TPU v7x, 32 devices: a whole 2x2x4 slice. The times are simulated.
32 devices in a mesh: shard: 2 (over y), context: 4 (over z), tensor: 4 (over x, core).
Axes of the slice: x: 2, y: 2, z: 4, core: 2. Of those that a mesh axis runs over, the one named last changes fastest.
Arguments:
- inputs: bfloat16 [6, 2048, 768], P('shard', 'context'), may hold values from -6 to 6
- w_query: bfloat16 [768, 768], P('shard', 'tensor'), may hold values from -0.21875 to 0.21875
- b_query: float32 [768], P('tensor'), may hold values from -3 to 3
- w_key: bfloat16 [768, 768], P('shard', 'tensor'), may hold values from -0.21875 to 0.21875
- w_value: bfloat16 [768, 768], P('shard', 'tensor'), may hold values from -0.21875 to 0.21875
- b_value: float32 [768], P('tensor'), may hold values from -3 to 3
- w_out: bfloat16 [768, 768], P('tensor', 'shard'), may hold values from -3.5 to 3.5
- b_out: float32 [768], replicated, may hold values from -3 to 3
- first_gain: float32 [768], replicated, may hold values from 0.5 to 1.5
- first_bias: float32 [768], replicated, may hold values from -2 to 2
- w_hidden: bfloat16 [768, 3072], P('shard', 'tensor'), may hold values from -0.21875 to 0.21875
- b_hidden: float32 [3072], P('tensor'), may hold values from -3 to 3
- w_down: bfloat16 [3072, 768], P('tensor', 'shard'), may hold values from -0.109375 to 0.109375
- b_down: float32 [768], replicated, may hold values from -3 to 3
- second_gain: float32 [768], replicated, may hold values from 0.5 to 1.5
- second_bias: float32 [768], replicated, may hold values from -2 to 2
- cotangent: bfloat16 [6, 2048, 768], P('shard', 'context'), may hold values from -6 to 6
Outputs:
- outputs: bfloat16 [6, 2048, 768], P('shard', 'context')
- input_grad: bfloat16 [6, 2048, 768], P('shard', 'context')
- grad_w_query: float32 [768, 768], P('shard', 'tensor')
- grad_b_query: float32 [768], P('tensor')
- grad_w_key: float32 [768, 768], P('shard', 'tensor')
- grad_w_value: float32 [768, 768], P('shard', 'tensor')
- grad_b_value: float32 [768], P('tensor')
- grad_w_out: float32 [768, 768], P('tensor', 'shard')
- grad_b_out: float32 [768], replicated
- grad_first_gain: float32 [768], replicated
- grad_first_bias: float32 [768], replicated
- grad_w_hidden: float32 [768, 3072], P('shard', 'tensor')
- grad_b_hidden: float32 [3072], P('tensor')
- grad_w_down: float32 [3072, 768], P('tensor', 'shard')
- grad_b_down: float32 [768], replicated
- grad_second_gain: float32 [768], replicated
- grad_second_bias: float32 [768], replicated
All inputs are finite; a program needn't handle non-finite values.
Results may differ from a plain program's by a relative error of at most 0.018.
Values may be sent and summed in bfloat16 or wider, within the bound.
No kernel may reach another device: no remote copies, remote signals or barrier semaphores. Data moves between devices by JAX's collectives and lax.ppermute only.
A program may use at most 256 MiB of HBM per device.

v0:
```python
import jax
import jax.numpy as jnp
from jax import lax
from jax.sharding import PartitionSpec as P

HEAD_DIM = 64
MICRO = 3


EPSILON = 1e-05


def layer_norm(values, gain, bias):
    centre = jnp.mean(values, axis=-1, keepdims=True)
    centred = values - centre
    inverse = lax.rsqrt(jnp.mean(centred * centred, axis=-1, keepdims=True) + EPSILON)
    normed = centred * inverse
    return (normed * gain + bias, normed, inverse)


def norm_back(grad, normed, inverse, gain):
    scaled = grad * gain
    return inverse * (
        scaled
        - jnp.mean(scaled, axis=-1, keepdims=True)
        - normed * jnp.mean(scaled * normed, axis=-1, keepdims=True)
    )


def gelu_exact(values):
    return jax.nn.gelu(values, approximate=False)


def attend(queries, keys, values, factor):
    heads_here = queries.shape[-1] // HEAD_DIM
    results = []
    totals = []
    for head in range(heads_here):
        lower = head * HEAD_DIM
        upper = lower + HEAD_DIM
        scores = (
            jnp.einsum(
                "sqd,skd->sqk",
                queries[..., lower:upper],
                keys[..., lower:upper],
                preferred_element_type=jnp.float32,
            )
            * factor
        )
        log_total = jax.nn.logsumexp(scores, axis=-1, keepdims=True)
        low_probs = jnp.exp(scores - log_total).astype(jnp.bfloat16)
        results.append(
            jnp.einsum(
                "sqk,skd->sqd",
                low_probs,
                values[..., lower:upper],
                preferred_element_type=jnp.float32,
            )
        )
        totals.append(log_total)
    return (jnp.concatenate(results, axis=-1).astype(jnp.bfloat16), totals)


def attend_back(queries, keys, values, grad_heads, totals, factor):
    heads_here = queries.shape[-1] // HEAD_DIM
    grad_queries = []
    grad_keys = []
    grad_values = []
    for head in range(heads_here):
        lower = head * HEAD_DIM
        upper = lower + HEAD_DIM
        query_head = queries[..., lower:upper]
        key_head = keys[..., lower:upper]
        grad_head = grad_heads[..., lower:upper]
        scores = (
            jnp.einsum("sqd,skd->sqk", query_head, key_head, preferred_element_type=jnp.float32)
            * factor
        )
        attn_probs = jnp.exp(scores - totals[head])
        low_probs = attn_probs.astype(jnp.bfloat16)
        grad_probs = jnp.einsum(
            "sqd,skd->sqk", grad_head, values[..., lower:upper], preferred_element_type=jnp.float32
        )
        grad_values.append(
            jnp.einsum("sqk,sqd->skd", low_probs, grad_head, preferred_element_type=jnp.float32)
        )
        weighted = jnp.sum(attn_probs * grad_probs, axis=-1, keepdims=True)
        grad_scores = (attn_probs * (grad_probs - weighted)).astype(jnp.bfloat16)
        grad_queries.append(
            jnp.einsum("sqk,skd->sqd", grad_scores, key_head, preferred_element_type=jnp.float32)
            * factor
        )
        grad_keys.append(
            jnp.einsum("sqk,sqd->skd", grad_scores, query_head, preferred_element_type=jnp.float32)
            * factor
        )
    return (
        jnp.concatenate(grad_queries, axis=-1),
        jnp.concatenate(grad_keys, axis=-1),
        jnp.concatenate(grad_values, axis=-1),
    )


def on_device(
    inputs,
    w_query,
    b_query,
    w_key,
    w_value,
    b_value,
    w_out,
    b_out,
    first_gain,
    first_bias,
    w_hidden,
    b_hidden,
    w_down,
    b_down,
    second_gain,
    second_bias,
    cotangent,
):
    seq_count, part_len, width = inputs.shape
    per_micro = seq_count // MICRO
    row_count = per_micro * part_len
    head_cols = w_query.shape[1]
    hidden_cols = w_hidden.shape[1]
    factor = HEAD_DIM ** (-0.5)
    acc_query = jnp.zeros((width, head_cols), jnp.float32)
    acc_key = jnp.zeros((width, head_cols), jnp.float32)
    acc_value = jnp.zeros((width, head_cols), jnp.float32)
    acc_out = jnp.zeros((head_cols, width), jnp.float32)
    acc_hidden = jnp.zeros((width, hidden_cols), jnp.float32)
    acc_down = jnp.zeros((hidden_cols, width), jnp.float32)
    sum_b_query = jnp.zeros((head_cols,), jnp.float32)
    sum_b_value = jnp.zeros((head_cols,), jnp.float32)
    sum_b_out = jnp.zeros((width,), jnp.float32)
    sum_first_gain = jnp.zeros((width,), jnp.float32)
    sum_first_bias = jnp.zeros((width,), jnp.float32)
    sum_b_hidden = jnp.zeros((hidden_cols,), jnp.float32)
    sum_b_down = jnp.zeros((width,), jnp.float32)
    sum_second_gain = jnp.zeros((width,), jnp.float32)
    sum_second_bias = jnp.zeros((width,), jnp.float32)
    result_parts = []
    input_parts = []
    for batch_index in range(MICRO):
        full = (
            lax.all_gather(w_query, "shard", axis=0, tiled=True),
            lax.all_gather(w_key, "shard", axis=0, tiled=True),
            lax.all_gather(w_value, "shard", axis=0, tiled=True),
            lax.all_gather(w_out, "shard", axis=1, tiled=True),
            lax.all_gather(w_hidden, "shard", axis=0, tiled=True),
            lax.all_gather(w_down, "shard", axis=1, tiled=True),
        )
        full_query, full_key, full_value, full_out, full_hidden, full_down = full
        begin = batch_index * per_micro
        token_rows = inputs[begin : begin + per_micro].reshape(row_count, width)
        query_low = (
            jnp.dot(token_rows, full_query, preferred_element_type=jnp.float32) + b_query
        ).astype(jnp.bfloat16)
        key_low = jnp.dot(token_rows, full_key, preferred_element_type=jnp.float32).astype(
            jnp.bfloat16
        )
        value_low = (
            jnp.dot(token_rows, full_value, preferred_element_type=jnp.float32) + b_value
        ).astype(jnp.bfloat16)
        queries = query_low.reshape(per_micro, part_len, head_cols)
        local_keys = key_low.reshape(per_micro, part_len, head_cols)
        local_values = value_low.reshape(per_micro, part_len, head_cols)
        all_keys, all_values = (
            lax.all_gather(local_keys, "context", axis=1, tiled=True),
            lax.all_gather(local_values, "context", axis=1, tiled=True),
        )
        attended, totals = attend(queries, all_keys, all_values, factor)
        attended_rows = attended.reshape(row_count, head_cols)
        branch = lax.psum(
            jnp.dot(attended_rows, full_out, preferred_element_type=jnp.float32), "tensor"
        )
        first, normed_first, inverse_first = layer_norm(
            token_rows.astype(jnp.float32) + branch + b_out, first_gain, first_bias
        )
        first_low = first.astype(jnp.bfloat16)
        inner = jnp.dot(first_low, full_hidden, preferred_element_type=jnp.float32) + b_hidden
        activated, gelu_back = jax.vjp(gelu_exact, inner)
        activated_low = activated.astype(jnp.bfloat16)
        ffn = lax.psum(
            jnp.dot(activated_low, full_down, preferred_element_type=jnp.float32), "tensor"
        )
        result, normed_second, inverse_second = layer_norm(
            first + ffn + b_down, second_gain, second_bias
        )
        result_parts.append(result.astype(jnp.bfloat16).reshape(per_micro, part_len, width))
        grad_result = (
            cotangent[begin : begin + per_micro].reshape(row_count, width).astype(jnp.float32)
        )
        sum_second_gain = sum_second_gain + jnp.sum(grad_result * normed_second, axis=0)
        sum_second_bias = sum_second_bias + jnp.sum(grad_result, axis=0)
        grad_second = norm_back(grad_result, normed_second, inverse_second, second_gain)
        sum_b_down = sum_b_down + jnp.sum(grad_second, axis=0)
        grad_ffn = grad_second.astype(jnp.bfloat16)
        acc_down = acc_down + jnp.einsum(
            "rf,rd->fd", activated_low, grad_ffn, preferred_element_type=jnp.float32
        )
        grad_act = jnp.einsum("rd,fd->rf", grad_ffn, full_down, preferred_element_type=jnp.float32)
        grad_inner = gelu_back(grad_act)[0].astype(jnp.bfloat16)
        sum_b_hidden = sum_b_hidden + jnp.sum(grad_inner.astype(jnp.float32), axis=0)
        acc_hidden = acc_hidden + jnp.einsum(
            "rd,rf->df", first_low, grad_inner, preferred_element_type=jnp.float32
        )
        grad_first = grad_second + lax.psum(
            jnp.einsum("rf,df->rd", grad_inner, full_hidden, preferred_element_type=jnp.float32),
            "tensor",
        )
        sum_first_gain = sum_first_gain + jnp.sum(grad_first * normed_first, axis=0)
        sum_first_bias = sum_first_bias + jnp.sum(grad_first, axis=0)
        grad_pre_first = norm_back(grad_first, normed_first, inverse_first, first_gain)
        sum_b_out = sum_b_out + jnp.sum(grad_pre_first, axis=0)
        grad_attn = grad_pre_first.astype(jnp.bfloat16)
        acc_out = acc_out + jnp.einsum(
            "rh,rd->hd", attended_rows, grad_attn, preferred_element_type=jnp.float32
        )
        grad_heads = jnp.einsum(
            "rd,hd->rh", grad_attn, full_out, preferred_element_type=jnp.float32
        ).astype(jnp.bfloat16)
        grad_heads = grad_heads.reshape(per_micro, part_len, head_cols)
        grad_queries, grad_keys, grad_values = attend_back(
            queries, all_keys, all_values, grad_heads, totals, factor
        )
        own_keys, own_values = (
            lax.psum_scatter(grad_keys, "context", scatter_dimension=1, tiled=True),
            lax.psum_scatter(grad_values, "context", scatter_dimension=1, tiled=True),
        )
        grad_query_low = grad_queries.astype(jnp.bfloat16).reshape(row_count, head_cols)
        grad_key_low = own_keys.astype(jnp.bfloat16).reshape(row_count, head_cols)
        grad_value_low = own_values.astype(jnp.bfloat16).reshape(row_count, head_cols)
        sum_b_query = sum_b_query + jnp.sum(grad_query_low.astype(jnp.float32), axis=0)
        sum_b_value = sum_b_value + jnp.sum(grad_value_low.astype(jnp.float32), axis=0)
        acc_query = acc_query + jnp.einsum(
            "rd,rh->dh", token_rows, grad_query_low, preferred_element_type=jnp.float32
        )
        acc_key = acc_key + jnp.einsum(
            "rd,rh->dh", token_rows, grad_key_low, preferred_element_type=jnp.float32
        )
        acc_value = acc_value + jnp.einsum(
            "rd,rh->dh", token_rows, grad_value_low, preferred_element_type=jnp.float32
        )
        back_rows = (
            jnp.einsum("rh,dh->rd", grad_query_low, full_query, preferred_element_type=jnp.float32)
            + jnp.einsum("rh,dh->rd", grad_key_low, full_key, preferred_element_type=jnp.float32)
            + jnp.einsum(
                "rh,dh->rd", grad_value_low, full_value, preferred_element_type=jnp.float32
            )
        )
        grad_input = grad_pre_first + lax.psum(back_rows, "tensor")
        input_parts.append(grad_input.astype(jnp.bfloat16).reshape(per_micro, part_len, width))
    matrices = (acc_query, acc_key, acc_value, acc_out, acc_hidden, acc_down)
    owned = (
        lax.psum_scatter(
            matrices[0].astype(jnp.bfloat16), "shard", scatter_dimension=0, tiled=True
        ).astype(jnp.float32),
        lax.psum_scatter(
            matrices[1].astype(jnp.bfloat16), "shard", scatter_dimension=0, tiled=True
        ).astype(jnp.float32),
        lax.psum_scatter(
            matrices[2].astype(jnp.bfloat16), "shard", scatter_dimension=0, tiled=True
        ).astype(jnp.float32),
        lax.psum_scatter(
            matrices[3].astype(jnp.bfloat16), "shard", scatter_dimension=1, tiled=True
        ).astype(jnp.float32),
        lax.psum_scatter(
            matrices[4].astype(jnp.bfloat16), "shard", scatter_dimension=0, tiled=True
        ).astype(jnp.float32),
        lax.psum_scatter(
            matrices[5].astype(jnp.bfloat16), "shard", scatter_dimension=1, tiled=True
        ).astype(jnp.float32),
    )
    owned = (
        lax.psum(owned[0].astype(jnp.bfloat16), "context").astype(jnp.float32),
        lax.psum(owned[1].astype(jnp.bfloat16), "context").astype(jnp.float32),
        lax.psum(owned[2].astype(jnp.bfloat16), "context").astype(jnp.float32),
        lax.psum(owned[3].astype(jnp.bfloat16), "context").astype(jnp.float32),
        lax.psum(owned[4].astype(jnp.bfloat16), "context").astype(jnp.float32),
        lax.psum(owned[5].astype(jnp.bfloat16), "context").astype(jnp.float32),
    )
    vectors = lax.psum(
        (
            sum_b_query,
            sum_b_value,
            sum_b_out,
            sum_first_gain,
            sum_first_bias,
            sum_b_hidden,
            sum_b_down,
            sum_second_gain,
            sum_second_bias,
        ),
        ("shard", "context"),
    )
    return (
        jnp.concatenate(result_parts, axis=0),
        jnp.concatenate(input_parts, axis=0),
        owned[0],
        vectors[0],
        owned[1],
        owned[2],
        vectors[1],
        owned[3],
        vectors[2],
        vectors[3],
        vectors[4],
        owned[4],
        vectors[5],
        owned[5],
        vectors[6],
        vectors[7],
        vectors[8],
    )


def solution(mesh):
    return jax.shard_map(
        on_device,
        mesh=mesh,
        in_specs=(
            P("shard", "context", None),
            P("shard", "tensor"),
            P("tensor"),
            P("shard", "tensor"),
            P("shard", "tensor"),
            P("tensor"),
            P("tensor", "shard"),
            P(),
            P(),
            P(),
            P("shard", "tensor"),
            P("tensor"),
            P("tensor", "shard"),
            P(),
            P(),
            P(),
            P("shard", "context", None),
        ),
        out_specs=(
            P("shard", "context", None),
            P("shard", "context", None),
            P("shard", "tensor"),
            P("tensor"),
            P("shard", "tensor"),
            P("shard", "tensor"),
            P("tensor"),
            P("tensor", "shard"),
            P(),
            P(),
            P(),
            P("shard", "tensor"),
            P("tensor"),
            P("tensor", "shard"),
            P(),
            P(),
            P(),
        ),
        check_vma=False,
    )
```

profile of v0, /device:TPU:0, one launch (start us, length us, event | category | flops | bytes accessed | tf_op | source)
XLA Modules:
  0.0 1056.1 jit_solution(5960588439616806110)
XLA Ops:
  8.1 7.7 all_gather.48
  19.7 5.8 all_gather.49
  26.8 5.8 all_gather.51
  33.9 18.1 %all-gather.4 = bf16[2048,192]{0,1:T(8,128)(2,1)S(1)} all-gather(bf16[512,192]{0,1:T(8,128)(2,1)S(1)} %convolution_convert_fusion.3), channel_id=6, replica_groups=mesh['shard'=2,'context'=4,'tensor'=4] {'context'}, dimensions={0}, use_global_device_ids=true | all-gather | bytes 983040 | tf_op jit(solution)/shard_map/all_gather | solution.py:171
  54.5 17.6 %all-gather.2 = bf16[2048,192]{0,1:T(8,128)(2,1)S(1)} all-gather(bf16[512,192]{0,1:T(8,128)(2,1)S(1)} %convolution_convert_fusion.4), channel_id=4, replica_groups=mesh['shard'=2,'context'=4,'tensor'=4] {'context'}, dimensions={0}, use_global_device_ids=true | all-gather | bytes 983040 | tf_op jit(solution)/shard_map/all_gather | solution.py:171
  74.5 15.7 %all-gather = bf16[2048,192]{0,1:T(8,128)(2,1)S(1)} all-gather(bf16[512,192]{0,1:T(8,128)(2,1)S(1)} %convolution_convert_fusion.5), channel_id=2, replica_groups=mesh['shard'=2,'context'=4,'tensor'=4] {'context'}, dimensions={0}, use_global_device_ids=true | all-gather | bytes 983040 | tf_op jit(solution)/shard_map/all_gather | solution.py:171
  93.0 5.8 all_gather.53
  98.8 17.9 %all-gather.1 = bf16[2048,192]{0,1:T(8,128)(2,1)S(1)} all-gather(bf16[512,192]{0,1:T(8,128)(2,1)S(1)} %fusion.71), channel_id=3, replica_groups=mesh['shard'=2,'context'=4,'tensor'=4] {'context'}, dimensions={0}, use_global_device_ids=true | all-gather | bytes 983040 | tf_op jit(solution)/shard_map/all_gather | solution.py:172
  116.7 19.4 %all-gather.3 = bf16[2048,192]{0,1:T(8,128)(2,1)S(1)} all-gather(bf16[512,192]{0,1:T(8,128)(2,1)S(1)} %fusion.73), channel_id=5, replica_groups=mesh['shard'=2,'context'=4,'tensor'=4] {'context'}, dimensions={0}, use_global_device_ids=true | all-gather | bytes 983040 | tf_op jit(solution)/shard_map/all_gather | solution.py:172
  136.1 15.8 %all-gather.5 = bf16[2048,192]{0,1:T(8,128)(2,1)S(1)} all-gather(bf16[512,192]{0,1:T(8,128)(2,1)S(1)} %fusion.75), channel_id=7, replica_groups=mesh['shard'=2,'context'=4,'tensor'=4] {'context'}, dimensions={0}, use_global_device_ids=true | all-gather | bytes 983040 | tf_op jit(solution)/shard_map/all_gather | solution.py:172
  174.4 93.1 %all-reduce.18.cloned.1.call-done = (f32[512,768]{1,0:T(8,128)}, f32[512,768]{1,0:T(8,128)}, f32[512,768]{1,0:T(8,128)}) async-done(((f32[512,768]{1,0:T(8,128)}, f32[512,768]{1,0:T(8,128)}, f32[512,768]{1,0:T(8,128)}), (f32[512,768]{1,0:T(8,128)}, f32[512,768]{1,0:T(8,128)}, f32[512,768]{1,0:T(8,128)})) %all-reduce.18.cloned.1.call-update) | async-done | bytes 4718608 | tf_op jit(solution)/shard_map/psum | solution.py:176
  267.5 3.8 fusion.259
  272.5 6.9 multiply_convert_fusion.10
  279.4 5.6 multiply_convert_fusion.9
  285.0 3.6 fusion.265
  290.6 5.5 multiply_convert_fusion.11
  299.2 94.5 %all-reduce.16.cloned.1.call-done = (f32[512,768]{1,0:T(8,128)}, f32[512,768]{1,0:T(8,128)}, f32[512,768]{1,0:T(8,128)}) async-done(((f32[512,768]{1,0:T(8,128)}, f32[512,768]{1,0:T(8,128)}, f32[512,768]{1,0:T(8,128)}), (f32[512,768]{1,0:T(8,128)}, f32[512,768]{1,0:T(8,128)}, f32[512,768]{1,0:T(8,128)})) %all-reduce.16.cloned.1.call-update) | async-done | bytes 4718608 | tf_op jit(solution)/shard_map/psum | solution.py:186
  393.7 3.6 fusion.255
  399.3 2.9 fusion.44
  402.3 2.2 fusion.246
  404.5 3.0 fusion.248
  409.9 2.0 fusion.269
  414.1 2.0 fusion.267
  421.8 94.4 %all-reduce.14.cloned.1.call-done = (f32[512,768]{1,0:T(8,128)}, f32[512,768]{1,0:T(8,128)}, f32[512,768]{1,0:T(8,128)}) async-done(((f32[512,768]{1,0:T(8,128)}, f32[512,768]{1,0:T(8,128)}, f32[512,768]{1,0:T(8,128)}), (f32[512,768]{1,0:T(8,128)}, f32[512,768]{1,0:T(8,128)}, f32[512,768]{1,0:T(8,128)})) %all-reduce.14.cloned.1.call-update) | async-done | bytes 4718608 | tf_op jit(solution)/shard_map/psum | solution.py:210
  516.2 3.9 multiply_reduce_fusion.20
  520.4 5.2 fusion.253
  533.0 4.1 fusion.252
  547.7 3.3 convolution_bitcast_fusion
  555.8 5.3 multiply_reduce_fusion.6
  561.0 4.0 multiply_reduce_fusion.7
  565.2 4.6 multiply_convert_fusion.6
  569.9 2.0 copy-done.55
  576.1 2.1 multiply_reduce_fusion.8
  582.3 5.3 multiply_reduce_fusion.3
  587.7 4.0 multiply_reduce_fusion.4
  591.9 4.6 multiply_convert_fusion.3
  596.6 2.0 copy-done.56
  602.6 2.1 multiply_reduce_fusion.5
  608.9 3.6 multiply_reduce_fusion
  612.6 2.3 multiply_convert_fusion
  615.9 2.1 fusion.17
  618.1 3.5 multiply_reduce_fusion.1
  630.0 2.6 fusion.139
  636.1 2.4 copy.42
  638.6 3.6 fusion.240
  647.2 2.7 fusion.87
  651.8 2.5 fusion.85
  674.0 4.0 reduce-scatter.23.cloned.1.call-done
  679.6 34.8 %reduce-scatter.27.cloned.1.call-done = f32[1,512,192]{1,2,0:T(8,128)} async-done(((f32[1,2048,192]{1,2,0:T(8,128)}), f32[1,512,192]{1,2,0:T(8,128)}) %reduce-scatter.27.cloned.1.call-update) | async-done | bytes 393232 | tf_op jit(solution)/shard_map/reduce_scatter | solution.py:230
  714.4 2.4 convolution_add_fusion.8
  716.8 34.0 %reduce-scatter.31.cloned.1.call-done = f32[1,512,192]{1,2,0:T(8,128)} async-done(((f32[1,2048,192]{1,2,0:T(8,128)}), f32[1,512,192]{1,2,0:T(8,128)}) %reduce-scatter.31.cloned.1.call-update) | async-done | bytes 393232 | tf_op jit(solution)/shard_map/reduce_scatter | solution.py:230
  753.6 2.3 fusion.243
  755.9 2.1 add_convert_fusion.1
  758.4 2.0 convert_reduce_fusion.1
  760.4 13.6 %reduce-scatter.45.cloned.1.call-done = bf16[384,768]{1,0:T(8,128)(2,1)} async-done(((bf16[768,768]{1,0:T(8,128)(2,1)}), bf16[384,768]{1,0:T(8,128)(2,1)}) %reduce-scatter.45.cloned.1.call-update) | async-done | bytes 589840
  774.0 2.2 copy.43
  778.6 10.8 %reduce-scatter.43.cloned.1.call-done = bf16[384,192]{1,0:T(8,128)(2,1)} async-done(((bf16[768,192]{1,0:T(8,128)(2,1)}), bf16[384,192]{1,0:T(8,128)(2,1)}) %reduce-scatter.43.cloned.1.call-update) | async-done | bytes 147472
  791.2 14.0 %reduce-scatter.37.cloned.1.call-done = bf16[384,192]{1,0:T(8,128)(2,1)} async-done(((bf16[768,192]{1,0:T(8,128)(2,1)}), bf16[384,192]{1,0:T(8,128)(2,1)}) %reduce-scatter.37.cloned.1.call-update) | async-done | bytes 147472
  806.9 13.7 %reduce-scatter.41.cloned.1.call-done = bf16[384,192]{1,0:T(8,128)(2,1)} async-done(((bf16[768,192]{1,0:T(8,128)(2,1)}), bf16[384,192]{1,0:T(8,128)(2,1)}) %reduce-scatter.41.cloned.1.call-update) | async-done | bytes 147472
  822.3 13.4 %reduce-scatter.39.cloned.1.call-done = bf16[384,192]{1,0:T(8,128)(2,1)} async-done(((bf16[768,192]{1,0:T(8,128)(2,1)}), bf16[384,192]{1,0:T(8,128)(2,1)}) %reduce-scatter.39.cloned.1.call-update) | async-done | bytes 147472
  837.4 22.9 %reduce-scatter.35.cloned.1.call-done = bf16[384,768]{1,0:T(8,128)(2,1)} async-done(((bf16[768,768]{1,0:T(8,128)(2,1)}), bf16[384,768]{1,0:T(8,128)(2,1)}) %reduce-scatter.35.cloned.1.call-update) | async-done | bytes 589840 | tf_op jit(solution)/shard_map/reduce_scatter | solution.py:270
  874.0 38.7 %all-reduce = (f32[192]{0:T(256)}, f32[192]{0:T(256)}, f32[768]{0:T(1024)}, f32[768]{0:T(1024)}, f32[768]{0:T(1024)}, /*index=5*/f32[768]{0:T(1024)}, f32[768]{0:T(1024)}, f32[768]{0:T(1024)}, f32[768]{0:T(1024)}) all-reduce(f32[192]{0:T(256)S(1)} %add_add_fusion.17, ...), channel_id=1, replica_groups=mesh['shard'=2,'context'=4,'tensor'=4] {'shard','context'}, use_global_device_ids=true, to_apply=%region_74.0 | all-reduce | flops 5760 | bytes 46080 | tf_op jit(solution)/shard_map/psum | solution.py:285
  912.7 30.0 %all-reduce.20.cloned.1.call-done = (bf16[384,192]{0,1:T(8,128)(2,1)}, bf16[384,192]{0,1:T(8,128)(2,1)}, bf16[384,192]{0,1:T(8,128)(2,1)}, bf16[192,384]{1,0:T(8...) async-done(((bf16[384,192]{0,1:T(8,128)(2,1)}, bf16[384,192]{0,1:T(8,128)(2,1)}, bf16[384,192]{0,1:T(8,128)(2,1)}, bf16[192,384]{1,0:T(8,128)(2,1)}, ...) | async-done | bytes 1769488 | tf_op jit(solution)/shard_map/psum | solution.py:278
  949.3 89.8 %all-reduce.12.cloned.1.call-done = (f32[512,768]{1,0:T(8,128)}, f32[512,768]{1,0:T(8,128)}, f32[512,768]{1,0:T(8,128)}) async-done(((f32[512,768]{1,0:T(8,128)}, f32[512,768]{1,0:T(8,128)}, f32[512,768]{1,0:T(8,128)}), (f32[512,768]{1,0:T(8,128)}, f32[512,768]{1,0:T(8,128)}, f32[512,768]{1,0:T(8,128)})) %all-reduce.12.cloned.1.call-update) | async-done | bytes 4718608 | tf_op jit(solution)/shard_map/psum | solution.py:254
  (652 shorter events, 176.1 us)
Async XLA Ops:
  8.0 9.5 copy-start.202
  8.0 259.5 %all-reduce.18.cloned.1.call-start = ((), (), s32[]{:S(2)}) async-start(), calls=%async_computation.29 | async-start | bytes 9437184 | tf_op jit(solution)/shard_map/psum | solution.py:176
  17.6 36.1 %copy-start.112 = (bf16[1,512,192]{1,2,0:T(8,128)(2,1)}, bf16[1,512,192]{1,2,0:T(8,128)(2,1)S(1)}, u32[]{:S(2)}) copy-start(bf16[1,512,192]{1,2,0:T(8,128)(2,1)S(1)} %fusion.82) | copy-start | bytes 589828
  19.2 54.5 %copy-start.114 = (bf16[1,512,192]{1,2,0:T(8,128)(2,1)}, bf16[1,512,192]{1,2,0:T(8,128)(2,1)S(1)}, u32[]{:S(2)}) copy-start(bf16[1,512,192]{1,2,0:T(8,128)(2,1)S(1)} %fusion.83) | copy-start | bytes 589828
  19.7 72.2 %copy-start.116 = (bf16[1,512,192]{1,2,0:T(8,128)(2,1)}, bf16[1,512,192]{1,2,0:T(8,128)(2,1)S(1)}, u32[]{:S(2)}) copy-start(bf16[1,512,192]{1,2,0:T(8,128)(2,1)S(1)} %fusion.84) | copy-start | bytes 589828
  52.8 100.8 %copy-start.6 = (f32[512,2048]{1,0:T(8,128)}, f32[512,2048]{1,0:T(8,128)S(1)}, u32[]{:S(2)}) copy-start(f32[512,2048]{1,0:T(8,128)S(1)} %get-tuple-element.131) | copy-start | bytes 12582916
  53.7 100.9 %copy-start.3 = (f32[512,2048]{1,0:T(8,128)}, f32[512,2048]{1,0:T(8,128)S(1)}, u32[]{:S(2)}) copy-start(f32[512,2048]{1,0:T(8,128)S(1)} %get-tuple-element.133) | copy-start | bytes 12582916
  54.5 101.9 %copy-start = (f32[512,2048]{1,0:T(8,128)}, f32[512,2048]{1,0:T(8,128)S(1)}, u32[]{:S(2)}) copy-start(f32[512,2048]{1,0:T(8,128)S(1)} %get-tuple-element.135) | copy-start | bytes 12582916
  72.9 86.1 %copy-start.15 = (f32[512,2048]{1,0:T(8,128)}, f32[512,2048]{1,0:T(8,128)S(1)}, u32[]{:S(2)}) copy-start(f32[512,2048]{1,0:T(8,128)S(1)} %get-tuple-element.137) | copy-start | bytes 12582916
  73.7 86.2 %copy-start.11 = (f32[512,2048]{1,0:T(8,128)}, f32[512,2048]{1,0:T(8,128)S(1)}, u32[]{:S(2)}) copy-start(f32[512,2048]{1,0:T(8,128)S(1)} %get-tuple-element.139) | copy-start | bytes 12582916
  74.5 87.2 %copy-start.8 = (f32[512,2048]{1,0:T(8,128)}, f32[512,2048]{1,0:T(8,128)S(1)}, u32[]{:S(2)}) copy-start(f32[512,2048]{1,0:T(8,128)S(1)} %get-tuple-element.141) | copy-start | bytes 12582916
  91.0 73.3 %copy-start.24 = (f32[512,2048]{1,0:T(8,128)}, f32[512,2048]{1,0:T(8,128)S(1)}, u32[]{:S(2)}) copy-start(f32[512,2048]{1,0:T(8,128)S(1)} %get-tuple-element.143) | copy-start | bytes 12582916
  91.9 73.4 %copy-start.20 = (f32[512,2048]{1,0:T(8,128)}, f32[512,2048]{1,0:T(8,128)S(1)}, u32[]{:S(2)}) copy-start(f32[512,2048]{1,0:T(8,128)S(1)} %get-tuple-element.145) | copy-start | bytes 12582916
  93.0 74.5 %copy-start.17 = (f32[512,2048]{1,0:T(8,128)}, f32[512,2048]{1,0:T(8,128)S(1)}, u32[]{:S(2)}) copy-start(f32[512,2048]{1,0:T(8,128)S(1)} %get-tuple-element.147) | copy-start | bytes 12582916
  116.7 50.8 %copy-start.72 = (bf16[2048,192]{0,1:T(8,128)(2,1)}, bf16[2048,192]{0,1:T(8,128)(2,1)S(1)}, u32[]{:S(2)}) copy-start(bf16[2048,192]{0,1:T(8,128)(2,1)S(1)} %all-gather.1) | copy-start | bytes 2359300
  136.1 25.6 %copy-start.71 = (bf16[2048,192]{0,1:T(8,128)(2,1)}, bf16[2048,192]{0,1:T(8,128)(2,1)S(1)}, u32[]{:S(2)}) copy-start(bf16[2048,192]{0,1:T(8,128)(2,1)S(1)} %all-gather.3) | copy-start | bytes 2359300
  153.6 397.4 %copy-start.165 = (f32[512]{0:T(512)}, f32[512]{0:T(512)S(1)}, u32[]{:S(2)}) copy-start(f32[512]{0:T(512)S(1)} %log_add_fusion.1) | copy-start | bytes 6148
  154.5 13.8 %copy-start.134 = (bf16[512,64]{0,1:T(8,128)(2,1)}, bf16[512,64]{0,1:T(8,128)(2,1)S(1)}, u32[]{:S(2)}) copy-start(bf16[512,64]{0,1:T(8,128)(2,1)S(1)} %convolution_convert_fusion.6) | copy-start | bytes 196612
  155.5 12.9 %copy-start.136 = (bf16[512,64]{0,1:T(8,128)(2,1)}, bf16[512,64]{0,1:T(8,128)(2,1)S(1)}, u32[]{:S(2)}) copy-start(bf16[512,64]{0,1:T(8,128)(2,1)S(1)} %convolution_convert_fusion.7) | copy-start | bytes 196612
  156.3 395.8 %copy-start.163 = (f32[512]{0:T(512)}, f32[512]{0:T(512)S(1)}, u32[]{:S(2)}) copy-start(f32[512]{0:T(512)S(1)} %log_add_fusion.2) | copy-start | bytes 6148
  157.3 11.1 %copy-start.138 = (bf16[512,64]{0,1:T(8,128)(2,1)}, bf16[512,64]{0,1:T(8,128)(2,1)S(1)}, u32[]{:S(2)}) copy-start(bf16[512,64]{0,1:T(8,128)(2,1)S(1)} %convolution_convert_fusion.8) | copy-start | bytes 196612
  159.9 10.1 copy-start.120
  160.8 9.1 copy-start.122
  162.6 7.4 copy-start.124
  173.2 94.4 %copy-start.191 = (f32[768]{0:T(1024)S(1)}, f32[768]{0:T(1024)}, u32[]{:S(2)}) copy-start(f32[768]{0:T(1024)} %param.24) | copy-start | bytes 9220
  173.2 99.3 %all-gather.9.cloned.1.call-start = ((), (), s32[]{:S(2)}) async-start(), calls=%async_computation.12 | async-start | bytes 1769472 | tf_op jit(solution)/shard_map/all_gather | solution.py:152
  173.8 111.3 %all-gather.11.cloned.1.call-start = ((), (), s32[]{:S(2)}) async-start(), calls=%async_computation.13 | async-start | bytes 1769472 | tf_op jit(solution)/shard_map/all_gather | solution.py:153
  174.4 219.3 %all-reduce.16.cloned.1.call-start = ((), (), s32[]{:S(2)}) async-start(), calls=%async_computation.28 | async-start | bytes 9437184 | tf_op jit(solution)/shard_map/psum | solution.py:186
  271.3 261.6 %copy-start.161 = (f32[512]{0:T(512)}, f32[512]{0:T(512)S(1)}, u32[]{:S(2)}) copy-start(f32[512]{0:T(512)S(1)} %broadcast_multiply_fusion.15) | copy-start | bytes 6148
  271.7 248.5 %copy-start.168 = (f32[512]{0:T(512)}, f32[512]{0:T(512)S(1)}, u32[]{:S(2)}) copy-start(f32[512]{0:T(512)S(1)} %add_rsqrt_fusion.5) | copy-start | bytes 6148
  272.5 260.5 %copy-start.170 = (f32[512]{0:T(512)}, f32[512]{0:T(512)S(1)}, u32[]{:S(2)}) copy-start(f32[512]{0:T(512)S(1)} %add_rsqrt_fusion.3) | copy-start | bytes 6148
  272.5 6.9 copy-start.196
  299.0 94.7 %copy-start.192 = (f32[768]{0:T(1024)S(1)}, f32[768]{0:T(1024)}, u32[]{:S(2)}) copy-start(f32[768]{0:T(1024)} %param.30) | copy-start | bytes 9220
  299.0 217.2 %all-reduce.14.cloned.1.call-start = ((), (), s32[]{:S(2)}) async-start(), calls=%async_computation.27 | async-start | bytes 9437184 | tf_op jit(solution)/shard_map/psum | solution.py:210
  404.5 11.7 %copy-start.57 = (f32[512,768]{1,0:T(8,128)}, f32[512,768]{1,0:T(8,128)S(1)}, u32[]{:S(2)}) copy-start(f32[512,768]{1,0:T(8,128)S(1)} %get-tuple-element.73) | copy-start | bytes 4718596
  421.5 246.6 %reduce-scatter.25.cloned.1.call-start = ((), (), s32[]{:S(2)}) async-start(), calls=%async_computation.15 | async-start | bytes 1966080 | tf_op jit(solution)/shard_map/reduce_scatter | solution.py:231
  532.8 136.9 %reduce-scatter.29.cloned.1.call-start = ((), (), s32[]{:S(2)}) async-start(), calls=%async_computation.17 | async-start | bytes 1966080 | tf_op jit(solution)/shard_map/reduce_scatter | solution.py:231
  545.4 126.0 %reduce-scatter.33.cloned.1.call-start = ((), (), s32[]{:S(2)}) async-start(), calls=%async_computation.19 | async-start | bytes 1966080 | tf_op jit(solution)/shard_map/reduce_scatter | solution.py:231
  565.1 112.9 %reduce-scatter.23.cloned.1.call-start = ((), (), s32[]{:S(2)}) async-start(), calls=%async_computation.14 | async-start | bytes 1966080 | tf_op jit(solution)/shard_map/reduce_scatter | solution.py:230
  565.2 6.7 copy-start.55
  591.7 122.7 %reduce-scatter.27.cloned.1.call-start = ((), (), s32[]{:S(2)}) async-start(), calls=%async_computation.16 | async-start | bytes 1966080 | tf_op jit(solution)/shard_map/reduce_scatter | solution.py:230
  615.0 135.8 %reduce-scatter.31.cloned.1.call-start = ((), (), s32[]{:S(2)}) async-start(), calls=%async_computation.18 | async-start | bytes 1966080 | tf_op jit(solution)/shard_map/reduce_scatter | solution.py:230
  629.9 144.1 %reduce-scatter.45.cloned.1.call-start = ((), (), s32[]{:S(2)}) async-start(), calls=%async_computation.25 | async-start | bytes 1769472
  642.2 147.2 %reduce-scatter.43.cloned.1.call-start = ((), (), s32[]{:S(2)}) async-start(), calls=%async_computation.24 | async-start | bytes 589824
  645.9 11.4 %copy-start.67 = (bf16[2048,192]{0,1:T(8,128)(2,1)S(1)}, bf16[2048,192]{0,1:T(8,128)(2,1)}, u32[]{:S(2)}) copy-start(bf16[2048,192]{0,1:T(8,128)(2,1)} %copy-done.66) | copy-start | bytes 2359300
  646.2 8.0 copy-start.65
  649.9 11.7 %copy-start.140 = (bf16[512,64]{0,1:T(8,128)(2,1)}, bf16[512,64]{0,1:T(8,128)(2,1)S(1)}, u32[]{:S(2)}) copy-start(bf16[512,64]{0,1:T(8,128)(2,1)S(1)} %fusion.87) | copy-start | bytes 196612
  651.8 9.8 copy-start.143
  659.1 119.1 %copy-start.100 = (bf16[512,64]{0,1:T(8,128)(2,1)}, bf16[512,64]{0,1:T(8,128)(2,1)S(1)}, u32[]{:S(2)}) copy-start(bf16[512,64]{0,1:T(8,128)(2,1)S(1)} %fusion.90) | copy-start | bytes 196612
  661.5 143.7 %reduce-scatter.37.cloned.1.call-start = ((), (), s32[]{:S(2)}) async-start(), calls=%async_computation.21 | async-start | bytes 589824
  668.0 152.5 %reduce-scatter.41.cloned.1.call-start = ((), (), s32[]{:S(2)}) async-start(), calls=%async_computation.23 | async-start | bytes 589824
  673.9 161.8 %reduce-scatter.39.cloned.1.call-start = ((), (), s32[]{:S(2)}) async-start(), calls=%async_computation.22 | async-start | bytes 589824
  716.8 36.7 %copy-start.29 = (f32[512,768]{1,0:T(8,128)S(1)}, f32[512,768]{1,0:T(8,128)}, u32[]{:S(2)}) copy-start(f32[512,768]{1,0:T(8,128)} %copy-done.26) | copy-start | bytes 4718596
  716.8 36.8 %copy-start.169 = (f32[512]{0:T(512)S(1)}, f32[512]{0:T(512)}, u32[]{:S(2)}) copy-start(f32[512]{0:T(512)} %copy-done.168) | copy-start | bytes 6148
  716.8 36.8 %copy-start.176 = (f32[768]{0:T(1024)S(1)}, f32[768]{0:T(1024)}, u32[]{:S(2)}) copy-start(f32[768]{0:T(1024)} %param.26) | copy-start | bytes 9220
  753.5 106.8 %reduce-scatter.35.cloned.1.call-start = ((), (), s32[]{:S(2)}) async-start(), calls=%async_computation.20 | async-start | bytes 1769472 | tf_op jit(solution)/shard_map/reduce_scatter | solution.py:270
  758.0 18.2 %copy-start.77 = (bf16[768,192]{0,1:T(8,128)(2,1)S(1)}, bf16[768,192]{0,1:T(8,128)(2,1)}, u32[]{:S(2)}) copy-start(bf16[768,192]{0,1:T(8,128)(2,1)} %copy-done.76) | copy-start | bytes 884740
  758.0 18.2 %copy-start.141 = (bf16[512,64]{0,1:T(8,128)(2,1)S(1)}, bf16[512,64]{0,1:T(8,128)(2,1)}, u32[]{:S(2)}) copy-start(bf16[512,64]{0,1:T(8,128)(2,1)} %copy-done.140) | copy-start | bytes 196612
  758.0 18.2 %copy-start.144 = (bf16[512,64]{0,1:T(8,128)(2,1)S(1)}, bf16[512,64]{0,1:T(8,128)(2,1)}, u32[]{:S(2)}) copy-start(bf16[512,64]{0,1:T(8,128)(2,1)} %copy-done.143) | copy-start | bytes 196612
  758.0 18.2 %copy-start.146 = (bf16[512,64]{0,1:T(8,128)(2,1)S(1)}, bf16[512,64]{0,1:T(8,128)(2,1)}, u32[]{:S(2)}) copy-start(bf16[512,64]{0,1:T(8,128)(2,1)} %fusion.85) | copy-start | bytes 196612
  758.1 184.6 %all-reduce.20.cloned.1.call-start = ((), (), s32[]{:S(2)}) async-start(), calls=%async_computation.30 | async-start | bytes 3538944 | tf_op jit(solution)/shard_map/psum | solution.py:278
  789.4 71.0 %copy-start.75 = (bf16[768,192]{0,1:T(8,128)(2,1)S(1)}, bf16[768,192]{0,1:T(8,128)(2,1)}, u32[]{:S(2)}) copy-start(bf16[768,192]{0,1:T(8,128)(2,1)} %copy-done.74) | copy-start | bytes 884740
  860.3 178.7 %all-reduce.12.cloned.1.call-start = ((), (), s32[]{:S(2)}) async-start(), calls=%async_computation.26 | async-start | bytes 9437184 | tf_op jit(solution)/shard_map/psum | solution.py:254
  873.5 165.6 %copy-start.32 = (f32[512,768]{1,0:T(8,128)S(1)}, f32[512,768]{1,0:T(8,128)}, u32[]{:S(2)}) copy-start(f32[512,768]{1,0:T(8,128)} %copy-done.31) | copy-start | bytes 4718596
  (167 other events, 402.9 us)
Sparse Core Ops, SparseCore 0:
  173.3 94.1 all-reduce.17
  299.1 94.5 all-reduce.15
  421.6 94.5 all-reduce.13
Sparse Core Ops, SparseCore 1:
  175.2 22.4 all-gather.8
  199.1 22.6 all-gather.10
  532.9 35.4 reduce-scatter.24
  570.7 34.1 reduce-scatter.28
  607.2 34.1 reduce-scatter.32
  643.8 34.2 reduce-scatter.22
  680.2 34.1 reduce-scatter.26
  716.5 34.1 reduce-scatter.30
  753.4 20.5 reduce-scatter.44
  776.4 13.0 reduce-scatter.42
  792.1 13.0 reduce-scatter.36
  807.5 13.0 reduce-scatter.40
  822.7 13.0 reduce-scatter.38
  838.6 21.6 reduce-scatter.34
  864.3 78.3 all-reduce.19
  946.0 93.0 all-reduce.11
where the time goes:
time: 1060 us
  waiting for transfers between devices  564 us (53%)
  blocking collectives  168 us (16%)
  matrix products  167 us (16%)
  other arithmetic  80.6 us (8%)
  local copies, waits for them, and re-layouts  54.3 us (5%)
  between operations  18.8 us (2%)
    psum x1, waiting for transfers between devices, on_device(): lax.psum(jnp.dot(activated_low, full_down, preferred_element_type=jnp.flo...  94.5 us
    psum x1, waiting for transfers between devices, on_device(): lax.psum(jnp.einsum('rf,df->rd', grad_inner, full_hidden, preferred_eleme...  94.4 us
    psum x1, waiting for transfers between devices, on_device(): lax.psum(jnp.dot(attended_rows, full_out, preferred_element_type=jnp.floa...  93.1 us
    psum x1, waiting for transfers between devices, on_device(): grad_input = grad_pre_first + lax.psum(back_rows, 'tensor')  89.8 us
    reduce_scatter x3, waiting for transfers between devices, on_device(): lax.psum_scatter(grad_keys, 'context', scatter_dimension=1, tiled=True)  72.8 us
    unnamed x24, waiting for transfers between devices  66.9 us
    unnamed x434, local copies, waits for them, and re-layouts  54.3 us
    all_gather x3, blocking collectives, on_device(): lax.all_gather(local_values, 'context', axis=1, tiled=True)  53.1 us
  transfers between devices with their start and end apart: 19, of which 14 were waited for; matrix products, arithmetic and copies ran while one was open for 16% of the time, Pallas kernels for 0%

commit v1 on v0

v1 whole, which is shorter than its diff:
```python
import functools
import jax
import jax.numpy as jnp
from jax import lax
from jax.experimental import pallas as pl
from jax.experimental.pallas import tpu as pltpu
from jax.sharding import PartitionSpec as P

HEAD_DIM = 64
EPSILON = 1e-05
F32 = jnp.float32
BF16 = jnp.bfloat16
VMEM_LIMIT = 56 << 20


def nn(a, b):
    return jnp.dot(a, b, preferred_element_type=F32)


def nt(a, b):
    return lax.dot_general(a, b, (((1,), (1,)), ((), ())), preferred_element_type=F32)


def head_lanes(shape, head):
    lane = lax.broadcasted_iota(jnp.int32, shape, len(shape) - 1)
    return (lane >= head * HEAD_DIM) & (lane < (head + 1) * HEAD_DIM)


def divisor(size, most):
    while size % most:
        most //= 2
    return most


def forward_body(heads, own, near, cross, sib, w_four, b_query, b_value, query, key, value, attended, log_total, keep, send):
    part, width = own.shape
    cols = heads * HEAD_DIM
    factor = HEAD_DIM**-0.5
    w_query, w_key, w_value, w_out = (w_four.at[i] for i in range(4))
    query[...] = ((nn(own[...], w_query[...]) + b_query[...]).astype(BF16).astype(F32) * factor).astype(BF16)
    row = 0
    for piece in (own, near, cross, sib):
        size = piece.shape[0]
        step = divisor(size, 256)

        def project(i, carry, piece=piece, row=row, step=step):
            rows = piece[pl.ds(i * step, step), :]
            out = pl.ds(row + i * step, step)
            key[out, :] = nn(rows, w_key[...]).astype(BF16)
            value[out, :] = (nn(rows, w_value[...]) + b_value[...]).astype(BF16)
            return carry

        lax.fori_loop(0, size // step, project, 0)
        row += size
    block = divisor(part, 128)
    lanes = lax.broadcasted_iota(jnp.int32, (block, 128), 1)

    def attend(i, carry):
        rows = pl.ds(pl.multiple_of(i * block, block), block)
        mine = query[rows, :].astype(F32)
        result = jnp.zeros((block, cols), F32)
        stats = jnp.zeros((block, 128), F32)
        for head in range(heads):
            mask = head_lanes((block, cols), head)
            masked = jnp.where(mask, mine, 0.0).astype(BF16)
            scores = nt(masked, key[...])
            top = jnp.max(scores, axis=-1, keepdims=True)
            powers = jnp.exp(scores - top)
            total = jnp.sum(powers, axis=-1, keepdims=True)
            mixed = nn(powers.astype(BF16), value[...])
            result = jnp.where(mask, mixed / total, result)
            stats = jnp.where(lanes == head, top + jnp.log(total), stats)
        attended[rows, :] = result.astype(BF16)
        turned = stats.T
        log_total[:, rows] = turned[:8, :]
        return carry

    lax.fori_loop(0, part // block, attend, 0)
    half = part // 2
    keep[...] = nt(attended[:half, :], w_out[...]).astype(BF16)
    send[...] = nt(attended[half:, :], w_out[...]).astype(BF16)


def backward_body(heads, nears, g_own, g_cross, g_sib, w_four, query, key, value, attended, log_total,
                  d_query, d_key, d_value, keep, send, d_out, sums, q_heads, g_heads, dq_turned):
    part, cols = query.shape
    width = w_four.shape[1]
    total = key.shape[0]
    quarter = part // 4
    factor = HEAD_DIM**-0.5
    w_query, w_key, w_value, w_out = (w_four.at[i] for i in range(4))
    grad = jnp.concatenate([g_own[...], g_cross[...], g_sib[...]], axis=0)
    grad_heads = nn(grad, w_out[...]).astype(BF16)
    att = attended[...]
    d_out[...] = nn(att.T, grad)
    product = grad_heads.astype(F32) * att.astype(F32)
    picks = jnp.concatenate(
        [jnp.where(head_lanes((1, cols), h), 1.0, 0.0) for h in range(heads)]
        + [jnp.zeros((8 - heads, cols), F32)], axis=0)
    weighted = lax.dot_general(picks, product, (((1,), (1,)), ((), ())), precision=lax.Precision.HIGHEST,
                               preferred_element_type=F32)
    for h in range(heads):
        mask = head_lanes((part, cols), h)
        q_heads[h] = jnp.where(mask, query[...].astype(F32), 0.0).astype(BF16)
        g_heads[h] = jnp.where(mask, grad_heads.astype(F32), 0.0).astype(BF16)
    dq_turned[...] = jnp.zeros_like(dq_turned)
    block = divisor(total, 256)

    def chunk(i, carry):
        rows = pl.ds(pl.multiple_of(i * block, block), block)
        keys = key[rows, :]
        values = value[rows, :]
        keys_turned = keys.T
        dk = jnp.zeros((block, cols), F32)
        dv = jnp.zeros((block, cols), F32)
        for h in range(heads):
            scores = nt(keys, q_heads[h])
            probs = jnp.exp(scores - log_total[h : h + 1, :])
            d_probs = nt(values, g_heads[h])
            d_scores = (probs * (d_probs - weighted[h : h + 1, :])).astype(BF16)
            dv = dv + nn(probs.astype(BF16), g_heads[h])
            dk = dk + nn(d_scores, q_heads[h])
            own = slice(h * HEAD_DIM, (h + 1) * HEAD_DIM)
            dq_turned[own, :] += nn(keys_turned[own, :], d_scores)
        d_key[rows, :] = dk.astype(BF16)
        d_value[rows, :] = dv.astype(BF16)
        return carry + jnp.sum(dv.astype(BF16).astype(F32), axis=0, keepdims=True)

    sum_value = lax.fori_loop(0, total // block, chunk, jnp.zeros((1, cols), F32))
    dq = (dq_turned[...] * factor).T.astype(BF16)
    d_query[...] = dq
    sums[...] = jnp.concatenate(
        [jnp.sum(dq.astype(F32), axis=0, keepdims=True), sum_value, jnp.zeros((6, cols), F32)], axis=0)

    def back(begin, size):
        rows = slice(begin, begin + size)
        return nt(d_key[rows, :], w_key[...]) + nt(d_value[rows, :], w_value[...])

    away = nears
    row = part
    for out, first in ((keep, 0), (send, 2)):
        for j in range(2):
            slot = first + j
            mine = slice(slot * quarter, (slot + 1) * quarter)
            begin = j * (quarter + away)
            out[begin : begin + quarter, :] = (back(slot * quarter, quarter) + nt(dq[mine, :], w_query[...])).astype(BF16)
            out[begin + quarter : begin + quarter + away, :] = back(row, away).astype(BF16)
            row += away


def vmem(n):
    return [pl.BlockSpec(memory_space=pltpu.VMEM)] * n


def attention_forward(own, near, cross, sib, w_four, b_query, b_value):
    part, width = own.shape
    cols = w_four.shape[-1]
    heads = cols // HEAD_DIM
    total = part + near.shape[0] + cross.shape[0] + sib.shape[0]
    shape = jax.ShapeDtypeStruct
    return pl.pallas_call(
        functools.partial(forward_body, heads),
        out_shape=(
            shape((part, cols), BF16),
            shape((total, cols), BF16),
            shape((total, cols), BF16),
            shape((part, cols), BF16),
            shape((8, part), F32),
            shape((part // 2, width), BF16),
            shape((part // 2, width), BF16),
        ),
        in_specs=vmem(7),
        out_specs=vmem(7),
        compiler_params=pltpu.CompilerParams(vmem_limit_bytes=VMEM_LIMIT),
        cost_estimate=pl.CostEstimate(
            flops=2 * total * width * 2 * cols + 4 * heads * 4 * part * total * HEAD_DIM,
            bytes_accessed=2 * (total * width + 3 * total * cols),
            transcendentals=heads * part * total,
        ),
        name="attention_forward",
    )(own, near, cross, sib, w_four, b_query, b_value)


def attention_backward(g_own, g_cross, g_sib, w_four, query, key, value, attended, log_total):
    part, cols = query.shape
    width = w_four.shape[1]
    heads = cols // HEAD_DIM
    total = key.shape[0]
    nears = (total - part) // 4
    shape = jax.ShapeDtypeStruct
    return pl.pallas_call(
        functools.partial(backward_body, heads, nears),
        out_shape=(
            shape((part, cols), BF16),
            shape((total, cols), BF16),
            shape((total, cols), BF16),
            shape((total // 2, width), BF16),
            shape((total // 2, width), BF16),
            shape((cols, width), F32),
            shape((8, cols), F32),
        ),
        in_specs=vmem(9),
        out_specs=vmem(7),
        scratch_shapes=[
            pltpu.VMEM((heads, part, cols), BF16),
            pltpu.VMEM((heads, part, cols), BF16),
            pltpu.VMEM((cols, part), F32),
        ],
        compiler_params=pltpu.CompilerParams(vmem_limit_bytes=VMEM_LIMIT),
        cost_estimate=pl.CostEstimate(
            flops=2 * total * width * 2 * cols + 10 * heads * 4 * part * total * HEAD_DIM,
            bytes_accessed=2 * (total * width + 5 * total * cols),
            transcendentals=heads * part * total,
        ),
        name="attention_backward",
    )(g_own, g_cross, g_sib, w_four, query, key, value, attended, log_total)


def rows_mean(a):
    return jnp.mean(a, axis=-1, keepdims=True)


def norm(values):
    centred = values - rows_mean(values)
    inverse = lax.rsqrt(rows_mean(centred * centred) + EPSILON)
    return centred * inverse, inverse


def norm_back(scaled, normed, inverse):
    return inverse * (scaled - rows_mean(scaled) - normed * rows_mean(scaled * normed))


def col_sum(a):
    return jnp.sum(a, axis=0, keepdims=True)


def feed_body(blocks, pieces, *refs):
    weights = refs[: blocks * pieces]
    inputs, branch_a, branch_b, cotangent, b_hidden, vectors = refs[blocks * pieces : blocks * pieces + 6]
    (result, grad_attn, grad_low, grads_keep, grads_send, sums, sums_hidden,
     up, down, act, slope, turned, sems) = refs[blocks * pieces + 6 :]
    rows, width = inputs.shape
    hidden = up.shape[-1]
    depth = width // pieces
    copies = []
    for b in range(blocks):
        for p in range(pieces):
            source = weights[b * pieces + p]
            spot = pl.ds(p * depth, depth)
            copies.append(pltpu.make_async_copy(source.at[pl.ds(0, depth), :], up.at[b, spot, :], sems.at[b, p, 0]))
            copies.append(pltpu.make_async_copy(source.at[pl.ds(depth, depth), :], down.at[b, spot, :], sems.at[b, p, 1]))
    for copy in copies:
        copy.start()
    b_out, gain_one, bias_one, b_down, gain_two, bias_two = (vectors[i : i + 1, :] for i in range(6))
    pre = inputs[...].astype(F32) + (branch_a[...].astype(F32) + branch_b[...].astype(F32)) + b_out
    normed_one, inverse_one = norm(pre)
    first = normed_one * gain_one + bias_one
    first_low = first.astype(BF16)
    turned[...] = first_low.T
    for copy in copies:
        copy.wait()

    def ahead(b, total):
        inner = nn(first_low, up[b]) + b_hidden[pl.ds(b, 1), :]
        shape = 0.5 * (1.0 + lax.erf(inner * (0.5**0.5)))
        act_low = (inner * shape).astype(BF16)
        act[b] = act_low
        slope[b] = shape + inner * (jnp.exp(-0.5 * inner * inner) * 0.3989422804014327)
        return total + nt(act_low, down[b])

    ffn = lax.fori_loop(0, blocks, ahead, jnp.zeros((rows, width), F32))
    normed_two, inverse_two = norm(first + ffn + b_down)
    result[...] = (normed_two * gain_two + bias_two).astype(BF16)
    grad = cotangent[...].astype(F32)
    grad_second = norm_back(grad * gain_two, normed_two, inverse_two)
    grad_ffn = grad_second.astype(BF16)
    grad_turned = grad_ffn.T

    def astern(offset, grads):
        def step(i, total):
            b = i + offset
            grad_inner = (nn(grad_ffn, down[b]) * slope[b]).astype(BF16)
            sums_hidden[pl.ds(b, 1), :] = col_sum(grad_inner.astype(F32))
            up_grad = nn(turned[...], grad_inner).astype(BF16)
            down_grad = nn(grad_turned, act[b]).astype(BF16)
            for p in range(pieces):
                grads[i, p, :depth, :] = up_grad[p * depth : (p + 1) * depth, :]
                grads[i, p, depth:, :] = down_grad[p * depth : (p + 1) * depth, :]
            return total + nt(grad_inner, up[b])

        return step

    grad_first = lax.fori_loop(0, blocks // 2, astern(blocks // 2, grads_send), grad_second)
    grad_first = lax.fori_loop(0, blocks // 2, astern(0, grads_keep), grad_first)
    grad_pre = norm_back(grad_first * gain_one, normed_one, inverse_one)
    grad_low[...] = grad_pre
    grad_attn[...] = grad_pre.astype(BF16)
    sums[...] = jnp.concatenate(
        [col_sum(grad_pre), col_sum(grad_first * normed_one), col_sum(grad_first), col_sum(grad_second),
         col_sum(grad * normed_two), col_sum(grad), jnp.zeros((2, width), F32)], axis=0)


def feed_forward(weights, inputs, branch_a, branch_b, cotangent, b_hidden, vectors):
    blocks = len(weights)
    pieces = len(weights[0])
    rows, width = inputs.shape
    hidden = weights[0][0].shape[-1]
    depth = width // pieces
    shape = jax.ShapeDtypeStruct
    flat = [w for block in weights for w in block]
    return pl.pallas_call(
        functools.partial(feed_body, blocks, pieces),
        out_shape=(
            shape((rows, width), BF16),
            shape((rows, width), BF16),
            shape((rows, width), F32),
            shape((blocks // 2, pieces, 2 * depth, hidden), BF16),
            shape((blocks // 2, pieces, 2 * depth, hidden), BF16),
            shape((8, width), F32),
            shape((8, hidden), F32),
        ),
        in_specs=[pl.BlockSpec(memory_space=pl.ANY)] * len(flat) + vmem(6),
        out_specs=vmem(7),
        scratch_shapes=[
            pltpu.VMEM((blocks, width, hidden), BF16),
            pltpu.VMEM((blocks, width, hidden), BF16),
            pltpu.VMEM((blocks, rows, hidden), BF16),
            pltpu.VMEM((blocks, rows, hidden), F32),
            pltpu.VMEM((width, rows), BF16),
            pltpu.SemaphoreType.DMA((blocks, pieces, 2)),
        ],
        compiler_params=pltpu.CompilerParams(vmem_limit_bytes=VMEM_LIMIT),
        cost_estimate=pl.CostEstimate(
            flops=12 * rows * width * hidden * blocks,
            bytes_accessed=8 * width * hidden * blocks,
            transcendentals=2 * rows * hidden * blocks,
        ),
        name="feed_forward",
    )(*flat, inputs, branch_a, branch_b, cotangent, b_hidden, vectors)


def gradients_body(own, near, cross, sib, d_query, d_key, d_value, out):
    out[0] = nn(d_query[...].T, own[...])
    row = 0
    for index, piece in enumerate((own, near, cross, sib)):
        rows = slice(row, row + piece.shape[0])
        for slot, grad in ((1, d_key), (2, d_value)):
            part = nn(grad[rows, :].T, piece[...])
            if index == 0:
                out[slot] = part
            else:
                out[slot] += part
        row += piece.shape[0]


def attention_gradients(own, near, cross, sib, d_query, d_key, d_value):
    cols = d_query.shape[1]
    width = own.shape[1]
    total = d_key.shape[0]
    return pl.pallas_call(
        gradients_body,
        out_shape=jax.ShapeDtypeStruct((3, cols, width), F32),
        in_specs=vmem(7),
        out_specs=pl.BlockSpec(memory_space=pltpu.VMEM),
        compiler_params=pltpu.CompilerParams(vmem_limit_bytes=VMEM_LIMIT),
        cost_estimate=pl.CostEstimate(
            flops=4 * total * cols * width, bytes_accessed=2 * total * (width + 2 * cols), transcendentals=0
        ),
        name="attention_gradients",
    )(own, near, cross, sib, d_query, d_key, d_value)


def rotated(value, axis, count, shift):
    return lax.ppermute(value, axis, [(i, (i + shift) % count) for i in range(count)])


def across(value):
    return lax.ppermute(value, "tensor", [(i, i ^ 2) for i in range(4)])


def sibling(value):
    return lax.ppermute(value, "tensor", [(i, i ^ 1) for i in range(4)])


def roll_columns(value, place, count):
    if count == 2:
        half = value.shape[-1] // 2
        turned = jnp.concatenate([value[..., half:], value[..., :half]], axis=-1)
        return jnp.where(place == 1, turned, value)
    size = value.shape[-1] // count
    twice = jnp.concatenate([value, value], axis=-1)
    return lax.dynamic_slice_in_dim(twice, place * size, value.shape[-1], axis=-1)


def on_device(shards, contexts, inputs, w_query, b_query, w_key, w_value, b_value, w_out, b_out,
              first_gain, first_bias, w_hidden, b_hidden, w_down, b_down, second_gain, second_bias, cotangent):
    seqs, part, width = inputs.shape
    cols = w_query.shape[1]
    hidden = w_hidden.shape[1]
    quarter = part // 4
    depth = width // shards
    shard = lax.axis_index("shard")
    tensor = lax.axis_index("tensor")
    places = [tensor ^ flip for flip in (0, 2, 1, 3)]
    unplace = (shards - shard) % shards

    def to_rel(value):
        return roll_columns(value, shard, shards)

    def from_rel(value):
        return roll_columns(value, unplace, shards)

    def block_of(value, axis, index, size):
        return lax.dynamic_slice_in_dim(value, index * size, size, axis=axis)

    four = jnp.stack([w_query, w_key, w_value, w_out.T])
    two = jnp.concatenate([w_hidden, w_down.T], axis=0)
    own = to_rel(jnp.concatenate([block_of(inputs, 1, p, quarter) for p in places], axis=1))

    nears = []
    for s in range(seqs):
        mine = own[s, :quarter]
        nears.append([rotated(mine, "context", contexts, -r) for r in range(1, contexts)])
    four_all = jnp.concatenate(
        [four] + [rotated(four, "shard", shards, -r) for r in range(1, shards)], axis=1)
    two_cross = across(two)
    two_pieces = [two] + [rotated(two, "shard", shards, -r) for r in range(1, shards)]
    cross_pieces = [two_cross] + [rotated(two_cross, "shard", shards, -r) for r in range(1, shards)]
    b_hidden_all = lax.all_gather(b_hidden, "tensor", axis=0)
    b_hidden_rel = jnp.concatenate([block_of(b_hidden_all, 0, p, 1) for p in places], axis=0)
    vectors = to_rel(jnp.stack([b_out, first_gain, first_bias, b_down, second_gain, second_bias, b_out, b_out]))
    cot_own = to_rel(block_of(cotangent, 1, tensor, quarter)).reshape(seqs * quarter, width)

    kept = []
    sums_a = []
    sums_b = []
    for s in range(seqs):
        near = jnp.concatenate(nears[s], axis=0)
        cross = across(near)
        sib = sibling(jnp.concatenate([near, cross], axis=0))
        query, key, value, attended, log_total, keep, send = attention_forward(
            own[s], near, cross, sib, four_all, b_query[None], b_value[None])
        kept.append((near, cross, sib, query, key, value, attended, log_total))
        both = keep.astype(F32) + sibling(send).astype(F32)
        sums_a.append(both[:quarter].astype(BF16))
        sums_b.append(across(both[quarter:].astype(BF16)))
    pieces = [two_pieces, cross_pieces, [sibling(p) for p in two_pieces], [sibling(p) for p in cross_pieces]]
    result, grad_attn, grad_low, grads_keep, grads_send, sums, sums_hidden = feed_forward(
        pieces, own[:, :quarter].reshape(seqs * quarter, width),
        jnp.concatenate(sums_a, axis=0), jnp.concatenate(sums_b, axis=0), cot_own, b_hidden_rel, vectors)

    def whole(value):
        return lax.all_gather(from_rel(value).reshape(seqs, quarter, width), "tensor", axis=1, tiled=True)

    outputs = whole(result)

    feed = grads_keep.astype(F32) + sibling(grads_send).astype(F32)
    feed_own = feed[:, 0]
    for r in range(1, shards):
        feed_own = feed_own + rotated(feed[:, r].astype(BF16), "shard", shards, r).astype(F32)
    feed_sum = feed_own[0] + across(feed_own[1].astype(BF16)).astype(F32)
    feed_sum = lax.psum(feed_sum.astype(BF16), "context").astype(F32)

    totals = []
    outs = []
    column_sums = []
    grad_parts = []
    for s in range(seqs):
        g_own = grad_attn[s * quarter : (s + 1) * quarter]
        g_cross = across(g_own)
        g_sib = sibling(jnp.concatenate([g_own, g_cross], axis=0))
        near, cross, sib, query, key, value, attended, log_total = kept[s]
        d_query, d_key, d_value, keep, send, d_out, summed = attention_backward(
            g_own, g_cross, g_sib, four_all, query, key, value, attended, log_total)
        outs.append(d_out)
        column_sums.append(summed)
        grad_parts.append((own[s], near, cross, sib, d_query, d_key, d_value))
        both = keep.astype(F32) + sibling(send).astype(F32)
        half = both.shape[0] // 2
        total = both[:half] + across(both[half:].astype(BF16)).astype(F32)
        total = total.reshape(contexts, quarter, width)
        grad = grad_low[s * quarter : (s + 1) * quarter] + total[0]
        for r in range(1, contexts):
            grad = grad + rotated(total[r].astype(BF16), "context", contexts, r).astype(F32)
        totals.append(grad.astype(BF16))
    input_grad = whole(jnp.concatenate(totals, axis=0))

    projections = [attention_gradients(*p) for p in grad_parts]
    projected = jnp.concatenate(
        [sum(projections[1:], projections[0]), sum(outs[1:], outs[0])[None]], axis=0)
    attn_sum = projected[:, :, :depth]
    for r in range(1, shards):
        away = projected[:, :, r * depth : (r + 1) * depth].astype(BF16)
        attn_sum = attn_sum + rotated(away, "shard", shards, r).astype(F32)
    attn_sum = lax.psum(attn_sum.astype(BF16), "context").astype(F32)

    summed = sum(column_sums[1:], column_sums[0])[:2]
    spread = lax.dynamic_update_slice(jnp.zeros((2, 4, cols), F32), summed[:, None], (0, tensor, 0))
    hidden_abs = jnp.concatenate([block_of(sums_hidden, 0, order, 1) for order in
                                  [(((tensor ^ t) & 2) >> 1) + (((tensor ^ t) & 1) << 1) for t in range(4)]], axis=0)
    packed = jnp.concatenate([from_rel(sums)[:6].reshape(-1), hidden_abs.reshape(-1), spread.reshape(-1)])
    packed = lax.psum(packed, ("shard", "context", "tensor"))
    wide = packed[: 6 * width].reshape(6, width)
    at = 6 * width
    grad_b_hidden = block_of(packed[at : at + 4 * hidden], 0, tensor, hidden)
    at += 4 * hidden
    grad_b_query = block_of(packed[at : at + 4 * cols], 0, tensor, cols)
    at += 4 * cols
    grad_b_value = block_of(packed[at : at + 4 * cols], 0, tensor, cols)
    return (
        outputs,
        input_grad,
        attn_sum[0].T,
        grad_b_query,
        attn_sum[1].T,
        attn_sum[2].T,
        grad_b_value,
        attn_sum[3],
        wide[0],
        wide[1],
        wide[2],
        feed_sum[:depth],
        grad_b_hidden,
        feed_sum[depth:].T,
        wide[3],
        wide[4],
        wide[5],
    )


def solution(mesh):
    shards = mesh.shape["shard"]
    contexts = mesh.shape["context"]
    rows = P("shard", "context", None)
    into = P("shard", "tensor")
    onto = P("tensor", "shard")
    heads = P("tensor")
    return jax.shard_map(
        functools.partial(on_device, shards, contexts),
        mesh=mesh,
        in_specs=(rows, into, heads, into, into, heads, onto, P(), P(), P(), into, heads, onto, P(), P(), P(), rows),
        out_specs=(rows, rows, into, heads, into, into, heads, onto, P(), P(), P(), into, heads, onto, P(), P(), P()),
        check_vma=False,
    )
```

time: 1060 us -> 576 us (0.54)
  waiting for transfers between devices: 564 us -> 191 us
  matrix products: 167 us -> 0 us
  Pallas kernels: 0 us -> 152 us
  blocking collectives: 168 us -> 50.9 us
  starting transfers between devices: 2.54 us -> 67.3 us
  other arithmetic: 80.6 us -> 44.8 us
    psum x5 -> x1, waiting for transfers between devices: 402 us -> 28.8 us  [on_device(): attn_sum = lax.psum(attn_sum.astype(BF16), 'context').astype(F32)]
    dot_general x108 -> x0, matrix products: 167 us -> none  [the longest x9 31.1 us: attend_back(): jnp.einsum('sqd,skd->sqk', grad_head, values[..., lower:upper], preferred...]
    ppermute x0 -> x54, waiting for transfers between devices: none -> 162 us  [the longest x14 113 us: across(): return lax.ppermute(value, 'tensor', [(i, i ^ 2) for i in range(4)])]
    pallas_call x0 -> x10, Pallas kernels: none -> 152 us  [the longest x3 56.4 us: attention_backward(): pl.pallas_call(functools.partial(backward_body, heads, nears), out_shape=...]
    all_gather x10 -> x1, blocking collectives: 130 us -> 9.94 us  [on_device(): b_hidden_all = lax.all_gather(b_hidden, 'tensor', axis=0)]
    reduce_scatter x7 -> x0, waiting for transfers between devices: 95.7 us -> none  [the longest x3 72.8 us: on_device(): lax.psum_scatter(grad_keys, 'context', scatter_dimension=1, tiled=True)]
    ppermute x0 -> x54, starting transfers between devices: none -> 66.9 us  [the longest x23 45.8 us: rotated(): lax.ppermute(value, axis, [(i, (i + shift) % count) for i in range(count)])]
    unnamed x24 -> x3, waiting for transfers between devices: 66.9 us -> 0.05 us
  transfers between devices with their start and end apart: 19 -> 57, of which waited for: 14 -> 21; matrix products, arithmetic and copies ran while one was open for 16% -> 11% of each run, Pallas kernels for 0% -> 22%
where the time goes in v1:
time: 576 us; the launch traced here: 570 us
  waiting for transfers between devices  191 us (33%)
  Pallas kernels  152 us (26%)
  starting transfers between devices  67.3 us (12%)
  blocking collectives  50.9 us (9%)
  local copies, waits for them, and re-layouts  46.7 us (8%)
  other arithmetic  44.8 us (8%)
  between operations  17 us (3%)
    ppermute x14, waiting for transfers between devices, across(): return lax.ppermute(value, 'tensor', [(i, i ^ 2) for i in range(4)])  113 us
    pallas_call x3, Pallas kernels, attention_backward(): pl.pallas_call(functools.partial(backward_body, heads, nears), out_shape=...  56.4 us
    pallas_call x3, Pallas kernels, attention_forward(): pl.pallas_call(functools.partial(forward_body, heads), out_shape=(shape((...  52 us
    ppermute x23, starting transfers between devices, rotated(): lax.ppermute(value, axis, [(i, (i + shift) % count) for i in range(count)])  45.8 us
    ppermute x23, waiting for transfers between devices, rotated(): lax.ppermute(value, axis, [(i, (i + shift) % count) for i in range(count)])  45 us
    psum x1, blocking collectives, on_device(): packed = lax.psum(packed, ('shard', 'context', 'tensor'))  41 us
    psum x1, waiting for transfers between devices, on_device(): attn_sum = lax.psum(attn_sum.astype(BF16), 'context').astype(F32)  28.8 us
    pallas_call x1, Pallas kernels, feed_forward(): pl.pallas_call(functools.partial(feed_body, blocks, pieces), out_shape=(s...  26.8 us
  transfers between devices with their start and end apart: 57, of which 21 were waited for; matrix products, arithmetic and copies ran while one was open for 11% of the time, Pallas kernels for 22%

profile of v1, /device:TPU:0, one launch (start us, length us, event | category | flops | bytes accessed | tf_op | source)
XLA Modules:
  0.0 569.9 jit_solution(9714405162231625877)
XLA Ops:
  8.1 1.8 constant_dynamic-slice_fusion.13
  10.9 1.7 fusion.29
  12.5 3.5 maximum_select_fusion
  16.8 5.0 collective-permute-start.7
  22.9 2.9 collective-permute-start.14
  31.6 2.2 pad_maximum_fusion.3.refs_0_
  40.9 5.8 %collective-permute-start.20 = (bf16[128,768]{1,0:T(8,128)(2,1)}, bf16[128,768]{1,0:T(8,128)(2,1)S(1)}, u32[]{:S(2)}, u32[]{:S(2)}) collective-permute-start(bf16[128,768]{1,0:T(8,128)(2,1)} %get-tuple-element.177), channel_id=1, source_target_pairs={{0,12},{4,0},{8,4},{12,8},{1,13},{5,1},{9,5},{13,9},{2,14},{6,2},{... | collective-permute-start | bytes 589832 | tf_op jit(solution)/shard_map/ppermute | solution.py:374
  48.5 1.6 collective-permute-start.10
  50.1 9.9 %all-gather.1 = f32[4,1,768]{2,1,0:T(1,128)S(1)} all-gather(f32[1,1,768]{2,1,0:T(1,128)S(1)} %reshape.105), channel_id=2, replica_groups=mesh['shard'=2,'context'=4,'tensor'=4] {'tensor'}, dimensions={0}, use_global_device_ids=true | all-gather | bytes 15360 | tf_op jit(solution)/shard_map/all_gather | solution.py:429
  60.0 6.5 %collective-permute-start.21 = (bf16[128,768]{1,0:T(8,128)(2,1)}, bf16[128,768]{1,0:T(8,128)(2,1)S(1)}, u32[]{:S(2)}, u32[]{:S(2)}) collective-permute-start(bf16[128,768]{1,0:T(8,128)(2,1)} %get-tuple-element.177), channel_id=1, source_target_pairs={{0,8},{4,12},{8,0},{12,4},{1,9},{5,13},{9,1},{13,5},{2,10},{6,14},... | collective-permute-start | bytes 589832 | tf_op jit(solution)/shard_map/ppermute | solution.py:374
  67.6 1.6 collective-permute-start.12
  70.2 1.6 collective-permute-start.1
  71.7 8.9 %collective-permute-done.21 = bf16[128,768]{1,0:T(8,128)(2,1)S(1)} collective-permute-done((bf16[128,768]{1,0:T(8,128)(2,1)}, bf16[128,768]{1,0:T(8,128)(2,1)S(1)}, u32[]{:S(2)}, u32[]{:S(2)}) %collective-permute-start.21) | collective-permute-done | bytes 196640 | tf_op jit(solution)/shard_map/ppermute | solution.py:374
  80.6 1.5 collective-permute-start.17
  82.2 2.4 pad_maximum_fusion.4
  85.2 26.7 %collective-permute-done.17.cross = bf16[384,768]{1,0:T(8,128)(2,1)S(1)} collective-permute-done((bf16[384,768]{1,0:T(8,128)(2,1)S(1)}, bf16[384,768]{1,0:T(8,128)(2,1)S(1)}, u32[]{:S(2)}, u32[]{:S(2)}) %collective-permute-start.17) | collective-permute-done | bytes 589856 | tf_op jit(solution)/shard_map/ppermute | solution.py:378
  111.9 2.3 pad_maximum_fusion.5
  114.9 8.5 %collective-permute-done.23.cross = bf16[384,768]{1,0:T(8,128)(2,1)S(1)} collective-permute-done((bf16[384,768]{1,0:T(8,128)(2,1)S(1)}, bf16[384,768]{1,0:T(8,128)(2,1)S(1)}, u32[]{:S(2)}, u32[]{:S(2)}) %collective-permute-start.23) | collective-permute-done | bytes 589856 | tf_op jit(solution)/shard_map/ppermute | solution.py:378
  125.5 2.1 maximum_select_fusion.1
  131.9 1.5 collective-permute-start.2
  133.5 17.6 %attention_forward.3 = (bf16[512,192]{1,0:T(8,128)(2,1)}, bf16[2048,192]{1,0:T(8,128)(2,1)}, bf16[2048,192]{1,0:T(8,128)(2,1)}, bf16[512,192]{1,0:T(8,128)(2,1)}...) custom-call(bf16[512,768]{1,0:T(8,128)(2,1)} %get-tuple-element.179.own, ...), custom_call_target="tpu_custom_call" | custom-call | flops 4429185024 | bytes 5505024 | tf_op jit(solution)/shard_map/attention_forward/pallas_call | solution.py:161
  151.1 17.2 %attention_forward.4 = (bf16[512,192]{1,0:T(8,128)(2,1)}, bf16[2048,192]{1,0:T(8,128)(2,1)}, bf16[2048,192]{1,0:T(8,128)(2,1)}, bf16[512,192]{1,0:T(8,128)(2,1)}...) custom-call(bf16[512,768]{1,0:T(8,128)(2,1)} %get-tuple-element.181.own, ...), custom_call_target="tpu_custom_call" | custom-call | flops 4429185024 | bytes 5505024 | tf_op jit(solution)/shard_map/attention_forward/pallas_call | solution.py:161
  168.8 17.2 %attention_forward.5 = (bf16[512,192]{1,0:T(8,128)(2,1)}, bf16[2048,192]{1,0:T(8,128)(2,1)}, bf16[2048,192]{1,0:T(8,128)(2,1)}, bf16[512,192]{1,0:T(8,128)(2,1)}...) custom-call(bf16[512,768]{1,0:T(8,128)(2,1)} %get-tuple-element.180.own, ...), custom_call_target="tpu_custom_call" | custom-call | flops 4429185024 | bytes 5505024 | tf_op jit(solution)/shard_map/attention_forward/pallas_call | solution.py:161
  187.4 3.6 collective-permute-done.25
  192.7 5.3 collective-permute-done.26
  198.0 1.5 collective-permute-start.27
  199.5 4.6 collective-permute-done.27
  207.1 2.7 collective-permute-done.28
  212.8 26.8 %feed_forward.1 = (bf16[384,768]{1,0:T(8,128)(2,1)}, bf16[384,768]{1,0:T(8,128)(2,1)}, f32[384,768]{1,0:T(8,128)}, bf16[2,2,768,768]{3,2,1,0:T(8,128)(2,1)}, bf1...) custom-call(bf16[768,768]{1,0:T(8,128)(2,1)} %pad_maximum_fusion.3.refs_0_, ...), custom_call_target="tpu_custom_call" | custom-call | flops 10871635968 | bytes 18874368 | tf_op jit(solution)/shard_map/feed_forward/pallas_call | solution.py:311
  240.8 1.6 collective-permute-start.36
  242.9 4.1 collective-permute-done.36.g_cross
  247.1 1.6 collective-permute-start.29
  249.3 5.2 collective-permute-done.29.g_cross
  255.3 18.9 %attention_backward.4 = (bf16[512,192]{1,0:T(8,128)(2,1)}, bf16[2048,192]{1,0:T(8,128)(2,1)}, bf16[2048,192]{1,0:T(8,128)(2,1)}, bf16[1024,768]{1,0:T(8,128)(2,1...) custom-call(bf16[128,768]{1,0:T(8,128)(2,1)} %copy-done.30, bf16[128,768]{1,0:T(8,128)(2,1)} %copy-done.43, ...), custom_call_target="tpu_custom_call" | custom-call | flops 9261023232 | bytes 7077888 | tf_op jit(solution)/shard_map/attention_backward/pallas_call | solution.py:191
  275.5 18.7 %attention_backward.5 = (bf16[512,192]{1,0:T(8,128)(2,1)}, bf16[2048,192]{1,0:T(8,128)(2,1)}, bf16[2048,192]{1,0:T(8,128)(2,1)}, bf16[1024,768]{1,0:T(8,128)(2,1...) custom-call(bf16[128,768]{1,0:T(8,128)(2,1)} %copy-done.29, bf16[128,768]{1,0:T(8,128)(2,1)} %copy-done.42, ...), custom_call_target="tpu_custom_call" | custom-call | flops 9261023232 | bytes 7077888 | tf_op jit(solution)/shard_map/attention_backward/pallas_call | solution.py:191
  295.0 18.8 %attention_backward.3 = (bf16[512,192]{1,0:T(8,128)(2,1)}, bf16[2048,192]{1,0:T(8,128)(2,1)}, bf16[2048,192]{1,0:T(8,128)(2,1)}, bf16[1024,768]{1,0:T(8,128)(2,1...) custom-call(bf16[128,768]{1,0:T(8,128)(2,1)} %copy-done.28, bf16[128,768]{1,0:T(8,128)(2,1)} %copy-done.41, ...), custom_call_target="tpu_custom_call" | custom-call | flops 9261023232 | bytes 7077888 | tf_op jit(solution)/shard_map/attention_backward/pallas_call | solution.py:191
  315.5 2.2 convert_add_fusion.2
  321.5 2.2 convert_add_fusion.1
  325.1 1.8 convert_add_fusion.3
  327.9 20.4 %collective-permute-done.39 = bf16[512,768]{1,0:T(8,128)(2,1)} collective-permute-done((bf16[512,768]{1,0:T(8,128)(2,1)}, bf16[512,768]{1,0:T(8,128)(2,1)}, u32[]{:S(2)}, u32[]{:S(2)}) %collective-permute-start.39) | collective-permute-done | bytes 786464 | tf_op jit(solution)/shard_map/ppermute | solution.py:378
  350.5 4.1 collective-permute-start.41
  354.6 14.1 %collective-permute-done.46 = bf16[512,768]{1,0:T(8,128)(2,1)S(1)} collective-permute-done((bf16[512,768]{1,0:T(8,128)(2,1)S(1)}, bf16[512,768]{1,0:T(8,128)(2,1)S(1)}, u32[]{:S(2)}, u32[]{:S(2)}) %collective-permute-start.46) | collective-permute-done | bytes 786464 | tf_op jit(solution)/shard_map/ppermute | solution.py:378
  368.8 3.5 collective-permute-start.42
  373.3 11.4 %collective-permute-done.32 = bf16[512,768]{1,0:T(8,128)(2,1)S(1)} collective-permute-done((bf16[512,768]{1,0:T(8,128)(2,1)S(1)}, bf16[512,768]{1,0:T(8,128)(2,1)S(1)}, u32[]{:S(2)}, u32[]{:S(2)}) %collective-permute-start.32) | collective-permute-done | bytes 786464 | tf_op jit(solution)/shard_map/ppermute | solution.py:378
  386.4 3.5 collective-permute-start.48
  389.9 3.3 convert_add_fusion
  393.3 1.6 fusion.1
  395.6 2.0 collective-permute-start.33
  397.6 5.5 collective-permute-done.48
  403.1 4.8 collective-permute-start.35
  407.8 1.9 collective-permute-done.49
  409.7 8.4 %collective-permute-done.34 = bf16[128,768]{1,0:T(8,128)(2,1)S(1)} collective-permute-done((bf16[128,768]{1,0:T(8,128)(2,1)S(1)}, bf16[128,768]{1,0:T(8,128)(2,1)S(1)}, u32[]{:S(2)}, u32[]{:S(2)}) %collective-permute-start.34) | collective-permute-done | bytes 196640 | tf_op jit(solution)/shard_map/ppermute | solution.py:374
  420.8 5.5 attention_gradients.4
  426.3 5.7 %attention_gradients.3 = f32[3,192,768]{2,1,0:T(8,128)} custom-call(bf16[512,768]{1,0:T(8,128)(2,1)} %get-tuple-element.179.own, bf16[384,768]{1,0:T(8,128)(2,1)} %copy-done.27, bf16[384,768]{1,0:T(8,128)(2,1)} %copy-done.7, bf16[768,768]{1,0:T(8,128)(2,1)} %collective-permute-done.11.sib, bf16[512,192]{1,0:T(8,128)(2,1)} %get-tuple-element.96.d_query, ...), custom_call_target="tpu_custom_call" | custom-call | flops 1207959552 | bytes 4718592 | tf_op jit(solution)/shard_map/attention_gradients/pallas_call | solution.py:360
  432.0 5.7 attention_gradients.5
  437.7 1.8 add_add_fusion
  439.5 7.5 %collective-permute-done.52 = bf16[2,768,768]{2,1,0:T(8,128)(2,1)} collective-permute-done((bf16[2,768,768]{2,1,0:T(8,128)(2,1)}, bf16[2,768,768]{2,1,0:T(8,128)(2,1)}, u32[]{:S(2)}, u32[]{:S(2)}) %collective-permute-start.52) | collective-permute-done | bytes 2359328 | tf_op jit(solution)/shard_map/ppermute | solution.py:374
  447.0 3.6 fusion
  450.7 1.6 collective-permute-start.53
  453.1 12.1 %collective-permute-done.50 = bf16[4,192,384]{2,1,0:T(8,128)(2,1)S(1)} collective-permute-done((bf16[4,192,384]{2,1,0:T(8,128)(2,1)S(1)}, bf16[4,192,384]{2,1,0:T(8,128)(2,1)S(1)}, u32[]{:S(2)}, u32[]{:S(2)}) %collective-permute-start.50) | collective-permute-done | bytes 589856 | tf_op jit(solution)/shard_map/ppermute | solution.py:374
  466.2 10.2 %collective-permute-done.53 = bf16[768,768]{1,0:T(8,128)(2,1)S(1)} collective-permute-done((bf16[768,768]{1,0:T(8,128)(2,1)S(1)}, bf16[768,768]{1,0:T(8,128)(2,1)S(1)}, u32[]{:S(2)}, u32[]{:S(2)}) %collective-permute-start.53) | collective-permute-done | bytes 1179680 | tf_op jit(solution)/shard_map/ppermute | solution.py:378
  479.4 41.0 %psum.22 = f32[9216]{0:T(1024)S(1)} all-reduce(f32[9216]{0:T(1024)S(1)} %pad_maximum_fusion.14), channel_id=1, replica_groups=mesh['shard'=2,'context'=4,'tensor'=4] {'shard','context','tensor'}, use_global_device_ids=true, to_apply=%region_1.2 | all-reduce | flops 9216 | bytes 73728 | tf_op jit(solution)/shard_map/psum | solution.py:502
  523.0 28.8 %all-reduce.3.cloned.1.call-done = (bf16[4,192,384]{2,1,0:T(8,128)(2,1)}, bf16[768,768]{1,0:T(8,128)(2,1)}) async-done(((bf16[4,192,384]{2,1,0:T(8,128)(2,1)}, bf16[768,768]{1,0:T(8,128)(2,1)}), (bf16[4,192,384]{2,1,0:T(8,128)(2,1)}, bf16[768,768]{1,0:T(8,128)(2,1)})) %all-reduce.3.cloned.1.call-update) | async-done | bytes 1769488 | tf_op jit(solution)/shard_map/psum | solution.py:495
  551.8 1.5 convert_element_type.172
  (303 shorter events, 73.8 us)
Async XLA Ops:
  8.0 515.0 %all-gather.5.cloned.1.call-start = ((), (), s32[]{:S(2)}) async-start(), calls=%async_computation | async-start | bytes 2949120 | tf_op jit(solution)/shard_map/all_gather | solution.py:453
  16.8 22.3 %collective-permute-start.7 = (bf16[128,768]{1,0:T(8,128)(2,1)}, bf16[128,768]{1,0:T(8,128)(2,1)}, u32[]{:S(2)}, u32[]{:S(2)}) collective-permute-start(bf16[128,768]{1,0:T(8,128)(2,1)} %get-tuple-element.176), channel_id=1, source_target_pairs={{0,12},{4,0},{8,4},{12,8},{1,13},{5,1},{9,5},{13,9},{2,14},{6,2},{... | collective-permute-start | bytes 589832 | tf_op jit(solution)/shard_map/ppermute | solution.py:374
  21.9 19.0 %collective-permute-start.8 = (bf16[128,768]{1,0:T(8,128)(2,1)}, bf16[128,768]{1,0:T(8,128)(2,1)}, u32[]{:S(2)}, u32[]{:S(2)}) collective-permute-start(bf16[128,768]{1,0:T(8,128)(2,1)} %get-tuple-element.176), channel_id=1, source_target_pairs={{0,8},{4,12},{8,0},{12,4},{1,9},{5,13},{9,1},{13,5},{2,10},{6,14},... | collective-permute-start | bytes 589832 | tf_op jit(solution)/shard_map/ppermute | solution.py:374
  21.9 25.7 %collective-permute-start.9 = (bf16[128,768]{1,0:T(8,128)(2,1)}, bf16[128,768]{1,0:T(8,128)(2,1)}, u32[]{:S(2)}, u32[]{:S(2)}) collective-permute-start(bf16[128,768]{1,0:T(8,128)(2,1)} %get-tuple-element.176), channel_id=1, source_target_pairs={{0,4},{4,8},{8,12},{12,0},{1,5},{5,9},{9,13},{13,1},{2,6},{6,10},{... | collective-permute-start | bytes 589832 | tf_op jit(solution)/shard_map/ppermute | solution.py:374
  22.9 37.1 %collective-permute-start.14 = (bf16[128,768]{1,0:T(8,128)(2,1)}, bf16[128,768]{1,0:T(8,128)(2,1)}, u32[]{:S(2)}, u32[]{:S(2)}) collective-permute-start(bf16[128,768]{1,0:T(8,128)(2,1)} %get-tuple-element.178), channel_id=1, source_target_pairs={{0,12},{4,0},{8,4},{12,8},{1,13},{5,1},{9,5},{13,9},{2,14},{6,2},{... | collective-permute-start | bytes 589832 | tf_op jit(solution)/shard_map/ppermute | solution.py:374
  25.8 41.8 %collective-permute-start.15 = (bf16[128,768]{1,0:T(8,128)(2,1)}, bf16[128,768]{1,0:T(8,128)(2,1)}, u32[]{:S(2)}, u32[]{:S(2)}) collective-permute-start(bf16[128,768]{1,0:T(8,128)(2,1)} %get-tuple-element.178), channel_id=1, source_target_pairs={{0,8},{4,12},{8,0},{12,4},{1,9},{5,13},{9,1},{13,5},{2,10},{6,14},... | collective-permute-start | bytes 589832 | tf_op jit(solution)/shard_map/ppermute | solution.py:374
  39.1 31.0 %collective-permute-start.16 = (bf16[128,768]{1,0:T(8,128)(2,1)}, bf16[128,768]{1,0:T(8,128)(2,1)S(1)}, u32[]{:S(2)}, u32[]{:S(2)}) collective-permute-start(bf16[128,768]{1,0:T(8,128)(2,1)} %get-tuple-element.178), channel_id=1, source_target_pairs={{0,4},{4,8},{8,12},{12,0},{1,5},{5,9},{9,13},{13,1},{2,6},{6,10},{... | collective-permute-start | bytes 589832 | tf_op jit(solution)/shard_map/ppermute | solution.py:374
  40.9 26.7 %collective-permute-start.20 = (bf16[128,768]{1,0:T(8,128)(2,1)}, bf16[128,768]{1,0:T(8,128)(2,1)S(1)}, u32[]{:S(2)}, u32[]{:S(2)}) collective-permute-start(bf16[128,768]{1,0:T(8,128)(2,1)} %get-tuple-element.177), channel_id=1, source_target_pairs={{0,12},{4,0},{8,4},{12,8},{1,13},{5,1},{9,5},{13,9},{2,14},{6,2},{... | collective-permute-start | bytes 589832 | tf_op jit(solution)/shard_map/ppermute | solution.py:374
  48.5 33.6 %copy-start.27 = (bf16[384,768]{1,0:T(8,128)(2,1)}, bf16[384,768]{1,0:T(8,128)(2,1)S(1)}, u32[]{:S(2)}) copy-start(bf16[384,768]{1,0:T(8,128)(2,1)S(1)} %constant_dynamic-update-slice_fusion.near) | copy-start | bytes 1769476
  48.5 33.6 %collective-permute-start.10 = (bf16[384,768]{1,0:T(8,128)(2,1)S(1)}, bf16[384,768]{1,0:T(8,128)(2,1)S(1)}, u32[]{:S(2)}, u32[]{:S(2)}) collective-permute-start(bf16[384,768]{1,0:T(8,128)(2,1)S(1)} %constant_dynamic-update-slice_fusion.near), channel_id=1, source_target_pairs={{0,2},{1,3},{2,0},{3,1},{4,6},{5,7},{6,4},{7,5},{8,10},{9,11},{10,... | collective-permute-start | bytes 1769480 | tf_op jit(solution)/shard_map/ppermute | solution.py:378
  60.0 20.6 %collective-permute-start.21 = (bf16[128,768]{1,0:T(8,128)(2,1)}, bf16[128,768]{1,0:T(8,128)(2,1)S(1)}, u32[]{:S(2)}, u32[]{:S(2)}) collective-permute-start(bf16[128,768]{1,0:T(8,128)(2,1)} %get-tuple-element.177), channel_id=1, source_target_pairs={{0,8},{4,12},{8,0},{12,4},{1,9},{5,13},{9,1},{13,5},{2,10},{6,14},... | collective-permute-start | bytes 589832 | tf_op jit(solution)/shard_map/ppermute | solution.py:374
  67.5 17.1 %collective-permute-start.22 = (bf16[128,768]{1,0:T(8,128)(2,1)}, bf16[128,768]{1,0:T(8,128)(2,1)S(1)}, u32[]{:S(2)}, u32[]{:S(2)}) collective-permute-start(bf16[128,768]{1,0:T(8,128)(2,1)} %get-tuple-element.177), channel_id=1, source_target_pairs={{0,4},{4,8},{8,12},{12,0},{1,5},{5,9},{9,13},{13,1},{2,6},{6,10},{... | collective-permute-start | bytes 589832 | tf_op jit(solution)/shard_map/ppermute | solution.py:374
  67.6 60.0 %collective-permute-start.12 = (bf16[4,384,192]{1,2,0:T(8,128)(2,1)}, bf16[4,384,192]{1,2,0:T(8,128)(2,1)S(1)}, u32[]{:S(2)}, u32[]{:S(2)}) collective-permute-start(bf16[4,384,192]{1,2,0:T(8,128)(2,1)} %copy.54), channel_id=1, source_target_pairs={{0,16},{16,0},{1,17},{17,1},{2,18},{18,2},{3,19},{19,3},{4,20},{20... | collective-permute-start | bytes 1769480 | tf_op jit(solution)/shard_map/ppermute | solution.py:374
  70.2 61.6 %collective-permute-start.1 = (bf16[768,768]{1,0:T(8,128)(2,1)}, bf16[768,768]{1,0:T(8,128)(2,1)}, u32[]{:S(2)}, u32[]{:S(2)}) collective-permute-start(bf16[768,768]{1,0:T(8,128)(2,1)} %pad_maximum_fusion.3.refs_0_), channel_id=1, source_target_pairs={{0,2},{1,3},{2,0},{3,1},{4,6},{5,7},{6,4},{7,5},{8,10},{9,11},{10,... | collective-permute-start | bytes 3538952 | tf_op jit(solution)/shard_map/ppermute | solution.py:378
  71.7 42.5 %copy-start.26 = (bf16[384,768]{1,0:T(8,128)(2,1)}, bf16[384,768]{1,0:T(8,128)(2,1)S(1)}, u32[]{:S(2)}) copy-start(bf16[384,768]{1,0:T(8,128)(2,1)S(1)} %constant_dynamic-update-slice_fusion.3.near) | copy-start | bytes 1769476
  80.6 31.3 %collective-permute-start.17 = (bf16[384,768]{1,0:T(8,128)(2,1)S(1)}, bf16[384,768]{1,0:T(8,128)(2,1)S(1)}, u32[]{:S(2)}, u32[]{:S(2)}) collective-permute-start(bf16[384,768]{1,0:T(8,128)(2,1)S(1)} %constant_dynamic-update-slice_fusion.3.near), channel_id=1, source_target_pairs={{0,2},{1,3},{2,0},{3,1},{4,6},{5,7},{6,4},{7,5},{8,10},{9,11},{10,... | collective-permute-start | bytes 1769480 | tf_op jit(solution)/shard_map/ppermute | solution.py:378
  82.1 32.1 %copy-start.7 = (bf16[384,768]{1,0:T(8,128)(2,1)}, bf16[384,768]{1,0:T(8,128)(2,1)S(1)}, u32[]{:S(2)}) copy-start(bf16[384,768]{1,0:T(8,128)(2,1)S(1)} %collective-permute-done.10.cross) | copy-start | bytes 1769476
  84.6 47.3 %collective-permute-start.11 = (bf16[768,768]{1,0:T(8,128)(2,1)}, bf16[768,768]{1,0:T(8,128)(2,1)}, u32[]{:S(2)}, u32[]{:S(2)}) collective-permute-start(bf16[768,768]{1,0:T(8,128)(2,1)} %pad_maximum_fusion.4), channel_id=1, source_target_pairs={{0,1},{1,0},{2,3},{3,2},{4,5},{5,4},{6,7},{7,6},{8,9},{9,8},{10,11... | collective-permute-start | bytes 3538952 | tf_op jit(solution)/shard_map/ppermute | solution.py:382
  84.6 39.9 %copy-start.25 = (bf16[384,768]{1,0:T(8,128)(2,1)}, bf16[384,768]{1,0:T(8,128)(2,1)S(1)}, u32[]{:S(2)}) copy-start(bf16[384,768]{1,0:T(8,128)(2,1)S(1)} %constant_dynamic-update-slice_fusion.6.near) | copy-start | bytes 1769476
  84.6 38.7 %collective-permute-start.23 = (bf16[384,768]{1,0:T(8,128)(2,1)S(1)}, bf16[384,768]{1,0:T(8,128)(2,1)S(1)}, u32[]{:S(2)}, u32[]{:S(2)}) collective-permute-start(bf16[384,768]{1,0:T(8,128)(2,1)S(1)} %constant_dynamic-update-slice_fusion.6.near), channel_id=1, source_target_pairs={{0,2},{1,3},{2,0},{3,1},{4,6},{5,7},{6,4},{7,5},{8,10},{9,11},{10,... | collective-permute-start | bytes 1769480 | tf_op jit(solution)/shard_map/ppermute | solution.py:378
  114.3 36.8 %collective-permute-start.18 = (bf16[768,768]{1,0:T(8,128)(2,1)}, bf16[768,768]{1,0:T(8,128)(2,1)}, u32[]{:S(2)}, u32[]{:S(2)}) collective-permute-start(bf16[768,768]{1,0:T(8,128)(2,1)} %pad_maximum_fusion.5), channel_id=1, source_target_pairs={{0,1},{1,0},{2,3},{3,2},{4,5},{5,4},{6,7},{7,6},{8,9},{9,8},{10,11... | collective-permute-start | bytes 3538952 | tf_op jit(solution)/shard_map/ppermute | solution.py:382
  124.6 43.7 %collective-permute-start.24 = (bf16[768,768]{1,0:T(8,128)(2,1)}, bf16[768,768]{1,0:T(8,128)(2,1)}, u32[]{:S(2)}, u32[]{:S(2)}) collective-permute-start(bf16[768,768]{1,0:T(8,128)(2,1)} %pad_maximum_fusion.6), channel_id=1, source_target_pairs={{0,1},{1,0},{2,3},{3,2},{4,5},{5,4},{6,7},{7,6},{8,9},{9,8},{10,11... | collective-permute-start | bytes 3538952 | tf_op jit(solution)/shard_map/ppermute | solution.py:382
  128.4 57.6 %collective-permute-start = (bf16[768,768]{1,0:T(8,128)(2,1)}, bf16[768,768]{1,0:T(8,128)(2,1)S(1)}, u32[]{:S(2)}, u32[]{:S(2)}) collective-permute-start(bf16[768,768]{1,0:T(8,128)(2,1)} %pad_maximum_fusion.3.refs_0_), channel_id=1, source_target_pairs={{0,16},{16,0},{1,17},{17,1},{2,18},{18,2},{3,19},{19,3},{4,20},{20... | collective-permute-start | bytes 3538952 | tf_op jit(solution)/shard_map/ppermute | solution.py:374
  131.7 78.9 %collective-permute-start.3 = (bf16[768,768]{1,0:T(8,128)(2,1)}, bf16[768,768]{1,0:T(8,128)(2,1)S(1)}, u32[]{:S(2)}, u32[]{:S(2)}) collective-permute-start(bf16[768,768]{1,0:T(8,128)(2,1)} %pad_maximum_fusion.3.refs_0_), channel_id=1, source_target_pairs={{0,1},{1,0},{2,3},{3,2},{4,5},{5,4},{6,7},{7,6},{8,9},{9,8},{10,11... | collective-permute-start | bytes 3538952 | tf_op jit(solution)/shard_map/ppermute | solution.py:382
  131.9 54.9 %collective-permute-start.2 = (bf16[768,768]{1,0:T(8,128)(2,1)}, bf16[768,768]{1,0:T(8,128)(2,1)S(1)}, u32[]{:S(2)}, u32[]{:S(2)}) collective-permute-start(bf16[768,768]{1,0:T(8,128)(2,1)} %collective-permute-done.1.refs_2_), channel_id=1, source_target_pairs={{0,16},{16,0},{1,17},{17,1},{2,18},{18,2},{3,19},{19,3},{4,20},{20... | collective-permute-start | bytes 3538952 | tf_op jit(solution)/shard_map/ppermute | solution.py:374
  151.1 35.0 %collective-permute-start.13 = (bf16[256,768]{1,0:T(8,128)(2,1)}, bf16[256,768]{1,0:T(8,128)(2,1)S(1)}, u32[]{:S(2)}, u32[]{:S(2)}) collective-permute-start(bf16[256,768]{1,0:T(8,128)(2,1)} %get-tuple-element.67), channel_id=1, source_target_pairs={{0,1},{1,0},{2,3},{3,2},{4,5},{5,4},{6,7},{7,6},{8,9},{9,8},{10,11... | collective-permute-start | bytes 1179656 | tf_op jit(solution)/shard_map/ppermute | solution.py:382
  168.3 18.4 %collective-permute-start.19 = (bf16[256,768]{1,0:T(8,128)(2,1)}, bf16[256,768]{1,0:T(8,128)(2,1)S(1)}, u32[]{:S(2)}, u32[]{:S(2)}) collective-permute-start(bf16[256,768]{1,0:T(8,128)(2,1)} %get-tuple-element.69), channel_id=1, source_target_pairs={{0,1},{1,0},{2,3},{3,2},{4,5},{5,4},{6,7},{7,6},{8,9},{9,8},{10,11... | collective-permute-start | bytes 1179656 | tf_op jit(solution)/shard_map/ppermute | solution.py:382
  186.0 24.6 %collective-permute-start.5 = (bf16[768,768]{1,0:T(8,128)(2,1)}, bf16[768,768]{1,0:T(8,128)(2,1)S(1)}, u32[]{:S(2)}, u32[]{:S(2)}) collective-permute-start(bf16[768,768]{1,0:T(8,128)(2,1)} %collective-permute-done.1.refs_2_), channel_id=1, source_target_pairs={{0,1},{1,0},{2,3},{3,2},{4,5},{5,4},{6,7},{7,6},{8,9},{9,8},{10,11... | collective-permute-start | bytes 3538952 | tf_op jit(solution)/shard_map/ppermute | solution.py:382
  186.1 24.6 %collective-permute-start.4 = (bf16[768,768]{1,0:T(8,128)(2,1)S(1)}, bf16[768,768]{1,0:T(8,128)(2,1)S(1)}, u32[]{:S(2)}, u32[]{:S(2)}) collective-permute-start(bf16[768,768]{1,0:T(8,128)(2,1)S(1)} %collective-permute-done.refs_1_), channel_id=1, source_target_pairs={{0,1},{1,0},{2,3},{3,2},{4,5},{5,4},{6,7},{7,6},{8,9},{9,8},{10,11... | collective-permute-start | bytes 3538952 | tf_op jit(solution)/shard_map/ppermute | solution.py:382
  186.7 4.4 collective-permute-start.25
  186.9 23.8 %collective-permute-start.6 = (bf16[768,768]{1,0:T(8,128)(2,1)S(1)}, bf16[768,768]{1,0:T(8,128)(2,1)S(1)}, u32[]{:S(2)}, u32[]{:S(2)}) collective-permute-start(bf16[768,768]{1,0:T(8,128)(2,1)S(1)} %collective-permute-done.2.refs_3_), channel_id=1, source_target_pairs={{0,1},{1,0},{2,3},{3,2},{4,5},{5,4},{6,7},{7,6},{8,9},{9,8},{10,11... | collective-permute-start | bytes 3538952 | tf_op jit(solution)/shard_map/ppermute | solution.py:382
  191.1 6.9 %collective-permute-start.26 = (bf16[128,768]{1,0:T(8,128)(2,1)S(1)}, bf16[128,768]{1,0:T(8,128)(2,1)S(1)}, u32[]{:S(2)}, u32[]{:S(2)}) collective-permute-start(bf16[128,768]{1,0:T(8,128)(2,1)S(1)} %get-tuple-element.211), channel_id=1, source_target_pairs={{0,2},{1,3},{2,0},{3,1},{4,6},{5,7},{6,4},{7,5},{8,10},{9,11},{10,... | collective-permute-start | bytes 589832 | tf_op jit(solution)/shard_map/ppermute | solution.py:378
  198.0 6.1 %collective-permute-start.27 = (bf16[128,768]{1,0:T(8,128)(2,1)S(1)}, bf16[128,768]{1,0:T(8,128)(2,1)S(1)}, u32[]{:S(2)}, u32[]{:S(2)}) collective-permute-start(bf16[128,768]{1,0:T(8,128)(2,1)S(1)} %get-tuple-element.213), channel_id=1, source_target_pairs={{0,2},{1,3},{2,0},{3,1},{4,6},{5,7},{6,4},{7,5},{8,10},{9,11},{10,... | collective-permute-start | bytes 589832 | tf_op jit(solution)/shard_map/ppermute | solution.py:378
  204.1 5.7 collective-permute-start.28
  240.8 33.4 %copy-start.28 = (bf16[128,768]{1,0:T(8,128)(2,1)}, bf16[128,768]{1,0:T(8,128)(2,1)S(1)}, u32[]{:S(2)}) copy-start(bf16[128,768]{1,0:T(8,128)(2,1)S(1)} %get-tuple-element.206.g_own) | copy-start | bytes 589828
  240.8 33.4 %copy-start.29 = (bf16[128,768]{1,0:T(8,128)(2,1)}, bf16[128,768]{1,0:T(8,128)(2,1)S(1)}, u32[]{:S(2)}) copy-start(bf16[128,768]{1,0:T(8,128)(2,1)S(1)} %get-tuple-element.207.g_own) | copy-start | bytes 589828
  240.8 6.2 %collective-permute-start.36 = (bf16[128,768]{1,0:T(8,128)(2,1)S(1)}, bf16[128,768]{1,0:T(8,128)(2,1)S(1)}, u32[]{:S(2)}, u32[]{:S(2)}) collective-permute-start(bf16[128,768]{1,0:T(8,128)(2,1)S(1)} %get-tuple-element.208.g_own), channel_id=1, source_target_pairs={{0,2},{1,3},{2,0},{3,1},{4,6},{5,7},{6,4},{7,5},{8,10},{9,11},{10,... | collective-permute-start | bytes 589832 | tf_op jit(solution)/shard_map/ppermute | solution.py:378
  242.3 6.8 %collective-permute-start.43 = (bf16[128,768]{1,0:T(8,128)(2,1)S(1)}, bf16[128,768]{1,0:T(8,128)(2,1)S(1)}, u32[]{:S(2)}, u32[]{:S(2)}) collective-permute-start(bf16[128,768]{1,0:T(8,128)(2,1)S(1)} %get-tuple-element.207.g_own), channel_id=1, source_target_pairs={{0,2},{1,3},{2,0},{3,1},{4,6},{5,7},{6,4},{7,5},{8,10},{9,11},{10,... | collective-permute-start | bytes 589832 | tf_op jit(solution)/shard_map/ppermute | solution.py:378
  247.0 7.5 %collective-permute-start.37 = (bf16[256,768]{1,0:T(8,128)(2,1)S(1)}, bf16[256,768]{1,0:T(8,128)(2,1)S(1)}, u32[]{:S(2)}, u32[]{:S(2)}) collective-permute-start(bf16[256,768]{1,0:T(8,128)(2,1)S(1)} %pad_maximum_fusion.12), channel_id=1, source_target_pairs={{0,1},{1,0},{2,3},{3,2},{4,5},{5,4},{6,7},{7,6},{8,9},{9,8},{10,11... | collective-permute-start | bytes 1179656 | tf_op jit(solution)/shard_map/ppermute | solution.py:382
  247.1 7.3 %collective-permute-start.29 = (bf16[128,768]{1,0:T(8,128)(2,1)S(1)}, bf16[128,768]{1,0:T(8,128)(2,1)S(1)}, u32[]{:S(2)}, u32[]{:S(2)}) collective-permute-start(bf16[128,768]{1,0:T(8,128)(2,1)S(1)} %get-tuple-element.206.g_own), channel_id=1, source_target_pairs={{0,2},{1,3},{2,0},{3,1},{4,6},{5,7},{6,4},{7,5},{8,10},{9,11},{10,... | collective-permute-start | bytes 589832 | tf_op jit(solution)/shard_map/ppermute | solution.py:378
  248.7 137.7 %collective-permute-start.51 = (bf16[2,2,768,768]{3,2,1,0:T(8,128)(2,1)}, bf16[2,2,768,768]{3,2,1,0:T(8,128)(2,1)}, u32[]{:S(2)}, u32[]{:S(2)}) collective-permute-start(bf16[2,2,768,768]{3,2,1,0:T(8,128)(2,1)} %get-tuple-element.114), channel_id=1, source_target_pairs={{0,1},{1,0},{2,3},{3,2},{4,5},{5,4},{6,7},{7,6},{8,9},{9,8},{10,11... | collective-permute-start | bytes 14155784 | tf_op jit(solution)/shard_map/ppermute | solution.py:382
  249.1 25.6 %collective-permute-start.44 = (bf16[256,768]{1,0:T(8,128)(2,1)S(1)}, bf16[256,768]{1,0:T(8,128)(2,1)S(1)}, u32[]{:S(2)}, u32[]{:S(2)}) collective-permute-start(bf16[256,768]{1,0:T(8,128)(2,1)S(1)} %pad_maximum_fusion.13), channel_id=1, source_target_pairs={{0,1},{1,0},{2,3},{3,2},{4,5},{5,4},{6,7},{7,6},{8,9},{9,8},{10,11... | collective-permute-start | bytes 1179656 | tf_op jit(solution)/shard_map/ppermute | solution.py:382
  254.5 39.8 %collective-permute-start.30 = (bf16[256,768]{1,0:T(8,128)(2,1)S(1)}, bf16[256,768]{1,0:T(8,128)(2,1)S(1)}, u32[]{:S(2)}, u32[]{:S(2)}) collective-permute-start(bf16[256,768]{1,0:T(8,128)(2,1)S(1)} %pad_maximum_fusion.11), channel_id=1, source_target_pairs={{0,1},{1,0},{2,3},{3,2},{4,5},{5,4},{6,7},{7,6},{8,9},{9,8},{10,11... | collective-permute-start | bytes 1179656 | tf_op jit(solution)/shard_map/ppermute | solution.py:382
  274.2 40.1 %collective-permute-start.38 = (bf16[1024,768]{1,0:T(8,128)(2,1)}, bf16[1024,768]{1,0:T(8,128)(2,1)S(1)}, u32[]{:S(2)}, u32[]{:S(2)}) collective-permute-start(bf16[1024,768]{1,0:T(8,128)(2,1)} %get-tuple-element.88), channel_id=1, source_target_pairs={{0,1},{1,0},{2,3},{3,2},{4,5},{5,4},{6,7},{7,6},{8,9},{9,8},{10,11... | collective-permute-start | bytes 4718600 | tf_op jit(solution)/shard_map/ppermute | solution.py:382
  294.2 27.3 %collective-permute-start.45 = (bf16[1024,768]{1,0:T(8,128)(2,1)}, bf16[1024,768]{1,0:T(8,128)(2,1)}, u32[]{:S(2)}, u32[]{:S(2)}) collective-permute-start(bf16[1024,768]{1,0:T(8,128)(2,1)} %get-tuple-element.95), channel_id=1, source_target_pairs={{0,1},{1,0},{2,3},{3,2},{4,5},{5,4},{6,7},{7,6},{8,9},{9,8},{10,11... | collective-permute-start | bytes 4718600 | tf_op jit(solution)/shard_map/ppermute | solution.py:382
  313.8 10.6 %collective-permute-start.31 = (bf16[1024,768]{1,0:T(8,128)(2,1)}, bf16[1024,768]{1,0:T(8,128)(2,1)}, u32[]{:S(2)}, u32[]{:S(2)}) collective-permute-start(bf16[1024,768]{1,0:T(8,128)(2,1)} %get-tuple-element.81), channel_id=1, source_target_pairs={{0,1},{1,0},{2,3},{3,2},{4,5},{5,4},{6,7},{7,6},{8,9},{9,8},{10,11... | collective-permute-start | bytes 4718600 | tf_op jit(solution)/shard_map/ppermute | solution.py:382
  318.7 29.5 %collective-permute-start.39 = (bf16[512,768]{1,0:T(8,128)(2,1)}, bf16[512,768]{1,0:T(8,128)(2,1)}, u32[]{:S(2)}, u32[]{:S(2)}) collective-permute-start(bf16[512,768]{1,0:T(8,128)(2,1)} %slice.479), channel_id=1, source_target_pairs={{0,2},{1,3},{2,0},{3,1},{4,6},{5,7},{6,4},{7,5},{8,10},{9,11},{10,... | collective-permute-start | bytes 2359304 | tf_op jit(solution)/shard_map/ppermute | solution.py:378
  321.2 201.8 %all-gather.7.cloned.1.call-start = ((), (), s32[]{:S(2)}) async-start(), calls=%async_computation.1 | async-start | bytes 2949120 | tf_op jit(solution)/shard_map/all_gather | solution.py:453
  323.8 45.0 %collective-permute-start.46 = (bf16[512,768]{1,0:T(8,128)(2,1)S(1)}, bf16[512,768]{1,0:T(8,128)(2,1)S(1)}, u32[]{:S(2)}, u32[]{:S(2)}) collective-permute-start(bf16[512,768]{1,0:T(8,128)(2,1)S(1)} %slice.478), channel_id=1, source_target_pairs={{0,2},{1,3},{2,0},{3,1},{4,6},{5,7},{6,4},{7,5},{8,10},{9,11},{10,... | collective-permute-start | bytes 2359304 | tf_op jit(solution)/shard_map/ppermute | solution.py:378
  327.1 57.7 %collective-permute-start.32 = (bf16[512,768]{1,0:T(8,128)(2,1)S(1)}, bf16[512,768]{1,0:T(8,128)(2,1)S(1)}, u32[]{:S(2)}, u32[]{:S(2)}) collective-permute-start(bf16[512,768]{1,0:T(8,128)(2,1)S(1)} %slice.480), channel_id=1, source_target_pairs={{0,2},{1,3},{2,0},{3,1},{4,6},{5,7},{6,4},{7,5},{8,10},{9,11},{10,... | collective-permute-start | bytes 2359304 | tf_op jit(solution)/shard_map/ppermute | solution.py:378
  348.2 41.7 %slice-start = ((s8[4718592]{0:T(1024)(128)(4,1)}), s8[4194304]{0:T(1024)(128)(4,1)S(1)}, s32[]{:S(2)}) async-start(s8[4718592]{0:T(1024)(128)(4,1)} %bitcast.72), calls=%async_computation.3 | async-start | bytes 8388608
  350.5 44.4 %collective-permute-start.40 = (bf16[128,768]{1,0:T(8,128)(2,1)}, bf16[128,768]{1,0:T(8,128)(2,1)S(1)}, u32[]{:S(2)}, u32[]{:S(2)}) collective-permute-start(bf16[128,768]{1,0:T(8,128)(2,1)} %get-tuple-element.198), channel_id=1, source_target_pairs={{0,4},{4,8},{8,12},{12,0},{1,5},{5,9},{9,13},{13,1},{2,6},{6,10},{... | collective-permute-start | bytes 589832 | tf_op jit(solution)/shard_map/ppermute | solution.py:374
  350.5 44.9 %collective-permute-start.41 = (bf16[128,768]{1,0:T(8,128)(2,1)}, bf16[128,768]{1,0:T(8,128)(2,1)S(1)}, u32[]{:S(2)}, u32[]{:S(2)}) collective-permute-start(bf16[128,768]{1,0:T(8,128)(2,1)} %get-tuple-element.200), channel_id=1, source_target_pairs={{0,8},{4,12},{8,0},{12,4},{1,9},{5,13},{9,1},{13,5},{2,10},{6,14},... | collective-permute-start | bytes 589832 | tf_op jit(solution)/shard_map/ppermute | solution.py:374
  368.8 26.8 %collective-permute-start.42 = (bf16[128,768]{1,0:T(8,128)(2,1)}, bf16[128,768]{1,0:T(8,128)(2,1)}, u32[]{:S(2)}, u32[]{:S(2)}) collective-permute-start(bf16[128,768]{1,0:T(8,128)(2,1)} %get-tuple-element.199), channel_id=1, source_target_pairs={{0,12},{4,0},{8,4},{12,8},{1,13},{5,1},{9,5},{13,9},{2,14},{6,2},{... | collective-permute-start | bytes 589832 | tf_op jit(solution)/shard_map/ppermute | solution.py:374
  384.7 12.9 %collective-permute-start.47 = (bf16[128,768]{1,0:T(8,128)(2,1)}, bf16[128,768]{1,0:T(8,128)(2,1)}, u32[]{:S(2)}, u32[]{:S(2)}) collective-permute-start(bf16[128,768]{1,0:T(8,128)(2,1)} %get-tuple-element.201), channel_id=1, source_target_pairs={{0,4},{4,8},{8,12},{12,0},{1,5},{5,9},{9,13},{13,1},{2,6},{6,10},{... | collective-permute-start | bytes 589832 | tf_op jit(solution)/shard_map/ppermute | solution.py:374
  386.4 16.7 %collective-permute-start.48 = (bf16[128,768]{1,0:T(8,128)(2,1)}, bf16[128,768]{1,0:T(8,128)(2,1)}, u32[]{:S(2)}, u32[]{:S(2)}) collective-permute-start(bf16[128,768]{1,0:T(8,128)(2,1)} %get-tuple-element.203), channel_id=1, source_target_pairs={{0,8},{4,12},{8,0},{12,4},{1,9},{5,13},{9,1},{13,5},{2,10},{6,14},... | collective-permute-start | bytes 589832 | tf_op jit(solution)/shard_map/ppermute | solution.py:374
  394.9 52.1 %collective-permute-start.52 = (bf16[2,768,768]{2,1,0:T(8,128)(2,1)}, bf16[2,768,768]{2,1,0:T(8,128)(2,1)}, u32[]{:S(2)}, u32[]{:S(2)}) collective-permute-start(bf16[2,768,768]{2,1,0:T(8,128)(2,1)} %fusion.1), channel_id=1, source_target_pairs={{0,16},{16,0},{1,17},{17,1},{2,18},{18,2},{3,19},{19,3},{4,20},{20... | collective-permute-start | bytes 7077896 | tf_op jit(solution)/shard_map/ppermute | solution.py:374
  395.5 14.2 %collective-permute-start.49 = (bf16[128,768]{1,0:T(8,128)(2,1)S(1)}, bf16[128,768]{1,0:T(8,128)(2,1)S(1)}, u32[]{:S(2)}, u32[]{:S(2)}) collective-permute-start(bf16[128,768]{1,0:T(8,128)(2,1)S(1)} %copy-done.40), channel_id=1, source_target_pairs={{0,12},{4,0},{8,4},{12,8},{1,13},{5,1},{9,5},{13,9},{2,14},{6,2},{... | collective-permute-start | bytes 589832 | tf_op jit(solution)/shard_map/ppermute | solution.py:374
  395.6 14.2 %collective-permute-start.33 = (bf16[128,768]{1,0:T(8,128)(2,1)S(1)}, bf16[128,768]{1,0:T(8,128)(2,1)S(1)}, u32[]{:S(2)}, u32[]{:S(2)}) collective-permute-start(bf16[128,768]{1,0:T(8,128)(2,1)S(1)} %get-tuple-element.195), channel_id=1, source_target_pairs={{0,4},{4,8},{8,12},{12,0},{1,5},{5,9},{9,13},{13,1},{2,6},{6,10},{... | collective-permute-start | bytes 589832 | tf_op jit(solution)/shard_map/ppermute | solution.py:374
  397.6 20.5 %collective-permute-start.34 = (bf16[128,768]{1,0:T(8,128)(2,1)S(1)}, bf16[128,768]{1,0:T(8,128)(2,1)S(1)}, u32[]{:S(2)}, u32[]{:S(2)}) collective-permute-start(bf16[128,768]{1,0:T(8,128)(2,1)S(1)} %get-tuple-element.197), channel_id=1, source_target_pairs={{0,8},{4,12},{8,0},{12,4},{1,9},{5,13},{9,1},{13,5},{2,10},{6,14},... | collective-permute-start | bytes 589832 | tf_op jit(solution)/shard_map/ppermute | solution.py:374
  403.1 15.1 %collective-permute-start.35 = (bf16[128,768]{1,0:T(8,128)(2,1)S(1)}, bf16[128,768]{1,0:T(8,128)(2,1)S(1)}, u32[]{:S(2)}, u32[]{:S(2)}) collective-permute-start(bf16[128,768]{1,0:T(8,128)(2,1)S(1)} %get-tuple-element.196), channel_id=1, source_target_pairs={{0,12},{4,0},{8,4},{12,8},{1,13},{5,1},{9,5},{13,9},{2,14},{6,2},{... | collective-permute-start | bytes 589832 | tf_op jit(solution)/shard_map/ppermute | solution.py:374
  420.7 131.1 %all-reduce.3.cloned.1.call-start = ((), (), s32[]{:S(2)}) async-start(), calls=%async_computation.2 | async-start | bytes 3538944 | tf_op jit(solution)/shard_map/psum | solution.py:495
  450.7 25.7 %collective-permute-start.53 = (bf16[768,768]{1,0:T(8,128)(2,1)S(1)}, bf16[768,768]{1,0:T(8,128)(2,1)S(1)}, u32[]{:S(2)}, u32[]{:S(2)}) collective-permute-start(bf16[768,768]{1,0:T(8,128)(2,1)S(1)} %fusion.7), channel_id=1, source_target_pairs={{0,2},{1,3},{2,0},{3,1},{4,6},{5,7},{6,4},{7,5},{8,10},{9,11},{10,... | collective-permute-start | bytes 3538952 | tf_op jit(solution)/shard_map/ppermute | solution.py:378
  452.5 12.7 %collective-permute-start.50 = (bf16[4,192,384]{2,1,0:T(8,128)(2,1)S(1)}, bf16[4,192,384]{2,1,0:T(8,128)(2,1)S(1)}, u32[]{:S(2)}, u32[]{:S(2)}) collective-permute-start(bf16[4,192,384]{2,1,0:T(8,128)(2,1)S(1)} %fusion.8), channel_id=1, source_target_pairs={{0,16},{16,0},{1,17},{17,1},{2,18},{18,2},{3,19},{19,3},{4,20},{20... | collective-permute-start | bytes 1769480 | tf_op jit(solution)/shard_map/ppermute | solution.py:374
  (58 other events, 351.1 us)
Sparse Core Ops, SparseCore 0:
  321.3 36.1 all-gather.4
  420.9 25.4 all-gather.6
Sparse Core Ops, SparseCore 1:
  477.8 73.9 all-reduce.2

commit v2 on v1

v2 whole, which is shorter than its diff:
```python
import functools

import jax
import jax.numpy as jnp
from jax import lax
from jax.experimental import pallas as pl
from jax.experimental.pallas import tpu as pltpu
from jax.sharding import PartitionSpec as P

HEAD_DIM = 64
EPSILON = 1e-05
F32 = jnp.float32
BF16 = jnp.bfloat16
VMEM_LIMIT = 56 << 20
EXTRA = 16
SUMS = 64
SMEM_SPEC = pl.BlockSpec(memory_space=pltpu.SMEM)
ANY_SPEC = pl.BlockSpec(memory_space=pl.ANY)


def nn(a, b):
    return jnp.dot(a, b, preferred_element_type=F32)


def nt(a, b):
    return lax.dot_general(a, b, (((1,), (1,)), ((), ())), preferred_element_type=F32)


def vmem(n):
    return [pl.BlockSpec(memory_space=pltpu.VMEM)] * n


def params():
    return pltpu.CompilerParams(vmem_limit_bytes=VMEM_LIMIT)


def head_lanes(shape, head):
    lane = lax.broadcasted_iota(jnp.int32, shape, len(shape) - 1)
    return (lane >= head * HEAD_DIM) & (lane < (head + 1) * HEAD_DIM)


def divisor(size, most):
    while size % most:
        most //= 2
    return most


def slot_rows(places, slot, size):
    return pl.ds(pl.multiple_of(places[slot] * size, size), size)


def forward_body(heads, index, places, inputs, near, cross, sib, w_four, b_query, b_value, query, key, value, attended, log_total, keep, send, q_heads, own, sem):
    fetch = pltpu.make_async_copy(inputs.at[index], own, sem)
    fetch.start()
    part, width = own.shape
    cols = heads * HEAD_DIM
    quarter = part // 4
    factor = HEAD_DIM**-0.5
    w_query, w_key, w_value, w_out = (w_four.at[i] for i in range(4))
    row = part
    for piece in (near, cross, sib, own):
        size = piece.shape[0]
        if piece is own:
            fetch.wait()
            query[...] = ((nt(own[...], w_query[...]) + b_query[...]).astype(BF16).astype(F32) * factor).astype(BF16)
            row = 0
        step = divisor(size, 512)

        def project(i, carry, piece=piece, row=row, step=step):
            rows = piece[pl.ds(i * step, step), :]
            out = pl.ds(row + i * step, step)
            key[out, :] = nt(rows, w_key[...]).astype(BF16)
            value[out, :] = (nt(rows, w_value[...]) + b_value[...]).astype(BF16)
            return carry

        lax.fori_loop(0, size // step, project, 0)
        row += size
    total = key.shape[0]
    block = divisor(total, 1024)
    for head in range(heads):
        mask = head_lanes((part, cols), head)
        q_heads[head] = jnp.where(mask, query[...].astype(F32), 0.0).astype(BF16)
    ones = jnp.ones((16, block), BF16)

    def attend(i, carry):
        rows = pl.ds(pl.multiple_of(i * block, block), block)
        keys = key[rows, :]
        turned = value[rows, :].T
        out = []
        for head in range(heads):
            top, mixed = carry[head]
            scores = nt(keys, q_heads[head])
            new_top = jnp.maximum(top, jnp.max(scores, axis=0, keepdims=True))
            powers = jnp.exp(scores - new_top).astype(BF16)
            values = jnp.concatenate([turned[head * HEAD_DIM : (head + 1) * HEAD_DIM, :], ones], axis=0)
            out.append((new_top, mixed * jnp.exp(top - new_top) + nn(values, powers)))
        return tuple(out)

    start = tuple((jnp.full((1, part), -jnp.inf, F32), jnp.zeros((HEAD_DIM + 16, part), F32)) for _ in range(heads))
    final = lax.fori_loop(0, total // block, attend, start)
    mixes = []
    logs = []
    for top, mixed in final:
        count = mixed[HEAD_DIM : HEAD_DIM + 1, :]
        mixes.append(mixed[:HEAD_DIM, :] / count)
        logs.append(top + jnp.log(count))
    attended[...] = jnp.concatenate(mixes, axis=0).T.astype(BF16)
    log_total[...] = jnp.concatenate(logs + [jnp.zeros((8 - heads, part), F32)], axis=0)
    for out, first in ((keep, 0), (send, 2)):
        for j in range(2):
            rows = attended[slot_rows(places, first + j, quarter), :]
            out[j * quarter : (j + 1) * quarter, :] = nn(rows, w_out[...]).astype(BF16)


def backward_body(heads, nears, index, places, g_own, g_cross, g_sib, w_four, query, key, value, attended, log_total,
                  d_query, d_key, d_value, keep, send, d_out, sums, grad, q_heads, g_heads, dq_turned):
    part, cols = query.shape
    total = key.shape[0]
    quarter = part // 4
    factor = HEAD_DIM**-0.5
    w_query, w_key, w_value, w_out = (w_four.at[i] for i in range(4))
    begin = index * quarter
    middle = g_own.shape[0]
    grad[slot_rows(places, 0, quarter), :] = g_own[begin : begin + quarter, :]
    grad[slot_rows(places, 1, quarter), :] = g_cross[begin : begin + quarter, :]
    grad[slot_rows(places, 2, quarter), :] = g_sib[begin : begin + quarter, :]
    grad[slot_rows(places, 3, quarter), :] = g_sib[middle + begin : middle + begin + quarter, :]
    grad_heads = nt(grad[...], w_out[...]).astype(BF16)
    att = attended[...]
    d_out[...] = nn(att.T, grad[...])
    product = grad_heads.astype(F32) * att.astype(F32)
    picks = jnp.concatenate(
        [jnp.where(head_lanes((1, cols), h), 1.0, 0.0) for h in range(heads)]
        + [jnp.zeros((8 - heads, cols), F32)], axis=0)
    weighted = lax.dot_general(picks, product, (((1,), (1,)), ((), ())), precision=lax.Precision.HIGHEST,
                               preferred_element_type=F32)
    for h in range(heads):
        mask = head_lanes((part, cols), h)
        q_heads[h] = jnp.where(mask, query[...].astype(F32), 0.0).astype(BF16)
        g_heads[h] = jnp.where(mask, grad_heads.astype(F32), 0.0).astype(BF16)
    dq_turned[...] = jnp.zeros_like(dq_turned)
    block = divisor(total, 1024)

    def chunk(i, carry):
        rows = pl.ds(pl.multiple_of(i * block, block), block)
        keys = key[rows, :]
        values = value[rows, :]
        keys_turned = keys.T
        dk = jnp.zeros((block, cols), F32)
        dv = jnp.zeros((block, cols), F32)
        for h in range(heads):
            scores = nt(keys, q_heads[h])
            probs = jnp.exp(scores - log_total[h : h + 1, :])
            d_probs = nt(values, g_heads[h])
            d_scores = (probs * (d_probs - weighted[h : h + 1, :])).astype(BF16)
            dv = dv + nn(probs.astype(BF16), g_heads[h])
            dk = dk + nn(d_scores, q_heads[h])
            own = slice(h * HEAD_DIM, (h + 1) * HEAD_DIM)
            dq_turned[own, :] += nn(keys_turned[own, :], d_scores)
        d_key[rows, :] = dk.astype(BF16)
        d_value[rows, :] = dv.astype(BF16)
        return carry + jnp.sum(dv.astype(BF16).astype(F32), axis=0, keepdims=True)

    sum_value = lax.fori_loop(0, total // block, chunk, jnp.zeros((1, cols), F32))
    dq = (dq_turned[...] * factor).T.astype(BF16)
    d_query[...] = dq
    sums[...] = jnp.concatenate(
        [jnp.sum(dq.astype(F32), axis=0, keepdims=True), sum_value, jnp.zeros((6, cols), F32)], axis=0)

    def back(rows):
        return nn(d_key[rows, :], w_key[...]) + nn(d_value[rows, :], w_value[...])

    row = part
    for out, first in ((keep, 0), (send, 2)):
        for j in range(2):
            mine = slot_rows(places, first + j, quarter)
            begin = j * (quarter + nears)
            out[begin : begin + quarter, :] = (back(mine) + nn(d_query[mine, :], w_query[...])).astype(BF16)
            out[begin + quarter : begin + quarter + nears, :] = back(pl.ds(row, nears)).astype(BF16)
            row += nears


def attention_forward(places, index, inputs, near, cross, sib, w_four, b_query, b_value):
    part, width = inputs.shape[1:]
    cols = w_four.shape[1]
    heads = cols // HEAD_DIM
    total = part + near.shape[0] + cross.shape[0] + sib.shape[0]
    shape = jax.ShapeDtypeStruct
    return pl.pallas_call(
        functools.partial(forward_body, heads, index),
        out_shape=(
            shape((part, cols), BF16),
            shape((total, cols), BF16),
            shape((total, cols), BF16),
            shape((part, cols), BF16),
            shape((8, part), F32),
            shape((part // 2, width), BF16),
            shape((part // 2, width), BF16),
        ),
        in_specs=[SMEM_SPEC, ANY_SPEC] + vmem(6),
        out_specs=vmem(7),
        scratch_shapes=[pltpu.VMEM((heads, part, cols), BF16), pltpu.VMEM((part, width), BF16), pltpu.SemaphoreType.DMA(())],
        compiler_params=params(),
        cost_estimate=pl.CostEstimate(
            flops=4 * total * width * cols + 16 * heads * part * total * HEAD_DIM,
            bytes_accessed=2 * (total * width + 3 * total * cols),
            transcendentals=heads * part * total,
        ),
        name="attention_forward",
    )(places, inputs, near, cross, sib, w_four, b_query, b_value)


def attention_backward(places, index, g_own, g_cross, g_sib, w_four, query, key, value, attended, log_total):
    part, cols = query.shape
    width = w_four.shape[2]
    heads = cols // HEAD_DIM
    total = key.shape[0]
    nears = (total - part) // 4
    shape = jax.ShapeDtypeStruct
    return pl.pallas_call(
        functools.partial(backward_body, heads, nears, index),
        out_shape=(
            shape((part, cols), BF16),
            shape((total, cols), BF16),
            shape((total, cols), BF16),
            shape((total // 2, width), BF16),
            shape((total // 2, width), BF16),
            shape((cols, width), F32),
            shape((8, cols), F32),
        ),
        in_specs=[SMEM_SPEC] + vmem(9),
        out_specs=vmem(7),
        scratch_shapes=[
            pltpu.VMEM((part, width), BF16),
            pltpu.VMEM((heads, part, cols), BF16),
            pltpu.VMEM((heads, part, cols), BF16),
            pltpu.VMEM((cols, part), F32),
        ],
        compiler_params=params(),
        cost_estimate=pl.CostEstimate(
            flops=4 * total * width * cols + 40 * heads * part * total * HEAD_DIM,
            bytes_accessed=2 * (total * width + 5 * total * cols),
            transcendentals=heads * part * total,
        ),
        name="attention_backward",
    )(places, g_own, g_cross, g_sib, w_four, query, key, value, attended, log_total)


def gradients_body(index, inputs, near, cross, sib, d_query, d_key, d_value, out, own, sem):
    fetch = pltpu.make_async_copy(inputs.at[index], own, sem)
    fetch.start()
    row = own.shape[0]
    for piece in (near, cross, sib, own):
        if piece is own:
            fetch.wait()
            row = 0
        rows = slice(row, row + piece.shape[0])
        for slot, grad in ((1, d_key), (2, d_value)):
            part = nn(grad[rows, :].T, piece[...])
            if piece is near:
                out[slot] = part
            else:
                out[slot] += part
        row += piece.shape[0]
    out[0] = nn(d_query[...].T, own[...])


def attention_gradients(index, inputs, near, cross, sib, d_query, d_key, d_value):
    cols = d_query.shape[1]
    width = inputs.shape[2]
    total = d_key.shape[0]
    return pl.pallas_call(
        functools.partial(gradients_body, index),
        out_shape=jax.ShapeDtypeStruct((3, cols, width), F32),
        in_specs=[ANY_SPEC] + vmem(6),
        out_specs=pl.BlockSpec(memory_space=pltpu.VMEM),
        scratch_shapes=[pltpu.VMEM(inputs.shape[1:], BF16), pltpu.SemaphoreType.DMA(())],
        compiler_params=params(),
        cost_estimate=pl.CostEstimate(
            flops=4 * total * cols * width, bytes_accessed=2 * total * (width + 2 * cols), transcendentals=0
        ),
        name="attention_gradients",
    )(inputs, near, cross, sib, d_query, d_key, d_value)


def rows_mean(a):
    return jnp.mean(a, axis=-1, keepdims=True)


def norm(values):
    centred = values - rows_mean(values)
    inverse = lax.rsqrt(rows_mean(centred * centred) + EPSILON)
    return centred * inverse, inverse


def norm_back(scaled, normed, inverse):
    return inverse * (scaled - rows_mean(scaled) - normed * rows_mean(scaled * normed))


def col_sum(a):
    return jnp.sum(a, axis=0, keepdims=True)


def feed_body(blocks, pieces, seqs, order, cotangents, *refs):
    count = blocks * pieces
    up_pieces, down_pieces, refs = refs[:count], refs[count : 2 * count], refs[2 * count :]
    shard = order[4]
    mine, keeps, gots, rests = (refs[i * seqs : (i + 1) * seqs] for i in range(4))
    vectors, result, grad_first_attn, grad_rest_attn = refs[4 * seqs : 4 * seqs + 4]
    (grad_low, act, d_inner, d_ffn, low, sums,
     up, down, bias, slope, cotangent, sems, cot_sems) = refs[4 * seqs + 4 :]
    rows, width = result.shape
    quarter = rows // seqs
    depth = width // pieces
    copies = []
    for b in range(blocks):
        for p in range(pieces):
            spot = pl.ds(pl.multiple_of(lax.rem(shard + p, pieces) * depth, depth), depth)
            source = up_pieces[b * pieces + p].at[pl.ds(0, depth), :]
            copies.append(pltpu.make_async_copy(source, up.at[b, spot, :], sems.at[b, p, 0]))
            copies.append(pltpu.make_async_copy(down_pieces[b * pieces + p], down.at[b, spot, :], sems.at[b, p, 1]))
        source = up_pieces[b * pieces].at[pl.ds(depth, EXTRA), :]
        copies.append(pltpu.make_async_copy(source, bias.at[b], sems.at[b, pieces, 0]))
    for i in range(seqs):
        source = cotangents.at[i, slot_rows(order, 0, quarter), :]
        copies.append(pltpu.make_async_copy(source, cotangent.at[pl.ds(i * quarter, quarter), :], cot_sems.at[i]))
    for copy in copies:
        copy.start()
    inputs = jnp.concatenate([r[...].astype(F32) for r in mine], axis=0)
    branch = jnp.concatenate(
        [keeps[i][:quarter, :].astype(F32) + gots[i][:quarter, :].astype(F32) + rests[i][...].astype(F32) for i in range(seqs)],
        axis=0)
    b_out, gain_one, bias_one, b_down, gain_two, bias_two = (vectors[i : i + 1, :] for i in range(6))
    pre = inputs + branch + b_out
    normed_one, inverse_one = norm(pre)
    first = normed_one * gain_one + bias_one
    first_low = first.astype(BF16)
    low[...] = first_low
    for copy in copies:
        copy.wait()

    def ahead(b, total):
        parts = bias[b].astype(F32)
        b_hidden = (parts[0:1, :] + parts[1:2, :]) + parts[2:3, :]
        inner = nn(first_low, up[b]) + b_hidden
        shape = 0.5 * (1.0 + lax.erf(inner * (0.5**0.5)))
        act_low = (inner * shape).astype(BF16)
        act[b] = act_low
        slope[b] = shape + inner * (jnp.exp(-0.5 * inner * inner) * 0.3989422804014327)
        return total + nt(act_low, down[b])

    ffn = lax.fori_loop(0, blocks, ahead, jnp.zeros((rows, width), F32))
    normed_two, inverse_two = norm(first + ffn + b_down)
    result[...] = (normed_two * gain_two + bias_two).astype(BF16)
    grad = cotangent[...].astype(F32)
    grad_second = norm_back(grad * gain_two, normed_two, inverse_two)
    grad_ffn = grad_second.astype(BF16)
    d_ffn[...] = grad_ffn

    def astern(b, total):
        grad_inner = (nn(grad_ffn, down[b]) * slope[b]).astype(BF16)
        d_inner[b] = grad_inner
        return total + nt(grad_inner, up[b])

    grad_first = lax.fori_loop(0, blocks, astern, grad_second)
    grad_pre = norm_back(grad_first * gain_one, normed_one, inverse_one)
    grad_low[...] = grad_pre
    grad_first_attn[...] = grad_pre[:quarter, :].astype(BF16)
    grad_rest_attn[...] = grad_pre[quarter:, :].astype(BF16)
    sums[...] = jnp.concatenate(
        [col_sum(grad_pre), col_sum(grad_first * normed_one), col_sum(grad_first), col_sum(grad_second),
         col_sum(grad * normed_two), col_sum(grad), jnp.zeros((2, width), F32)], axis=0)


def feed_forward(order, ups, downs, cotangents, mine, keeps, gots, rests, vectors):
    seqs = len(mine)
    blocks = len(ups)
    pieces = len(ups[0])
    flat = [w for block in ups for w in block] + [w for block in downs for w in block]
    quarter, width = mine[0].shape
    rows = quarter * seqs
    hidden = ups[0][0].shape[-1]
    shape = jax.ShapeDtypeStruct
    return pl.pallas_call(
        functools.partial(feed_body, blocks, pieces, seqs),
        out_shape=(
            shape((rows, width), BF16),
            shape((quarter, width), BF16),
            shape((rows - quarter, width), BF16),
            shape((rows, width), F32),
            shape((blocks, rows, hidden), BF16),
            shape((blocks, rows, hidden), BF16),
            shape((rows, width), BF16),
            shape((rows, width), BF16),
            shape((8, width), F32),
        ),
        in_specs=[SMEM_SPEC] + [ANY_SPEC] * (1 + len(flat)) + vmem(4 * seqs + 1),
        out_specs=vmem(9),
        scratch_shapes=[
            pltpu.VMEM((blocks, width, hidden), BF16),
            pltpu.VMEM((blocks, width, hidden), BF16),
            pltpu.VMEM((blocks, EXTRA, hidden), BF16),
            pltpu.VMEM((blocks, rows, hidden), F32),
            pltpu.VMEM((rows, width), BF16),
            pltpu.SemaphoreType.DMA((blocks, pieces + 1, 2)),
            pltpu.SemaphoreType.DMA((seqs,)),
        ],
        compiler_params=params(),
        cost_estimate=pl.CostEstimate(
            flops=8 * rows * width * hidden * blocks,
            bytes_accessed=6 * width * hidden * blocks,
            transcendentals=2 * rows * hidden * blocks,
        ),
        name="feed_forward",
    )(order, cotangents, *flat, *mine, *keeps, *gots, *rests, vectors)


def feed_gradients_body(pieces, order, act, d_inner, d_ffn, low, sums, ups, downs, low_turned, ffn_turned):
    depth = low.shape[1] // pieces
    hidden = act.shape[-1]
    shard = order[4]
    grad_inner = d_inner[0]

    @pl.when(pl.program_id(0) == 0)
    def _():
        low_turned[...] = low[...].T
        ffn_turned[...] = d_ffn[...].T

    up = nn(low_turned[...], grad_inner)
    down = nn(ffn_turned[...], act[0])
    extra = jnp.concatenate(
        [sums[:6, :], col_sum(grad_inner.astype(F32)), jnp.zeros((SUMS - 7, hidden), F32)], axis=0).astype(BF16)
    for p in range(pieces):
        spot = lax.rem(p - shard + pieces, pieces)
        ups[0, spot, :depth, :] = up[p * depth : (p + 1) * depth, :].astype(BF16)
        ups[0, spot, depth:, :] = extra
        downs[0, spot, :, :] = down[p * depth : (p + 1) * depth, :].astype(BF16)


def feed_gradients(pieces, first, order, act, d_inner, d_ffn, low, sums):
    blocks, rows, hidden = act.shape
    width = low.shape[1]
    depth = width // pieces
    shape = jax.ShapeDtypeStruct
    pick = pl.BlockSpec((1, rows, hidden), lambda i, order: (first + i, 0, 0))
    whole = pl.BlockSpec((rows, width), lambda i, order: (0, 0))
    return pl.pallas_call(
        functools.partial(feed_gradients_body, pieces),
        out_shape=(shape((2, pieces, depth + SUMS, hidden), BF16), shape((2, pieces, depth, hidden), BF16)),
        grid_spec=pltpu.PrefetchScalarGridSpec(
            num_scalar_prefetch=1,
            grid=(2,),
            in_specs=[pick, pick, whole, whole, pl.BlockSpec((8, width), lambda i, order: (0, 0))],
            out_specs=[
                pl.BlockSpec((1, pieces, depth + SUMS, hidden), lambda i, order: (i, 0, 0, 0)),
                pl.BlockSpec((1, pieces, depth, hidden), lambda i, order: (i, 0, 0, 0)),
            ],
            scratch_shapes=[pltpu.VMEM((width, rows), BF16), pltpu.VMEM((width, rows), BF16)],
        ),
        compiler_params=params(),
        cost_estimate=pl.CostEstimate(
            flops=8 * rows * width * hidden, bytes_accessed=8 * width * hidden, transcendentals=0
        ),
        name="feed_gradients",
    )(order, act, d_inner, d_ffn, low, sums)


def rotated(value, axis, count, shift):
    return lax.ppermute(value, axis, [(i, (i + shift) % count) for i in range(count)])


def across(value):
    return lax.ppermute(value, "tensor", [(i, i ^ 2) for i in range(4)])


def sibling(value):
    return lax.ppermute(value, "tensor", [(i, i ^ 1) for i in range(4)])


def stage(*values):
    return lax.optimization_barrier(values)


def added(*values):
    total = values[0].astype(F32)
    for value in values[1:]:
        total = total + value.astype(F32)
    return total


def rounded(value):
    return lax.reduce_precision(value, 8, 7)


def low_sum(*values):
    return added(*values).astype(BF16)


def thirds(value):
    high = value.astype(BF16)
    rest = value - high.astype(F32)
    middle = rest.astype(BF16)
    return high, middle, (rest - middle.astype(F32)).astype(BF16)


def on_device(shards, contexts, inputs, w_query, b_query, w_key, w_value, b_value, w_out, b_out,
              first_gain, first_bias, w_hidden, b_hidden, w_down, b_down, second_gain, second_bias, cotangent):
    seqs, part, width = inputs.shape
    cols = w_query.shape[1]
    quarter = part // 4
    depth = width // shards
    shard = lax.axis_index("shard")
    context = lax.axis_index("context")
    tensor = lax.axis_index("tensor")
    masks = [1 << i for i in range(contexts.bit_length() - 1)]
    hops = len(masks)
    places = jnp.stack([tensor ^ flip for flip in (0, 2, 1, 3)]).astype(jnp.int32)
    order = jnp.concatenate([places, shard[None].astype(jnp.int32)])

    def along(value, mask):
        return lax.ppermute(value, "context", [(i, i ^ mask) for i in range(contexts)])

    def from_shards(value):
        return [rotated(value, "shard", shards, -r) for r in range(1, shards)]

    def to_shards(parts):
        return [rotated(value, "shard", shards, r) for r, value in enumerate(parts, 1)]

    mine = [lax.dynamic_slice_in_dim(inputs[s], tensor * quarter, quarter, axis=0) for s in range(seqs)]
    nears = [[m] for m in mine]
    cross = [None] * seqs
    four = jnp.stack([w_query.T, w_key.T, w_value.T, w_out])
    line = lax.broadcasted_iota(jnp.int32, (EXTRA, w_hidden.shape[1]), 0)
    biases = jnp.zeros((EXTRA, w_hidden.shape[1]), BF16)
    for i, third in enumerate(thirds(b_hidden)):
        biases = jnp.where(line == i, third[None], biases)
    up_own = jnp.concatenate([w_hidden, lax.optimization_barrier(biases)], axis=0)
    down_own = w_down.T
    vectors = jnp.concatenate([b_out, first_gain, first_bias, b_down, second_gain, second_bias]).reshape(6, width)
    up_x = up_y = up_xy = down_x = down_y = down_xy = other = None
    up_beside, down_beside = {}, {}
    saved = [None] * seqs
    sibs = [None] * seqs
    joined = [None] * seqs
    held = [None] * seqs
    gots = []
    rests = []
    rest = None
    four_all = None
    for j in range(hops + 1 + seqs):
        flights = {}
        found = ()
        s = j - hops - 1
        if s >= 0:
            sibs[s] = sibling(jnp.concatenate([joined[s], cross[s]], axis=0))
            if s >= 1:
                gots.append(sibling(held[s - 1][1]))
                rest = low_sum(held[s - 1][0][quarter:], gots[-1][quarter:])
                sibs[s], rest = stage(sibs[s], rest)
                flights["rest"] = across(rest)
            query, key, value, attended, log_total, keep, send = attention_forward(
                places, s, inputs, joined[s], cross[s], sibs[s], four_all, b_query[None], b_value[None])
            saved[s] = (query, key, value, attended, log_total)
            found = (keep, send)
        for q in range(seqs):
            k = j - q
            if 0 <= k < hops:
                flights[f"z{q}"] = along(jnp.concatenate(nears[q], axis=0), masks[hops - 1 - k])
            if k == hops:
                joined[q] = jnp.concatenate(nears[q][1:], axis=0)
                flights[f"x{q}"] = across(joined[q])
        if j == hops - 1:
            flights["up_x"] = across(up_own)
            flights["four"] = from_shards(four)
        if j == hops:
            flights["up_y"] = from_shards(up_own)
        if j == hops + 1:
            flights["down_y"] = from_shards(down_own)
            flights["down_x"] = across(stage(down_own, sibs[0])[0])
        if j == hops + 2:
            flights["up_xy"] = from_shards(up_x)
            flights["up_c"] = sibling(up_own)
        if j == hops + 3:
            flights["down_xy"] = from_shards(down_x)
            flights["down_c"] = sibling(down_own)
        flights, found, four, up_own, down_own, vectors, nears, up_x, up_y, up_xy, down_x, down_y = stage(
            flights, found, four, up_own, down_own, vectors, nears, up_x, up_y, up_xy, down_x, down_y)
        for q in range(seqs):
            if f"z{q}" in flights:
                nears[q] = nears[q] + [flights[f"z{q}"]]
            if f"x{q}" in flights:
                cross[q] = flights[f"x{q}"]
        if s >= 0:
            held[s] = found
            if s >= 1:
                rests.append(flights["rest"])
        if j == hops - 1:
            up_x, other = flights["up_x"], flights["four"]
            if shards == 2:
                left = jnp.where(shard == 0, four, other[0])
                right = jnp.where(shard == 0, other[0], four)
                four_all = jnp.concatenate([left, right], axis=2)
            else:
                four_all = lax.all_gather(four, "shard", axis=2, tiled=True)
        if j == hops:
            up_y = flights["up_y"]
        if j == hops + 1:
            down_x, down_y = flights["down_x"], flights["down_y"]
        if j == hops + 2:
            up_xy, up_c = flights["up_xy"], flights["up_c"]
        if j == hops + 3:
            down_xy, down_c = flights["down_xy"], flights["down_c"]
    gots.append(sibling(held[seqs - 1][1]))
    rests.append(across(low_sum(held[seqs - 1][0][quarter:], gots[-1][quarter:])))
    ups = [[up_own] + up_y, [up_x] + up_xy, [up_c] + [sibling(w) for w in up_y], [sibling(w) for w in [up_x] + up_xy]]
    downs = [[down_own] + down_y, [down_x] + down_xy, [down_c] + [sibling(w) for w in down_y],
             [sibling(w) for w in [down_x] + down_xy]]
    result, g_first, g_rest, grad_low, act, d_inner, d_ffn, low, sums = feed_forward(
        order, ups, downs, cotangent, mine, [h[0] for h in held], gots, rests, vectors)

    up_send, down_send = feed_gradients(shards, 2, order, act, d_inner, d_ffn, low, sums)
    g_first_x, up_send, down_send, d_inner, g_rest = stage(across(g_first), up_send, down_send, d_inner, g_rest)
    up_keep, down_keep = feed_gradients(shards, 0, order, act, d_inner, d_ffn, low, sums)
    g_first_c, g_rest_x, up_got, down_got, up_keep, down_keep, result = stage(
        sibling(jnp.concatenate([g_first, g_first_x], axis=0)), across(g_rest),
        sibling(up_send), sibling(down_send), up_keep, down_keep, result)
    up_leave = low_sum(up_keep[1], up_got[1])
    down_leave = [low_sum(down_keep[:, r], down_got[:, r]) for r in range(1, shards)]
    up_pair = rounded(added(up_keep[0], up_got[0]))
    down_pair = rounded(added(down_keep[:, 0], down_got[:, 0]))

    def project(s, found):
        return attention_gradients(s, inputs, joined[s], cross[s], sibs[s], *found[:3])

    def leaving(terms):
        half = terms[-1].shape[0] // 2
        return low_sum(*[t[half : 2 * half] for t in terms])

    def settle(s, terms):
        return low_sum(grad_low[s * quarter : (s + 1) * quarter], *[t[:quarter] for t in terms])

    def paired(parts):
        own = parts.reshape(parts.shape[0] // quarter, quarter, width)
        return own, across(own)

    def whole(own, swapped):
        count = own.shape[0]
        beside = sibling(jnp.stack([own, swapped]))
        row, side = tensor // 2, tensor % 2
        blocks = []
        for r in range(2):
            for c in range(2):
                here = jnp.where(side == c, own, beside[0])
                there = jnp.where(side == c, swapped, beside[1])
                blocks.append(jnp.where(row == r, here, there))
        return jnp.stack(blocks, axis=1).reshape(count, part, width)

    def split(value, mask):
        half = value.shape[0] // 2
        bit = (context & mask) // mask
        stay = lax.dynamic_slice_in_dim(value, bit * half, half, axis=0)
        return stay, lax.dynamic_slice_in_dim(value, (1 - bit) * half, half, axis=0).astype(BF16)

    def join(value, got, mask):
        lower = (context & mask) == 0
        return jnp.concatenate([jnp.where(lower, value, got), jnp.where(lower, got, value)], axis=0)

    columns = []
    outs = []
    projections = []

    def work(s, *gradient):
        found = attention_backward(places, max(s - 1, 0), *gradient, four_all, *saved[s])
        columns.append(found[6])
        outs.append(found[5])
        return found

    g_first, up_leave, down_leave = stage(g_first, up_leave, down_leave)
    found = work(0, g_first, g_first_x, g_first_c)
    up_far, down_far, g_rest_c, projection, keep, send = stage(
        across(up_leave), to_shards(down_leave), sibling(jnp.concatenate([g_rest, g_rest_x], axis=0)),
        project(0, found), found[3], found[4])
    projections.append(projection)
    got = sibling(send)
    up_leave = [low_sum(up_pair[r], up_far[r]) for r in range(1, shards)]
    down_leave = low_sum(down_pair[1], *[d[1] for d in down_far])
    up_pair = rounded(added(up_pair[0], up_far[0]))
    down_pair = rounded(added(down_pair[0], *[d[0] for d in down_far]))
    terms0 = [keep, got]
    leave = leaving(terms0)
    g_rest, leave, up_leave, down_leave = stage(g_rest, leave, up_leave, down_leave)
    found = work(1, g_rest, g_rest_x, g_rest_c)
    up_far, down_far, found = stage(to_shards(up_leave), across(down_leave), found)
    feed = jnp.concatenate([low_sum(up_pair, *up_far), low_sum(down_pair, down_far)], axis=0)
    feed_stay, feed_leave = split(feed, masks[0])
    flight, projection, keep, send, feed_stay, feed_leave = stage(
        across(leave), project(1, found), found[3], found[4], feed_stay, feed_leave)
    projections.append(projection)
    terms0 = terms0 + [flight]
    z_leave = leaving(terms0)
    terms1 = [keep, sibling(send)]
    leave = leaving(terms1)
    g_rest, leave, z_leave = stage(g_rest, leave, z_leave)
    found = work(2, g_rest, g_rest_x, g_rest_c)
    flight, z0, feed_got, found = stage(across(leave), along(z_leave, masks[0]), along(feed_leave, masks[0]), found)
    terms0 = terms0 + [z0]
    terms1 = terms1 + [flight]
    z0_leave, z1_leave = leaving(terms0), leaving(terms1)
    feed_parts = split(low_sum(feed_stay, feed_got), masks[1])
    got = sibling(found[4])
    found, z0_leave, z1_leave = stage(found, z0_leave, z1_leave)
    terms1 = terms1 + [along(z1_leave, masks[0])]
    terms0 = terms0 + [along(z0_leave, masks[1])]
    projections.append(project(2, found))
    got, projections[2] = stage(got, projections[2])
    terms2 = [found[3], got]
    leave = leaving(terms2)
    half = leave.shape[0] // 2
    flight_first = across(leave[half:])
    flight = across(leave[:half])

    def scatter(parts, hop):
        return parts[0], along(parts[1], masks[hop])

    def collect(value, hop):
        return along(value, masks[hop])

    def merge(value, got, hop):
        return join(value, got, masks[hop])

    feed_parts, leave = stage(feed_parts, leave)
    feed = scatter(feed_parts, 1)
    projected = jnp.concatenate([added(*projections), added(*outs)[None]], axis=0)
    biases = added(*columns)[:2].reshape(-1)
    lines = EXTRA * contexts
    biases = jnp.pad(biases, (0, lines * depth - biases.shape[0])).reshape(lines, depth)

    def lined(value):
        return jnp.concatenate([value.reshape(4 * cols, depth), biases], axis=0).astype(BF16)

    if shards == 2:
        left, right = projected[..., :depth], projected[..., depth:]
        staying = lined(jnp.where(shard == 0, left, right))
        attn = (staying, rotated(lined(jnp.where(shard == 0, right, left)), "shard", 2, 1))
    else:
        stacked = jnp.stack([lined(projected[..., r * depth : (r + 1) * depth]) for r in range(shards)])
        attn = (lax.psum_scatter(stacked, "shard", scatter_dimension=0),)
    terms1, staying = stage(terms1, attn[0])
    attn = (staying,) + attn[1:]
    z1_leave = leaving(terms1)
    terms1 = terms1 + [along(z1_leave, masks[1])]
    flight_first, z1_leave = stage(flight_first, z1_leave)
    z2_leave = leaving([t[: 2 * half] for t in terms2[:2]] + [jnp.concatenate([flight_first, flight_first], axis=0)])
    z2 = along(z2_leave, masks[0])
    terms0, feed, z2_leave = stage(terms0, feed, z2_leave)
    early = [settle(0, terms0)]
    feed = low_sum(*feed)
    feed_got = collect(feed, hops - 1)
    attn, early, feed = stage(attn, early, feed)
    attn = split(low_sum(*attn), masks[0])
    attn_got = along(attn[1], masks[0])
    terms1, attn_leave = stage(terms1, attn[1])
    early = jnp.concatenate(early + [settle(1, terms1)], axis=0)
    early_x = paired(early)[1]
    result, early = stage(result, early)
    result_x = paired(result)[1]
    z2, flight, early = stage(z2, flight, early)
    terms2 = terms2 + [flight, z2]
    z2_leave = leaving(terms2)
    z2 = along(z2_leave, masks[1])
    attn_got, z2_leave = stage(attn_got, z2_leave)
    attn = split(low_sum(attn[0], attn_got), masks[1])
    attn_got = along(attn[1], masks[1])
    feed_got, early_x, attn_leave = stage(feed_got, early_x, attn[1])
    feed = merge(feed, feed_got, hops - 1)
    feed_got = collect(feed, 0)
    z2, feed, early_x = stage(z2, feed, early_x)
    last = settle(2, terms2 + [z2])
    last_x = paired(last)[1]
    attn_got, last = stage(attn_got, last)
    attn = low_sum(attn[0], attn_got)
    attn_got = collect(attn, 1)
    result_x, attn, early, early_x = stage(result_x, attn, early, early_x)
    early = whole(early.reshape(early_x.shape), early_x)
    last_x, attn_got, early = stage(last_x, attn_got, early)
    attn = merge(attn, attn_got, 1)
    attn_got = collect(attn, 0)
    last = whole(last.reshape(last_x.shape), last_x)
    feed_got, last = stage(feed_got, last)
    feed = merge(feed, feed_got, 0)
    outputs = whole(result.reshape(result_x.shape), result_x)
    attn_got, outputs, last, feed = stage(attn_got, outputs, last, feed)
    attn = merge(attn, attn_got, 0)
    input_grad = jnp.concatenate([early, last], axis=0)

    feed, attn = feed.astype(F32), attn.astype(F32)
    vector_sums = feed[depth : depth + 7]
    bias_sums = attn[4 * cols :].reshape(-1)[: 2 * cols]
    matrices = attn[: 4 * cols].reshape(4, cols, depth)
    return (
        outputs,
        input_grad,
        matrices[0].T,
        bias_sums[:cols],
        matrices[1].T,
        matrices[2].T,
        bias_sums[cols:],
        matrices[3],
        vector_sums[0],
        vector_sums[1],
        vector_sums[2],
        feed[:depth],
        vector_sums[6],
        feed[depth + SUMS :].T,
        vector_sums[3],
        vector_sums[4],
        vector_sums[5],
    )


def solution(mesh):
    shards = mesh.shape["shard"]
    contexts = mesh.shape["context"]
    rows = P("shard", "context", None)
    into = P("shard", "tensor")
    onto = P("tensor", "shard")
    heads = P("tensor")
    return jax.shard_map(
        functools.partial(on_device, shards, contexts),
        mesh=mesh,
        in_specs=(rows, into, heads, into, into, heads, onto, P(), P(), P(), into, heads, onto, P(), P(), P(), rows),
        out_specs=(rows, rows, into, heads, into, into, heads, onto, P(), P(), P(), into, heads, onto, P(), P(), P()),
        check_vma=False,
    )
```

time: 576 us -> 410 us (0.71)
  waiting for transfers between devices: 191 us -> 124 us
  blocking collectives: 50.9 us -> 0 us
  local copies, waits for them, and re-layouts: 46.7 us -> 20.3 us
  between operations: 17 us -> 2.31 us
  Pallas kernels: 152 us -> 140 us
  other arithmetic: 44.8 us -> 52.9 us
    ppermute x0 -> x20, waiting for transfers between devices: none -> 79.9 us  [along(): lax.ppermute(value, 'context', [(i, i ^ mask) for i in range(contexts)])]
    ppermute x14 -> x19, waiting for transfers between devices: 113 us -> 34.2 us  [across(): return lax.ppermute(value, 'tensor', [(i, i ^ 2) for i in range(4)])]
    psum x1 -> x0, blocking collectives: 41 us -> none  [on_device(): packed = lax.psum(packed, ('shard', 'context', 'tensor'))]
    ppermute x23 -> x8, waiting for transfers between devices: 45 us -> 5.15 us  [rotated(): lax.ppermute(value, axis, [(i, (i + shift) % count) for i in range(count)])]
    ppermute x23 -> x8, starting transfers between devices: 45.8 us -> 10.4 us  [rotated(): lax.ppermute(value, axis, [(i, (i + shift) % count) for i in range(count)])]
    ppermute x0 -> x20, starting transfers between devices: none -> 31.2 us  [along(): lax.ppermute(value, 'context', [(i, i ^ mask) for i in range(contexts)])]
    psum x1 -> x0, waiting for transfers between devices: 28.8 us -> none  [on_device(): attn_sum = lax.psum(attn_sum.astype(BF16), 'context').astype(F32)]
    convert_element_type x5 -> x28, other arithmetic: 5.37 us -> 28.9 us  [the longest x25 28.6 us: low_sum(): return added(*values).astype(BF16)]
  transfers between devices with their start and end apart: 57 -> 71, of which waited for: 21 -> 32; matrix products, arithmetic and copies ran while one was open for 11% -> 12% of each run, Pallas kernels for 22% -> 29%
where the time goes in v2:
time: 410 us; the launch traced here: 406 us
  Pallas kernels  140 us (34%)
  waiting for transfers between devices  124 us (30%)
  starting transfers between devices  66.7 us (16%)
  other arithmetic  52.9 us (13%)
  local copies, waits for them, and re-layouts  20.3 us (5%)
    ppermute x20, waiting for transfers between devices, along(): lax.ppermute(value, 'context', [(i, i ^ mask) for i in range(contexts)])  79.9 us
    pallas_call x3, Pallas kernels, attention_backward(): pl.pallas_call(functools.partial(backward_body, heads, nears, index), out...  46 us
    pallas_call x3, Pallas kernels, attention_forward(): pl.pallas_call(functools.partial(forward_body, heads, index), out_shape=(...  41.6 us
    ppermute x19, waiting for transfers between devices, across(): return lax.ppermute(value, 'tensor', [(i, i ^ 2) for i in range(4)])  34.2 us
    ppermute x20, starting transfers between devices, along(): lax.ppermute(value, 'context', [(i, i ^ mask) for i in range(contexts)])  31.2 us
    convert_element_type x25, other arithmetic, low_sum(): return added(*values).astype(BF16)  28.6 us
    pallas_call x1, Pallas kernels, feed_forward(): pl.pallas_call(functools.partial(feed_body, blocks, pieces, seqs), out_sh...  21.1 us
    ppermute x19, starting transfers between devices, across(): return lax.ppermute(value, 'tensor', [(i, i ^ 2) for i in range(4)])  21.1 us
  transfers between devices with their start and end apart: 71, of which 32 were waited for; matrix products, arithmetic and copies ran while one was open for 12% of the time, Pallas kernels for 29%

profile of v2, /device:TPU:0, one launch (start us, length us, event | category | flops | bytes accessed | tf_op | source)
XLA Modules:
  0.0 406.1 jit_solution(11960401931203122301)
XLA Ops:
  0.7 1.8 fusion.27
  2.6 4.1 %collective-permute-start = (bf16[128,768]{1,0:T(8,128)(2,1)S(1)}, bf16[128,768]{1,0:T(8,128)(2,1)S(1)}, u32[]{:S(2)}, u32[]{:S(2)}) collective-permute-start(bf16[128,768]{1,0:T(8,128)(2,1)S(1)} %dynamic-slice_bitcast_fusion.2.refs_16_), channel_id=1, source_target_pairs={{0,8},{4,12},{8,0},{12,4},{1,9},{5,13},{9,1},{13,5},{2,10},{6,14},... | collective-permute-start | bytes 589832 | tf_op jit(solution)/shard_map/ppermute | solution.py:521
  11.3 4.5 %collective-permute-done = bf16[128,768]{1,0:T(8,128)(2,1)S(1)} collective-permute-done((bf16[128,768]{1,0:T(8,128)(2,1)S(1)}, bf16[128,768]{1,0:T(8,128)(2,1)S(1)}, u32[]{:S(2)}, u32[]{:S(2)}) %collective-permute-start) | collective-permute-done | bytes 196640 | tf_op jit(solution)/shard_map/ppermute | solution.py:521
  19.7 3.4 collective-permute-start.4
  23.0 8.8 %collective-permute-done.4 = bf16[128,768]{1,0:T(8,128)(2,1)S(1)} collective-permute-done((bf16[128,768]{1,0:T(8,128)(2,1)S(1)}, bf16[128,768]{1,0:T(8,128)(2,1)S(1)}, u32[]{:S(2)}, u32[]{:S(2)}) %collective-permute-start.4) | collective-permute-done | bytes 196640 | tf_op jit(solution)/shard_map/ppermute | solution.py:521
  34.2 3.2 collective-permute-start.7
  37.3 1.8 collective-permute-start.8
  39.1 9.3 %collective-permute-done.8 = bf16[128,768]{1,0:T(8,128)(2,1)S(1)} collective-permute-done((bf16[128,768]{1,0:T(8,128)(2,1)S(1)}, bf16[128,768]{1,0:T(8,128)(2,1)S(1)}, u32[]{:S(2)}, u32[]{:S(2)}) %collective-permute-start.8) | collective-permute-done | bytes 196640 | tf_op jit(solution)/shard_map/ppermute | solution.py:521
  52.3 1.6 collective-permute-start.12
  57.0 2.0 collective-permute-start.13
  59.1 13.9 %attention_forward.3 = (bf16[512,192]{1,0:T(8,128)(2,1)}, bf16[2048,192]{1,0:T(8,128)(2,1)}, bf16[2048,192]{1,0:T(8,128)(2,1)}, bf16[512,192]{1,0:T(8,128)(2,1)}...) custom-call(s32[4]{0:T(128)} %pad_add_fusion.places, bf16[3,512,768]{2,1,0:T(8,128)(2,1)} %inputs.11, ...), custom_call_target="tpu_custom_call" | custom-call | flops 4429185024 | bytes 5505024 | tf_op jit(solution)/shard_map/attention_forward/pallas_call | solution.py:189
  73.0 7.8 %collective-permute-done.10.refs_10_ = bf16[384,768]{1,0:T(8,128)(2,1)} collective-permute-done((bf16[384,768]{1,0:T(8,128)(2,1)S(1)}, bf16[384,768]{1,0:T(8,128)(2,1)}, u32[]{:S(2)}, u32[]{:S(2)}) %collective-permute-start.10) | collective-permute-done | bytes 589856 | tf_op jit(solution)/shard_map/ppermute | solution.py:473
  81.6 1.6 collective-permute-start.19
  86.0 13.8 %attention_forward.4 = (bf16[512,192]{1,0:T(8,128)(2,1)}, bf16[2048,192]{1,0:T(8,128)(2,1)}, bf16[2048,192]{1,0:T(8,128)(2,1)}, bf16[512,192]{1,0:T(8,128)(2,1)}...) custom-call(s32[4]{0:T(128)} %pad_add_fusion.places, bf16[3,512,768]{2,1,0:T(8,128)(2,1)} %inputs.11, ...), custom_call_target="tpu_custom_call" | custom-call | flops 4429185024 | bytes 5505024 | tf_op jit(solution)/shard_map/attention_forward/pallas_call | solution.py:189
  106.4 13.9 %attention_forward.5 = (bf16[512,192]{1,0:T(8,128)(2,1)}, bf16[2048,192]{1,0:T(8,128)(2,1)}, bf16[2048,192]{1,0:T(8,128)(2,1)}, bf16[512,192]{1,0:T(8,128)(2,1)}...) custom-call(s32[4]{0:T(128)} %pad_add_fusion.places, bf16[3,512,768]{2,1,0:T(8,128)(2,1)} %inputs.11, ...), custom_call_target="tpu_custom_call" | custom-call | flops 4429185024 | bytes 5505024 | tf_op jit(solution)/shard_map/attention_forward/pallas_call | solution.py:189
  125.2 5.3 %collective-permute-done.32.refs_27_ = bf16[128,768]{1,0:T(8,128)(2,1)S(1)} collective-permute-done((bf16[128,768]{1,0:T(8,128)(2,1)S(1)}, bf16[128,768]{1,0:T(8,128)(2,1)S(1)}, u32[]{:S(2)}, u32[]{:S(2)}) %collective-permute-start.32) | collective-permute-done | bytes 196640 | tf_op jit(solution)/shard_map/ppermute | solution.py:473
  135.6 21.1 %feed_forward.1 = (bf16[384,768]{1,0:T(8,128)(2,1)}, bf16[128,768]{1,0:T(8,128)(2,1)}, bf16[256,768]{1,0:T(8,128)(2,1)}, f32[384,768]{1,0:T(8,128)}, bf16[4,384,...) custom-call(s32[5]{0:T(128)} %concatenate.81.order, ...), custom_call_target="tpu_custom_call" | custom-call | flops 7247757312 | bytes 14155776 | tf_op jit(solution)/shard_map/feed_forward/pallas_call | solution.py:384
  157.8 7.0 %feed_gradients.2 = (bf16[2,2,448,768]{3,2,1,0:T(8,128)(2,1)}, bf16[2,2,384,768]{3,2,1,0:T(8,128)(2,1)}) custom-call(s32[5]{0:T(128)} %concatenate.81.order, bf16[4,384,768]{2,1,0:T(8,128)(2,1)} %get-tuple-element.330.act, bf16[4,384,768]{2,1,0:T(8,128)(2,1)} %get-tuple-element.342.d_inner, bf16[384,768]{1,0:T(8,128)(2,1)} %get-tuple-element.332.d_ffn, ...), custom_call_target="tpu_custom_call" | custom-call | flops 1811939328 | bytes 4718592 | tf_op jit(solution)/shard_map/feed_gradients/pallas_call | solution.py:447
  164.9 2.0 copy.35
  168.6 7.4 %feed_gradients.3 = (bf16[2,2,448,768]{3,2,1,0:T(8,128)(2,1)}, bf16[2,2,384,768]{3,2,1,0:T(8,128)(2,1)}) custom-call(s32[5]{0:T(128)} %concatenate.81.order, bf16[4,384,768]{2,1,0:T(8,128)(2,1)} %get-tuple-element.330.act, bf16[4,384,768]{2,1,0:T(8,128)(2,1)} %get-tuple-element.342.d_inner, bf16[384,768]{1,0:T(8,128)(2,1)} %get-tuple-element.332.d_ffn, ...), custom_call_target="tpu_custom_call" | custom-call | flops 1811939328 | bytes 4718592 | tf_op jit(solution)/shard_map/feed_gradients/pallas_call | solution.py:447
  176.0 3.0 collective-permute-done.35.g_cross
  179.0 3.1 fusion.9
  185.6 15.2 %attention_backward.3 = (bf16[512,192]{1,0:T(8,128)(2,1)}, bf16[2048,192]{1,0:T(8,128)(2,1)}, bf16[2048,192]{1,0:T(8,128)(2,1)}, bf16[1024,768]{1,0:T(8,128)(2,1...) custom-call(s32[4]{0:T(128)} %pad_add_fusion.places, ...), custom_call_target="tpu_custom_call" | custom-call | flops 9261023232 | bytes 7077888 | tf_op jit(solution)/shard_map/attention_backward/pallas_call | solution.py:220
  200.8 5.4 %attention_gradients.3 = f32[3,192,768]{2,1,0:T(8,128)} custom-call(bf16[3,512,768]{2,1,0:T(8,128)(2,1)} %inputs.11, bf16[384,768]{1,0:T(8,128)(2,1)} %copy-done.25, bf16[384,768]{1,0:T(8,128)(2,1)} %copy-done.8, bf16[768,768]{1,0:T(8,128)(2,1)} %copy-done.23, bf16[512,192]{1,0:T(8,128)(2,1)} %get-tuple-element.361.d_query, ...), custom_call_target="tpu_custom_call" | custom-call | flops 1207959552 | bytes 4718592 | tf_op jit(solution)/shard_map/attention_gradients/pallas_call | solution.py:272
  206.2 5.1 %collective-permute-done.39 = bf16[2,384,768]{2,1,0:T(8,128)(2,1)} collective-permute-done((bf16[2,384,768]{2,1,0:T(8,128)(2,1)}, bf16[2,384,768]{2,1,0:T(8,128)(2,1)}, u32[]{:S(2)}, u32[]{:S(2)}) %collective-permute-start.39) | collective-permute-done | bytes 1179680 | tf_op jit(solution)/shard_map/ppermute | solution.py:469
  211.4 3.2 collective-permute-done.38
  215.7 1.9 fusion
  217.6 2.1 fusion.21
  221.1 2.3 add_convert_fusion.4
  223.4 1.6 collective-permute-start.43
  227.0 15.4 %attention_backward.4 = (bf16[512,192]{1,0:T(8,128)(2,1)}, bf16[2048,192]{1,0:T(8,128)(2,1)}, bf16[2048,192]{1,0:T(8,128)(2,1)}, bf16[1024,768]{1,0:T(8,128)(2,1...) custom-call(s32[4]{0:T(128)} %pad_add_fusion.places, ...), custom_call_target="tpu_custom_call" | custom-call | flops 9261023232 | bytes 7077888 | tf_op jit(solution)/shard_map/attention_backward/pallas_call | solution.py:220
  243.5 5.5 %attention_gradients.4 = f32[3,192,768]{2,1,0:T(8,128)} custom-call(bf16[3,512,768]{2,1,0:T(8,128)(2,1)} %inputs.11, bf16[384,768]{1,0:T(8,128)(2,1)} %copy-done.26, bf16[384,768]{1,0:T(8,128)(2,1)} %copy-done.7, bf16[768,768]{1,0:T(8,128)(2,1)} %copy-done.22, bf16[512,192]{1,0:T(8,128)(2,1)} %get-tuple-element.387.d_query, ...), custom_call_target="tpu_custom_call" | custom-call | flops 1207959552 | bytes 4718592 | tf_op jit(solution)/shard_map/attention_gradients/pallas_call | solution.py:272
  249.0 1.6 fusion.15
  251.2 2.6 fusion.19
  253.8 3.7 collective-permute-done.42
  257.5 1.8 collective-permute-start.48
  259.3 1.9 add_convert_fusion.9
  261.2 2.3 add_convert_fusion.3
  264.5 1.8 collective-permute-start.47
  266.3 15.4 %attention_backward.5 = (bf16[512,192]{1,0:T(8,128)(2,1)}, bf16[2048,192]{1,0:T(8,128)(2,1)}, bf16[2048,192]{1,0:T(8,128)(2,1)}, bf16[1024,768]{1,0:T(8,128)(2,1...) custom-call(s32[4]{0:T(128)} %pad_add_fusion.places, ...), custom_call_target="tpu_custom_call" | custom-call | flops 9261023232 | bytes 7077888 | tf_op jit(solution)/shard_map/attention_backward/pallas_call | solution.py:220
  283.5 1.6 add_bitcast_fusion
  285.2 1.7 add_convert_fusion.17
  286.9 2.0 add_convert_fusion.8
  288.9 1.8 collective-permute-start.49
  290.6 1.7 collective-permute-start.52
  292.4 5.6 %attention_gradients.5 = f32[3,192,768]{2,1,0:T(8,128)} custom-call(bf16[3,512,768]{2,1,0:T(8,128)(2,1)} %inputs.11, bf16[384,768]{1,0:T(8,128)(2,1)} %copy-done.27, bf16[384,768]{1,0:T(8,128)(2,1)} %copy-done.6, bf16[768,768]{1,0:T(8,128)(2,1)} %copy-done.21, bf16[512,192]{1,0:T(8,128)(2,1)} %get-tuple-element.423.d_query, ...), custom_call_target="tpu_custom_call" | custom-call | flops 1207959552 | bytes 4718592 | tf_op jit(solution)/shard_map/attention_gradients/pallas_call | solution.py:272
  302.7 2.1 collective-permute-done.49
  307.7 1.9 collective-permute-start.55
  309.6 2.4 collective-permute-done.54
  315.3 11.2 %collective-permute-done.53 = bf16[208,768]{1,0:T(8,128)(2,1)S(1)} collective-permute-done((bf16[208,768]{1,0:T(8,128)(2,1)S(1)}, bf16[208,768]{1,0:T(8,128)(2,1)S(1)}, u32[]{:S(2)}, u32[]{:S(2)}) %collective-permute-start.53) | collective-permute-done | bytes 319520 | tf_op jit(solution)/shard_map/ppermute | solution.py:521
  328.1 2.3 collective-permute-start.57
  330.4 7.2 %collective-permute-done.55 = bf16[128,768]{1,0:T(8,128)(2,1)S(1)} collective-permute-done((bf16[128,768]{1,0:T(8,128)(2,1)S(1)}, bf16[128,768]{1,0:T(8,128)(2,1)S(1)}, u32[]{:S(2)}, u32[]{:S(2)}) %collective-permute-start.55) | collective-permute-done | bytes 196640 | tf_op jit(solution)/shard_map/ppermute | solution.py:521
  342.0 7.1 %collective-permute-done.57 = bf16[416,384]{1,0:T(8,128)(2,1)S(1)} collective-permute-done((bf16[416,384]{1,0:T(8,128)(2,1)S(1)}, bf16[416,384]{1,0:T(8,128)(2,1)S(1)}, u32[]{:S(2)}, u32[]{:S(2)}) %collective-permute-start.57) | collective-permute-done | bytes 319520 | tf_op jit(solution)/shard_map/ppermute | solution.py:521
  349.3 1.6 collective-permute-done.63
  351.0 4.8 %collective-permute-done.61 = bf16[128,768]{1,0:T(8,128)(2,1)S(1)} collective-permute-done((bf16[128,768]{1,0:T(8,128)(2,1)S(1)}, bf16[128,768]{1,0:T(8,128)(2,1)S(1)}, u32[]{:S(2)}, u32[]{:S(2)}) %collective-permute-start.61) | collective-permute-done | bytes 196640 | tf_op jit(solution)/shard_map/ppermute | solution.py:521
  356.9 2.3 collective-permute-done.60
  359.3 2.4 collective-permute-done.56
  366.9 3.1 collective-permute-done.64
  370.0 3.9 collective-permute-done.65
  375.8 2.1 collective-permute-start.67
  378.1 13.9 %collective-permute-done.69 = bf16[416,768]{1,0:T(8,128)(2,1)S(1)} collective-permute-done((bf16[416,768]{1,0:T(8,128)(2,1)S(1)}, bf16[416,768]{1,0:T(8,128)(2,1)S(1)}, u32[]{:S(2)}, u32[]{:S(2)}) %collective-permute-start.69) | collective-permute-done | bytes 639008 | tf_op jit(solution)/shard_map/ppermute | solution.py:521
  393.7 1.6 copy.39
  395.5 2.8 collective-permute-done.67
  404.2 1.6 pad_maximum_fusion.1
  (344 shorter events, 86.0 us)
Async XLA Ops:
  2.6 13.2 %collective-permute-start = (bf16[128,768]{1,0:T(8,128)(2,1)S(1)}, bf16[128,768]{1,0:T(8,128)(2,1)S(1)}, u32[]{:S(2)}, u32[]{:S(2)}) collective-permute-start(bf16[128,768]{1,0:T(8,128)(2,1)S(1)} %dynamic-slice_bitcast_fusion.2.refs_16_), channel_id=1, source_target_pairs={{0,8},{4,12},{8,0},{12,4},{1,9},{5,13},{9,1},{13,5},{2,10},{6,14},... | collective-permute-start | bytes 589832 | tf_op jit(solution)/shard_map/ppermute | solution.py:521
  15.8 16.8 %collective-permute-start.2 = (bf16[400,768]{1,0:T(8,128)(2,1)S(1)}, bf16[400,768]{1,0:T(8,128)(2,1)}, u32[]{:S(2)}, u32[]{:S(2)}) collective-permute-start(bf16[400,768]{1,0:T(8,128)(2,1)S(1)} %pad_maximum_fusion.16.refs_0_), channel_id=1, source_target_pairs={{0,2},{1,3},{2,0},{3,1},{4,6},{5,7},{6,4},{7,5},{8,10},{9,11},{10,... | collective-permute-start | bytes 1843208 | tf_op jit(solution)/shard_map/ppermute | solution.py:473
  17.4 15.3 %collective-permute-start.1 = (bf16[4,192,384]{2,1,0:T(8,128)(2,1)S(1)}, bf16[4,192,384]{2,1,0:T(8,128)(2,1)S(1)}, u32[]{:S(2)}, u32[]{:S(2)}) collective-permute-start(bf16[4,192,384]{2,1,0:T(8,128)(2,1)S(1)} %pad_maximum_fusion.17), channel_id=1, source_target_pairs={{0,16},{16,0},{1,17},{17,1},{2,18},{18,2},{3,19},{19,3},{4,20},{20... | collective-permute-start | bytes 1769480 | tf_op jit(solution)/shard_map/ppermute | solution.py:469
  18.9 13.7 %collective-permute-start.3 = (bf16[256,768]{1,0:T(8,128)(2,1)S(1)}, bf16[256,768]{1,0:T(8,128)(2,1)S(1)}, u32[]{:S(2)}, u32[]{:S(2)}) collective-permute-start(bf16[256,768]{1,0:T(8,128)(2,1)S(1)} %pad_maximum_fusion.18), channel_id=1, source_target_pairs={{0,4},{4,0},{8,12},{12,8},{1,5},{5,1},{9,13},{13,9},{2,6},{6,2},{1... | collective-permute-start | bytes 1179656 | tf_op jit(solution)/shard_map/ppermute | solution.py:521
  19.7 12.2 %collective-permute-start.4 = (bf16[128,768]{1,0:T(8,128)(2,1)S(1)}, bf16[128,768]{1,0:T(8,128)(2,1)S(1)}, u32[]{:S(2)}, u32[]{:S(2)}) collective-permute-start(bf16[128,768]{1,0:T(8,128)(2,1)S(1)} %get-tuple-element.262.refs_17_), channel_id=1, source_target_pairs={{0,8},{4,12},{8,0},{12,4},{1,9},{5,13},{9,1},{13,5},{2,10},{6,14},... | collective-permute-start | bytes 589832 | tf_op jit(solution)/shard_map/ppermute | solution.py:521
  32.7 16.5 %collective-permute-start.5 = (bf16[400,768]{1,0:T(8,128)(2,1)S(1)}, bf16[400,768]{1,0:T(8,128)(2,1)}, u32[]{:S(2)}, u32[]{:S(2)}) collective-permute-start(bf16[400,768]{1,0:T(8,128)(2,1)S(1)} %pad_maximum_fusion.16.refs_0_), channel_id=1, source_target_pairs={{0,16},{16,0},{1,17},{17,1},{2,18},{18,2},{3,19},{19,3},{4,20},{20... | collective-permute-start | bytes 1843208 | tf_op jit(solution)/shard_map/ppermute | solution.py:469
  33.3 15.8 %collective-permute-start.6 = (bf16[384,768]{1,0:T(8,128)(2,1)S(1)}, bf16[384,768]{1,0:T(8,128)(2,1)S(1)}, u32[]{:S(2)}, u32[]{:S(2)}) collective-permute-start(bf16[384,768]{1,0:T(8,128)(2,1)S(1)} %constant_dynamic-update-slice_fusion.1.near), channel_id=1, source_target_pairs={{0,2},{1,3},{2,0},{3,1},{4,6},{5,7},{6,4},{7,5},{8,10},{9,11},{10,... | collective-permute-start | bytes 1769480 | tf_op jit(solution)/shard_map/ppermute | solution.py:473
  34.2 15.0 %collective-permute-start.7 = (bf16[256,768]{1,0:T(8,128)(2,1)S(1)}, bf16[256,768]{1,0:T(8,128)(2,1)S(1)}, u32[]{:S(2)}, u32[]{:S(2)}) collective-permute-start(bf16[256,768]{1,0:T(8,128)(2,1)S(1)} %pad_maximum_fusion.19), channel_id=1, source_target_pairs={{0,4},{4,0},{8,12},{12,8},{1,5},{5,1},{9,13},{13,9},{2,6},{6,2},{1... | collective-permute-start | bytes 1179656 | tf_op jit(solution)/shard_map/ppermute | solution.py:521
  37.3 11.0 %collective-permute-start.8 = (bf16[128,768]{1,0:T(8,128)(2,1)S(1)}, bf16[128,768]{1,0:T(8,128)(2,1)S(1)}, u32[]{:S(2)}, u32[]{:S(2)}) collective-permute-start(bf16[128,768]{1,0:T(8,128)(2,1)S(1)} %get-tuple-element.274.refs_18_), channel_id=1, source_target_pairs={{0,8},{4,12},{8,0},{12,4},{1,9},{5,13},{9,1},{13,5},{2,10},{6,14},... | collective-permute-start | bytes 589832 | tf_op jit(solution)/shard_map/ppermute | solution.py:521
  50.3 5.0 %collective-permute-start.9 = (bf16[768,768]{1,0:T(8,128)(2,1)}, bf16[768,768]{1,0:T(8,128)(2,1)S(1)}, u32[]{:S(2)}, u32[]{:S(2)}) collective-permute-start(bf16[768,768]{1,0:T(8,128)(2,1)} %pad_maximum_fusion.5), channel_id=1, source_target_pairs={{0,1},{1,0},{2,3},{3,2},{4,5},{5,4},{6,7},{7,6},{8,9},{9,8},{10,11... | collective-permute-start | bytes 3538952 | tf_op jit(solution)/shard_map/ppermute | solution.py:477
  52.3 20.7 %collective-permute-start.12 = (bf16[384,768]{1,0:T(8,128)(2,1)S(1)}, bf16[384,768]{1,0:T(8,128)(2,1)S(1)}, u32[]{:S(2)}, u32[]{:S(2)}) collective-permute-start(bf16[384,768]{1,0:T(8,128)(2,1)S(1)} %constant_dynamic-update-slice_fusion.3.near), channel_id=1, source_target_pairs={{0,2},{1,3},{2,0},{3,1},{4,6},{5,7},{6,4},{7,5},{8,10},{9,11},{10,... | collective-permute-start | bytes 1769480 | tf_op jit(solution)/shard_map/ppermute | solution.py:473
  53.8 19.2 %collective-permute-start.11 = (bf16[384,768]{1,0:T(8,128)(2,1)S(1)}, bf16[384,768]{1,0:T(8,128)(2,1)}, u32[]{:S(2)}, u32[]{:S(2)}) collective-permute-start(bf16[384,768]{1,0:T(8,128)(2,1)S(1)} %bitcast.253), channel_id=1, source_target_pairs={{0,16},{16,0},{1,17},{17,1},{2,18},{18,2},{3,19},{19,3},{4,20},{20... | collective-permute-start | bytes 1769480 | tf_op jit(solution)/shard_map/ppermute | solution.py:469
  55.4 25.5 %collective-permute-start.10 = (bf16[384,768]{1,0:T(8,128)(2,1)S(1)}, bf16[384,768]{1,0:T(8,128)(2,1)}, u32[]{:S(2)}, u32[]{:S(2)}) collective-permute-start(bf16[384,768]{1,0:T(8,128)(2,1)S(1)} %bitcast.254), channel_id=1, source_target_pairs={{0,2},{1,3},{2,0},{3,1},{4,6},{5,7},{6,4},{7,5},{8,10},{9,11},{10,... | collective-permute-start | bytes 1769480 | tf_op jit(solution)/shard_map/ppermute | solution.py:473
  57.0 15.9 %collective-permute-start.13 = (bf16[256,768]{1,0:T(8,128)(2,1)S(1)}, bf16[256,768]{1,0:T(8,128)(2,1)S(1)}, u32[]{:S(2)}, u32[]{:S(2)}) collective-permute-start(bf16[256,768]{1,0:T(8,128)(2,1)S(1)} %pad_maximum_fusion.20), channel_id=1, source_target_pairs={{0,4},{4,0},{8,12},{12,8},{1,5},{5,1},{9,13},{13,9},{2,6},{6,2},{1... | collective-permute-start | bytes 1179656 | tf_op jit(solution)/shard_map/ppermute | solution.py:521
  80.9 3.8 collective-permute-start.14
  81.0 3.6 collective-permute-start.15
  81.6 18.3 %collective-permute-start.19 = (bf16[384,768]{1,0:T(8,128)(2,1)S(1)}, bf16[384,768]{1,0:T(8,128)(2,1)S(1)}, u32[]{:S(2)}, u32[]{:S(2)}) collective-permute-start(bf16[384,768]{1,0:T(8,128)(2,1)S(1)} %constant_dynamic-update-slice_fusion.5.near), channel_id=1, source_target_pairs={{0,2},{1,3},{2,0},{3,1},{4,6},{5,7},{6,4},{7,5},{8,10},{9,11},{10,... | collective-permute-start | bytes 1769480 | tf_op jit(solution)/shard_map/ppermute | solution.py:473
  83.1 16.7 %collective-permute-start.17 = (bf16[400,768]{1,0:T(8,128)(2,1)S(1)}, bf16[400,768]{1,0:T(8,128)(2,1)S(1)}, u32[]{:S(2)}, u32[]{:S(2)}) collective-permute-start(bf16[400,768]{1,0:T(8,128)(2,1)S(1)} %copy-done.35), channel_id=1, source_target_pairs={{0,1},{1,0},{2,3},{3,2},{4,5},{5,4},{6,7},{7,6},{8,9},{9,8},{10,11... | collective-permute-start | bytes 1843208 | tf_op jit(solution)/shard_map/ppermute | solution.py:477
  83.1 16.7 %collective-permute-start.18 = (bf16[400,768]{1,0:T(8,128)(2,1)}, bf16[400,768]{1,0:T(8,128)(2,1)}, u32[]{:S(2)}, u32[]{:S(2)}) collective-permute-start(bf16[400,768]{1,0:T(8,128)(2,1)} %collective-permute-done.2.refs_2_), channel_id=1, source_target_pairs={{0,16},{16,0},{1,17},{17,1},{2,18},{18,2},{3,19},{19,3},{4,20},{20... | collective-permute-start | bytes 1843208 | tf_op jit(solution)/shard_map/ppermute | solution.py:469
  84.7 16.4 %collective-permute-start.16 = (bf16[128,768]{1,0:T(8,128)(2,1)S(1)}, bf16[128,768]{1,0:T(8,128)(2,1)S(1)}, u32[]{:S(2)}, u32[]{:S(2)}) collective-permute-start(bf16[128,768]{1,0:T(8,128)(2,1)S(1)} %add_convert_fusion.20), channel_id=1, source_target_pairs={{0,2},{1,3},{2,0},{3,1},{4,6},{5,7},{6,4},{7,5},{8,10},{9,11},{10,... | collective-permute-start | bytes 589832 | tf_op jit(solution)/shard_map/ppermute | solution.py:473
  101.8 18.5 %collective-permute-start.20 = (bf16[384,768]{1,0:T(8,128)(2,1)S(1)}, bf16[384,768]{1,0:T(8,128)(2,1)S(1)}, u32[]{:S(2)}, u32[]{:S(2)}) collective-permute-start(bf16[384,768]{1,0:T(8,128)(2,1)S(1)} %bitcast.255), channel_id=1, source_target_pairs={{0,1},{1,0},{2,3},{3,2},{4,5},{5,4},{6,7},{7,6},{8,9},{9,8},{10,11... | collective-permute-start | bytes 1769480 | tf_op jit(solution)/shard_map/ppermute | solution.py:477
  101.9 18.4 %collective-permute-start.21 = (bf16[384,768]{1,0:T(8,128)(2,1)}, bf16[384,768]{1,0:T(8,128)(2,1)S(1)}, u32[]{:S(2)}, u32[]{:S(2)}) collective-permute-start(bf16[384,768]{1,0:T(8,128)(2,1)} %collective-permute-done.10.refs_10_), channel_id=1, source_target_pairs={{0,16},{16,0},{1,17},{17,1},{2,18},{18,2},{3,19},{19,3},{4,20},{20... | collective-permute-start | bytes 1769480 | tf_op jit(solution)/shard_map/ppermute | solution.py:469
  104.8 15.6 %collective-permute-start.24 = (bf16[128,768]{1,0:T(8,128)(2,1)S(1)}, bf16[128,768]{1,0:T(8,128)(2,1)S(1)}, u32[]{:S(2)}, u32[]{:S(2)}) collective-permute-start(bf16[128,768]{1,0:T(8,128)(2,1)S(1)} %add_convert_fusion.19), channel_id=1, source_target_pairs={{0,2},{1,3},{2,0},{3,1},{4,6},{5,7},{6,4},{7,5},{8,10},{9,11},{10,... | collective-permute-start | bytes 589832 | tf_op jit(solution)/shard_map/ppermute | solution.py:473
  120.5 10.1 %collective-permute-start.28 = (bf16[384,768]{1,0:T(8,128)(2,1)}, bf16[384,768]{1,0:T(8,128)(2,1)S(1)}, u32[]{:S(2)}, u32[]{:S(2)}) collective-permute-start(bf16[384,768]{1,0:T(8,128)(2,1)} %collective-permute-done.11.refs_9_), channel_id=1, source_target_pairs={{0,1},{1,0},{2,3},{3,2},{4,5},{5,4},{6,7},{7,6},{8,9},{9,8},{10,11... | collective-permute-start | bytes 1769480 | tf_op jit(solution)/shard_map/ppermute | solution.py:477
  123.5 7.0 %collective-permute-start.32 = (bf16[128,768]{1,0:T(8,128)(2,1)S(1)}, bf16[128,768]{1,0:T(8,128)(2,1)S(1)}, u32[]{:S(2)}, u32[]{:S(2)}) collective-permute-start(bf16[128,768]{1,0:T(8,128)(2,1)S(1)} %add_convert_fusion.18), channel_id=1, source_target_pairs={{0,2},{1,3},{2,0},{3,1},{4,6},{5,7},{6,4},{7,5},{8,10},{9,11},{10,... | collective-permute-start | bytes 589832 | tf_op jit(solution)/shard_map/ppermute | solution.py:473
  124.6 9.1 %collective-permute-start.25 = (bf16[400,768]{1,0:T(8,128)(2,1)}, bf16[400,768]{1,0:T(8,128)(2,1)S(1)}, u32[]{:S(2)}, u32[]{:S(2)}) collective-permute-start(bf16[400,768]{1,0:T(8,128)(2,1)} %collective-permute-done.5.refs_1_), channel_id=1, source_target_pairs={{0,1},{1,0},{2,3},{3,2},{4,5},{5,4},{6,7},{7,6},{8,9},{9,8},{10,11... | collective-permute-start | bytes 1843208 | tf_op jit(solution)/shard_map/ppermute | solution.py:477
  124.6 9.1 %collective-permute-start.26 = (bf16[400,768]{1,0:T(8,128)(2,1)}, bf16[400,768]{1,0:T(8,128)(2,1)S(1)}, u32[]{:S(2)}, u32[]{:S(2)}) collective-permute-start(bf16[400,768]{1,0:T(8,128)(2,1)} %collective-permute-done.2.refs_2_), channel_id=1, source_target_pairs={{0,1},{1,0},{2,3},{3,2},{4,5},{5,4},{6,7},{7,6},{8,9},{9,8},{10,11... | collective-permute-start | bytes 1843208 | tf_op jit(solution)/shard_map/ppermute | solution.py:477
  125.1 8.6 %collective-permute-start.27 = (bf16[400,768]{1,0:T(8,128)(2,1)}, bf16[400,768]{1,0:T(8,128)(2,1)S(1)}, u32[]{:S(2)}, u32[]{:S(2)}) collective-permute-start(bf16[400,768]{1,0:T(8,128)(2,1)} %collective-permute-done.18.refs_3_), channel_id=1, source_target_pairs={{0,1},{1,0},{2,3},{3,2},{4,5},{5,4},{6,7},{7,6},{8,9},{9,8},{10,11... | collective-permute-start | bytes 1843208 | tf_op jit(solution)/shard_map/ppermute | solution.py:477
  156.7 8.1 %collective-permute-start.33 = (bf16[128,768]{1,0:T(8,128)(2,1)}, bf16[128,768]{1,0:T(8,128)(2,1)S(1)}, u32[]{:S(2)}, u32[]{:S(2)}) collective-permute-start(bf16[128,768]{1,0:T(8,128)(2,1)} %get-tuple-element.354.g_own), channel_id=1, source_target_pairs={{0,2},{1,3},{2,0},{3,1},{4,6},{5,7},{6,4},{7,5},{8,10},{9,11},{10,... | collective-permute-start | bytes 589832 | tf_op jit(solution)/shard_map/ppermute | solution.py:473
  164.9 14.1 %collective-permute-start.36 = (bf16[2,2,448,768]{3,2,1,0:T(8,128)(2,1)}, bf16[2,2,448,768]{3,2,1,0:T(8,128)(2,1)S(1)}, u32[]{:S(2)}, u32[]{:S(2)}) collective-permute-start(bf16[2,2,448,768]{3,2,1,0:T(8,128)(2,1)} %get-tuple-element.340), channel_id=1, source_target_pairs={{0,1},{1,0},{2,3},{3,2},{4,5},{5,4},{6,7},{7,6},{8,9},{9,8},{10,11... | collective-permute-start | bytes 8257544 | tf_op jit(solution)/shard_map/ppermute | solution.py:477
  166.9 12.0 %collective-permute-start.37 = (bf16[2,2,384,768]{3,2,0,1:T(8,128)(2,1)S(1)}, bf16[2,2,384,768]{3,2,0,1:T(8,128)(2,1)}, u32[]{:S(2)}, u32[]{:S(2)}) collective-permute-start(bf16[2,2,384,768]{3,2,0,1:T(8,128)(2,1)S(1)} %copy.35), channel_id=1, source_target_pairs={{0,1},{1,0},{2,3},{3,2},{4,5},{5,4},{6,7},{7,6},{8,9},{9,8},{10,11... | collective-permute-start | bytes 7077896 | tf_op jit(solution)/shard_map/ppermute | solution.py:477
  167.4 8.6 %collective-permute-start.34 = (bf16[256,768]{1,0:T(8,128)(2,1)S(1)}, bf16[256,768]{1,0:T(8,128)(2,1)S(1)}, u32[]{:S(2)}, u32[]{:S(2)}) collective-permute-start(bf16[256,768]{1,0:T(8,128)(2,1)S(1)} %pad_maximum_fusion.21), channel_id=1, source_target_pairs={{0,1},{1,0},{2,3},{3,2},{4,5},{5,4},{6,7},{7,6},{8,9},{9,8},{10,11... | collective-permute-start | bytes 1179656 | tf_op jit(solution)/shard_map/ppermute | solution.py:477
  167.6 11.4 %collective-permute-start.35 = (bf16[256,768]{1,0:T(8,128)(2,1)S(1)}, bf16[256,768]{1,0:T(8,128)(2,1)S(1)}, u32[]{:S(2)}, u32[]{:S(2)}) collective-permute-start(bf16[256,768]{1,0:T(8,128)(2,1)S(1)} %copy-done.41), channel_id=1, source_target_pairs={{0,2},{1,3},{2,0},{3,1},{4,6},{5,7},{6,4},{7,5},{8,10},{9,11},{10,... | collective-permute-start | bytes 1179656 | tf_op jit(solution)/shard_map/ppermute | solution.py:473
  182.9 31.7 %collective-permute-start.38 = (bf16[2,448,768]{2,1,0:T(8,128)(2,1)S(1)}, bf16[2,448,768]{2,1,0:T(8,128)(2,1)S(1)}, u32[]{:S(2)}, u32[]{:S(2)}) collective-permute-start(bf16[2,448,768]{2,1,0:T(8,128)(2,1)S(1)} %get-tuple-element.351), channel_id=1, source_target_pairs={{0,2},{1,3},{2,0},{3,1},{4,6},{5,7},{6,4},{7,5},{8,10},{9,11},{10,... | collective-permute-start | bytes 4128776 | tf_op jit(solution)/shard_map/ppermute | solution.py:473
  183.9 27.4 %collective-permute-start.39 = (bf16[2,384,768]{2,1,0:T(8,128)(2,1)}, bf16[2,384,768]{2,1,0:T(8,128)(2,1)}, u32[]{:S(2)}, u32[]{:S(2)}) collective-permute-start(bf16[2,384,768]{2,1,0:T(8,128)(2,1)} %fusion.9), channel_id=1, source_target_pairs={{0,16},{16,0},{1,17},{17,1},{2,18},{18,2},{3,19},{19,3},{4,20},{20... | collective-permute-start | bytes 3538952 | tf_op jit(solution)/shard_map/ppermute | solution.py:469
  185.5 20.7 %collective-permute-start.40 = (bf16[512,768]{1,0:T(8,128)(2,1)S(1)}, bf16[512,768]{1,0:T(8,128)(2,1)S(1)}, u32[]{:S(2)}, u32[]{:S(2)}) collective-permute-start(bf16[512,768]{1,0:T(8,128)(2,1)S(1)} %pad_maximum_fusion.12), channel_id=1, source_target_pairs={{0,1},{1,0},{2,3},{3,2},{4,5},{5,4},{6,7},{7,6},{8,9},{9,8},{10,11... | collective-permute-start | bytes 2359304 | tf_op jit(solution)/shard_map/ppermute | solution.py:477
  215.7 4.2 %collective-permute-start.41 = (bf16[1024,768]{1,0:T(8,128)(2,1)}, bf16[1024,768]{1,0:T(8,128)(2,1)}, u32[]{:S(2)}, u32[]{:S(2)}) collective-permute-start(bf16[1024,768]{1,0:T(8,128)(2,1)} %get-tuple-element.367), channel_id=1, source_target_pairs={{0,1},{1,0},{2,3},{3,2},{4,5},{5,4},{6,7},{7,6},{8,9},{9,8},{10,11... | collective-permute-start | bytes 4718600 | tf_op jit(solution)/shard_map/ppermute | solution.py:477
  223.4 19.0 %collective-permute-start.43 = (bf16[448,768]{1,0:T(8,128)(2,1)S(1)}, bf16[448,768]{1,0:T(8,128)(2,1)S(1)}, u32[]{:S(2)}, u32[]{:S(2)}) collective-permute-start(bf16[448,768]{1,0:T(8,128)(2,1)S(1)} %fusion.18), channel_id=1, source_target_pairs={{0,16},{16,0},{1,17},{17,1},{2,18},{18,2},{3,19},{19,3},{4,20},{20... | collective-permute-start | bytes 2064392 | tf_op jit(solution)/shard_map/ppermute | solution.py:469
  225.0 17.5 %collective-permute-start.44 = (bf16[384,768]{1,0:T(8,128)(2,1)}, bf16[384,768]{1,0:T(8,128)(2,1)S(1)}, u32[]{:S(2)}, u32[]{:S(2)}) collective-permute-start(bf16[384,768]{1,0:T(8,128)(2,1)} %fusion.21), channel_id=1, source_target_pairs={{0,2},{1,3},{2,0},{3,1},{4,6},{5,7},{6,4},{7,5},{8,10},{9,11},{10,... | collective-permute-start | bytes 1769480 | tf_op jit(solution)/shard_map/ppermute | solution.py:473
  225.9 31.6 %collective-permute-start.42 = (bf16[512,768]{1,0:T(8,128)(2,1)}, bf16[512,768]{1,0:T(8,128)(2,1)S(1)}, u32[]{:S(2)}, u32[]{:S(2)}) collective-permute-start(bf16[512,768]{1,0:T(8,128)(2,1)} %add_convert_fusion.4), channel_id=1, source_target_pairs={{0,2},{1,3},{2,0},{3,1},{4,6},{5,7},{6,4},{7,5},{8,10},{9,11},{10,... | collective-permute-start | bytes 2359304 | tf_op jit(solution)/shard_map/ppermute | solution.py:473
  257.5 3.8 collective-permute-start.45
  257.5 25.0 %collective-permute-start.48 = (bf16[416,768]{1,0:T(8,128)(2,1)}, bf16[416,768]{1,0:T(8,128)(2,1)}, u32[]{:S(2)}, u32[]{:S(2)}) collective-permute-start(bf16[416,768]{1,0:T(8,128)(2,1)} %get-tuple-element.399), channel_id=1, source_target_pairs={{0,4},{4,0},{8,12},{12,8},{1,5},{5,1},{9,13},{13,9},{2,6},{6,2},{1... | collective-permute-start | bytes 1916936 | tf_op jit(solution)/shard_map/ppermute | solution.py:521
  263.5 20.0 %collective-permute-start.46 = (bf16[512,768]{1,0:T(8,128)(2,1)}, bf16[512,768]{1,0:T(8,128)(2,1)}, u32[]{:S(2)}, u32[]{:S(2)}) collective-permute-start(bf16[512,768]{1,0:T(8,128)(2,1)} %add_convert_fusion.3), channel_id=1, source_target_pairs={{0,2},{1,3},{2,0},{3,1},{4,6},{5,7},{6,4},{7,5},{8,10},{9,11},{10,... | collective-permute-start | bytes 2359304 | tf_op jit(solution)/shard_map/ppermute | solution.py:473
  264.5 18.5 %collective-permute-start.47 = (bf16[256,768]{1,0:T(8,128)(2,1)}, bf16[256,768]{1,0:T(8,128)(2,1)S(1)}, u32[]{:S(2)}, u32[]{:S(2)}) collective-permute-start(bf16[256,768]{1,0:T(8,128)(2,1)} %add_convert_fusion.9), channel_id=1, source_target_pairs={{0,4},{4,0},{8,12},{12,8},{1,5},{5,1},{9,13},{13,9},{2,6},{6,2},{1... | collective-permute-start | bytes 1179656 | tf_op jit(solution)/shard_map/ppermute | solution.py:521
  283.5 15.9 %collective-permute-start.50 = (bf16[1024,768]{1,0:T(8,128)(2,1)}, bf16[1024,768]{1,0:T(8,128)(2,1)}, u32[]{:S(2)}, u32[]{:S(2)}) collective-permute-start(bf16[1024,768]{1,0:T(8,128)(2,1)} %get-tuple-element.418), channel_id=1, source_target_pairs={{0,1},{1,0},{2,3},{3,2},{4,5},{5,4},{6,7},{7,6},{8,9},{9,8},{10,11... | collective-permute-start | bytes 4718600 | tf_op jit(solution)/shard_map/ppermute | solution.py:477
  288.9 16.0 %collective-permute-start.49 = (bf16[256,768]{1,0:T(8,128)(2,1)}, bf16[256,768]{1,0:T(8,128)(2,1)S(1)}, u32[]{:S(2)}, u32[]{:S(2)}) collective-permute-start(bf16[256,768]{1,0:T(8,128)(2,1)} %add_convert_fusion.8), channel_id=1, source_target_pairs={{0,4},{4,0},{8,12},{12,8},{1,5},{5,1},{9,13},{13,9},{2,6},{6,2},{1... | collective-permute-start | bytes 1179656 | tf_op jit(solution)/shard_map/ppermute | solution.py:521
  290.6 23.4 %collective-permute-start.52 = (bf16[128,768]{1,0:T(8,128)(2,1)}, bf16[128,768]{1,0:T(8,128)(2,1)}, u32[]{:S(2)}, u32[]{:S(2)}) collective-permute-start(bf16[128,768]{1,0:T(8,128)(2,1)} %add_convert_fusion.17), channel_id=1, source_target_pairs={{0,8},{4,12},{8,0},{12,4},{1,9},{5,13},{9,1},{13,5},{2,10},{6,14},... | collective-permute-start | bytes 589832 | tf_op jit(solution)/shard_map/ppermute | solution.py:521
  300.9 11.0 %collective-permute-start.54 = (bf16[256,768]{1,0:T(8,128)(2,1)S(1)}, bf16[256,768]{1,0:T(8,128)(2,1)S(1)}, u32[]{:S(2)}, u32[]{:S(2)}) collective-permute-start(bf16[256,768]{1,0:T(8,128)(2,1)S(1)} %get-tuple-element.538), channel_id=1, source_target_pairs={{0,2},{1,3},{2,0},{3,1},{4,6},{5,7},{6,4},{7,5},{8,10},{9,11},{10,... | collective-permute-start | bytes 1179656 | tf_op jit(solution)/shard_map/ppermute | solution.py:473
  304.8 21.6 %collective-permute-start.53 = (bf16[208,768]{1,0:T(8,128)(2,1)S(1)}, bf16[208,768]{1,0:T(8,128)(2,1)S(1)}, u32[]{:S(2)}, u32[]{:S(2)}) collective-permute-start(bf16[208,768]{1,0:T(8,128)(2,1)S(1)} %get-tuple-element.437), channel_id=1, source_target_pairs={{0,8},{4,12},{8,0},{12,4},{1,9},{5,13},{9,1},{13,5},{2,10},{6,14},... | collective-permute-start | bytes 958472 | tf_op jit(solution)/shard_map/ppermute | solution.py:521
  305.9 21.9 %collective-permute-start.51 = (bf16[832,384]{1,0:T(8,128)(2,1)S(1)}, bf16[832,384]{1,0:T(8,128)(2,1)S(1)}, u32[]{:S(2)}, u32[]{:S(2)}) collective-permute-start(bf16[832,384]{1,0:T(8,128)(2,1)S(1)} %get-tuple-element.549), channel_id=1, source_target_pairs={{0,16},{16,0},{1,17},{17,1},{2,18},{18,2},{3,19},{19,3},{4,20},{20... | collective-permute-start | bytes 1916936 | tf_op jit(solution)/shard_map/ppermute | solution.py:469
  307.7 29.9 %collective-permute-start.55 = (bf16[128,768]{1,0:T(8,128)(2,1)S(1)}, bf16[128,768]{1,0:T(8,128)(2,1)S(1)}, u32[]{:S(2)}, u32[]{:S(2)}) collective-permute-start(bf16[128,768]{1,0:T(8,128)(2,1)S(1)} %add_convert_fusion.16), channel_id=1, source_target_pairs={{0,8},{4,12},{8,0},{12,4},{1,9},{5,13},{9,1},{13,5},{2,10},{6,14},... | collective-permute-start | bytes 589832 | tf_op jit(solution)/shard_map/ppermute | solution.py:521
  312.0 27.8 %collective-permute-start.59 = (bf16[256,768]{1,0:T(8,128)(2,1)S(1)}, bf16[256,768]{1,0:T(8,128)(2,1)S(1)}, u32[]{:S(2)}, u32[]{:S(2)}) collective-permute-start(bf16[256,768]{1,0:T(8,128)(2,1)S(1)} %get-tuple-element.537), channel_id=1, source_target_pairs={{0,2},{1,3},{2,0},{3,1},{4,6},{5,7},{6,4},{7,5},{8,10},{9,11},{10,... | collective-permute-start | bytes 1179656 | tf_op jit(solution)/shard_map/ppermute | solution.py:473
  314.1 26.8 %collective-permute-start.58 = (bf16[256,768]{1,0:T(8,128)(2,1)S(1)}, bf16[256,768]{1,0:T(8,128)(2,1)S(1)}, u32[]{:S(2)}, u32[]{:S(2)}) collective-permute-start(bf16[256,768]{1,0:T(8,128)(2,1)S(1)} %add_convert_fusion.7), channel_id=1, source_target_pairs={{0,4},{4,0},{8,12},{12,8},{1,5},{5,1},{9,13},{13,9},{2,6},{6,2},{1... | collective-permute-start | bytes 1179656 | tf_op jit(solution)/shard_map/ppermute | solution.py:521
  326.5 22.8 %collective-permute-start.62 = (bf16[208,768]{1,0:T(8,128)(2,1)S(1)}, bf16[208,768]{1,0:T(8,128)(2,1)S(1)}, u32[]{:S(2)}, u32[]{:S(2)}) collective-permute-start(bf16[208,768]{1,0:T(8,128)(2,1)S(1)} %add_convert_fusion.11), channel_id=1, source_target_pairs={{0,8},{4,12},{8,0},{12,4},{1,9},{5,13},{9,1},{13,5},{2,10},{6,14},... | collective-permute-start | bytes 958472 | tf_op jit(solution)/shard_map/ppermute | solution.py:521
  328.1 21.0 %collective-permute-start.57 = (bf16[416,384]{1,0:T(8,128)(2,1)S(1)}, bf16[416,384]{1,0:T(8,128)(2,1)S(1)}, u32[]{:S(2)}, u32[]{:S(2)}) collective-permute-start(bf16[416,384]{1,0:T(8,128)(2,1)S(1)} %constant_dynamic-slice_fusion.1), channel_id=1, source_target_pairs={{0,4},{4,0},{8,12},{12,8},{1,5},{5,1},{9,13},{13,9},{2,6},{6,2},{1... | collective-permute-start | bytes 958472 | tf_op jit(solution)/shard_map/ppermute | solution.py:521
  338.8 12.1 %collective-permute-start.63 = (bf16[2,128,768]{2,1,0:T(8,128)(2,1)S(1)}, bf16[2,128,768]{2,1,0:T(8,128)(2,1)S(1)}, u32[]{:S(2)}, u32[]{:S(2)}) collective-permute-start(bf16[2,128,768]{2,1,0:T(8,128)(2,1)S(1)} %bitcast.237), channel_id=1, source_target_pairs={{0,2},{1,3},{2,0},{3,1},{4,6},{5,7},{6,4},{7,5},{8,10},{9,11},{10,... | collective-permute-start | bytes 1179656 | tf_op jit(solution)/shard_map/ppermute | solution.py:473
  339.8 21.9 %collective-permute-start.56 = (bf16[3,128,768]{2,1,0:T(8,128)(2,1)S(1)}, bf16[3,128,768]{2,1,0:T(8,128)(2,1)S(1)}, u32[]{:S(2)}, u32[]{:S(2)}) collective-permute-start(bf16[3,128,768]{2,1,0:T(8,128)(2,1)S(1)} %bitcast.244), channel_id=1, source_target_pairs={{0,2},{1,3},{2,0},{3,1},{4,6},{5,7},{6,4},{7,5},{8,10},{9,11},{10,... | collective-permute-start | bytes 1769480 | tf_op jit(solution)/shard_map/ppermute | solution.py:473
  341.9 13.9 %collective-permute-start.61 = (bf16[128,768]{1,0:T(8,128)(2,1)S(1)}, bf16[128,768]{1,0:T(8,128)(2,1)S(1)}, u32[]{:S(2)}, u32[]{:S(2)}) collective-permute-start(bf16[128,768]{1,0:T(8,128)(2,1)S(1)} %add_convert_fusion.13), channel_id=1, source_target_pairs={{0,8},{4,12},{8,0},{12,4},{1,9},{5,13},{9,1},{13,5},{2,10},{6,14},... | collective-permute-start | bytes 589832 | tf_op jit(solution)/shard_map/ppermute | solution.py:521
  349.2 10.0 %collective-permute-start.60 = (bf16[208,384]{1,0:T(8,128)(2,1)S(1)}, bf16[208,384]{1,0:T(8,128)(2,1)S(1)}, u32[]{:S(2)}, u32[]{:S(2)}) collective-permute-start(bf16[208,384]{1,0:T(8,128)(2,1)S(1)} %constant_dynamic-slice_fusion), channel_id=1, source_target_pairs={{0,8},{4,12},{8,0},{12,4},{1,9},{5,13},{9,1},{13,5},{2,10},{6,14},... | collective-permute-start | bytes 479240 | tf_op jit(solution)/shard_map/ppermute | solution.py:521
  362.7 7.3 %collective-permute-start.64 = (bf16[1,128,768]{2,1,0:T(8,128)(2,1)S(1)}, bf16[1,128,768]{2,1,0:T(8,128)(2,1)S(1)}, u32[]{:S(2)}, u32[]{:S(2)}) collective-permute-start(bf16[1,128,768]{2,1,0:T(8,128)(2,1)S(1)} %bitcast.248), channel_id=1, source_target_pairs={{0,2},{1,3},{2,0},{3,1},{4,6},{5,7},{6,4},{7,5},{8,10},{9,11},{10,... | collective-permute-start | bytes 589832 | tf_op jit(solution)/shard_map/ppermute | solution.py:473
  363.7 10.2 %collective-permute-start.65 = (bf16[208,384]{1,0:T(8,128)(2,1)S(1)}, bf16[208,384]{1,0:T(8,128)(2,1)S(1)}, u32[]{:S(2)}, u32[]{:S(2)}) collective-permute-start(bf16[208,384]{1,0:T(8,128)(2,1)S(1)} %add_convert_fusion.21), channel_id=1, source_target_pairs={{0,8},{4,12},{8,0},{12,4},{1,9},{5,13},{9,1},{13,5},{2,10},{6,14},... | collective-permute-start | bytes 479240 | tf_op jit(solution)/shard_map/ppermute | solution.py:521
  364.8 27.2 %collective-permute-start.68 = (bf16[2,3,128,768]{3,2,1,0:T(8,128)(2,1)}, bf16[2,3,128,768]{3,2,1,0:T(8,128)(2,1)}, u32[]{:S(2)}, u32[]{:S(2)}) collective-permute-start(bf16[2,3,128,768]{3,2,1,0:T(8,128)(2,1)} %pad_maximum_fusion.9), channel_id=1, source_target_pairs={{0,1},{1,0},{2,3},{3,2},{4,5},{5,4},{6,7},{7,6},{8,9},{9,8},{10,11... | collective-permute-start | bytes 3538952 | tf_op jit(solution)/shard_map/ppermute | solution.py:477
  374.7 17.2 %collective-permute-start.69 = (bf16[416,768]{1,0:T(8,128)(2,1)S(1)}, bf16[416,768]{1,0:T(8,128)(2,1)S(1)}, u32[]{:S(2)}, u32[]{:S(2)}) collective-permute-start(bf16[416,768]{1,0:T(8,128)(2,1)S(1)} %pad_maximum_fusion.15), channel_id=1, source_target_pairs={{0,4},{4,0},{8,12},{12,8},{1,5},{5,1},{9,13},{13,9},{2,6},{6,2},{1... | collective-permute-start | bytes 1916936 | tf_op jit(solution)/shard_map/ppermute | solution.py:521
  375.8 22.5 %collective-permute-start.67 = (bf16[416,384]{1,0:T(8,128)(2,1)S(1)}, bf16[416,384]{1,0:T(8,128)(2,1)S(1)}, u32[]{:S(2)}, u32[]{:S(2)}) collective-permute-start(bf16[416,384]{1,0:T(8,128)(2,1)S(1)} %pad_maximum_fusion.24), channel_id=1, source_target_pairs={{0,4},{4,0},{8,12},{12,8},{1,5},{5,1},{9,13},{13,9},{2,6},{6,2},{1... | collective-permute-start | bytes 958472 | tf_op jit(solution)/shard_map/ppermute | solution.py:521
  (81 other events, 572.9 us)

commit v3 on v2

--- a/solution.py
+++ b/solution.py
@@ -246,7 +246,14 @@
     )(places, g_own, g_cross, g_sib, w_four, query, key, value, attended, log_total)
 
 
-def gradients_body(index, inputs, near, cross, sib, d_query, d_key, d_value, out, own, sem):
+def gradients_body(index, adds, last, *refs):
+    inputs, near, cross, sib, d_query, d_key, d_value = refs[:7]
+    previous, refs = refs[7 : 7 + adds], refs[7 + adds :]
+    if last:
+        order, biases, d_outs = refs[0], refs[1], refs[2:5]
+        staying, leaving, out, own, sem = refs[5:]
+    else:
+        out, own, sem = refs
     fetch = pltpu.make_async_copy(inputs.at[index], own, sem)
     fetch.start()
     row = own.shape[0]
@@ -257,30 +264,50 @@
         rows = slice(row, row + piece.shape[0])
         for slot, grad in ((1, d_key), (2, d_value)):
             part = nn(grad[rows, :].T, piece[...])
-            if piece is near:
+            if piece is not near:
+                out[slot] += part
+            elif previous:
+                out[slot] = previous[0][slot] + part
+            else:
                 out[slot] = part
-            else:
-                out[slot] += part
         row += piece.shape[0]
-    out[0] = nn(d_query[...].T, own[...])
-
-
-def attention_gradients(index, inputs, near, cross, sib, d_query, d_key, d_value):
+    part = nn(d_query[...].T, own[...])
+    out[0] = previous[0][0] + part if previous else part
+    if not last:
+        return
+    cols, width = part.shape
+    depth = width // 2
+    swap = order[4] == 1
+    for slot in range(4):
+        total = out[slot] if slot < 3 else d_outs[0][...] + d_outs[1][...] + d_outs[2][...]
+        left, right = total[:, :depth], total[:, depth:]
+        spot = slice(slot * cols, (slot + 1) * cols)
+        staying[spot, :] = jnp.where(swap, right, left).astype(BF16)
+        leaving[spot, :] = jnp.where(swap, left, right).astype(BF16)
+    staying[4 * cols :, :] = biases[...]
+    leaving[4 * cols :, :] = biases[...]
+
+
+def attention_gradients(index, inputs, near, cross, sib, d_query, d_key, d_value, previous=(), final=()):
     cols = d_query.shape[1]
     width = inputs.shape[2]
     total = d_key.shape[0]
+    shape = jax.ShapeDtypeStruct
+    sums = shape((3, cols, width), F32)
+    half = shape((4 * cols + final[1].shape[0], width // 2), BF16) if final else None
+    scratch = [pltpu.VMEM(inputs.shape[1:], BF16), pltpu.SemaphoreType.DMA(())]
     return pl.pallas_call(
-        functools.partial(gradients_body, index),
-        out_shape=jax.ShapeDtypeStruct((3, cols, width), F32),
-        in_specs=[ANY_SPEC] + vmem(6),
-        out_specs=pl.BlockSpec(memory_space=pltpu.VMEM),
-        scratch_shapes=[pltpu.VMEM(inputs.shape[1:], BF16), pltpu.SemaphoreType.DMA(())],
+        functools.partial(gradients_body, index, len(previous), bool(final)),
+        out_shape=(half, half) if final else sums,
+        in_specs=[ANY_SPEC] + vmem(6 + len(previous)) + ([SMEM_SPEC] + vmem(4) if final else []),
+        out_specs=vmem(2) if final else vmem(1)[0],
+        scratch_shapes=[pltpu.VMEM(sums.shape, F32)] + scratch if final else scratch,
         compiler_params=params(),
         cost_estimate=pl.CostEstimate(
             flops=4 * total * cols * width, bytes_accessed=2 * total * (width + 2 * cols), transcendentals=0
         ),
         name="attention_gradients",
-    )(inputs, near, cross, sib, d_query, d_key, d_value)
+    )(inputs, near, cross, sib, d_query, d_key, d_value, *previous, *final)
 
 
 def rows_mean(a):
@@ -557,7 +584,8 @@
                 gots.append(sibling(held[s - 1][1]))
                 rest = low_sum(held[s - 1][0][quarter:], gots[-1][quarter:])
                 sibs[s], rest = stage(sibs[s], rest)
-                flights["rest"] = across(rest)
+            if s >= 2:
+                flights["rest"] = [across(r) for r in rests + [rest]]
             query, key, value, attended, log_total, keep, send = attention_forward(
                 places, s, inputs, joined[s], cross[s], sibs[s], four_all, b_query[None], b_value[None])
             saved[s] = (query, key, value, attended, log_total)
@@ -574,12 +602,14 @@
             flights["four"] = from_shards(four)
         if j == hops:
             flights["up_y"] = from_shards(up_own)
+            flights["four_all"] = four_all
         if j == hops + 1:
             flights["down_y"] = from_shards(down_own)
-            flights["down_x"] = across(stage(down_own, sibs[0])[0])
+            flights["down_x1"] = across(stage(down_own[: depth // 2], sibs[0])[0])
         if j == hops + 2:
             flights["up_xy"] = from_shards(up_x)
             flights["up_c"] = sibling(up_own)
+            flights["down_x2"] = across(stage(down_own[depth // 2 :], sibs[1])[0])
         if j == hops + 3:
             flights["down_xy"] = from_shards(down_x)
             flights["down_c"] = sibling(down_own)
@@ -593,7 +623,9 @@
         if s >= 0:
             held[s] = found
             if s >= 1:
-                rests.append(flights["rest"])
+                rests.append(rest)
+            if s >= 2:
+                rests = flights["rest"]
         if j == hops - 1:
             up_x, other = flights["up_x"], flights["four"]
             if shards == 2:
@@ -603,11 +635,12 @@
             else:
                 four_all = lax.all_gather(four, "shard", axis=2, tiled=True)
         if j == hops:
-            up_y = flights["up_y"]
+            up_y, four_all = flights["up_y"], flights["four_all"]
         if j == hops + 1:
-            down_x, down_y = flights["down_x"], flights["down_y"]
+            down_x1, down_y = flights["down_x1"], flights["down_y"]
         if j == hops + 2:
             up_xy, up_c = flights["up_xy"], flights["up_c"]
+            down_x = jnp.concatenate([down_x1, flights["down_x2"]], axis=0)
         if j == hops + 3:
             down_xy, down_c = flights["down_xy"], flights["down_c"]
     gots.append(sibling(held[seqs - 1][1]))
@@ -621,16 +654,18 @@
     up_send, down_send = feed_gradients(shards, 2, order, act, d_inner, d_ffn, low, sums)
     g_first_x, up_send, down_send, d_inner, g_rest = stage(across(g_first), up_send, down_send, d_inner, g_rest)
     up_keep, down_keep = feed_gradients(shards, 0, order, act, d_inner, d_ffn, low, sums)
-    g_first_c, g_rest_x, up_got, down_got, up_keep, down_keep, result = stage(
-        sibling(jnp.concatenate([g_first, g_first_x], axis=0)), across(g_rest),
-        sibling(up_send), sibling(down_send), up_keep, down_keep, result)
-    up_leave = low_sum(up_keep[1], up_got[1])
-    down_leave = [low_sum(down_keep[:, r], down_got[:, r]) for r in range(1, shards)]
-    up_pair = rounded(added(up_keep[0], up_got[0]))
-    down_pair = rounded(added(down_keep[:, 0], down_got[:, 0]))
-
-    def project(s, found):
-        return attention_gradients(s, inputs, joined[s], cross[s], sibs[s], *found[:3])
+    g_first_c, up_got, down_got, up_keep, down_keep, result = stage(
+        sibling(jnp.concatenate([g_first, g_first_x], axis=0)), sibling(up_send), sibling(down_send),
+        up_keep, down_keep, result)
+
+    def up_pair(p):
+        return rounded(added(up_keep[0, p], up_got[0, p]))
+
+    def down_pair(slot):
+        return rounded(added(down_keep[slot, 0], down_got[slot, 0]))
+
+    def project(s, found, previous=(), final=()):
+        return attention_gradients(s, inputs, joined[s], cross[s], sibs[s], *found[:3], previous, final)
 
     def leaving(terms):
         half = terms[-1].shape[0] // 2
@@ -675,122 +710,120 @@
         outs.append(found[5])
         return found
 
-    g_first, up_leave, down_leave = stage(g_first, up_leave, down_leave)
-    found = work(0, g_first, g_first_x, g_first_c)
-    up_far, down_far, g_rest_c, projection, keep, send = stage(
-        across(up_leave), to_shards(down_leave), sibling(jnp.concatenate([g_rest, g_rest_x], axis=0)),
-        project(0, found), found[3], found[4])
-    projections.append(projection)
-    got = sibling(send)
-    up_leave = [low_sum(up_pair[r], up_far[r]) for r in range(1, shards)]
-    down_leave = low_sum(down_pair[1], *[d[1] for d in down_far])
-    up_pair = rounded(added(up_pair[0], up_far[0]))
-    down_pair = rounded(added(down_pair[0], *[d[0] for d in down_far]))
-    terms0 = [keep, got]
+    up_leave = [low_sum(up_keep[1, p], up_got[1, p]) for p in range(1, shards)]
+    down_leave = [low_sum(down_keep[1, p], down_got[1, p]) for p in range(1, shards)]
+    g_first, g_rest, g_rest_x, up_leave, down_leave = stage(g_first, g_rest, across(g_rest), up_leave, down_leave)
+    found0 = work(0, g_first, g_first_x, g_first_c)
+    up_far, down_far, g_rest_c, found0 = stage(
+        [across(u) for u in up_leave], to_shards(down_leave), sibling(jnp.concatenate([g_rest, g_rest_x], axis=0)), found0)
+    got0 = sibling(found0[4])
+    up_second = [low_sum(up_pair(p), up_far[p - 1]) for p in range(1, shards)]
+    down_second = low_sum(down_pair(1), *down_far)
+    up_leave = low_sum(up_keep[1, 0], up_got[1, 0])
+    down_leave = [low_sum(down_keep[0, p], down_got[0, p]) for p in range(1, shards)]
+    g_rest, up_second, down_second, up_leave, down_leave = stage(g_rest, up_second, down_second, up_leave, down_leave)
+    found1 = work(1, g_rest, g_rest_x, g_rest_c)
+    up_far, down_far, got0, found1 = stage(across(up_leave), to_shards(down_leave), got0, found1)
+    terms0 = [found0[3], got0]
     leave = leaving(terms0)
-    g_rest, leave, up_leave, down_leave = stage(g_rest, leave, up_leave, down_leave)
-    found = work(1, g_rest, g_rest_x, g_rest_c)
-    up_far, down_far, found = stage(to_shards(up_leave), across(down_leave), found)
-    feed = jnp.concatenate([low_sum(up_pair, *up_far), low_sum(down_pair, down_far)], axis=0)
+    found0, leave, up_second, down_second, found1 = stage(found0, leave, up_second, down_second, found1)
+    up_last = to_shards(up_second)
+    down_last = across(down_second)
+    flight0 = across(leave)
+    projection = project(0, found0)
+    got1, projection = stage(sibling(found1[4]), projection)
+    terms1 = [found1[3], got1]
+    leave = leaving(terms1)
+    found1, leave = stage(found1, leave)
+    flight1 = across(leave)
+    projection = project(1, found1, [projection])
+    up_last, down_last, projection = stage(up_last, down_last, projection)
+    feed = jnp.concatenate(
+        [low_sum(rounded(up_pair(0) + up_far.astype(F32)), *up_last),
+         low_sum(rounded(added(down_pair(0), *down_far)), down_last)], axis=0)
     feed_stay, feed_leave = split(feed, masks[0])
-    flight, projection, keep, send, feed_stay, feed_leave = stage(
-        across(leave), project(1, found), found[3], found[4], feed_stay, feed_leave)
-    projections.append(projection)
-    terms0 = terms0 + [flight]
+    g_rest, feed_leave, feed_stay = stage(g_rest, feed_leave, feed_stay)
+    found = work(2, g_rest, g_rest_x, g_rest_c)
+    feed_got, flight0, found = stage(along(feed_leave, masks[0]), flight0, found)
+    got = sibling(found[4])
+    terms0 = terms0 + [flight0]
     z_leave = leaving(terms0)
-    terms1 = [keep, sibling(send)]
-    leave = leaving(terms1)
-    g_rest, leave, z_leave = stage(g_rest, leave, z_leave)
-    found = work(2, g_rest, g_rest_x, g_rest_c)
-    flight, z0, feed_got, found = stage(across(leave), along(z_leave, masks[0]), along(feed_leave, masks[0]), found)
-    terms0 = terms0 + [z0]
-    terms1 = terms1 + [flight]
-    z0_leave, z1_leave = leaving(terms0), leaving(terms1)
-    feed_parts = split(low_sum(feed_stay, feed_got), masks[1])
-    got = sibling(found[4])
-    found, z0_leave, z1_leave = stage(found, z0_leave, z1_leave)
-    terms1 = terms1 + [along(z1_leave, masks[0])]
-    terms0 = terms0 + [along(z0_leave, masks[1])]
-    projections.append(project(2, found))
-    got, projections[2] = stage(got, projections[2])
+    feed_stay, feed_leave = split(low_sum(feed_stay, feed_got), masks[1])
+    found, z_leave, feed_leave = stage(found, z_leave, feed_leave)
+    terms0 = terms0 + [along(z_leave, masks[0])]
+    feed_got = along(feed_leave, masks[1])
+    biases = added(*columns)[:2].reshape(-1)
+    lines = EXTRA * contexts
+    biases = jnp.pad(biases, (0, lines * depth - biases.shape[0])).reshape(lines, depth).astype(BF16)
+    if shards == 2:
+        staying, leave = project(2, found, [projection], (order, biases, *outs))
+        got, staying, leave = stage(got, staying, leave)
+        attn_got = rotated(leave, "shard", 2, 1)
+    else:
+        projected = jnp.concatenate([project(2, found, [projection]), added(*outs)[None]], axis=0)
+        stacked = jnp.stack([
+            jnp.concatenate([projected[..., r * depth : (r + 1) * depth].reshape(4 * cols, depth).astype(BF16), biases], axis=0)
+            for r in range(shards)])
+        staying = lax.psum_scatter(stacked, "shard", scatter_dimension=0)
+        attn_got = jnp.zeros_like(staying)
+        got, staying = stage(got, staying)
     terms2 = [found[3], got]
     leave = leaving(terms2)
     half = leave.shape[0] // 2
     flight_first = across(leave[half:])
     flight = across(leave[:half])
-
-    def scatter(parts, hop):
-        return parts[0], along(parts[1], masks[hop])
-
-    def collect(value, hop):
-        return along(value, masks[hop])
-
-    def merge(value, got, hop):
-        return join(value, got, masks[hop])
-
-    feed_parts, leave = stage(feed_parts, leave)
-    feed = scatter(feed_parts, 1)
-    projected = jnp.concatenate([added(*projections), added(*outs)[None]], axis=0)
-    biases = added(*columns)[:2].reshape(-1)
-    lines = EXTRA * contexts
-    biases = jnp.pad(biases, (0, lines * depth - biases.shape[0])).reshape(lines, depth)
-
-    def lined(value):
-        return jnp.concatenate([value.reshape(4 * cols, depth), biases], axis=0).astype(BF16)
-
-    if shards == 2:
-        left, right = projected[..., :depth], projected[..., depth:]
-        staying = lined(jnp.where(shard == 0, left, right))
-        attn = (staying, rotated(lined(jnp.where(shard == 0, right, left)), "shard", 2, 1))
-    else:
-        stacked = jnp.stack([lined(projected[..., r * depth : (r + 1) * depth]) for r in range(shards)])
-        attn = (lax.psum_scatter(stacked, "shard", scatter_dimension=0),)
-    terms1, staying = stage(terms1, attn[0])
-    attn = (staying,) + attn[1:]
+    flight1, leave = stage(flight1, leave)
+    terms1 = terms1 + [flight1]
+    z1_leave = leaving(terms1)
+    terms1 = terms1 + [along(z1_leave, masks[0])]
+    terms0, z1_leave = stage(terms0, z1_leave)
+    z0_leave = leaving(terms0)
+    terms0 = terms0 + [along(z0_leave, masks[1])]
+    feed_got, z0_leave = stage(feed_got, z0_leave)
+    feed = low_sum(feed_stay, feed_got)
+    feed_got = along(feed, masks[1])
+    flight_first, feed = stage(flight_first, feed)
+    z2_leave = leaving([t[: 2 * half] for t in terms2[:2]] + [jnp.concatenate([flight_first, flight_first], axis=0)])
+    z2 = along(z2_leave, masks[0])
+    terms1, z2_leave = stage(terms1, z2_leave)
     z1_leave = leaving(terms1)
     terms1 = terms1 + [along(z1_leave, masks[1])]
-    flight_first, z1_leave = stage(flight_first, z1_leave)
-    z2_leave = leaving([t[: 2 * half] for t in terms2[:2]] + [jnp.concatenate([flight_first, flight_first], axis=0)])
-    z2 = along(z2_leave, masks[0])
-    terms0, feed, z2_leave = stage(terms0, feed, z2_leave)
-    early = [settle(0, terms0)]
-    feed = low_sum(*feed)
-    feed_got = collect(feed, hops - 1)
-    attn, early, feed = stage(attn, early, feed)
-    attn = split(low_sum(*attn), masks[0])
+    attn_got, z1_leave = stage(attn_got, z1_leave)
+    attn = split(low_sum(staying, attn_got), masks[0])
     attn_got = along(attn[1], masks[0])
+    z2, flight, attn_leave = stage(z2, flight, attn[1])
+    terms2 = terms2 + [flight, z2]
+    z2_leave = leaving(terms2)
+    z2 = along(z2_leave, masks[1])
+    feed_got, terms0, z2_leave = stage(feed_got, terms0, z2_leave)
+    feed = join(feed, feed_got, masks[1])
+    feed_got = along(feed, masks[0])
+    early = settle(0, terms0)
+    attn_got, feed, early = stage(attn_got, feed, early)
+    attn = split(low_sum(attn[0], attn_got), masks[1])
+    attn_got = along(attn[1], masks[1])
     terms1, attn_leave = stage(terms1, attn[1])
-    early = jnp.concatenate(early + [settle(1, terms1)], axis=0)
+    early = jnp.concatenate([early, settle(1, terms1)], axis=0)
     early_x = paired(early)[1]
     result, early = stage(result, early)
     result_x = paired(result)[1]
-    z2, flight, early = stage(z2, flight, early)
-    terms2 = terms2 + [flight, z2]
-    z2_leave = leaving(terms2)
-    z2 = along(z2_leave, masks[1])
-    attn_got, z2_leave = stage(attn_got, z2_leave)
-    attn = split(low_sum(attn[0], attn_got), masks[1])
-    attn_got = along(attn[1], masks[1])
-    feed_got, early_x, attn_leave = stage(feed_got, early_x, attn[1])
-    feed = merge(feed, feed_got, hops - 1)
-    feed_got = collect(feed, 0)
-    z2, feed, early_x = stage(z2, feed, early_x)
+    z2, early = stage(z2, early)
     last = settle(2, terms2 + [z2])
     last_x = paired(last)[1]
+    attn_got, early_x, last = stage(attn_got, early_x, last)
+    attn = low_sum(attn[0], attn_got)
+    attn_got = along(attn, masks[1])
+    early = whole(early.reshape(early_x.shape), early_x)
+    last_x, early, attn = stage(last_x, early, attn)
+    last = whole(last.reshape(last_x.shape), last_x)
     attn_got, last = stage(attn_got, last)
-    attn = low_sum(attn[0], attn_got)
-    attn_got = collect(attn, 1)
-    result_x, attn, early, early_x = stage(result_x, attn, early, early_x)
-    early = whole(early.reshape(early_x.shape), early_x)
-    last_x, attn_got, early = stage(last_x, attn_got, early)
-    attn = merge(attn, attn_got, 1)
-    attn_got = collect(attn, 0)
-    last = whole(last.reshape(last_x.shape), last_x)
-    feed_got, last = stage(feed_got, last)
-    feed = merge(feed, feed_got, 0)
+    attn = join(attn, attn_got, masks[1])
+    attn_got = along(attn, masks[0])
+    result_x, feed_got, attn = stage(result_x, feed_got, attn)
+    feed = join(feed, feed_got, masks[0])
     outputs = whole(result.reshape(result_x.shape), result_x)
     attn_got, outputs, last, feed = stage(attn_got, outputs, last, feed)
-    attn = merge(attn, attn_got, 0)
+    attn = join(attn, attn_got, masks[0])
     input_grad = jnp.concatenate([early, last], axis=0)
 
     feed, attn = feed.astype(F32), attn.astype(F32)

time: 410 us -> 389 us (0.949)
  waiting for transfers between devices: 124 us -> 97.1 us
  starting transfers between devices: 66.7 us -> 71.3 us
    ppermute x19 -> x21, waiting for transfers between devices: 34.2 us -> 22.2 us  [across(): return lax.ppermute(value, 'tensor', [(i, i ^ 2) for i in range(4)])]
    ppermute x20, waiting for transfers between devices: 79.9 us -> 68 us  [along(): lax.ppermute(value, 'context', [(i, i ^ mask) for i in range(contexts)])]
    ppermute x19 -> x21, starting transfers between devices: 21.1 us -> 23.4 us  [across(): return lax.ppermute(value, 'tensor', [(i, i ^ 2) for i in range(4)])]
    convert_element_type x25 -> x26, other arithmetic: 28.6 us -> 30.9 us  [low_sum(): return added(*values).astype(BF16)]
    ppermute x8 -> x9, starting transfers between devices: 10.4 us -> 12.4 us  [rotated(): lax.ppermute(value, axis, [(i, (i + shift) % count) for i in range(count)])]
    unnamed x158 -> x157, local copies, waits for them, and re-layouts: 9.7 us -> 10 us
  transfers between devices with their start and end apart: 71 -> 74, of which waited for: 32 -> 28; matrix products, arithmetic and copies ran while one was open for 12% -> 14% of each run, Pallas kernels for 29% -> 31%
where the time goes in v3:
time: 389 us; the launch traced here: 385 us
  Pallas kernels  141 us (36%)
  waiting for transfers between devices  97.1 us (25%)
  starting transfers between devices  71.3 us (18%)
  other arithmetic  51.4 us (13%)
  local copies, waits for them, and re-layouts  21.8 us (6%)
    ppermute x20, waiting for transfers between devices, along(): lax.ppermute(value, 'context', [(i, i ^ mask) for i in range(contexts)])  68 us
    pallas_call x3, Pallas kernels, attention_backward(): pl.pallas_call(functools.partial(backward_body, heads, nears, index), out...  45.8 us
    pallas_call x3, Pallas kernels, attention_forward(): pl.pallas_call(functools.partial(forward_body, heads, index), out_shape=(...  41.6 us
    ppermute x20, starting transfers between devices, along(): lax.ppermute(value, 'context', [(i, i ^ mask) for i in range(contexts)])  31.4 us
    convert_element_type x26, other arithmetic, low_sum(): return added(*values).astype(BF16)  30.9 us
    ppermute x21, starting transfers between devices, across(): return lax.ppermute(value, 'tensor', [(i, i ^ 2) for i in range(4)])  23.4 us
    ppermute x21, waiting for transfers between devices, across(): return lax.ppermute(value, 'tensor', [(i, i ^ 2) for i in range(4)])  22.2 us
    pallas_call x1, Pallas kernels, feed_forward(): pl.pallas_call(functools.partial(feed_body, blocks, pieces, seqs), out_sh...  21.3 us
  transfers between devices with their start and end apart: 74, of which 28 were waited for; matrix products, arithmetic and copies ran while one was open for 14% of the time, Pallas kernels for 31%

profile of v3, /device:TPU:0, one launch (start us, length us, event | category | flops | bytes accessed | tf_op | source)
XLA Modules:
  0.0 385.1 jit_solution(14968799948142380090)
XLA Ops:
  0.7 1.8 fusion.20
  2.6 4.1 %collective-permute-start = (bf16[128,768]{1,0:T(8,128)(2,1)S(1)}, bf16[128,768]{1,0:T(8,128)(2,1)S(1)}, u32[]{:S(2)}, u32[]{:S(2)}) collective-permute-start(bf16[128,768]{1,0:T(8,128)(2,1)S(1)} %dynamic-slice_bitcast_fusion.2.refs_16_), channel_id=1, source_target_pairs={{0,8},{4,12},{8,0},{12,4},{1,9},{5,13},{9,1},{13,5},{2,10},{6,14},... | collective-permute-start | bytes 589832 | tf_op jit(solution)/shard_map/ppermute | solution.py:548
  10.8 2.0 pad_maximum_fusion.13.refs_0_
  12.8 3.0 collective-permute-done
  15.8 1.5 collective-permute-start.2
  17.3 1.5 collective-permute-start.1
  19.6 3.4 collective-permute-start.4
  23.0 8.8 %collective-permute-done.4 = bf16[128,768]{1,0:T(8,128)(2,1)S(1)} collective-permute-done((bf16[128,768]{1,0:T(8,128)(2,1)S(1)}, bf16[128,768]{1,0:T(8,128)(2,1)S(1)}, u32[]{:S(2)}, u32[]{:S(2)}) %collective-permute-start.4) | collective-permute-done | bytes 196640 | tf_op jit(solution)/shard_map/ppermute | solution.py:548
  35.5 3.2 collective-permute-start.7
  38.7 1.9 collective-permute-start.8
  42.9 6.9 %collective-permute-done.8 = bf16[128,768]{1,0:T(8,128)(2,1)S(1)} collective-permute-done((bf16[128,768]{1,0:T(8,128)(2,1)}, bf16[128,768]{1,0:T(8,128)(2,1)S(1)}, u32[]{:S(2)}, u32[]{:S(2)}) %collective-permute-start.8) | collective-permute-done | bytes 196640 | tf_op jit(solution)/shard_map/ppermute | solution.py:548
  52.7 1.6 collective-permute-start.12
  54.3 1.5 collective-permute-start.11
  57.4 1.9 collective-permute-start.13
  59.9 13.9 %attention_forward.3 = (bf16[512,192]{1,0:T(8,128)(2,1)}, bf16[2048,192]{1,0:T(8,128)(2,1)}, bf16[2048,192]{1,0:T(8,128)(2,1)}, bf16[512,192]{1,0:T(8,128)(2,1)}...) custom-call(s32[4]{0:T(128)} %pad_add_fusion.places, bf16[3,512,768]{2,1,0:T(8,128)(2,1)} %refs_0_.5, ...), custom_call_target="tpu_custom_call" | custom-call | flops 4429185024 | bytes 5505024 | tf_op jit(solution)/shard_map/attention_forward/pallas_call | solution.py:189
  75.6 1.6 collective-permute-start.19
  77.3 1.6 collective-permute-start.18
  79.6 1.6 collective-permute-start.16
  81.2 13.8 %attention_forward.4 = (bf16[512,192]{1,0:T(8,128)(2,1)}, bf16[2048,192]{1,0:T(8,128)(2,1)}, bf16[2048,192]{1,0:T(8,128)(2,1)}, bf16[512,192]{1,0:T(8,128)(2,1)}...) custom-call(s32[4]{0:T(128)} %pad_add_fusion.places, bf16[3,512,768]{2,1,0:T(8,128)(2,1)} %refs_0_.5, ...), custom_call_target="tpu_custom_call" | custom-call | flops 4429185024 | bytes 5505024 | tf_op jit(solution)/shard_map/attention_forward/pallas_call | solution.py:189
  95.1 2.2 collective-permute-done.16
  98.0 1.6 collective-permute-start.22
  99.6 1.6 collective-permute-start.21
  102.5 13.9 %attention_forward.5 = (bf16[512,192]{1,0:T(8,128)(2,1)}, bf16[2048,192]{1,0:T(8,128)(2,1)}, bf16[2048,192]{1,0:T(8,128)(2,1)}, bf16[512,192]{1,0:T(8,128)(2,1)}...) custom-call(s32[4]{0:T(128)} %pad_add_fusion.places, bf16[3,512,768]{2,1,0:T(8,128)(2,1)} %refs_0_.5, ...), custom_call_target="tpu_custom_call" | custom-call | flops 4429185024 | bytes 5505024 | tf_op jit(solution)/shard_map/attention_forward/pallas_call | solution.py:189
  118.7 1.9 collective-permute-done.32.refs_24_
  124.5 4.9 %collective-permute-done.33.refs_27_ = bf16[128,768]{1,0:T(8,128)(2,1)S(1)} collective-permute-done((bf16[128,768]{1,0:T(8,128)(2,1)S(1)}, bf16[128,768]{1,0:T(8,128)(2,1)S(1)}, u32[]{:S(2)}, u32[]{:S(2)}) %collective-permute-start.33) | collective-permute-done | bytes 196640 | tf_op jit(solution)/shard_map/ppermute | solution.py:500
  131.3 21.3 %feed_forward.1 = (bf16[384,768]{1,0:T(8,128)(2,1)}, bf16[128,768]{1,0:T(8,128)(2,1)}, bf16[256,768]{1,0:T(8,128)(2,1)}, f32[384,768]{1,0:T(8,128)}, bf16[4,384,...) custom-call(s32[5]{0:T(128)} %concatenate.73.order.refs_8_, ...), custom_call_target="tpu_custom_call" | custom-call | flops 7247757312 | bytes 14155776 | tf_op jit(solution)/shard_map/feed_forward/pallas_call | solution.py:411
  153.6 7.2 %feed_gradients.2 = (bf16[2,2,448,768]{3,2,1,0:T(8,128)(2,1)}, bf16[2,2,384,768]{3,2,1,0:T(8,128)(2,1)}) custom-call(s32[5]{0:T(128)} %concatenate.73.order.refs_8_, bf16[4,384,768]{2,1,0:T(8,128)(2,1)} %get-tuple-element.354.act, bf16[4,384,768]{2,1,0:T(8,128)(2,1)} %get-tuple-element.366.d_inner, bf16[384,768]{1,0:T(8,128)(2,1)} %get-tuple-element.356.d_ffn, ...), custom_call_target="tpu_custom_call" | custom-call | flops 1811939328 | bytes 4718592 | tf_op jit(solution)/shard_map/feed_gradients/pallas_call | solution.py:474
  162.7 7.4 %feed_gradients.3 = (bf16[2,2,448,768]{3,2,1,0:T(8,128)(2,1)}, bf16[2,2,384,768]{3,2,1,0:T(8,128)(2,1)}) custom-call(s32[5]{0:T(128)} %concatenate.73.order.refs_8_, bf16[4,384,768]{2,1,0:T(8,128)(2,1)} %get-tuple-element.354.act, bf16[4,384,768]{2,1,0:T(8,128)(2,1)} %get-tuple-element.366.d_inner, bf16[384,768]{1,0:T(8,128)(2,1)} %get-tuple-element.356.d_ffn, ...), custom_call_target="tpu_custom_call" | custom-call | flops 1811939328 | bytes 4718592 | tf_op jit(solution)/shard_map/feed_gradients/pallas_call | solution.py:474
  170.9 3.0 fusion.13
  176.9 1.5 collective-permute-start.40
  178.4 15.0 %attention_backward.3 = (bf16[512,192]{1,0:T(8,128)(2,1)}, bf16[2048,192]{1,0:T(8,128)(2,1)}, bf16[2048,192]{1,0:T(8,128)(2,1)}, bf16[1024,768]{1,0:T(8,128)(2,1...) custom-call(s32[4]{0:T(128)} %pad_add_fusion.places, ...), custom_call_target="tpu_custom_call" | custom-call | flops 9261023232 | bytes 7077888 | tf_op jit(solution)/shard_map/attention_backward/pallas_call | solution.py:220
  193.7 2.5 fusion.7
  198.2 1.5 collective-permute-start.43
  199.7 15.4 %attention_backward.4 = (bf16[512,192]{1,0:T(8,128)(2,1)}, bf16[2048,192]{1,0:T(8,128)(2,1)}, bf16[2048,192]{1,0:T(8,128)(2,1)}, bf16[1024,768]{1,0:T(8,128)(2,1...) custom-call(s32[4]{0:T(128)} %pad_add_fusion.places, ...), custom_call_target="tpu_custom_call" | custom-call | flops 9261023232 | bytes 7077888 | tf_op jit(solution)/shard_map/attention_backward/pallas_call | solution.py:220
  220.3 5.4 %attention_gradients.3.refs_7_ = f32[3,192,768]{2,1,0:T(8,128)} custom-call(bf16[3,512,768]{2,1,0:T(8,128)(2,1)} %refs_0_.5, bf16[384,768]{1,0:T(8,128)(2,1)} %constant_dynamic-update-slice_fusion.1.near.refs_1_, bf16[384,768]{1,0:T(8,128)(2,1)} %copy-done.1, bf16[768,768]{1,0:T(8,128)(2,1)} %collective-permute-done.9.sib.refs_3_, ...), custom_call_target="tpu_custom_call" | custom-call | flops 1207959552 | bytes 4718592 | tf_op jit(solution)/shard_map/attention_gradients/pallas_call | solution.py:299
  225.8 2.2 add_convert_fusion.1
  228.0 6.1 %attention_gradients.4.refs_7_ = f32[3,192,768]{2,1,0:T(8,128)} custom-call(bf16[3,512,768]{2,1,0:T(8,128)(2,1)} %refs_0_.5, bf16[384,768]{1,0:T(8,128)(2,1)} %copy-done.22, bf16[384,768]{1,0:T(8,128)(2,1)} %copy-done.8, bf16[768,768]{1,0:T(8,128)(2,1)} %copy-done.21, bf16[512,192]{1,0:T(8,128)(2,1)} %get-tuple-element.435.refs_4_, ...), custom_call_target="tpu_custom_call" | custom-call | flops 1207959552 | bytes 4718592 | tf_op jit(solution)/shard_map/attention_gradients/pallas_call | solution.py:299
  235.0 1.8 fusion.6
  236.8 1.8 fusion.2
  238.6 1.8 fusion.10
  240.3 1.9 collective-permute-start.48
  242.2 15.4 %attention_backward.5 = (bf16[512,192]{1,0:T(8,128)(2,1)}, bf16[2048,192]{1,0:T(8,128)(2,1)}, bf16[2048,192]{1,0:T(8,128)(2,1)}, bf16[1024,768]{1,0:T(8,128)(2,1...) custom-call(s32[4]{0:T(128)} %pad_add_fusion.places, ...), custom_call_target="tpu_custom_call" | custom-call | flops 9261023232 | bytes 7077888 | tf_op jit(solution)/shard_map/attention_backward/pallas_call | solution.py:220
  263.0 1.9 add_convert_fusion.11
  265.3 2.5 collective-permute-start.52
  267.8 6.5 %attention_gradients.5 = (bf16[832,384]{1,0:T(8,128)(2,1)}, bf16[832,384]{1,0:T(8,128)(2,1)}) custom-call(bf16[3,512,768]{2,1,0:T(8,128)(2,1)} %refs_0_.5, bf16[384,768]{1,0:T(8,128)(2,1)} %copy-done.23, bf16[384,768]{1,0:T(8,128)(2,1)} %copy-done.7, bf16[768,768]{1,0:T(8,128)(2,1)} %copy-done.20, bf16[512,192]{1,0:T(8,128)(2,1)} %get-tuple-element.466.refs_4_, ...), custom_call_target="tpu_custom_call" | custom-call | flops 1207959552 | bytes 4718592 | tf_op jit(solution)/shard_map/attention_gradients/pallas_call | solution.py:299
  274.3 1.4 add_convert_fusion
  275.7 4.5 %collective-permute-done.54 = bf16[512,768]{1,0:T(8,128)(2,1)S(1)} collective-permute-done((bf16[512,768]{1,0:T(8,128)(2,1)}, bf16[512,768]{1,0:T(8,128)(2,1)S(1)}, u32[]{:S(2)}, u32[]{:S(2)}) %collective-permute-start.54) | collective-permute-done | bytes 786464 | tf_op jit(solution)/shard_map/ppermute | solution.py:500
  286.6 1.5 collective-permute-start.57
  290.1 5.2 %collective-permute-done.51 = bf16[256,768]{1,0:T(8,128)(2,1)S(1)} collective-permute-done((bf16[256,768]{1,0:T(8,128)(2,1)S(1)}, bf16[256,768]{1,0:T(8,128)(2,1)S(1)}, u32[]{:S(2)}, u32[]{:S(2)}) %collective-permute-start.51) | collective-permute-done | bytes 393248 | tf_op jit(solution)/shard_map/ppermute | solution.py:500
  295.2 1.4 collective-permute-start.61
  297.8 1.5 collective-permute-start.55
  300.3 1.4 collective-permute-done.57
  301.7 1.6 collective-permute-start.63
  304.2 18.2 %collective-permute-done.55 = bf16[256,768]{1,0:T(8,128)(2,1)S(1)} collective-permute-done((bf16[256,768]{1,0:T(8,128)(2,1)S(1)}, bf16[256,768]{1,0:T(8,128)(2,1)S(1)}, u32[]{:S(2)}, u32[]{:S(2)}) %collective-permute-start.55) | collective-permute-done | bytes 393248 | tf_op jit(solution)/shard_map/ppermute | solution.py:548
  324.8 1.5 collective-permute-done.60
  330.0 6.5 %collective-permute-done.59 = bf16[128,768]{1,0:T(8,128)(2,1)S(1)} collective-permute-done((bf16[128,768]{1,0:T(8,128)(2,1)S(1)}, bf16[128,768]{1,0:T(8,128)(2,1)S(1)}, u32[]{:S(2)}, u32[]{:S(2)}) %collective-permute-start.59) | collective-permute-done | bytes 196640 | tf_op jit(solution)/shard_map/ppermute | solution.py:548
  342.4 3.3 collective-permute-done.64
  346.9 2.2 collective-permute-start.68
  349.4 14.5 %collective-permute-done.68 = bf16[208,384]{1,0:T(8,128)(2,1)S(1)} collective-permute-done((bf16[208,384]{1,0:T(8,128)(2,1)S(1)}, bf16[208,384]{1,0:T(8,128)(2,1)S(1)}, u32[]{:S(2)}, u32[]{:S(2)}) %collective-permute-start.68) | collective-permute-done | bytes 159776 | tf_op jit(solution)/shard_map/ppermute | solution.py:548
  363.9 2.1 collective-permute-done.72
  370.7 1.5 select_bitcast_fusion.3
  372.5 1.6 copy.36
  374.0 3.4 collective-permute-done.70
  383.3 1.6 pad_maximum_fusion.1
  (346 shorter events, 84.2 us)
Async XLA Ops:
  2.6 13.2 %collective-permute-start = (bf16[128,768]{1,0:T(8,128)(2,1)S(1)}, bf16[128,768]{1,0:T(8,128)(2,1)S(1)}, u32[]{:S(2)}, u32[]{:S(2)}) collective-permute-start(bf16[128,768]{1,0:T(8,128)(2,1)S(1)} %dynamic-slice_bitcast_fusion.2.refs_16_), channel_id=1, source_target_pairs={{0,8},{4,12},{8,0},{12,4},{1,9},{5,13},{9,1},{13,5},{2,10},{6,14},... | collective-permute-start | bytes 589832 | tf_op jit(solution)/shard_map/ppermute | solution.py:548
  15.8 16.8 %collective-permute-start.2 = (bf16[400,768]{1,0:T(8,128)(2,1)}, bf16[400,768]{1,0:T(8,128)(2,1)}, u32[]{:S(2)}, u32[]{:S(2)}) collective-permute-start(bf16[400,768]{1,0:T(8,128)(2,1)} %pad_maximum_fusion.13.refs_0_), channel_id=1, source_target_pairs={{0,2},{1,3},{2,0},{3,1},{4,6},{5,7},{6,4},{7,5},{8,10},{9,11},{10,... | collective-permute-start | bytes 1843208 | tf_op jit(solution)/shard_map/ppermute | solution.py:500
  17.3 15.3 %collective-permute-start.1 = (bf16[4,192,384]{2,1,0:T(8,128)(2,1)S(1)}, bf16[4,192,384]{2,1,0:T(8,128)(2,1)S(1)}, u32[]{:S(2)}, u32[]{:S(2)}) collective-permute-start(bf16[4,192,384]{2,1,0:T(8,128)(2,1)S(1)} %pad_maximum_fusion.14), channel_id=1, source_target_pairs={{0,16},{16,0},{1,17},{17,1},{2,18},{18,2},{3,19},{19,3},{4,20},{20... | collective-permute-start | bytes 1769480 | tf_op jit(solution)/shard_map/ppermute | solution.py:496
  18.9 13.7 %collective-permute-start.3 = (bf16[256,768]{1,0:T(8,128)(2,1)S(1)}, bf16[256,768]{1,0:T(8,128)(2,1)S(1)}, u32[]{:S(2)}, u32[]{:S(2)}) collective-permute-start(bf16[256,768]{1,0:T(8,128)(2,1)S(1)} %pad_maximum_fusion.15), channel_id=1, source_target_pairs={{0,4},{4,0},{8,12},{12,8},{1,5},{5,1},{9,13},{13,9},{2,6},{6,2},{1... | collective-permute-start | bytes 1179656 | tf_op jit(solution)/shard_map/ppermute | solution.py:548
  19.6 12.2 %collective-permute-start.4 = (bf16[128,768]{1,0:T(8,128)(2,1)S(1)}, bf16[128,768]{1,0:T(8,128)(2,1)S(1)}, u32[]{:S(2)}, u32[]{:S(2)}) collective-permute-start(bf16[128,768]{1,0:T(8,128)(2,1)S(1)} %get-tuple-element.285.refs_17_), channel_id=1, source_target_pairs={{0,8},{4,12},{8,0},{12,4},{1,9},{5,13},{9,1},{13,5},{2,10},{6,14},... | collective-permute-start | bytes 589832 | tf_op jit(solution)/shard_map/ppermute | solution.py:548
  33.3 17.1 %collective-permute-start.5 = (bf16[400,768]{1,0:T(8,128)(2,1)}, bf16[400,768]{1,0:T(8,128)(2,1)}, u32[]{:S(2)}, u32[]{:S(2)}) collective-permute-start(bf16[400,768]{1,0:T(8,128)(2,1)} %pad_maximum_fusion.13.refs_0_), channel_id=1, source_target_pairs={{0,16},{16,0},{1,17},{17,1},{2,18},{18,2},{3,19},{19,3},{4,20},{20... | collective-permute-start | bytes 1843208 | tf_op jit(solution)/shard_map/ppermute | solution.py:496
  34.6 15.8 %collective-permute-start.6 = (bf16[384,768]{1,0:T(8,128)(2,1)}, bf16[384,768]{1,0:T(8,128)(2,1)S(1)}, u32[]{:S(2)}, u32[]{:S(2)}) collective-permute-start(bf16[384,768]{1,0:T(8,128)(2,1)} %constant_dynamic-update-slice_fusion.1.near.refs_1_), channel_id=1, source_target_pairs={{0,2},{1,3},{2,0},{3,1},{4,6},{5,7},{6,4},{7,5},{8,10},{9,11},{10,... | collective-permute-start | bytes 1769480 | tf_op jit(solution)/shard_map/ppermute | solution.py:500
  35.5 15.0 %collective-permute-start.7 = (bf16[256,768]{1,0:T(8,128)(2,1)S(1)}, bf16[256,768]{1,0:T(8,128)(2,1)S(1)}, u32[]{:S(2)}, u32[]{:S(2)}) collective-permute-start(bf16[256,768]{1,0:T(8,128)(2,1)S(1)} %pad_maximum_fusion.16), channel_id=1, source_target_pairs={{0,4},{4,0},{8,12},{12,8},{1,5},{5,1},{9,13},{13,9},{2,6},{6,2},{1... | collective-permute-start | bytes 1179656 | tf_op jit(solution)/shard_map/ppermute | solution.py:548
  38.7 11.1 %collective-permute-start.8 = (bf16[128,768]{1,0:T(8,128)(2,1)}, bf16[128,768]{1,0:T(8,128)(2,1)S(1)}, u32[]{:S(2)}, u32[]{:S(2)}) collective-permute-start(bf16[128,768]{1,0:T(8,128)(2,1)} %get-tuple-element.296.refs_18_), channel_id=1, source_target_pairs={{0,8},{4,12},{8,0},{12,4},{1,9},{5,13},{9,1},{13,5},{2,10},{6,14},... | collective-permute-start | bytes 589832 | tf_op jit(solution)/shard_map/ppermute | solution.py:548
  51.7 7.6 %collective-permute-start.9 = (bf16[768,768]{1,0:T(8,128)(2,1)}, bf16[768,768]{1,0:T(8,128)(2,1)}, u32[]{:S(2)}, u32[]{:S(2)}) collective-permute-start(bf16[768,768]{1,0:T(8,128)(2,1)} %pad_maximum_fusion.5), channel_id=1, source_target_pairs={{0,1},{1,0},{2,3},{3,2},{4,5},{5,4},{6,7},{7,6},{8,9},{9,8},{10,11... | collective-permute-start | bytes 3538952 | tf_op jit(solution)/shard_map/ppermute | solution.py:504
  52.7 21.2 %collective-permute-start.12 = (bf16[384,768]{1,0:T(8,128)(2,1)S(1)}, bf16[384,768]{1,0:T(8,128)(2,1)S(1)}, u32[]{:S(2)}, u32[]{:S(2)}) collective-permute-start(bf16[384,768]{1,0:T(8,128)(2,1)S(1)} %constant_dynamic-update-slice_fusion.3.near.refs_1_), channel_id=1, source_target_pairs={{0,2},{1,3},{2,0},{3,1},{4,6},{5,7},{6,4},{7,5},{8,10},{9,11},{10,... | collective-permute-start | bytes 1769480 | tf_op jit(solution)/shard_map/ppermute | solution.py:500
  54.3 19.6 %collective-permute-start.11 = (bf16[384,768]{1,0:T(8,128)(2,1)S(1)}, bf16[384,768]{1,0:T(8,128)(2,1)S(1)}, u32[]{:S(2)}, u32[]{:S(2)}) collective-permute-start(bf16[384,768]{1,0:T(8,128)(2,1)S(1)} %bitcast.207), channel_id=1, source_target_pairs={{0,16},{16,0},{1,17},{17,1},{2,18},{18,2},{3,19},{19,3},{4,20},{20... | collective-permute-start | bytes 1769480 | tf_op jit(solution)/shard_map/ppermute | solution.py:496
  57.4 16.5 %collective-permute-start.13 = (bf16[256,768]{1,0:T(8,128)(2,1)S(1)}, bf16[256,768]{1,0:T(8,128)(2,1)S(1)}, u32[]{:S(2)}, u32[]{:S(2)}) collective-permute-start(bf16[256,768]{1,0:T(8,128)(2,1)S(1)} %pad_maximum_fusion.17), channel_id=1, source_target_pairs={{0,4},{4,0},{8,12},{12,8},{1,5},{5,1},{9,13},{13,9},{2,6},{6,2},{1... | collective-permute-start | bytes 1179656 | tf_op jit(solution)/shard_map/ppermute | solution.py:548
  59.3 15.6 %collective-permute-start.10 = (bf16[192,768]{1,0:T(8,128)(2,1)S(1)}, bf16[192,768]{1,0:T(8,128)(2,1)S(1)}, u32[]{:S(2)}, u32[]{:S(2)}) collective-permute-start(bf16[192,768]{1,0:T(8,128)(2,1)S(1)} %slice.331), channel_id=1, source_target_pairs={{0,2},{1,3},{2,0},{3,1},{4,6},{5,7},{6,4},{7,5},{8,10},{9,11},{10,... | collective-permute-start | bytes 884744 | tf_op jit(solution)/shard_map/ppermute | solution.py:500
  74.9 4.7 %collective-permute-start.14 = (bf16[768,768]{1,0:T(8,128)(2,1)S(1)}, bf16[768,768]{1,0:T(8,128)(2,1)S(1)}, u32[]{:S(2)}, u32[]{:S(2)}) collective-permute-start(bf16[768,768]{1,0:T(8,128)(2,1)S(1)} %pad_maximum_fusion.6), channel_id=1, source_target_pairs={{0,1},{1,0},{2,3},{3,2},{4,5},{5,4},{6,7},{7,6},{8,9},{9,8},{10,11... | collective-permute-start | bytes 3538952 | tf_op jit(solution)/shard_map/ppermute | solution.py:504
  75.6 19.4 %collective-permute-start.19 = (bf16[384,768]{1,0:T(8,128)(2,1)S(1)}, bf16[384,768]{1,0:T(8,128)(2,1)S(1)}, u32[]{:S(2)}, u32[]{:S(2)}) collective-permute-start(bf16[384,768]{1,0:T(8,128)(2,1)S(1)} %constant_dynamic-update-slice_fusion.5.near.refs_1_), channel_id=1, source_target_pairs={{0,2},{1,3},{2,0},{3,1},{4,6},{5,7},{6,4},{7,5},{8,10},{9,11},{10,... | collective-permute-start | bytes 1769480 | tf_op jit(solution)/shard_map/ppermute | solution.py:500
  77.2 17.9 %collective-permute-start.17 = (bf16[400,768]{1,0:T(8,128)(2,1)}, bf16[400,768]{1,0:T(8,128)(2,1)S(1)}, u32[]{:S(2)}, u32[]{:S(2)}) collective-permute-start(bf16[400,768]{1,0:T(8,128)(2,1)} %pad_maximum_fusion.13.refs_0_), channel_id=1, source_target_pairs={{0,1},{1,0},{2,3},{3,2},{4,5},{5,4},{6,7},{7,6},{8,9},{9,8},{10,11... | collective-permute-start | bytes 1843208 | tf_op jit(solution)/shard_map/ppermute | solution.py:504
  77.3 17.8 %collective-permute-start.18 = (bf16[400,768]{1,0:T(8,128)(2,1)}, bf16[400,768]{1,0:T(8,128)(2,1)}, u32[]{:S(2)}, u32[]{:S(2)}) collective-permute-start(bf16[400,768]{1,0:T(8,128)(2,1)} %collective-permute-done.2.refs_2_), channel_id=1, source_target_pairs={{0,16},{16,0},{1,17},{17,1},{2,18},{18,2},{3,19},{19,3},{4,20},{20... | collective-permute-start | bytes 1843208 | tf_op jit(solution)/shard_map/ppermute | solution.py:496
  79.6 17.7 %collective-permute-start.16 = (bf16[192,768]{1,0:T(8,128)(2,1)S(1)}, bf16[192,768]{1,0:T(8,128)(2,1)S(1)}, u32[]{:S(2)}, u32[]{:S(2)}) collective-permute-start(bf16[192,768]{1,0:T(8,128)(2,1)S(1)} %slice.332), channel_id=1, source_target_pairs={{0,2},{1,3},{2,0},{3,1},{4,6},{5,7},{6,4},{7,5},{8,10},{9,11},{10,... | collective-permute-start | bytes 884744 | tf_op jit(solution)/shard_map/ppermute | solution.py:500
  98.0 18.5 %collective-permute-start.22 = (bf16[128,768]{1,0:T(8,128)(2,1)S(1)}, bf16[128,768]{1,0:T(8,128)(2,1)S(1)}, u32[]{:S(2)}, u32[]{:S(2)}) collective-permute-start(bf16[128,768]{1,0:T(8,128)(2,1)S(1)} %add_convert_fusion.22), channel_id=1, source_target_pairs={{0,2},{1,3},{2,0},{3,1},{4,6},{5,7},{6,4},{7,5},{8,10},{9,11},{10,... | collective-permute-start | bytes 589832 | tf_op jit(solution)/shard_map/ppermute | solution.py:500
  99.6 16.9 %collective-permute-start.21 = (bf16[384,768]{1,0:T(8,128)(2,1)S(1)}, bf16[384,768]{1,0:T(8,128)(2,1)}, u32[]{:S(2)}, u32[]{:S(2)}) collective-permute-start(bf16[384,768]{1,0:T(8,128)(2,1)S(1)} %constant_dynamic-update-slice_fusion.7.refs_10_), channel_id=1, source_target_pairs={{0,16},{16,0},{1,17},{17,1},{2,18},{18,2},{3,19},{19,3},{4,20},{20... | collective-permute-start | bytes 1769480 | tf_op jit(solution)/shard_map/ppermute | solution.py:496
  101.2 15.3 %collective-permute-start.20 = (bf16[384,768]{1,0:T(8,128)(2,1)S(1)}, bf16[384,768]{1,0:T(8,128)(2,1)S(1)}, u32[]{:S(2)}, u32[]{:S(2)}) collective-permute-start(bf16[384,768]{1,0:T(8,128)(2,1)S(1)} %bitcast.210), channel_id=1, source_target_pairs={{0,1},{1,0},{2,3},{3,2},{4,5},{5,4},{6,7},{7,6},{8,9},{9,8},{10,11... | collective-permute-start | bytes 1769480 | tf_op jit(solution)/shard_map/ppermute | solution.py:504
  101.3 15.2 %collective-permute-start.25 = (bf16[128,768]{1,0:T(8,128)(2,1)S(1)}, bf16[128,768]{1,0:T(8,128)(2,1)S(1)}, u32[]{:S(2)}, u32[]{:S(2)}) collective-permute-start(bf16[128,768]{1,0:T(8,128)(2,1)S(1)} %add_convert_fusion.21), channel_id=1, source_target_pairs={{0,2},{1,3},{2,0},{3,1},{4,6},{5,7},{6,4},{7,5},{8,10},{9,11},{10,... | collective-permute-start | bytes 589832 | tf_op jit(solution)/shard_map/ppermute | solution.py:500
  118.2 11.2 %collective-permute-start.26 = (bf16[400,768]{1,0:T(8,128)(2,1)}, bf16[400,768]{1,0:T(8,128)(2,1)S(1)}, u32[]{:S(2)}, u32[]{:S(2)}) collective-permute-start(bf16[400,768]{1,0:T(8,128)(2,1)} %collective-permute-done.5.refs_1_), channel_id=1, source_target_pairs={{0,1},{1,0},{2,3},{3,2},{4,5},{5,4},{6,7},{7,6},{8,9},{9,8},{10,11... | collective-permute-start | bytes 1843208 | tf_op jit(solution)/shard_map/ppermute | solution.py:504
  118.3 11.1 %collective-permute-start.27 = (bf16[400,768]{1,0:T(8,128)(2,1)}, bf16[400,768]{1,0:T(8,128)(2,1)S(1)}, u32[]{:S(2)}, u32[]{:S(2)}) collective-permute-start(bf16[400,768]{1,0:T(8,128)(2,1)} %collective-permute-done.2.refs_2_), channel_id=1, source_target_pairs={{0,1},{1,0},{2,3},{3,2},{4,5},{5,4},{6,7},{7,6},{8,9},{9,8},{10,11... | collective-permute-start | bytes 1843208 | tf_op jit(solution)/shard_map/ppermute | solution.py:504
  120.6 8.8 %collective-permute-start.28 = (bf16[400,768]{1,0:T(8,128)(2,1)}, bf16[400,768]{1,0:T(8,128)(2,1)S(1)}, u32[]{:S(2)}, u32[]{:S(2)}) collective-permute-start(bf16[400,768]{1,0:T(8,128)(2,1)} %collective-permute-done.18.refs_3_), channel_id=1, source_target_pairs={{0,1},{1,0},{2,3},{3,2},{4,5},{5,4},{6,7},{7,6},{8,9},{9,8},{10,11... | collective-permute-start | bytes 1843208 | tf_op jit(solution)/shard_map/ppermute | solution.py:504
  122.2 7.2 %collective-permute-start.33 = (bf16[128,768]{1,0:T(8,128)(2,1)S(1)}, bf16[128,768]{1,0:T(8,128)(2,1)S(1)}, u32[]{:S(2)}, u32[]{:S(2)}) collective-permute-start(bf16[128,768]{1,0:T(8,128)(2,1)S(1)} %add_convert_fusion.20), channel_id=1, source_target_pairs={{0,2},{1,3},{2,0},{3,1},{4,6},{5,7},{6,4},{7,5},{8,10},{9,11},{10,... | collective-permute-start | bytes 589832 | tf_op jit(solution)/shard_map/ppermute | solution.py:500
  152.6 8.1 %collective-permute-start.34 = (bf16[128,768]{1,0:T(8,128)(2,1)}, bf16[128,768]{1,0:T(8,128)(2,1)S(1)}, u32[]{:S(2)}, u32[]{:S(2)}) collective-permute-start(bf16[128,768]{1,0:T(8,128)(2,1)} %get-tuple-element.378.g_own), channel_id=1, source_target_pairs={{0,2},{1,3},{2,0},{3,1},{4,6},{5,7},{6,4},{7,5},{8,10},{9,11},{10,... | collective-permute-start | bytes 589832 | tf_op jit(solution)/shard_map/ppermute | solution.py:500
  160.7 9.4 %collective-permute-start.37 = (bf16[2,2,448,768]{3,2,1,0:T(8,128)(2,1)}, bf16[2,2,448,768]{3,2,1,0:T(8,128)(2,1)S(1)}, u32[]{:S(2)}, u32[]{:S(2)}) collective-permute-start(bf16[2,2,448,768]{3,2,1,0:T(8,128)(2,1)} %get-tuple-element.364), channel_id=1, source_target_pairs={{0,1},{1,0},{2,3},{3,2},{4,5},{5,4},{6,7},{7,6},{8,9},{9,8},{10,11... | collective-permute-start | bytes 8257544 | tf_op jit(solution)/shard_map/ppermute | solution.py:504
  160.8 9.3 %collective-permute-start.38 = (bf16[2,2,384,768]{3,2,1,0:T(8,128)(2,1)}, bf16[2,2,384,768]{3,2,1,0:T(8,128)(2,1)}, u32[]{:S(2)}, u32[]{:S(2)}) collective-permute-start(bf16[2,2,384,768]{3,2,1,0:T(8,128)(2,1)} %get-tuple-element.365), channel_id=1, source_target_pairs={{0,1},{1,0},{2,3},{3,2},{4,5},{5,4},{6,7},{7,6},{8,9},{9,8},{10,11... | collective-permute-start | bytes 7077896 | tf_op jit(solution)/shard_map/ppermute | solution.py:504
  161.3 8.8 %collective-permute-start.36 = (bf16[256,768]{1,0:T(8,128)(2,1)S(1)}, bf16[256,768]{1,0:T(8,128)(2,1)S(1)}, u32[]{:S(2)}, u32[]{:S(2)}) collective-permute-start(bf16[256,768]{1,0:T(8,128)(2,1)S(1)} %pad_maximum_fusion.18), channel_id=1, source_target_pairs={{0,1},{1,0},{2,3},{3,2},{4,5},{5,4},{6,7},{7,6},{8,9},{9,8},{10,11... | collective-permute-start | bytes 1179656 | tf_op jit(solution)/shard_map/ppermute | solution.py:504
  161.5 13.6 %collective-permute-start.35 = (bf16[256,768]{1,0:T(8,128)(2,1)S(1)}, bf16[256,768]{1,0:T(8,128)(2,1)S(1)}, u32[]{:S(2)}, u32[]{:S(2)}) collective-permute-start(bf16[256,768]{1,0:T(8,128)(2,1)S(1)} %copy-done.37), channel_id=1, source_target_pairs={{0,2},{1,3},{2,0},{3,1},{4,6},{5,7},{6,4},{7,5},{8,10},{9,11},{10,... | collective-permute-start | bytes 1179656 | tf_op jit(solution)/shard_map/ppermute | solution.py:500
  175.8 17.9 %collective-permute-start.41 = (bf16[512,768]{1,0:T(8,128)(2,1)S(1)}, bf16[512,768]{1,0:T(8,128)(2,1)}, u32[]{:S(2)}, u32[]{:S(2)}) collective-permute-start(bf16[512,768]{1,0:T(8,128)(2,1)S(1)} %pad_maximum_fusion.9), channel_id=1, source_target_pairs={{0,1},{1,0},{2,3},{3,2},{4,5},{5,4},{6,7},{7,6},{8,9},{9,8},{10,11... | collective-permute-start | bytes 2359304 | tf_op jit(solution)/shard_map/ppermute | solution.py:504
  176.0 17.7 %collective-permute-start.39 = (bf16[448,768]{1,0:T(8,128)(2,1)S(1)}, bf16[448,768]{1,0:T(8,128)(2,1)S(1)}, u32[]{:S(2)}, u32[]{:S(2)}) collective-permute-start(bf16[448,768]{1,0:T(8,128)(2,1)S(1)} %get-tuple-element.375), channel_id=1, source_target_pairs={{0,2},{1,3},{2,0},{3,1},{4,6},{5,7},{6,4},{7,5},{8,10},{9,11},{10,... | collective-permute-start | bytes 2064392 | tf_op jit(solution)/shard_map/ppermute | solution.py:500
  176.9 16.5 %collective-permute-start.40 = (bf16[384,768]{1,0:T(8,128)(2,1)}, bf16[384,768]{1,0:T(8,128)(2,1)}, u32[]{:S(2)}, u32[]{:S(2)}) collective-permute-start(bf16[384,768]{1,0:T(8,128)(2,1)} %get-tuple-element.376), channel_id=1, source_target_pairs={{0,16},{16,0},{1,17},{17,1},{2,18},{18,2},{3,19},{19,3},{4,20},{20... | collective-permute-start | bytes 1769480 | tf_op jit(solution)/shard_map/ppermute | solution.py:496
  193.7 21.7 %collective-permute-start.44 = (bf16[1024,768]{1,0:T(8,128)(2,1)}, bf16[1024,768]{1,0:T(8,128)(2,1)S(1)}, u32[]{:S(2)}, u32[]{:S(2)}) collective-permute-start(bf16[1024,768]{1,0:T(8,128)(2,1)} %get-tuple-element.397), channel_id=1, source_target_pairs={{0,1},{1,0},{2,3},{3,2},{4,5},{5,4},{6,7},{7,6},{8,9},{9,8},{10,11... | collective-permute-start | bytes 4718600 | tf_op jit(solution)/shard_map/ppermute | solution.py:504
  197.3 18.1 %collective-permute-start.42 = (bf16[448,768]{1,0:T(8,128)(2,1)}, bf16[448,768]{1,0:T(8,128)(2,1)S(1)}, u32[]{:S(2)}, u32[]{:S(2)}) collective-permute-start(bf16[448,768]{1,0:T(8,128)(2,1)} %get-tuple-element.395), channel_id=1, source_target_pairs={{0,2},{1,3},{2,0},{3,1},{4,6},{5,7},{6,4},{7,5},{8,10},{9,11},{10,... | collective-permute-start | bytes 2064392 | tf_op jit(solution)/shard_map/ppermute | solution.py:500
  198.2 16.9 %collective-permute-start.43 = (bf16[384,768]{1,0:T(8,128)(2,1)}, bf16[384,768]{1,0:T(8,128)(2,1)S(1)}, u32[]{:S(2)}, u32[]{:S(2)}) collective-permute-start(bf16[384,768]{1,0:T(8,128)(2,1)} %get-tuple-element.396), channel_id=1, source_target_pairs={{0,16},{16,0},{1,17},{17,1},{2,18},{18,2},{3,19},{19,3},{4,20},{20... | collective-permute-start | bytes 1769480 | tf_op jit(solution)/shard_map/ppermute | solution.py:496
  216.9 8.9 %collective-permute-start.47 = (bf16[1024,768]{1,0:T(8,128)(2,1)}, bf16[1024,768]{1,0:T(8,128)(2,1)}, u32[]{:S(2)}, u32[]{:S(2)}) collective-permute-start(bf16[1024,768]{1,0:T(8,128)(2,1)} %get-tuple-element.430), channel_id=1, source_target_pairs={{0,1},{1,0},{2,3},{3,2},{4,5},{5,4},{6,7},{7,6},{8,9},{9,8},{10,11... | collective-permute-start | bytes 4718600 | tf_op jit(solution)/shard_map/ppermute | solution.py:504
  217.0 18.0 %collective-permute-start.45 = (bf16[448,768]{1,0:T(8,128)(2,1)}, bf16[448,768]{1,0:T(8,128)(2,1)}, u32[]{:S(2)}, u32[]{:S(2)}) collective-permute-start(bf16[448,768]{1,0:T(8,128)(2,1)} %fusion.3), channel_id=1, source_target_pairs={{0,16},{16,0},{1,17},{17,1},{2,18},{18,2},{3,19},{19,3},{4,20},{20... | collective-permute-start | bytes 2064392 | tf_op jit(solution)/shard_map/ppermute | solution.py:496
  218.3 16.5 %collective-permute-start.46 = (bf16[384,768]{1,0:T(8,128)(2,1)}, bf16[384,768]{1,0:T(8,128)(2,1)}, u32[]{:S(2)}, u32[]{:S(2)}) collective-permute-start(bf16[384,768]{1,0:T(8,128)(2,1)} %fusion.7), channel_id=1, source_target_pairs={{0,2},{1,3},{2,0},{3,1},{4,6},{5,7},{6,4},{7,5},{8,10},{9,11},{10,... | collective-permute-start | bytes 1769480 | tf_op jit(solution)/shard_map/ppermute | solution.py:500
  219.4 38.2 %collective-permute-start.49 = (bf16[512,768]{1,0:T(8,128)(2,1)}, bf16[512,768]{1,0:T(8,128)(2,1)S(1)}, u32[]{:S(2)}, u32[]{:S(2)}) collective-permute-start(bf16[512,768]{1,0:T(8,128)(2,1)} %add_convert_fusion.2), channel_id=1, source_target_pairs={{0,2},{1,3},{2,0},{3,1},{4,6},{5,7},{6,4},{7,5},{8,10},{9,11},{10,... | collective-permute-start | bytes 2359304 | tf_op jit(solution)/shard_map/ppermute | solution.py:500
  240.3 17.3 %collective-permute-start.48 = (bf16[416,768]{1,0:T(8,128)(2,1)S(1)}, bf16[416,768]{1,0:T(8,128)(2,1)S(1)}, u32[]{:S(2)}, u32[]{:S(2)}) collective-permute-start(bf16[416,768]{1,0:T(8,128)(2,1)S(1)} %get-tuple-element.442), channel_id=1, source_target_pairs={{0,4},{4,0},{8,12},{12,8},{1,5},{5,1},{9,13},{13,9},{2,6},{6,2},{1... | collective-permute-start | bytes 1916936 | tf_op jit(solution)/shard_map/ppermute | solution.py:548
  258.5 15.7 %collective-permute-start.50 = (bf16[1024,768]{1,0:T(8,128)(2,1)}, bf16[1024,768]{1,0:T(8,128)(2,1)}, u32[]{:S(2)}, u32[]{:S(2)}) collective-permute-start(bf16[1024,768]{1,0:T(8,128)(2,1)} %get-tuple-element.461), channel_id=1, source_target_pairs={{0,1},{1,0},{2,3},{3,2},{4,5},{5,4},{6,7},{7,6},{8,9},{9,8},{10,11... | collective-permute-start | bytes 4718600 | tf_op jit(solution)/shard_map/ppermute | solution.py:504
  260.1 20.1 %collective-permute-start.54 = (bf16[512,768]{1,0:T(8,128)(2,1)}, bf16[512,768]{1,0:T(8,128)(2,1)S(1)}, u32[]{:S(2)}, u32[]{:S(2)}) collective-permute-start(bf16[512,768]{1,0:T(8,128)(2,1)} %add_convert_fusion.1), channel_id=1, source_target_pairs={{0,2},{1,3},{2,0},{3,1},{4,6},{5,7},{6,4},{7,5},{8,10},{9,11},{10,... | collective-permute-start | bytes 2359304 | tf_op jit(solution)/shard_map/ppermute | solution.py:500
  264.9 18.2 %collective-permute-start.53 = (bf16[256,768]{1,0:T(8,128)(2,1)}, bf16[256,768]{1,0:T(8,128)(2,1)S(1)}, u32[]{:S(2)}, u32[]{:S(2)}) collective-permute-start(bf16[256,768]{1,0:T(8,128)(2,1)} %add_convert_fusion.11), channel_id=1, source_target_pairs={{0,4},{4,0},{8,12},{12,8},{1,5},{5,1},{9,13},{13,9},{2,6},{6,2},{1... | collective-permute-start | bytes 1179656 | tf_op jit(solution)/shard_map/ppermute | solution.py:548
  265.3 21.3 %collective-permute-start.52 = (bf16[208,768]{1,0:T(8,128)(2,1)}, bf16[208,768]{1,0:T(8,128)(2,1)}, u32[]{:S(2)}, u32[]{:S(2)}) collective-permute-start(bf16[208,768]{1,0:T(8,128)(2,1)} %constant_dynamic-slice_fusion.2), channel_id=1, source_target_pairs={{0,8},{4,12},{8,0},{12,4},{1,9},{5,13},{9,1},{13,5},{2,10},{6,14},... | collective-permute-start | bytes 958472 | tf_op jit(solution)/shard_map/ppermute | solution.py:548
  281.7 16.1 %collective-permute-start.58 = (bf16[256,768]{1,0:T(8,128)(2,1)S(1)}, bf16[256,768]{1,0:T(8,128)(2,1)S(1)}, u32[]{:S(2)}, u32[]{:S(2)}) collective-permute-start(bf16[256,768]{1,0:T(8,128)(2,1)S(1)} %add_convert_fusion.10), channel_id=1, source_target_pairs={{0,4},{4,0},{8,12},{12,8},{1,5},{5,1},{9,13},{13,9},{2,6},{6,2},{1... | collective-permute-start | bytes 1179656 | tf_op jit(solution)/shard_map/ppermute | solution.py:548
  283.2 12.1 %collective-permute-start.51 = (bf16[256,768]{1,0:T(8,128)(2,1)S(1)}, bf16[256,768]{1,0:T(8,128)(2,1)S(1)}, u32[]{:S(2)}, u32[]{:S(2)}) collective-permute-start(bf16[256,768]{1,0:T(8,128)(2,1)S(1)} %get-tuple-element.580), channel_id=1, source_target_pairs={{0,2},{1,3},{2,0},{3,1},{4,6},{5,7},{6,4},{7,5},{8,10},{9,11},{10,... | collective-permute-start | bytes 1179656 | tf_op jit(solution)/shard_map/ppermute | solution.py:500
  285.3 38.2 %collective-permute-start.62 = (bf16[128,768]{1,0:T(8,128)(2,1)S(1)}, bf16[128,768]{1,0:T(8,128)(2,1)S(1)}, u32[]{:S(2)}, u32[]{:S(2)}) collective-permute-start(bf16[128,768]{1,0:T(8,128)(2,1)S(1)} %add_convert_fusion.19), channel_id=1, source_target_pairs={{0,8},{4,12},{8,0},{12,4},{1,9},{5,13},{9,1},{13,5},{2,10},{6,14},... | collective-permute-start | bytes 589832 | tf_op jit(solution)/shard_map/ppermute | solution.py:548
  286.6 15.1 %collective-permute-start.57 = (bf16[832,384]{1,0:T(8,128)(2,1)S(1)}, bf16[832,384]{1,0:T(8,128)(2,1)S(1)}, u32[]{:S(2)}, u32[]{:S(2)}) collective-permute-start(bf16[832,384]{1,0:T(8,128)(2,1)S(1)} %copy-done.58), channel_id=1, source_target_pairs={{0,16},{16,0},{1,17},{17,1},{2,18},{18,2},{3,19},{19,3},{4,20},{20... | collective-permute-start | bytes 1916936 | tf_op jit(solution)/shard_map/ppermute | solution.py:496
  288.1 15.5 %collective-permute-start.56 = (bf16[256,768]{1,0:T(8,128)(2,1)S(1)}, bf16[256,768]{1,0:T(8,128)(2,1)S(1)}, u32[]{:S(2)}, u32[]{:S(2)}) collective-permute-start(bf16[256,768]{1,0:T(8,128)(2,1)S(1)} %get-tuple-element.579), channel_id=1, source_target_pairs={{0,2},{1,3},{2,0},{3,1},{4,6},{5,7},{6,4},{7,5},{8,10},{9,11},{10,... | collective-permute-start | bytes 1179656 | tf_op jit(solution)/shard_map/ppermute | solution.py:500
  295.2 28.3 %collective-permute-start.61 = (bf16[208,768]{1,0:T(8,128)(2,1)S(1)}, bf16[208,768]{1,0:T(8,128)(2,1)S(1)}, u32[]{:S(2)}, u32[]{:S(2)}) collective-permute-start(bf16[208,768]{1,0:T(8,128)(2,1)S(1)} %add_convert_fusion.13), channel_id=1, source_target_pairs={{0,8},{4,12},{8,0},{12,4},{1,9},{5,13},{9,1},{13,5},{2,10},{6,14},... | collective-permute-start | bytes 958472 | tf_op jit(solution)/shard_map/ppermute | solution.py:548
  297.8 24.5 %collective-permute-start.55 = (bf16[256,768]{1,0:T(8,128)(2,1)S(1)}, bf16[256,768]{1,0:T(8,128)(2,1)S(1)}, u32[]{:S(2)}, u32[]{:S(2)}) collective-permute-start(bf16[256,768]{1,0:T(8,128)(2,1)S(1)} %add_convert_fusion.9), channel_id=1, source_target_pairs={{0,4},{4,0},{8,12},{12,8},{1,5},{5,1},{9,13},{13,9},{2,6},{6,2},{1... | collective-permute-start | bytes 1179656 | tf_op jit(solution)/shard_map/ppermute | solution.py:548
  301.7 24.7 %collective-permute-start.63 = (bf16[128,768]{1,0:T(8,128)(2,1)S(1)}, bf16[128,768]{1,0:T(8,128)(2,1)S(1)}, u32[]{:S(2)}, u32[]{:S(2)}) collective-permute-start(bf16[128,768]{1,0:T(8,128)(2,1)S(1)} %add_convert_fusion.18), channel_id=1, source_target_pairs={{0,8},{4,12},{8,0},{12,4},{1,9},{5,13},{9,1},{13,5},{2,10},{6,14},... | collective-permute-start | bytes 589832 | tf_op jit(solution)/shard_map/ppermute | solution.py:548
  303.6 22.7 %collective-permute-start.60 = (bf16[416,384]{1,0:T(8,128)(2,1)S(1)}, bf16[416,384]{1,0:T(8,128)(2,1)S(1)}, u32[]{:S(2)}, u32[]{:S(2)}) collective-permute-start(bf16[416,384]{1,0:T(8,128)(2,1)S(1)} %constant_dynamic-slice_fusion.1), channel_id=1, source_target_pairs={{0,4},{4,0},{8,12},{12,8},{1,5},{5,1},{9,13},{13,9},{2,6},{6,2},{1... | collective-permute-start | bytes 958472 | tf_op jit(solution)/shard_map/ppermute | solution.py:548
  323.4 13.1 %collective-permute-start.59 = (bf16[128,768]{1,0:T(8,128)(2,1)S(1)}, bf16[128,768]{1,0:T(8,128)(2,1)S(1)}, u32[]{:S(2)}, u32[]{:S(2)}) collective-permute-start(bf16[128,768]{1,0:T(8,128)(2,1)S(1)} %add_convert_fusion.17), channel_id=1, source_target_pairs={{0,8},{4,12},{8,0},{12,4},{1,9},{5,13},{9,1},{13,5},{2,10},{6,14},... | collective-permute-start | bytes 589832 | tf_op jit(solution)/shard_map/ppermute | solution.py:548
  327.6 10.7 %collective-permute-start.66 = (bf16[2,128,768]{2,1,0:T(8,128)(2,1)S(1)}, bf16[2,128,768]{2,1,0:T(8,128)(2,1)S(1)}, u32[]{:S(2)}, u32[]{:S(2)}) collective-permute-start(bf16[2,128,768]{2,1,0:T(8,128)(2,1)S(1)} %bitcast.202), channel_id=1, source_target_pairs={{0,2},{1,3},{2,0},{3,1},{4,6},{5,7},{6,4},{7,5},{8,10},{9,11},{10,... | collective-permute-start | bytes 1179656 | tf_op jit(solution)/shard_map/ppermute | solution.py:500
  328.6 9.6 %collective-permute-start.65 = (bf16[208,384]{1,0:T(8,128)(2,1)S(1)}, bf16[208,384]{1,0:T(8,128)(2,1)S(1)}, u32[]{:S(2)}, u32[]{:S(2)}) collective-permute-start(bf16[208,384]{1,0:T(8,128)(2,1)S(1)} %constant_dynamic-slice_fusion), channel_id=1, source_target_pairs={{0,8},{4,12},{8,0},{12,4},{1,9},{5,13},{9,1},{13,5},{2,10},{6,14},... | collective-permute-start | bytes 479240 | tf_op jit(solution)/shard_map/ppermute | solution.py:548
  338.4 7.3 %collective-permute-start.64 = (bf16[1,128,768]{2,1,0:T(8,128)(2,1)S(1)}, bf16[1,128,768]{2,1,0:T(8,128)(2,1)S(1)}, u32[]{:S(2)}, u32[]{:S(2)}) collective-permute-start(bf16[1,128,768]{2,1,0:T(8,128)(2,1)S(1)} %bitcast.216), channel_id=1, source_target_pairs={{0,2},{1,3},{2,0},{3,1},{4,6},{5,7},{6,4},{7,5},{8,10},{9,11},{10,... | collective-permute-start | bytes 589832 | tf_op jit(solution)/shard_map/ppermute | solution.py:500
  345.8 20.2 %collective-permute-start.72 = (bf16[416,768]{1,0:T(8,128)(2,1)S(1)}, bf16[416,768]{1,0:T(8,128)(2,1)S(1)}, u32[]{:S(2)}, u32[]{:S(2)}) collective-permute-start(bf16[416,768]{1,0:T(8,128)(2,1)S(1)} %pad_maximum_fusion.12), channel_id=1, source_target_pairs={{0,4},{4,0},{8,12},{12,8},{1,5},{5,1},{9,13},{13,9},{2,6},{6,2},{1... | collective-permute-start | bytes 1916936 | tf_op jit(solution)/shard_map/ppermute | solution.py:548
  345.9 20.1 %collective-permute-start.71 = (bf16[3,128,768]{2,1,0:T(8,128)(2,1)S(1)}, bf16[3,128,768]{2,1,0:T(8,128)(2,1)S(1)}, u32[]{:S(2)}, u32[]{:S(2)}) collective-permute-start(bf16[3,128,768]{2,1,0:T(8,128)(2,1)S(1)} %bitcast.212), channel_id=1, source_target_pairs={{0,2},{1,3},{2,0},{3,1},{4,6},{5,7},{6,4},{7,5},{8,10},{9,11},{10,... | collective-permute-start | bytes 1769480 | tf_op jit(solution)/shard_map/ppermute | solution.py:500
  346.9 16.9 %collective-permute-start.68 = (bf16[208,384]{1,0:T(8,128)(2,1)S(1)}, bf16[208,384]{1,0:T(8,128)(2,1)S(1)}, u32[]{:S(2)}, u32[]{:S(2)}) collective-permute-start(bf16[208,384]{1,0:T(8,128)(2,1)S(1)} %add_convert_fusion.23), channel_id=1, source_target_pairs={{0,8},{4,12},{8,0},{12,4},{1,9},{5,13},{9,1},{13,5},{2,10},{6,14},... | collective-permute-start | bytes 479240 | tf_op jit(solution)/shard_map/ppermute | solution.py:548
  367.5 9.9 %collective-permute-start.70 = (bf16[416,384]{1,0:T(8,128)(2,1)S(1)}, bf16[416,384]{1,0:T(8,128)(2,1)S(1)}, u32[]{:S(2)}, u32[]{:S(2)}) collective-permute-start(bf16[416,384]{1,0:T(8,128)(2,1)S(1)} %pad_maximum_fusion.21), channel_id=1, source_target_pairs={{0,4},{4,0},{8,12},{12,8},{1,5},{5,1},{9,13},{13,9},{2,6},{6,2},{1... | collective-permute-start | bytes 958472 | tf_op jit(solution)/shard_map/ppermute | solution.py:548
  (83 other events, 660.6 us)

commit v4 on v3

--- a/solution.py
+++ b/solution.py
@@ -814,12 +814,11 @@
     attn = low_sum(attn[0], attn_got)
     attn_got = along(attn, masks[1])
     early = whole(early.reshape(early_x.shape), early_x)
-    last_x, early, attn = stage(last_x, early, attn)
-    last = whole(last.reshape(last_x.shape), last_x)
-    attn_got, last = stage(attn_got, last)
+    last_x, attn_got, early, result_x = stage(last_x, attn_got, early, result_x)
     attn = join(attn, attn_got, masks[1])
     attn_got = along(attn, masks[0])
-    result_x, feed_got, attn = stage(result_x, feed_got, attn)
+    last = whole(last.reshape(last_x.shape), last_x)
+    feed_got, last = stage(feed_got, last)
     feed = join(feed, feed_got, masks[0])
     outputs = whole(result.reshape(result_x.shape), result_x)
     attn_got, outputs, last, feed = stage(attn_got, outputs, last, feed)

time: 389 us -> 379 us (0.974)
  waiting for transfers between devices: 97.1 us -> 90.1 us
  other arithmetic: 51.4 us -> 45.2 us
    ppermute x20, waiting for transfers between devices: 68 us -> 50.3 us  [along(): lax.ppermute(value, 'context', [(i, i ^ mask) for i in range(contexts)])]
    ppermute x21, waiting for transfers between devices: 22.2 us -> 34 us  [across(): return lax.ppermute(value, 'tensor', [(i, i ^ 2) for i in range(4)])]
    unnamed x157 -> x149, local copies, waits for them, and re-layouts: 10 us -> 10.2 us
  transfers between devices with their start and end apart: 74 -> 74, of which waited for: 28 -> 24; matrix products, arithmetic and copies ran while one was open for 14% -> 13% of each run, Pallas kernels for 31% -> 32%
where the time goes in v4:
time: 379 us; the launch traced here: 375 us
  Pallas kernels  141 us (37%)
  waiting for transfers between devices  90.1 us (24%)
  starting transfers between devices  74.6 us (20%)
  other arithmetic  45.2 us (12%)
  local copies, waits for them, and re-layouts  21.9 us (6%)
    ppermute x20, waiting for transfers between devices, along(): lax.ppermute(value, 'context', [(i, i ^ mask) for i in range(contexts)])  50.3 us
    pallas_call x3, Pallas kernels, attention_backward(): pl.pallas_call(functools.partial(backward_body, heads, nears, index), out...  45.8 us
    pallas_call x3, Pallas kernels, attention_forward(): pl.pallas_call(functools.partial(forward_body, heads, index), out_shape=(...  41.5 us
    ppermute x21, waiting for transfers between devices, across(): return lax.ppermute(value, 'tensor', [(i, i ^ 2) for i in range(4)])  34 us
    ppermute x20, starting transfers between devices, along(): lax.ppermute(value, 'context', [(i, i ^ mask) for i in range(contexts)])  33.9 us
    convert_element_type x26, other arithmetic, low_sum(): return added(*values).astype(BF16)  28.2 us
    ppermute x21, starting transfers between devices, across(): return lax.ppermute(value, 'tensor', [(i, i ^ 2) for i in range(4)])  23.5 us
    pallas_call x1, Pallas kernels, feed_forward(): pl.pallas_call(functools.partial(feed_body, blocks, pieces, seqs), out_sh...  21.2 us
  transfers between devices with their start and end apart: 74, of which 24 were waited for; matrix products, arithmetic and copies ran while one was open for 13% of the time, Pallas kernels for 32%

profile of v4, /device:TPU:0, one launch (start us, length us, event | category | flops | bytes accessed | tf_op | source)
XLA Modules:
  0.0 375.2 jit_solution(13830067303041026422)
XLA Ops:
  0.7 1.8 fusion.20
  2.6 4.1 %collective-permute-start = (bf16[128,768]{1,0:T(8,128)(2,1)S(1)}, bf16[128,768]{1,0:T(8,128)(2,1)S(1)}, u32[]{:S(2)}, u32[]{:S(2)}) collective-permute-start(bf16[128,768]{1,0:T(8,128)(2,1)S(1)} %dynamic-slice_bitcast_fusion.2.refs_16_), channel_id=1, source_target_pairs={{0,8},{4,12},{8,0},{12,4},{1,9},{5,13},{9,1},{13,5},{2,10},{6,14},... | collective-permute-start | bytes 589832 | tf_op jit(solution)/shard_map/ppermute | solution.py:548
  10.7 2.0 pad_maximum_fusion.13.refs_0_
  12.7 3.1 collective-permute-done
  15.8 1.5 collective-permute-start.2
  17.3 1.5 collective-permute-start.1
  19.6 3.4 collective-permute-start.4
  23.0 8.8 %collective-permute-done.4 = bf16[128,768]{1,0:T(8,128)(2,1)S(1)} collective-permute-done((bf16[128,768]{1,0:T(8,128)(2,1)S(1)}, bf16[128,768]{1,0:T(8,128)(2,1)S(1)}, u32[]{:S(2)}, u32[]{:S(2)}) %collective-permute-start.4) | collective-permute-done | bytes 196640 | tf_op jit(solution)/shard_map/ppermute | solution.py:548
  35.4 3.2 collective-permute-start.7
  38.6 2.0 collective-permute-start.8
  42.9 6.9 %collective-permute-done.8 = bf16[128,768]{1,0:T(8,128)(2,1)S(1)} collective-permute-done((bf16[128,768]{1,0:T(8,128)(2,1)}, bf16[128,768]{1,0:T(8,128)(2,1)S(1)}, u32[]{:S(2)}, u32[]{:S(2)}) %collective-permute-start.8) | collective-permute-done | bytes 196640 | tf_op jit(solution)/shard_map/ppermute | solution.py:548
  52.7 1.6 collective-permute-start.12
  54.3 1.5 collective-permute-start.11
  57.3 1.9 collective-permute-start.13
  59.9 13.9 %attention_forward.3 = (bf16[512,192]{1,0:T(8,128)(2,1)}, bf16[2048,192]{1,0:T(8,128)(2,1)}, bf16[2048,192]{1,0:T(8,128)(2,1)}, bf16[512,192]{1,0:T(8,128)(2,1)}...) custom-call(s32[4]{0:T(128)} %pad_add_fusion.places, bf16[3,512,768]{2,1,0:T(8,128)(2,1)} %refs_0_.5, ...), custom_call_target="tpu_custom_call" | custom-call | flops 4429185024 | bytes 5505024 | tf_op jit(solution)/shard_map/attention_forward/pallas_call | solution.py:189
  75.6 1.6 collective-permute-start.19
  77.2 1.6 collective-permute-start.18
  79.6 1.6 collective-permute-start.16
  81.2 13.7 %attention_forward.4 = (bf16[512,192]{1,0:T(8,128)(2,1)}, bf16[2048,192]{1,0:T(8,128)(2,1)}, bf16[2048,192]{1,0:T(8,128)(2,1)}, bf16[512,192]{1,0:T(8,128)(2,1)}...) custom-call(s32[4]{0:T(128)} %pad_add_fusion.places, bf16[3,512,768]{2,1,0:T(8,128)(2,1)} %refs_0_.5, ...), custom_call_target="tpu_custom_call" | custom-call | flops 4429185024 | bytes 5505024 | tf_op jit(solution)/shard_map/attention_forward/pallas_call | solution.py:189
  95.0 2.3 collective-permute-done.16
  97.9 1.6 collective-permute-start.22
  99.6 1.6 collective-permute-start.21
  102.5 13.9 %attention_forward.5 = (bf16[512,192]{1,0:T(8,128)(2,1)}, bf16[2048,192]{1,0:T(8,128)(2,1)}, bf16[2048,192]{1,0:T(8,128)(2,1)}, bf16[512,192]{1,0:T(8,128)(2,1)}...) custom-call(s32[4]{0:T(128)} %pad_add_fusion.places, bf16[3,512,768]{2,1,0:T(8,128)(2,1)} %refs_0_.5, ...), custom_call_target="tpu_custom_call" | custom-call | flops 4429185024 | bytes 5505024 | tf_op jit(solution)/shard_map/attention_forward/pallas_call | solution.py:189
  118.6 1.9 collective-permute-done.32.refs_24_
  124.4 4.9 %collective-permute-done.33.refs_27_ = bf16[128,768]{1,0:T(8,128)(2,1)S(1)} collective-permute-done((bf16[128,768]{1,0:T(8,128)(2,1)S(1)}, bf16[128,768]{1,0:T(8,128)(2,1)S(1)}, u32[]{:S(2)}, u32[]{:S(2)}) %collective-permute-start.33) | collective-permute-done | bytes 196640 | tf_op jit(solution)/shard_map/ppermute | solution.py:500
  131.3 21.2 %feed_forward.1 = (bf16[384,768]{1,0:T(8,128)(2,1)}, bf16[128,768]{1,0:T(8,128)(2,1)}, bf16[256,768]{1,0:T(8,128)(2,1)}, f32[384,768]{1,0:T(8,128)}, bf16[4,384,...) custom-call(s32[5]{0:T(128)} %concatenate.73.order.refs_8_, ...), custom_call_target="tpu_custom_call" | custom-call | flops 7247757312 | bytes 14155776 | tf_op jit(solution)/shard_map/feed_forward/pallas_call | solution.py:411
  153.5 7.1 %feed_gradients.2 = (bf16[2,2,448,768]{3,2,1,0:T(8,128)(2,1)}, bf16[2,2,384,768]{3,2,1,0:T(8,128)(2,1)}) custom-call(s32[5]{0:T(128)} %concatenate.73.order.refs_8_, bf16[4,384,768]{2,1,0:T(8,128)(2,1)} %get-tuple-element.351.act, bf16[4,384,768]{2,1,0:T(8,128)(2,1)} %get-tuple-element.363.d_inner, bf16[384,768]{1,0:T(8,128)(2,1)} %get-tuple-element.353.d_ffn, ...), custom_call_target="tpu_custom_call" | custom-call | flops 1811939328 | bytes 4718592 | tf_op jit(solution)/shard_map/feed_gradients/pallas_call | solution.py:474
  162.5 7.5 %feed_gradients.3 = (bf16[2,2,448,768]{3,2,1,0:T(8,128)(2,1)}, bf16[2,2,384,768]{3,2,1,0:T(8,128)(2,1)}) custom-call(s32[5]{0:T(128)} %concatenate.73.order.refs_8_, bf16[4,384,768]{2,1,0:T(8,128)(2,1)} %get-tuple-element.351.act, bf16[4,384,768]{2,1,0:T(8,128)(2,1)} %get-tuple-element.363.d_inner, bf16[384,768]{1,0:T(8,128)(2,1)} %get-tuple-element.353.d_ffn, ...), custom_call_target="tpu_custom_call" | custom-call | flops 1811939328 | bytes 4718592 | tf_op jit(solution)/shard_map/feed_gradients/pallas_call | solution.py:474
  170.7 3.0 fusion.13
  176.7 1.5 collective-permute-start.40
  178.2 15.0 %attention_backward.3 = (bf16[512,192]{1,0:T(8,128)(2,1)}, bf16[2048,192]{1,0:T(8,128)(2,1)}, bf16[2048,192]{1,0:T(8,128)(2,1)}, bf16[1024,768]{1,0:T(8,128)(2,1...) custom-call(s32[4]{0:T(128)} %pad_add_fusion.places, ...), custom_call_target="tpu_custom_call" | custom-call | flops 9261023232 | bytes 7077888 | tf_op jit(solution)/shard_map/attention_backward/pallas_call | solution.py:220
  193.6 2.5 fusion.7
  198.1 1.5 collective-permute-start.43
  199.6 15.5 %attention_backward.4 = (bf16[512,192]{1,0:T(8,128)(2,1)}, bf16[2048,192]{1,0:T(8,128)(2,1)}, bf16[2048,192]{1,0:T(8,128)(2,1)}, bf16[1024,768]{1,0:T(8,128)(2,1...) custom-call(s32[4]{0:T(128)} %pad_add_fusion.places, ...), custom_call_target="tpu_custom_call" | custom-call | flops 9261023232 | bytes 7077888 | tf_op jit(solution)/shard_map/attention_backward/pallas_call | solution.py:220
  220.1 5.4 %attention_gradients.3.refs_7_ = f32[3,192,768]{2,1,0:T(8,128)} custom-call(bf16[3,512,768]{2,1,0:T(8,128)(2,1)} %refs_0_.5, bf16[384,768]{1,0:T(8,128)(2,1)} %constant_dynamic-update-slice_fusion.1.near.refs_1_, bf16[384,768]{1,0:T(8,128)(2,1)} %copy-done.3, bf16[768,768]{1,0:T(8,128)(2,1)} %collective-permute-done.9.sib.refs_3_, ...), custom_call_target="tpu_custom_call" | custom-call | flops 1207959552 | bytes 4718592 | tf_op jit(solution)/shard_map/attention_gradients/pallas_call | solution.py:299
  225.6 2.3 add_convert_fusion.1
  227.8 6.1 %attention_gradients.4.refs_7_ = f32[3,192,768]{2,1,0:T(8,128)} custom-call(bf16[3,512,768]{2,1,0:T(8,128)(2,1)} %refs_0_.5, bf16[384,768]{1,0:T(8,128)(2,1)} %copy-done.22, bf16[384,768]{1,0:T(8,128)(2,1)} %copy-done.8, bf16[768,768]{1,0:T(8,128)(2,1)} %copy-done.21, bf16[512,192]{1,0:T(8,128)(2,1)} %get-tuple-element.432.refs_4_, ...), custom_call_target="tpu_custom_call" | custom-call | flops 1207959552 | bytes 4718592 | tf_op jit(solution)/shard_map/attention_gradients/pallas_call | solution.py:299
  234.9 1.8 fusion.6
  236.7 1.8 fusion.2
  238.4 1.8 fusion.10
  240.2 1.9 collective-permute-start.48
  242.1 15.4 %attention_backward.5 = (bf16[512,192]{1,0:T(8,128)(2,1)}, bf16[2048,192]{1,0:T(8,128)(2,1)}, bf16[2048,192]{1,0:T(8,128)(2,1)}, bf16[1024,768]{1,0:T(8,128)(2,1...) custom-call(s32[4]{0:T(128)} %pad_add_fusion.places, ...), custom_call_target="tpu_custom_call" | custom-call | flops 9261023232 | bytes 7077888 | tf_op jit(solution)/shard_map/attention_backward/pallas_call | solution.py:220
  262.8 2.0 add_convert_fusion.11
  265.2 2.3 collective-permute-start.55
  267.6 6.5 %attention_gradients.5 = (bf16[832,384]{1,0:T(8,128)(2,1)}, bf16[832,384]{1,0:T(8,128)(2,1)}) custom-call(bf16[3,512,768]{2,1,0:T(8,128)(2,1)} %refs_0_.5, bf16[384,768]{1,0:T(8,128)(2,1)} %copy-done.23, bf16[384,768]{1,0:T(8,128)(2,1)} %copy-done.7, bf16[768,768]{1,0:T(8,128)(2,1)} %copy-done.20, bf16[512,192]{1,0:T(8,128)(2,1)} %get-tuple-element.462.refs_4_, ...), custom_call_target="tpu_custom_call" | custom-call | flops 1207959552 | bytes 4718592 | tf_op jit(solution)/shard_map/attention_gradients/pallas_call | solution.py:299
  274.3 5.7 %collective-permute-done.52 = bf16[512,768]{1,0:T(8,128)(2,1)S(1)} collective-permute-done((bf16[512,768]{1,0:T(8,128)(2,1)}, bf16[512,768]{1,0:T(8,128)(2,1)S(1)}, u32[]{:S(2)}, u32[]{:S(2)}) %collective-permute-start.52) | collective-permute-done | bytes 786464 | tf_op jit(solution)/shard_map/ppermute | solution.py:500
  280.0 1.4 add_convert_fusion.10
  286.5 1.5 collective-permute-start.51
  289.9 5.3 %collective-permute-done.54 = bf16[256,768]{1,0:T(8,128)(2,1)S(1)} collective-permute-done((bf16[256,768]{1,0:T(8,128)(2,1)S(1)}, bf16[256,768]{1,0:T(8,128)(2,1)S(1)}, u32[]{:S(2)}, u32[]{:S(2)}) %collective-permute-start.54) | collective-permute-done | bytes 393248 | tf_op jit(solution)/shard_map/ppermute | solution.py:500
  296.6 1.5 collective-permute-start.60
  299.2 2.5 collective-permute-done.51
  301.6 1.7 collective-permute-start.63
  304.1 14.5 %collective-permute-done.60 = bf16[256,768]{1,0:T(8,128)(2,1)S(1)} collective-permute-done((bf16[256,768]{1,0:T(8,128)(2,1)S(1)}, bf16[256,768]{1,0:T(8,128)(2,1)S(1)}, u32[]{:S(2)}, u32[]{:S(2)}) %collective-permute-start.60) | collective-permute-done | bytes 393248 | tf_op jit(solution)/shard_map/ppermute | solution.py:548
  318.7 3.0 collective-permute-start.65
  321.9 1.4 add_convert_fusion.16
  323.3 4.3 %collective-permute-done.57 = bf16[416,384]{1,0:T(8,128)(2,1)S(1)} collective-permute-done((bf16[416,384]{1,0:T(8,128)(2,1)S(1)}, bf16[416,384]{1,0:T(8,128)(2,1)S(1)}, u32[]{:S(2)}, u32[]{:S(2)}) %collective-permute-start.57) | collective-permute-done | bytes 319520 | tf_op jit(solution)/shard_map/ppermute | solution.py:548
  331.1 5.8 %collective-permute-done.62 = bf16[208,384]{1,0:T(8,128)(2,1)S(1)} collective-permute-done((bf16[208,384]{1,0:T(8,128)(2,1)S(1)}, bf16[208,384]{1,0:T(8,128)(2,1)S(1)}, u32[]{:S(2)}, u32[]{:S(2)}) %collective-permute-start.62) | collective-permute-done | bytes 159776 | tf_op jit(solution)/shard_map/ppermute | solution.py:548
  339.3 2.4 collective-permute-start.67
  343.3 13.8 %collective-permute-done.66 = bf16[1,128,768]{2,1,0:T(8,128)(2,1)S(1)} collective-permute-done((bf16[1,128,768]{2,1,0:T(8,128)(2,1)S(1)}, bf16[1,128,768]{2,1,0:T(8,128)(2,1)S(1)}, u32[]{:S(2)}, u32[]{:S(2)}) %collective-permute-start.66) | collective-permute-done | bytes 196640 | tf_op jit(solution)/shard_map/ppermute | solution.py:500
  358.0 1.7 collective-permute-start.70
  361.6 1.6 copy.36
  363.2 4.3 %collective-permute-done.70 = bf16[416,384]{1,0:T(8,128)(2,1)S(1)} collective-permute-done((bf16[416,384]{1,0:T(8,128)(2,1)S(1)}, bf16[416,384]{1,0:T(8,128)(2,1)S(1)}, u32[]{:S(2)}, u32[]{:S(2)}) %collective-permute-start.70) | collective-permute-done | bytes 319520 | tf_op jit(solution)/shard_map/ppermute | solution.py:548
  372.0 1.4 copy.37
  373.4 1.6 pad_maximum_fusion.1
  (338 shorter events, 73.9 us)
Async XLA Ops:
  2.6 13.2 %collective-permute-start = (bf16[128,768]{1,0:T(8,128)(2,1)S(1)}, bf16[128,768]{1,0:T(8,128)(2,1)S(1)}, u32[]{:S(2)}, u32[]{:S(2)}) collective-permute-start(bf16[128,768]{1,0:T(8,128)(2,1)S(1)} %dynamic-slice_bitcast_fusion.2.refs_16_), channel_id=1, source_target_pairs={{0,8},{4,12},{8,0},{12,4},{1,9},{5,13},{9,1},{13,5},{2,10},{6,14},... | collective-permute-start | bytes 589832 | tf_op jit(solution)/shard_map/ppermute | solution.py:548
  15.8 16.8 %collective-permute-start.2 = (bf16[400,768]{1,0:T(8,128)(2,1)}, bf16[400,768]{1,0:T(8,128)(2,1)}, u32[]{:S(2)}, u32[]{:S(2)}) collective-permute-start(bf16[400,768]{1,0:T(8,128)(2,1)} %pad_maximum_fusion.13.refs_0_), channel_id=1, source_target_pairs={{0,2},{1,3},{2,0},{3,1},{4,6},{5,7},{6,4},{7,5},{8,10},{9,11},{10,... | collective-permute-start | bytes 1843208 | tf_op jit(solution)/shard_map/ppermute | solution.py:500
  17.3 15.3 %collective-permute-start.1 = (bf16[4,192,384]{2,1,0:T(8,128)(2,1)S(1)}, bf16[4,192,384]{2,1,0:T(8,128)(2,1)S(1)}, u32[]{:S(2)}, u32[]{:S(2)}) collective-permute-start(bf16[4,192,384]{2,1,0:T(8,128)(2,1)S(1)} %pad_maximum_fusion.14), channel_id=1, source_target_pairs={{0,16},{16,0},{1,17},{17,1},{2,18},{18,2},{3,19},{19,3},{4,20},{20... | collective-permute-start | bytes 1769480 | tf_op jit(solution)/shard_map/ppermute | solution.py:496
  18.9 13.7 %collective-permute-start.3 = (bf16[256,768]{1,0:T(8,128)(2,1)S(1)}, bf16[256,768]{1,0:T(8,128)(2,1)S(1)}, u32[]{:S(2)}, u32[]{:S(2)}) collective-permute-start(bf16[256,768]{1,0:T(8,128)(2,1)S(1)} %pad_maximum_fusion.15), channel_id=1, source_target_pairs={{0,4},{4,0},{8,12},{12,8},{1,5},{5,1},{9,13},{13,9},{2,6},{6,2},{1... | collective-permute-start | bytes 1179656 | tf_op jit(solution)/shard_map/ppermute | solution.py:548
  19.6 12.2 %collective-permute-start.4 = (bf16[128,768]{1,0:T(8,128)(2,1)S(1)}, bf16[128,768]{1,0:T(8,128)(2,1)S(1)}, u32[]{:S(2)}, u32[]{:S(2)}) collective-permute-start(bf16[128,768]{1,0:T(8,128)(2,1)S(1)} %get-tuple-element.283.refs_17_), channel_id=1, source_target_pairs={{0,8},{4,12},{8,0},{12,4},{1,9},{5,13},{9,1},{13,5},{2,10},{6,14},... | collective-permute-start | bytes 589832 | tf_op jit(solution)/shard_map/ppermute | solution.py:548
  33.3 17.1 %collective-permute-start.5 = (bf16[400,768]{1,0:T(8,128)(2,1)}, bf16[400,768]{1,0:T(8,128)(2,1)}, u32[]{:S(2)}, u32[]{:S(2)}) collective-permute-start(bf16[400,768]{1,0:T(8,128)(2,1)} %pad_maximum_fusion.13.refs_0_), channel_id=1, source_target_pairs={{0,16},{16,0},{1,17},{17,1},{2,18},{18,2},{3,19},{19,3},{4,20},{20... | collective-permute-start | bytes 1843208 | tf_op jit(solution)/shard_map/ppermute | solution.py:496
  34.6 15.8 %collective-permute-start.6 = (bf16[384,768]{1,0:T(8,128)(2,1)}, bf16[384,768]{1,0:T(8,128)(2,1)S(1)}, u32[]{:S(2)}, u32[]{:S(2)}) collective-permute-start(bf16[384,768]{1,0:T(8,128)(2,1)} %constant_dynamic-update-slice_fusion.1.near.refs_1_), channel_id=1, source_target_pairs={{0,2},{1,3},{2,0},{3,1},{4,6},{5,7},{6,4},{7,5},{8,10},{9,11},{10,... | collective-permute-start | bytes 1769480 | tf_op jit(solution)/shard_map/ppermute | solution.py:500
  35.4 15.0 %collective-permute-start.7 = (bf16[256,768]{1,0:T(8,128)(2,1)S(1)}, bf16[256,768]{1,0:T(8,128)(2,1)S(1)}, u32[]{:S(2)}, u32[]{:S(2)}) collective-permute-start(bf16[256,768]{1,0:T(8,128)(2,1)S(1)} %pad_maximum_fusion.16), channel_id=1, source_target_pairs={{0,4},{4,0},{8,12},{12,8},{1,5},{5,1},{9,13},{13,9},{2,6},{6,2},{1... | collective-permute-start | bytes 1179656 | tf_op jit(solution)/shard_map/ppermute | solution.py:548
  38.6 11.1 %collective-permute-start.8 = (bf16[128,768]{1,0:T(8,128)(2,1)}, bf16[128,768]{1,0:T(8,128)(2,1)S(1)}, u32[]{:S(2)}, u32[]{:S(2)}) collective-permute-start(bf16[128,768]{1,0:T(8,128)(2,1)} %get-tuple-element.294.refs_18_), channel_id=1, source_target_pairs={{0,8},{4,12},{8,0},{12,4},{1,9},{5,13},{9,1},{13,5},{2,10},{6,14},... | collective-permute-start | bytes 589832 | tf_op jit(solution)/shard_map/ppermute | solution.py:548
  51.6 7.6 %collective-permute-start.9 = (bf16[768,768]{1,0:T(8,128)(2,1)}, bf16[768,768]{1,0:T(8,128)(2,1)}, u32[]{:S(2)}, u32[]{:S(2)}) collective-permute-start(bf16[768,768]{1,0:T(8,128)(2,1)} %pad_maximum_fusion.5), channel_id=1, source_target_pairs={{0,1},{1,0},{2,3},{3,2},{4,5},{5,4},{6,7},{7,6},{8,9},{9,8},{10,11... | collective-permute-start | bytes 3538952 | tf_op jit(solution)/shard_map/ppermute | solution.py:504
  52.7 21.2 %collective-permute-start.12 = (bf16[384,768]{1,0:T(8,128)(2,1)S(1)}, bf16[384,768]{1,0:T(8,128)(2,1)S(1)}, u32[]{:S(2)}, u32[]{:S(2)}) collective-permute-start(bf16[384,768]{1,0:T(8,128)(2,1)S(1)} %constant_dynamic-update-slice_fusion.3.near.refs_1_), channel_id=1, source_target_pairs={{0,2},{1,3},{2,0},{3,1},{4,6},{5,7},{6,4},{7,5},{8,10},{9,11},{10,... | collective-permute-start | bytes 1769480 | tf_op jit(solution)/shard_map/ppermute | solution.py:500
  54.3 19.6 %collective-permute-start.11 = (bf16[384,768]{1,0:T(8,128)(2,1)S(1)}, bf16[384,768]{1,0:T(8,128)(2,1)S(1)}, u32[]{:S(2)}, u32[]{:S(2)}) collective-permute-start(bf16[384,768]{1,0:T(8,128)(2,1)S(1)} %bitcast.207), channel_id=1, source_target_pairs={{0,16},{16,0},{1,17},{17,1},{2,18},{18,2},{3,19},{19,3},{4,20},{20... | collective-permute-start | bytes 1769480 | tf_op jit(solution)/shard_map/ppermute | solution.py:496
  57.3 16.5 %collective-permute-start.13 = (bf16[256,768]{1,0:T(8,128)(2,1)S(1)}, bf16[256,768]{1,0:T(8,128)(2,1)S(1)}, u32[]{:S(2)}, u32[]{:S(2)}) collective-permute-start(bf16[256,768]{1,0:T(8,128)(2,1)S(1)} %pad_maximum_fusion.17), channel_id=1, source_target_pairs={{0,4},{4,0},{8,12},{12,8},{1,5},{5,1},{9,13},{13,9},{2,6},{6,2},{1... | collective-permute-start | bytes 1179656 | tf_op jit(solution)/shard_map/ppermute | solution.py:548
  59.2 15.6 %collective-permute-start.10 = (bf16[192,768]{1,0:T(8,128)(2,1)S(1)}, bf16[192,768]{1,0:T(8,128)(2,1)S(1)}, u32[]{:S(2)}, u32[]{:S(2)}) collective-permute-start(bf16[192,768]{1,0:T(8,128)(2,1)S(1)} %slice.331), channel_id=1, source_target_pairs={{0,2},{1,3},{2,0},{3,1},{4,6},{5,7},{6,4},{7,5},{8,10},{9,11},{10,... | collective-permute-start | bytes 884744 | tf_op jit(solution)/shard_map/ppermute | solution.py:500
  75.6 19.4 %collective-permute-start.19 = (bf16[384,768]{1,0:T(8,128)(2,1)S(1)}, bf16[384,768]{1,0:T(8,128)(2,1)S(1)}, u32[]{:S(2)}, u32[]{:S(2)}) collective-permute-start(bf16[384,768]{1,0:T(8,128)(2,1)S(1)} %constant_dynamic-update-slice_fusion.5.near.refs_1_), channel_id=1, source_target_pairs={{0,2},{1,3},{2,0},{3,1},{4,6},{5,7},{6,4},{7,5},{8,10},{9,11},{10,... | collective-permute-start | bytes 1769480 | tf_op jit(solution)/shard_map/ppermute | solution.py:500
  77.1 17.8 %collective-permute-start.17 = (bf16[400,768]{1,0:T(8,128)(2,1)}, bf16[400,768]{1,0:T(8,128)(2,1)S(1)}, u32[]{:S(2)}, u32[]{:S(2)}) collective-permute-start(bf16[400,768]{1,0:T(8,128)(2,1)} %pad_maximum_fusion.13.refs_0_), channel_id=1, source_target_pairs={{0,1},{1,0},{2,3},{3,2},{4,5},{5,4},{6,7},{7,6},{8,9},{9,8},{10,11... | collective-permute-start | bytes 1843208 | tf_op jit(solution)/shard_map/ppermute | solution.py:504
  77.2 17.8 %collective-permute-start.18 = (bf16[400,768]{1,0:T(8,128)(2,1)}, bf16[400,768]{1,0:T(8,128)(2,1)}, u32[]{:S(2)}, u32[]{:S(2)}) collective-permute-start(bf16[400,768]{1,0:T(8,128)(2,1)} %collective-permute-done.2.refs_2_), channel_id=1, source_target_pairs={{0,16},{16,0},{1,17},{17,1},{2,18},{18,2},{3,19},{19,3},{4,20},{20... | collective-permute-start | bytes 1843208 | tf_op jit(solution)/shard_map/ppermute | solution.py:496
  79.6 17.7 %collective-permute-start.16 = (bf16[192,768]{1,0:T(8,128)(2,1)S(1)}, bf16[192,768]{1,0:T(8,128)(2,1)S(1)}, u32[]{:S(2)}, u32[]{:S(2)}) collective-permute-start(bf16[192,768]{1,0:T(8,128)(2,1)S(1)} %slice.332), channel_id=1, source_target_pairs={{0,2},{1,3},{2,0},{3,1},{4,6},{5,7},{6,4},{7,5},{8,10},{9,11},{10,... | collective-permute-start | bytes 884744 | tf_op jit(solution)/shard_map/ppermute | solution.py:500
  97.9 18.4 %collective-permute-start.22 = (bf16[128,768]{1,0:T(8,128)(2,1)S(1)}, bf16[128,768]{1,0:T(8,128)(2,1)S(1)}, u32[]{:S(2)}, u32[]{:S(2)}) collective-permute-start(bf16[128,768]{1,0:T(8,128)(2,1)S(1)} %add_convert_fusion.22), channel_id=1, source_target_pairs={{0,2},{1,3},{2,0},{3,1},{4,6},{5,7},{6,4},{7,5},{8,10},{9,11},{10,... | collective-permute-start | bytes 589832 | tf_op jit(solution)/shard_map/ppermute | solution.py:500
  99.6 16.9 %collective-permute-start.21 = (bf16[384,768]{1,0:T(8,128)(2,1)S(1)}, bf16[384,768]{1,0:T(8,128)(2,1)}, u32[]{:S(2)}, u32[]{:S(2)}) collective-permute-start(bf16[384,768]{1,0:T(8,128)(2,1)S(1)} %constant_dynamic-update-slice_fusion.7.refs_10_), channel_id=1, source_target_pairs={{0,16},{16,0},{1,17},{17,1},{2,18},{18,2},{3,19},{19,3},{4,20},{20... | collective-permute-start | bytes 1769480 | tf_op jit(solution)/shard_map/ppermute | solution.py:496
  101.1 15.3 %collective-permute-start.20 = (bf16[384,768]{1,0:T(8,128)(2,1)S(1)}, bf16[384,768]{1,0:T(8,128)(2,1)S(1)}, u32[]{:S(2)}, u32[]{:S(2)}) collective-permute-start(bf16[384,768]{1,0:T(8,128)(2,1)S(1)} %bitcast.210), channel_id=1, source_target_pairs={{0,1},{1,0},{2,3},{3,2},{4,5},{5,4},{6,7},{7,6},{8,9},{9,8},{10,11... | collective-permute-start | bytes 1769480 | tf_op jit(solution)/shard_map/ppermute | solution.py:504
  101.3 15.2 %collective-permute-start.25 = (bf16[128,768]{1,0:T(8,128)(2,1)S(1)}, bf16[128,768]{1,0:T(8,128)(2,1)S(1)}, u32[]{:S(2)}, u32[]{:S(2)}) collective-permute-start(bf16[128,768]{1,0:T(8,128)(2,1)S(1)} %add_convert_fusion.21), channel_id=1, source_target_pairs={{0,2},{1,3},{2,0},{3,1},{4,6},{5,7},{6,4},{7,5},{8,10},{9,11},{10,... | collective-permute-start | bytes 589832 | tf_op jit(solution)/shard_map/ppermute | solution.py:500
  118.1 11.2 %collective-permute-start.26 = (bf16[400,768]{1,0:T(8,128)(2,1)}, bf16[400,768]{1,0:T(8,128)(2,1)S(1)}, u32[]{:S(2)}, u32[]{:S(2)}) collective-permute-start(bf16[400,768]{1,0:T(8,128)(2,1)} %collective-permute-done.5.refs_1_), channel_id=1, source_target_pairs={{0,1},{1,0},{2,3},{3,2},{4,5},{5,4},{6,7},{7,6},{8,9},{9,8},{10,11... | collective-permute-start | bytes 1843208 | tf_op jit(solution)/shard_map/ppermute | solution.py:504
  118.2 11.1 %collective-permute-start.27 = (bf16[400,768]{1,0:T(8,128)(2,1)}, bf16[400,768]{1,0:T(8,128)(2,1)S(1)}, u32[]{:S(2)}, u32[]{:S(2)}) collective-permute-start(bf16[400,768]{1,0:T(8,128)(2,1)} %collective-permute-done.2.refs_2_), channel_id=1, source_target_pairs={{0,1},{1,0},{2,3},{3,2},{4,5},{5,4},{6,7},{7,6},{8,9},{9,8},{10,11... | collective-permute-start | bytes 1843208 | tf_op jit(solution)/shard_map/ppermute | solution.py:504
  120.6 8.8 %collective-permute-start.28 = (bf16[400,768]{1,0:T(8,128)(2,1)}, bf16[400,768]{1,0:T(8,128)(2,1)S(1)}, u32[]{:S(2)}, u32[]{:S(2)}) collective-permute-start(bf16[400,768]{1,0:T(8,128)(2,1)} %collective-permute-done.18.refs_3_), channel_id=1, source_target_pairs={{0,1},{1,0},{2,3},{3,2},{4,5},{5,4},{6,7},{7,6},{8,9},{9,8},{10,11... | collective-permute-start | bytes 1843208 | tf_op jit(solution)/shard_map/ppermute | solution.py:504
  122.2 7.2 %collective-permute-start.33 = (bf16[128,768]{1,0:T(8,128)(2,1)S(1)}, bf16[128,768]{1,0:T(8,128)(2,1)S(1)}, u32[]{:S(2)}, u32[]{:S(2)}) collective-permute-start(bf16[128,768]{1,0:T(8,128)(2,1)S(1)} %add_convert_fusion.20), channel_id=1, source_target_pairs={{0,2},{1,3},{2,0},{3,1},{4,6},{5,7},{6,4},{7,5},{8,10},{9,11},{10,... | collective-permute-start | bytes 589832 | tf_op jit(solution)/shard_map/ppermute | solution.py:500
  152.5 8.1 %collective-permute-start.34 = (bf16[128,768]{1,0:T(8,128)(2,1)}, bf16[128,768]{1,0:T(8,128)(2,1)S(1)}, u32[]{:S(2)}, u32[]{:S(2)}) collective-permute-start(bf16[128,768]{1,0:T(8,128)(2,1)} %get-tuple-element.375.g_own), channel_id=1, source_target_pairs={{0,2},{1,3},{2,0},{3,1},{4,6},{5,7},{6,4},{7,5},{8,10},{9,11},{10,... | collective-permute-start | bytes 589832 | tf_op jit(solution)/shard_map/ppermute | solution.py:500
  160.6 9.4 %collective-permute-start.37 = (bf16[2,2,448,768]{3,2,1,0:T(8,128)(2,1)}, bf16[2,2,448,768]{3,2,1,0:T(8,128)(2,1)S(1)}, u32[]{:S(2)}, u32[]{:S(2)}) collective-permute-start(bf16[2,2,448,768]{3,2,1,0:T(8,128)(2,1)} %get-tuple-element.361), channel_id=1, source_target_pairs={{0,1},{1,0},{2,3},{3,2},{4,5},{5,4},{6,7},{7,6},{8,9},{9,8},{10,11... | collective-permute-start | bytes 8257544 | tf_op jit(solution)/shard_map/ppermute | solution.py:504
  160.7 9.3 %collective-permute-start.38 = (bf16[2,2,384,768]{3,2,1,0:T(8,128)(2,1)}, bf16[2,2,384,768]{3,2,1,0:T(8,128)(2,1)}, u32[]{:S(2)}, u32[]{:S(2)}) collective-permute-start(bf16[2,2,384,768]{3,2,1,0:T(8,128)(2,1)} %get-tuple-element.362), channel_id=1, source_target_pairs={{0,1},{1,0},{2,3},{3,2},{4,5},{5,4},{6,7},{7,6},{8,9},{9,8},{10,11... | collective-permute-start | bytes 7077896 | tf_op jit(solution)/shard_map/ppermute | solution.py:504
  161.2 8.8 %collective-permute-start.36 = (bf16[256,768]{1,0:T(8,128)(2,1)S(1)}, bf16[256,768]{1,0:T(8,128)(2,1)S(1)}, u32[]{:S(2)}, u32[]{:S(2)}) collective-permute-start(bf16[256,768]{1,0:T(8,128)(2,1)S(1)} %pad_maximum_fusion.18), channel_id=1, source_target_pairs={{0,1},{1,0},{2,3},{3,2},{4,5},{5,4},{6,7},{7,6},{8,9},{9,8},{10,11... | collective-permute-start | bytes 1179656 | tf_op jit(solution)/shard_map/ppermute | solution.py:504
  161.3 13.6 %collective-permute-start.35 = (bf16[256,768]{1,0:T(8,128)(2,1)S(1)}, bf16[256,768]{1,0:T(8,128)(2,1)S(1)}, u32[]{:S(2)}, u32[]{:S(2)}) collective-permute-start(bf16[256,768]{1,0:T(8,128)(2,1)S(1)} %copy-done.35), channel_id=1, source_target_pairs={{0,2},{1,3},{2,0},{3,1},{4,6},{5,7},{6,4},{7,5},{8,10},{9,11},{10,... | collective-permute-start | bytes 1179656 | tf_op jit(solution)/shard_map/ppermute | solution.py:500
  175.7 17.9 %collective-permute-start.41 = (bf16[512,768]{1,0:T(8,128)(2,1)S(1)}, bf16[512,768]{1,0:T(8,128)(2,1)}, u32[]{:S(2)}, u32[]{:S(2)}) collective-permute-start(bf16[512,768]{1,0:T(8,128)(2,1)S(1)} %pad_maximum_fusion.9), channel_id=1, source_target_pairs={{0,1},{1,0},{2,3},{3,2},{4,5},{5,4},{6,7},{7,6},{8,9},{9,8},{10,11... | collective-permute-start | bytes 2359304 | tf_op jit(solution)/shard_map/ppermute | solution.py:504
  175.9 17.7 %collective-permute-start.39 = (bf16[448,768]{1,0:T(8,128)(2,1)S(1)}, bf16[448,768]{1,0:T(8,128)(2,1)S(1)}, u32[]{:S(2)}, u32[]{:S(2)}) collective-permute-start(bf16[448,768]{1,0:T(8,128)(2,1)S(1)} %get-tuple-element.372), channel_id=1, source_target_pairs={{0,2},{1,3},{2,0},{3,1},{4,6},{5,7},{6,4},{7,5},{8,10},{9,11},{10,... | collective-permute-start | bytes 2064392 | tf_op jit(solution)/shard_map/ppermute | solution.py:500
  176.7 16.5 %collective-permute-start.40 = (bf16[384,768]{1,0:T(8,128)(2,1)}, bf16[384,768]{1,0:T(8,128)(2,1)}, u32[]{:S(2)}, u32[]{:S(2)}) collective-permute-start(bf16[384,768]{1,0:T(8,128)(2,1)} %get-tuple-element.373), channel_id=1, source_target_pairs={{0,16},{16,0},{1,17},{17,1},{2,18},{18,2},{3,19},{19,3},{4,20},{20... | collective-permute-start | bytes 1769480 | tf_op jit(solution)/shard_map/ppermute | solution.py:496
  193.6 21.7 %collective-permute-start.44 = (bf16[1024,768]{1,0:T(8,128)(2,1)}, bf16[1024,768]{1,0:T(8,128)(2,1)S(1)}, u32[]{:S(2)}, u32[]{:S(2)}) collective-permute-start(bf16[1024,768]{1,0:T(8,128)(2,1)} %get-tuple-element.394), channel_id=1, source_target_pairs={{0,1},{1,0},{2,3},{3,2},{4,5},{5,4},{6,7},{7,6},{8,9},{9,8},{10,11... | collective-permute-start | bytes 4718600 | tf_op jit(solution)/shard_map/ppermute | solution.py:504
  197.2 18.1 %collective-permute-start.42 = (bf16[448,768]{1,0:T(8,128)(2,1)}, bf16[448,768]{1,0:T(8,128)(2,1)S(1)}, u32[]{:S(2)}, u32[]{:S(2)}) collective-permute-start(bf16[448,768]{1,0:T(8,128)(2,1)} %get-tuple-element.392), channel_id=1, source_target_pairs={{0,2},{1,3},{2,0},{3,1},{4,6},{5,7},{6,4},{7,5},{8,10},{9,11},{10,... | collective-permute-start | bytes 2064392 | tf_op jit(solution)/shard_map/ppermute | solution.py:500
  198.1 17.0 %collective-permute-start.43 = (bf16[384,768]{1,0:T(8,128)(2,1)}, bf16[384,768]{1,0:T(8,128)(2,1)S(1)}, u32[]{:S(2)}, u32[]{:S(2)}) collective-permute-start(bf16[384,768]{1,0:T(8,128)(2,1)} %get-tuple-element.393), channel_id=1, source_target_pairs={{0,16},{16,0},{1,17},{17,1},{2,18},{18,2},{3,19},{19,3},{4,20},{20... | collective-permute-start | bytes 1769480 | tf_op jit(solution)/shard_map/ppermute | solution.py:496
  216.7 8.9 %collective-permute-start.47 = (bf16[1024,768]{1,0:T(8,128)(2,1)}, bf16[1024,768]{1,0:T(8,128)(2,1)}, u32[]{:S(2)}, u32[]{:S(2)}) collective-permute-start(bf16[1024,768]{1,0:T(8,128)(2,1)} %get-tuple-element.427), channel_id=1, source_target_pairs={{0,1},{1,0},{2,3},{3,2},{4,5},{5,4},{6,7},{7,6},{8,9},{9,8},{10,11... | collective-permute-start | bytes 4718600 | tf_op jit(solution)/shard_map/ppermute | solution.py:504
  216.9 18.0 %collective-permute-start.45 = (bf16[448,768]{1,0:T(8,128)(2,1)}, bf16[448,768]{1,0:T(8,128)(2,1)}, u32[]{:S(2)}, u32[]{:S(2)}) collective-permute-start(bf16[448,768]{1,0:T(8,128)(2,1)} %fusion.3), channel_id=1, source_target_pairs={{0,16},{16,0},{1,17},{17,1},{2,18},{18,2},{3,19},{19,3},{4,20},{20... | collective-permute-start | bytes 2064392 | tf_op jit(solution)/shard_map/ppermute | solution.py:496
  218.1 16.5 %collective-permute-start.46 = (bf16[384,768]{1,0:T(8,128)(2,1)}, bf16[384,768]{1,0:T(8,128)(2,1)}, u32[]{:S(2)}, u32[]{:S(2)}) collective-permute-start(bf16[384,768]{1,0:T(8,128)(2,1)} %fusion.7), channel_id=1, source_target_pairs={{0,2},{1,3},{2,0},{3,1},{4,6},{5,7},{6,4},{7,5},{8,10},{9,11},{10,... | collective-permute-start | bytes 1769480 | tf_op jit(solution)/shard_map/ppermute | solution.py:500
  219.2 38.2 %collective-permute-start.49 = (bf16[512,768]{1,0:T(8,128)(2,1)}, bf16[512,768]{1,0:T(8,128)(2,1)S(1)}, u32[]{:S(2)}, u32[]{:S(2)}) collective-permute-start(bf16[512,768]{1,0:T(8,128)(2,1)} %add_convert_fusion.2), channel_id=1, source_target_pairs={{0,2},{1,3},{2,0},{3,1},{4,6},{5,7},{6,4},{7,5},{8,10},{9,11},{10,... | collective-permute-start | bytes 2359304 | tf_op jit(solution)/shard_map/ppermute | solution.py:500
  240.2 17.3 %collective-permute-start.48 = (bf16[416,768]{1,0:T(8,128)(2,1)S(1)}, bf16[416,768]{1,0:T(8,128)(2,1)S(1)}, u32[]{:S(2)}, u32[]{:S(2)}) collective-permute-start(bf16[416,768]{1,0:T(8,128)(2,1)S(1)} %get-tuple-element.439), channel_id=1, source_target_pairs={{0,4},{4,0},{8,12},{12,8},{1,5},{5,1},{9,13},{13,9},{2,6},{6,2},{1... | collective-permute-start | bytes 1916936 | tf_op jit(solution)/shard_map/ppermute | solution.py:548
  258.3 15.7 %collective-permute-start.50 = (bf16[1024,768]{1,0:T(8,128)(2,1)}, bf16[1024,768]{1,0:T(8,128)(2,1)S(1)}, u32[]{:S(2)}, u32[]{:S(2)}) collective-permute-start(bf16[1024,768]{1,0:T(8,128)(2,1)} %get-tuple-element.454), channel_id=1, source_target_pairs={{0,1},{1,0},{2,3},{3,2},{4,5},{5,4},{6,7},{7,6},{8,9},{9,8},{10,11... | collective-permute-start | bytes 4718600 | tf_op jit(solution)/shard_map/ppermute | solution.py:504
  259.8 20.2 %collective-permute-start.52 = (bf16[512,768]{1,0:T(8,128)(2,1)}, bf16[512,768]{1,0:T(8,128)(2,1)S(1)}, u32[]{:S(2)}, u32[]{:S(2)}) collective-permute-start(bf16[512,768]{1,0:T(8,128)(2,1)} %add_convert_fusion.1), channel_id=1, source_target_pairs={{0,2},{1,3},{2,0},{3,1},{4,6},{5,7},{6,4},{7,5},{8,10},{9,11},{10,... | collective-permute-start | bytes 2359304 | tf_op jit(solution)/shard_map/ppermute | solution.py:500
  264.8 18.3 %collective-permute-start.56 = (bf16[256,768]{1,0:T(8,128)(2,1)}, bf16[256,768]{1,0:T(8,128)(2,1)S(1)}, u32[]{:S(2)}, u32[]{:S(2)}) collective-permute-start(bf16[256,768]{1,0:T(8,128)(2,1)} %add_convert_fusion.11), channel_id=1, source_target_pairs={{0,4},{4,0},{8,12},{12,8},{1,5},{5,1},{9,13},{13,9},{2,6},{6,2},{1... | collective-permute-start | bytes 1179656 | tf_op jit(solution)/shard_map/ppermute | solution.py:548
  265.2 21.2 %collective-permute-start.55 = (bf16[208,768]{1,0:T(8,128)(2,1)}, bf16[208,768]{1,0:T(8,128)(2,1)}, u32[]{:S(2)}, u32[]{:S(2)}) collective-permute-start(bf16[208,768]{1,0:T(8,128)(2,1)} %constant_dynamic-slice_fusion.2), channel_id=1, source_target_pairs={{0,8},{4,12},{8,0},{12,4},{1,9},{5,13},{9,1},{13,5},{2,10},{6,14},... | collective-permute-start | bytes 958472 | tf_op jit(solution)/shard_map/ppermute | solution.py:548
  281.4 15.2 %collective-permute-start.53 = (bf16[256,768]{1,0:T(8,128)(2,1)S(1)}, bf16[256,768]{1,0:T(8,128)(2,1)S(1)}, u32[]{:S(2)}, u32[]{:S(2)}) collective-permute-start(bf16[256,768]{1,0:T(8,128)(2,1)S(1)} %add_convert_fusion.10), channel_id=1, source_target_pairs={{0,4},{4,0},{8,12},{12,8},{1,5},{5,1},{9,13},{13,9},{2,6},{6,2},{1... | collective-permute-start | bytes 1179656 | tf_op jit(solution)/shard_map/ppermute | solution.py:548
  283.1 12.1 %collective-permute-start.54 = (bf16[256,768]{1,0:T(8,128)(2,1)S(1)}, bf16[256,768]{1,0:T(8,128)(2,1)S(1)}, u32[]{:S(2)}, u32[]{:S(2)}) collective-permute-start(bf16[256,768]{1,0:T(8,128)(2,1)S(1)} %get-tuple-element.576), channel_id=1, source_target_pairs={{0,2},{1,3},{2,0},{3,1},{4,6},{5,7},{6,4},{7,5},{8,10},{9,11},{10,... | collective-permute-start | bytes 1179656 | tf_op jit(solution)/shard_map/ppermute | solution.py:500
  285.3 36.5 %collective-permute-start.59 = (bf16[128,768]{1,0:T(8,128)(2,1)S(1)}, bf16[128,768]{1,0:T(8,128)(2,1)S(1)}, u32[]{:S(2)}, u32[]{:S(2)}) collective-permute-start(bf16[128,768]{1,0:T(8,128)(2,1)S(1)} %add_convert_fusion.19), channel_id=1, source_target_pairs={{0,8},{4,12},{8,0},{12,4},{1,9},{5,13},{9,1},{13,5},{2,10},{6,14},... | collective-permute-start | bytes 589832 | tf_op jit(solution)/shard_map/ppermute | solution.py:548
  286.5 15.2 %collective-permute-start.51 = (bf16[832,384]{1,0:T(8,128)(2,1)S(1)}, bf16[832,384]{1,0:T(8,128)(2,1)S(1)}, u32[]{:S(2)}, u32[]{:S(2)}) collective-permute-start(bf16[832,384]{1,0:T(8,128)(2,1)S(1)} %copy-done.54), channel_id=1, source_target_pairs={{0,16},{16,0},{1,17},{17,1},{2,18},{18,2},{3,19},{19,3},{4,20},{20... | collective-permute-start | bytes 1916936 | tf_op jit(solution)/shard_map/ppermute | solution.py:496
  288.0 15.7 %collective-permute-start.61 = (bf16[256,768]{1,0:T(8,128)(2,1)S(1)}, bf16[256,768]{1,0:T(8,128)(2,1)S(1)}, u32[]{:S(2)}, u32[]{:S(2)}) collective-permute-start(bf16[256,768]{1,0:T(8,128)(2,1)S(1)} %get-tuple-element.575), channel_id=1, source_target_pairs={{0,2},{1,3},{2,0},{3,1},{4,6},{5,7},{6,4},{7,5},{8,10},{9,11},{10,... | collective-permute-start | bytes 1179656 | tf_op jit(solution)/shard_map/ppermute | solution.py:500
  295.1 26.6 %collective-permute-start.58 = (bf16[208,768]{1,0:T(8,128)(2,1)S(1)}, bf16[208,768]{1,0:T(8,128)(2,1)S(1)}, u32[]{:S(2)}, u32[]{:S(2)}) collective-permute-start(bf16[208,768]{1,0:T(8,128)(2,1)S(1)} %add_convert_fusion.13), channel_id=1, source_target_pairs={{0,8},{4,12},{8,0},{12,4},{1,9},{5,13},{9,1},{13,5},{2,10},{6,14},... | collective-permute-start | bytes 958472 | tf_op jit(solution)/shard_map/ppermute | solution.py:548
  296.6 22.0 %collective-permute-start.60 = (bf16[256,768]{1,0:T(8,128)(2,1)S(1)}, bf16[256,768]{1,0:T(8,128)(2,1)S(1)}, u32[]{:S(2)}, u32[]{:S(2)}) collective-permute-start(bf16[256,768]{1,0:T(8,128)(2,1)S(1)} %add_convert_fusion.9), channel_id=1, source_target_pairs={{0,4},{4,0},{8,12},{12,8},{1,5},{5,1},{9,13},{13,9},{2,6},{6,2},{1... | collective-permute-start | bytes 1179656 | tf_op jit(solution)/shard_map/ppermute | solution.py:548
  301.6 26.1 %collective-permute-start.63 = (bf16[128,768]{1,0:T(8,128)(2,1)S(1)}, bf16[128,768]{1,0:T(8,128)(2,1)S(1)}, u32[]{:S(2)}, u32[]{:S(2)}) collective-permute-start(bf16[128,768]{1,0:T(8,128)(2,1)S(1)} %add_convert_fusion.18), channel_id=1, source_target_pairs={{0,8},{4,12},{8,0},{12,4},{1,9},{5,13},{9,1},{13,5},{2,10},{6,14},... | collective-permute-start | bytes 589832 | tf_op jit(solution)/shard_map/ppermute | solution.py:548
  303.6 24.0 %collective-permute-start.57 = (bf16[416,384]{1,0:T(8,128)(2,1)S(1)}, bf16[416,384]{1,0:T(8,128)(2,1)S(1)}, u32[]{:S(2)}, u32[]{:S(2)}) collective-permute-start(bf16[416,384]{1,0:T(8,128)(2,1)S(1)} %constant_dynamic-slice_fusion.1), channel_id=1, source_target_pairs={{0,4},{4,0},{8,12},{12,8},{1,5},{5,1},{9,13},{13,9},{2,6},{6,2},{1... | collective-permute-start | bytes 958472 | tf_op jit(solution)/shard_map/ppermute | solution.py:548
  318.7 11.3 %collective-permute-start.65 = (bf16[128,768]{1,0:T(8,128)(2,1)S(1)}, bf16[128,768]{1,0:T(8,128)(2,1)S(1)}, u32[]{:S(2)}, u32[]{:S(2)}) collective-permute-start(bf16[128,768]{1,0:T(8,128)(2,1)S(1)} %add_convert_fusion.17), channel_id=1, source_target_pairs={{0,8},{4,12},{8,0},{12,4},{1,9},{5,13},{9,1},{13,5},{2,10},{6,14},... | collective-permute-start | bytes 589832 | tf_op jit(solution)/shard_map/ppermute | solution.py:548
  328.9 8.0 %collective-permute-start.64 = (bf16[2,128,768]{2,1,0:T(8,128)(2,1)S(1)}, bf16[2,128,768]{2,1,0:T(8,128)(2,1)S(1)}, u32[]{:S(2)}, u32[]{:S(2)}) collective-permute-start(bf16[2,128,768]{2,1,0:T(8,128)(2,1)S(1)} %bitcast.202), channel_id=1, source_target_pairs={{0,2},{1,3},{2,0},{3,1},{4,6},{5,7},{6,4},{7,5},{8,10},{9,11},{10,... | collective-permute-start | bytes 1179656 | tf_op jit(solution)/shard_map/ppermute | solution.py:500
  330.0 6.9 %collective-permute-start.62 = (bf16[208,384]{1,0:T(8,128)(2,1)S(1)}, bf16[208,384]{1,0:T(8,128)(2,1)S(1)}, u32[]{:S(2)}, u32[]{:S(2)}) collective-permute-start(bf16[208,384]{1,0:T(8,128)(2,1)S(1)} %constant_dynamic-slice_fusion), channel_id=1, source_target_pairs={{0,8},{4,12},{8,0},{12,4},{1,9},{5,13},{9,1},{13,5},{2,10},{6,14},... | collective-permute-start | bytes 479240 | tf_op jit(solution)/shard_map/ppermute | solution.py:548
  337.0 4.8 %collective-permute-start.68 = (bf16[2,2,128,768]{3,2,1,0:T(8,128)(2,1)S(1)}, bf16[2,2,128,768]{3,2,1,0:T(8,128)(2,1)}, u32[]{:S(2)}, u32[]{:S(2)}) collective-permute-start(bf16[2,2,128,768]{3,2,1,0:T(8,128)(2,1)S(1)} %pad_maximum_fusion.10), channel_id=1, source_target_pairs={{0,1},{1,0},{2,3},{3,2},{4,5},{5,4},{6,7},{7,6},{8,9},{9,8},{10,11... | collective-permute-start | bytes 2359304 | tf_op jit(solution)/shard_map/ppermute | solution.py:504
  337.1 22.8 %collective-permute-start.72 = (bf16[416,768]{1,0:T(8,128)(2,1)S(1)}, bf16[416,768]{1,0:T(8,128)(2,1)S(1)}, u32[]{:S(2)}, u32[]{:S(2)}) collective-permute-start(bf16[416,768]{1,0:T(8,128)(2,1)S(1)} %pad_maximum_fusion.12), channel_id=1, source_target_pairs={{0,4},{4,0},{8,12},{12,8},{1,5},{5,1},{9,13},{13,9},{2,6},{6,2},{1... | collective-permute-start | bytes 1916936 | tf_op jit(solution)/shard_map/ppermute | solution.py:548
  337.2 19.9 %collective-permute-start.69 = (bf16[3,128,768]{2,1,0:T(8,128)(2,1)S(1)}, bf16[3,128,768]{2,1,0:T(8,128)(2,1)S(1)}, u32[]{:S(2)}, u32[]{:S(2)}) collective-permute-start(bf16[3,128,768]{2,1,0:T(8,128)(2,1)S(1)} %bitcast.212), channel_id=1, source_target_pairs={{0,2},{1,3},{2,0},{3,1},{4,6},{5,7},{6,4},{7,5},{8,10},{9,11},{10,... | collective-permute-start | bytes 1769480 | tf_op jit(solution)/shard_map/ppermute | solution.py:500
  338.5 18.5 %collective-permute-start.66 = (bf16[1,128,768]{2,1,0:T(8,128)(2,1)S(1)}, bf16[1,128,768]{2,1,0:T(8,128)(2,1)S(1)}, u32[]{:S(2)}, u32[]{:S(2)}) collective-permute-start(bf16[1,128,768]{2,1,0:T(8,128)(2,1)S(1)} %bitcast.216), channel_id=1, source_target_pairs={{0,2},{1,3},{2,0},{3,1},{4,6},{5,7},{6,4},{7,5},{8,10},{9,11},{10,... | collective-permute-start | bytes 589832 | tf_op jit(solution)/shard_map/ppermute | solution.py:500
  339.3 17.7 %collective-permute-start.67 = (bf16[208,384]{1,0:T(8,128)(2,1)S(1)}, bf16[208,384]{1,0:T(8,128)(2,1)S(1)}, u32[]{:S(2)}, u32[]{:S(2)}) collective-permute-start(bf16[208,384]{1,0:T(8,128)(2,1)S(1)} %add_convert_fusion.23), channel_id=1, source_target_pairs={{0,8},{4,12},{8,0},{12,4},{1,9},{5,13},{9,1},{13,5},{2,10},{6,14},... | collective-permute-start | bytes 479240 | tf_op jit(solution)/shard_map/ppermute | solution.py:548
  358.0 9.5 %collective-permute-start.70 = (bf16[416,384]{1,0:T(8,128)(2,1)S(1)}, bf16[416,384]{1,0:T(8,128)(2,1)S(1)}, u32[]{:S(2)}, u32[]{:S(2)}) collective-permute-start(bf16[416,384]{1,0:T(8,128)(2,1)S(1)} %pad_maximum_fusion.21), channel_id=1, source_target_pairs={{0,4},{4,0},{8,12},{12,8},{1,5},{5,1},{9,13},{13,9},{2,6},{6,2},{1... | collective-permute-start | bytes 958472 | tf_op jit(solution)/shard_map/ppermute | solution.py:548
  (79 other events, 654.5 us)

commit v5 on v4

--- a/solution.py
+++ b/solution.py
@@ -11,7 +11,7 @@
 EPSILON = 1e-05
 F32 = jnp.float32
 BF16 = jnp.bfloat16
-VMEM_LIMIT = 56 << 20
+VMEM_LIMIT = 53 << 20
 EXTRA = 16
 SUMS = 64
 SMEM_SPEC = pl.BlockSpec(memory_space=pltpu.SMEM)

time: 379 us -> 375 us (0.989)
  waiting for transfers between devices: 90.1 us -> 97.8 us
  other arithmetic: 45.2 us -> 39.1 us
    unnamed x149 -> x163, local copies, waits for them, and re-layouts: 10.2 us -> 8.84 us
  transfers between devices with their start and end apart: 74 -> 74, of which waited for: 24 -> 28; matrix products, arithmetic and copies ran while one was open for 13% -> 11% of each run, Pallas kernels for 32% -> 32%
where the time goes in v5:
time: 375 us; the launch traced here: 371 us
  Pallas kernels  139 us (37%)
  waiting for transfers between devices  97.8 us (26%)
  starting transfers between devices  72.7 us (19%)
  other arithmetic  39.1 us (10%)
  local copies, waits for them, and re-layouts  20.4 us (5%)
    ppermute x20, waiting for transfers between devices, along(): lax.ppermute(value, 'context', [(i, i ^ mask) for i in range(contexts)])  51.9 us
    pallas_call x3, Pallas kernels, attention_backward(): pl.pallas_call(functools.partial(backward_body, heads, nears, index), out...  45.7 us
    pallas_call x3, Pallas kernels, attention_forward(): pl.pallas_call(functools.partial(forward_body, heads, index), out_shape=(...  41.3 us
    ppermute x21, waiting for transfers between devices, across(): return lax.ppermute(value, 'tensor', [(i, i ^ 2) for i in range(4)])  37.1 us
    ppermute x20, starting transfers between devices, along(): lax.ppermute(value, 'context', [(i, i ^ mask) for i in range(contexts)])  35.1 us
    convert_element_type x26, other arithmetic, low_sum(): return added(*values).astype(BF16)  25.4 us
    ppermute x21, starting transfers between devices, across(): return lax.ppermute(value, 'tensor', [(i, i ^ 2) for i in range(4)])  23.2 us
    pallas_call x1, Pallas kernels, feed_forward(): pl.pallas_call(functools.partial(feed_body, blocks, pieces, seqs), out_sh...  20.5 us
  transfers between devices with their start and end apart: 74, of which 28 were waited for; matrix products, arithmetic and copies ran while one was open for 11% of the time, Pallas kernels for 32%

profile of v5, /device:TPU:0, one launch (start us, length us, event | category | flops | bytes accessed | tf_op | source)
XLA Modules:
  0.0 371.3 jit_solution(12297684643679391652)
XLA Ops:
  0.7 2.7 fusion.20
  3.5 4.1 %collective-permute-start = (bf16[128,768]{1,0:T(8,128)(2,1)S(1)}, bf16[128,768]{1,0:T(8,128)(2,1)S(1)}, u32[]{:S(2)}, u32[]{:S(2)}) collective-permute-start(bf16[128,768]{1,0:T(8,128)(2,1)S(1)} %dynamic-slice_bitcast_fusion.2.refs_16_), channel_id=1, source_target_pairs={{0,8},{4,12},{8,0},{12,4},{1,9},{5,13},{9,1},{13,5},{2,10},{6,14},... | collective-permute-start | bytes 589832 | tf_op jit(solution)/shard_map/ppermute | solution.py:548
  11.9 4.8 %collective-permute-done = bf16[128,768]{1,0:T(8,128)(2,1)S(1)} collective-permute-done((bf16[128,768]{1,0:T(8,128)(2,1)S(1)}, bf16[128,768]{1,0:T(8,128)(2,1)S(1)}, u32[]{:S(2)}, u32[]{:S(2)}) %collective-permute-start) | collective-permute-done | bytes 196640 | tf_op jit(solution)/shard_map/ppermute | solution.py:548
  16.7 1.5 collective-permute-start.2
  18.2 1.5 collective-permute-start.1
  20.5 3.4 collective-permute-start.4
  23.9 8.8 %collective-permute-done.4 = bf16[128,768]{1,0:T(8,128)(2,1)S(1)} collective-permute-done((bf16[128,768]{1,0:T(8,128)(2,1)S(1)}, bf16[128,768]{1,0:T(8,128)(2,1)S(1)}, u32[]{:S(2)}, u32[]{:S(2)}) %collective-permute-start.4) | collective-permute-done | bytes 196640 | tf_op jit(solution)/shard_map/ppermute | solution.py:548
  35.1 3.3 collective-permute-start.7
  38.4 1.8 collective-permute-start.8
  42.5 7.2 %collective-permute-done.8 = bf16[128,768]{1,0:T(8,128)(2,1)S(1)} collective-permute-done((bf16[128,768]{1,0:T(8,128)(2,1)S(1)}, bf16[128,768]{1,0:T(8,128)(2,1)S(1)}, u32[]{:S(2)}, u32[]{:S(2)}) %collective-permute-start.8) | collective-permute-done | bytes 196640 | tf_op jit(solution)/shard_map/ppermute | solution.py:548
  52.7 1.6 collective-permute-start.12
  56.5 1.9 collective-permute-start.13
  59.1 13.9 %attention_forward.3 = (bf16[512,192]{1,0:T(8,128)(2,1)S(1)}, bf16[2048,192]{1,0:T(8,128)(2,1)}, bf16[2048,192]{1,0:T(8,128)(2,1)}, bf16[512,192]{1,0:T(8,128)(2...) custom-call(s32[4]{0:T(128)S(1)} %pad_add_fusion.places, ...), custom_call_target="tpu_custom_call" | custom-call | flops 4429185024 | bytes 5505024 | tf_op jit(solution)/shard_map/attention_forward/pallas_call | solution.py:189
  73.0 1.8 collective-permute-done.10
  75.6 1.6 collective-permute-start.19
  81.1 13.6 %attention_forward.4 = (bf16[512,192]{1,0:T(8,128)(2,1)S(1)}, bf16[2048,192]{1,0:T(8,128)(2,1)}, bf16[2048,192]{1,0:T(8,128)(2,1)}, bf16[512,192]{1,0:T(8,128)(2...) custom-call(s32[4]{0:T(128)S(1)} %pad_add_fusion.places, ...), custom_call_target="tpu_custom_call" | custom-call | flops 4429185024 | bytes 5505024 | tf_op jit(solution)/shard_map/attention_forward/pallas_call | solution.py:189
  94.9 2.4 collective-permute-done.16
  98.0 1.6 collective-permute-start.22
  100.9 1.6 collective-permute-start.25
  102.5 13.8 %attention_forward.5 = (bf16[512,192]{1,0:T(8,128)(2,1)S(1)}, bf16[2048,192]{1,0:T(8,128)(2,1)}, bf16[2048,192]{1,0:T(8,128)(2,1)}, bf16[512,192]{1,0:T(8,128)(2...) custom-call(s32[4]{0:T(128)S(1)} %pad_add_fusion.places, ...), custom_call_target="tpu_custom_call" | custom-call | flops 4429185024 | bytes 5505024 | tf_op jit(solution)/shard_map/attention_forward/pallas_call | solution.py:189
  117.6 2.7 collective-permute-done.32.refs_24_
  122.3 1.5 collective-permute-done.31.refs_15_
  123.8 4.2 %collective-permute-done.33.refs_27_ = bf16[128,768]{1,0:T(8,128)(2,1)S(1)} collective-permute-done((bf16[128,768]{1,0:T(8,128)(2,1)S(1)}, bf16[128,768]{1,0:T(8,128)(2,1)S(1)}, u32[]{:S(2)}, u32[]{:S(2)}) %collective-permute-start.33) | collective-permute-done | bytes 196640 | tf_op jit(solution)/shard_map/ppermute | solution.py:500
  128.7 20.5 %feed_forward.1 = (bf16[384,768]{1,0:T(8,128)(2,1)}, bf16[128,768]{1,0:T(8,128)(2,1)S(1)}, bf16[256,768]{1,0:T(8,128)(2,1)}, f32[384,768]{1,0:T(8,128)}, bf16[4,...) custom-call(s32[5]{0:T(128)S(1)} %concatenate.73.order.refs_8_, ...), custom_call_target="tpu_custom_call" | custom-call | flops 7247757312 | bytes 14155776 | tf_op jit(solution)/shard_map/feed_forward/pallas_call | solution.py:411
  151.4 6.7 %feed_gradients.2 = (bf16[2,2,448,768]{3,2,1,0:T(8,128)(2,1)}, bf16[2,2,384,768]{3,2,1,0:T(8,128)(2,1)}) custom-call(s32[5]{0:T(128)S(1)} %concatenate.73.order.refs_8_, bf16[4,384,768]{2,1,0:T(8,128)(2,1)} %get-tuple-element.351.act, bf16[4,384,768]{2,1,0:T(8,128)(2,1)} %get-tuple-element.363.d_inner, bf16[384,768]{1,0:T(8,128)(2,1)S(1)} %copy-done.11, ...), custom_call_target="tpu_custom_call" | custom-call | flops 1811939328 | bytes 4718592 | tf_op jit(solution)/shard_map/feed_gradients/pallas_call | solution.py:474
  159.8 7.1 %feed_gradients.3 = (bf16[2,2,448,768]{3,2,1,0:T(8,128)(2,1)}, bf16[2,2,384,768]{3,2,1,0:T(8,128)(2,1)}) custom-call(s32[5]{0:T(128)S(1)} %concatenate.73.order.refs_8_, bf16[4,384,768]{2,1,0:T(8,128)(2,1)} %get-tuple-element.351.act, bf16[4,384,768]{2,1,0:T(8,128)(2,1)} %get-tuple-element.363.d_inner, bf16[384,768]{1,0:T(8,128)(2,1)S(1)} %copy-done.11, ...), custom_call_target="tpu_custom_call" | custom-call | flops 1811939328 | bytes 4718592 | tf_op jit(solution)/shard_map/feed_gradients/pallas_call | solution.py:474
  167.9 2.3 fusion.13
  170.8 1.4 fusion.9
  174.6 14.9 %attention_backward.3 = (bf16[512,192]{1,0:T(8,128)(2,1)S(1)}, bf16[2048,192]{1,0:T(8,128)(2,1)}, bf16[2048,192]{1,0:T(8,128)(2,1)}, bf16[1024,768]{1,0:T(8,128)...) custom-call(s32[4]{0:T(128)S(1)} %pad_add_fusion.places, ...), custom_call_target="tpu_custom_call" | custom-call | flops 9261023232 | bytes 7077888 | tf_op jit(solution)/shard_map/attention_backward/pallas_call | solution.py:220
  190.4 2.5 fusion.7
  196.1 15.5 %attention_backward.4 = (bf16[512,192]{1,0:T(8,128)(2,1)S(1)}, bf16[2048,192]{1,0:T(8,128)(2,1)}, bf16[2048,192]{1,0:T(8,128)(2,1)}, bf16[1024,768]{1,0:T(8,128)...) custom-call(s32[4]{0:T(128)S(1)} %pad_add_fusion.places, ...), custom_call_target="tpu_custom_call" | custom-call | flops 9261023232 | bytes 7077888 | tf_op jit(solution)/shard_map/attention_backward/pallas_call | solution.py:220
  211.9 1.6 add_convert_fusion.2
  216.8 5.5 %attention_gradients.3.refs_7_ = f32[3,192,768]{2,1,0:T(8,128)} custom-call(bf16[3,512,768]{2,1,0:T(8,128)(2,1)} %refs_0_.5, bf16[384,768]{1,0:T(8,128)(2,1)S(1)} %copy-done.1, bf16[384,768]{1,0:T(8,128)(2,1)} %copy-done.17, bf16[768,768]{1,0:T(8,128)(2,1)} %collective-permute-done.9.sib.refs_3_, bf16[512,192]{1,0:T(8,128)(2,1)S(1)} %get-tuple-element.428.refs_4_, ...), custom_call_target="tpu_custom_call" | custom-call | flops 1207959552 | bytes 4718592 | tf_op jit(solution)/shard_map/attention_gradients/pallas_call | solution.py:299
  222.3 2.3 add_convert_fusion.1
  224.6 5.9 %attention_gradients.4.refs_7_ = f32[3,192,768]{2,1,0:T(8,128)} custom-call(bf16[3,512,768]{2,1,0:T(8,128)(2,1)} %refs_0_.5, bf16[384,768]{1,0:T(8,128)(2,1)S(1)} %copy-done.3, bf16[384,768]{1,0:T(8,128)(2,1)} %copy-done.21, bf16[768,768]{1,0:T(8,128)(2,1)} %copy-done.35, bf16[512,192]{1,0:T(8,128)(2,1)S(1)} %get-tuple-element.432.refs_4_, ...), custom_call_target="tpu_custom_call" | custom-call | flops 1207959552 | bytes 4718592 | tf_op jit(solution)/shard_map/attention_gradients/pallas_call | solution.py:299
  231.7 1.8 fusion.6
  233.6 1.9 fusion.2
  235.5 1.8 fusion.10
  237.3 1.9 collective-permute-start.48
  239.2 15.4 %attention_backward.5 = (bf16[512,192]{1,0:T(8,128)(2,1)S(1)}, bf16[2048,192]{1,0:T(8,128)(2,1)}, bf16[2048,192]{1,0:T(8,128)(2,1)}, bf16[1024,768]{1,0:T(8,128)...) custom-call(s32[4]{0:T(128)S(1)} %pad_add_fusion.places, ...), custom_call_target="tpu_custom_call" | custom-call | flops 9261023232 | bytes 7077888 | tf_op jit(solution)/shard_map/attention_backward/pallas_call | solution.py:220
  257.0 1.2 add_convert_fusion.6
  258.3 1.3 add_convert_fusion.11
  260.0 2.5 collective-permute-start.55
  262.5 6.2 %attention_gradients.5 = (bf16[832,384]{1,0:T(8,128)(2,1)}, bf16[832,384]{1,0:T(8,128)(2,1)}) custom-call(bf16[3,512,768]{2,1,0:T(8,128)(2,1)} %refs_0_.5, bf16[384,768]{1,0:T(8,128)(2,1)S(1)} %copy-done.5, bf16[384,768]{1,0:T(8,128)(2,1)} %copy-done.20, bf16[768,768]{1,0:T(8,128)(2,1)} %copy-done.34, bf16[512,192]{1,0:T(8,128)(2,1)S(1)} %get-tuple-element.462.refs_4_, ...), custom_call_target="tpu_custom_call" | custom-call | flops 1207959552 | bytes 4718592 | tf_op jit(solution)/shard_map/attention_gradients/pallas_call | solution.py:299
  269.0 7.1 %collective-permute-done.52 = bf16[512,768]{1,0:T(8,128)(2,1)S(1)} collective-permute-done((bf16[512,768]{1,0:T(8,128)(2,1)}, bf16[512,768]{1,0:T(8,128)(2,1)S(1)}, u32[]{:S(2)}, u32[]{:S(2)}) %collective-permute-start.52) | collective-permute-done | bytes 786464 | tf_op jit(solution)/shard_map/ppermute | solution.py:500
  279.9 2.6 collective-permute-start.59
  284.5 5.3 %collective-permute-done.54 = bf16[256,768]{1,0:T(8,128)(2,1)S(1)} collective-permute-done((bf16[256,768]{1,0:T(8,128)(2,1)S(1)}, bf16[256,768]{1,0:T(8,128)(2,1)S(1)}, u32[]{:S(2)}, u32[]{:S(2)}) %collective-permute-start.54) | collective-permute-done | bytes 393248 | tf_op jit(solution)/shard_map/ppermute | solution.py:500
  289.8 2.4 collective-permute-start.58
  294.4 3.2 collective-permute-done.51
  298.3 1.7 collective-permute-start.57
  300.1 14.7 %collective-permute-done.60 = bf16[256,768]{1,0:T(8,128)(2,1)S(1)} collective-permute-done((bf16[256,768]{1,0:T(8,128)(2,1)S(1)}, bf16[256,768]{1,0:T(8,128)(2,1)S(1)}, u32[]{:S(2)}, u32[]{:S(2)}) %collective-permute-start.60) | collective-permute-done | bytes 393248 | tf_op jit(solution)/shard_map/ppermute | solution.py:548
  314.9 2.6 collective-permute-start.65
  317.7 1.4 add_convert_fusion.16
  319.1 4.4 %collective-permute-done.57 = bf16[416,384]{1,0:T(8,128)(2,1)S(1)} collective-permute-done((bf16[416,384]{1,0:T(8,128)(2,1)S(1)}, bf16[416,384]{1,0:T(8,128)(2,1)S(1)}, u32[]{:S(2)}, u32[]{:S(2)}) %collective-permute-start.57) | collective-permute-done | bytes 319520 | tf_op jit(solution)/shard_map/ppermute | solution.py:548
  326.9 5.8 %collective-permute-done.62 = bf16[208,384]{1,0:T(8,128)(2,1)S(1)} collective-permute-done((bf16[208,384]{1,0:T(8,128)(2,1)S(1)}, bf16[208,384]{1,0:T(8,128)(2,1)S(1)}, u32[]{:S(2)}, u32[]{:S(2)}) %collective-permute-start.62) | collective-permute-done | bytes 159776 | tf_op jit(solution)/shard_map/ppermute | solution.py:548
  333.2 1.2 collective-permute-start.69
  335.4 2.3 collective-permute-start.67
  337.6 1.2 select_bitcast_fusion.7
  339.2 13.9 %collective-permute-done.66 = bf16[1,128,768]{2,1,0:T(8,128)(2,1)S(1)} collective-permute-done((bf16[1,128,768]{2,1,0:T(8,128)(2,1)S(1)}, bf16[1,128,768]{2,1,0:T(8,128)(2,1)S(1)}, u32[]{:S(2)}, u32[]{:S(2)}) %collective-permute-start.66) | collective-permute-done | bytes 196640 | tf_op jit(solution)/shard_map/ppermute | solution.py:500
  354.0 1.7 collective-permute-start.70
  357.6 1.6 copy.36
  359.2 4.3 %collective-permute-done.70 = bf16[416,384]{1,0:T(8,128)(2,1)S(1)} collective-permute-done((bf16[416,384]{1,0:T(8,128)(2,1)S(1)}, bf16[416,384]{1,0:T(8,128)(2,1)S(1)}, u32[]{:S(2)}, u32[]{:S(2)}) %collective-permute-start.70) | collective-permute-done | bytes 319520 | tf_op jit(solution)/shard_map/ppermute | solution.py:548
  368.1 1.4 copy.37
  369.5 1.6 pad_maximum_fusion.1
  (352 shorter events, 67.0 us)
Async XLA Ops:
  3.5 13.2 %collective-permute-start = (bf16[128,768]{1,0:T(8,128)(2,1)S(1)}, bf16[128,768]{1,0:T(8,128)(2,1)S(1)}, u32[]{:S(2)}, u32[]{:S(2)}) collective-permute-start(bf16[128,768]{1,0:T(8,128)(2,1)S(1)} %dynamic-slice_bitcast_fusion.2.refs_16_), channel_id=1, source_target_pairs={{0,8},{4,12},{8,0},{12,4},{1,9},{5,13},{9,1},{13,5},{2,10},{6,14},... | collective-permute-start | bytes 589832 | tf_op jit(solution)/shard_map/ppermute | solution.py:548
  16.7 16.8 %collective-permute-start.2 = (bf16[400,768]{1,0:T(8,128)(2,1)}, bf16[400,768]{1,0:T(8,128)(2,1)}, u32[]{:S(2)}, u32[]{:S(2)}) collective-permute-start(bf16[400,768]{1,0:T(8,128)(2,1)} %pad_maximum_fusion.13.refs_0_), channel_id=1, source_target_pairs={{0,2},{1,3},{2,0},{3,1},{4,6},{5,7},{6,4},{7,5},{8,10},{9,11},{10,... | collective-permute-start | bytes 1843208 | tf_op jit(solution)/shard_map/ppermute | solution.py:500
  18.2 15.3 %collective-permute-start.1 = (bf16[4,192,384]{2,1,0:T(8,128)(2,1)S(1)}, bf16[4,192,384]{2,1,0:T(8,128)(2,1)S(1)}, u32[]{:S(2)}, u32[]{:S(2)}) collective-permute-start(bf16[4,192,384]{2,1,0:T(8,128)(2,1)S(1)} %pad_maximum_fusion.14), channel_id=1, source_target_pairs={{0,16},{16,0},{1,17},{17,1},{2,18},{18,2},{3,19},{19,3},{4,20},{20... | collective-permute-start | bytes 1769480 | tf_op jit(solution)/shard_map/ppermute | solution.py:496
  19.8 13.7 %collective-permute-start.3 = (bf16[256,768]{1,0:T(8,128)(2,1)S(1)}, bf16[256,768]{1,0:T(8,128)(2,1)S(1)}, u32[]{:S(2)}, u32[]{:S(2)}) collective-permute-start(bf16[256,768]{1,0:T(8,128)(2,1)S(1)} %pad_maximum_fusion.15), channel_id=1, source_target_pairs={{0,4},{4,0},{8,12},{12,8},{1,5},{5,1},{9,13},{13,9},{2,6},{6,2},{1... | collective-permute-start | bytes 1179656 | tf_op jit(solution)/shard_map/ppermute | solution.py:548
  20.5 12.2 %collective-permute-start.4 = (bf16[128,768]{1,0:T(8,128)(2,1)S(1)}, bf16[128,768]{1,0:T(8,128)(2,1)S(1)}, u32[]{:S(2)}, u32[]{:S(2)}) collective-permute-start(bf16[128,768]{1,0:T(8,128)(2,1)S(1)} %get-tuple-element.283.refs_17_), channel_id=1, source_target_pairs={{0,8},{4,12},{8,0},{12,4},{1,9},{5,13},{9,1},{13,5},{2,10},{6,14},... | collective-permute-start | bytes 589832 | tf_op jit(solution)/shard_map/ppermute | solution.py:548
  33.6 16.9 %collective-permute-start.5 = (bf16[400,768]{1,0:T(8,128)(2,1)}, bf16[400,768]{1,0:T(8,128)(2,1)}, u32[]{:S(2)}, u32[]{:S(2)}) collective-permute-start(bf16[400,768]{1,0:T(8,128)(2,1)} %pad_maximum_fusion.13.refs_0_), channel_id=1, source_target_pairs={{0,16},{16,0},{1,17},{17,1},{2,18},{18,2},{3,19},{19,3},{4,20},{20... | collective-permute-start | bytes 1843208 | tf_op jit(solution)/shard_map/ppermute | solution.py:496
  34.4 16.1 %collective-permute-start.6 = (bf16[384,768]{1,0:T(8,128)(2,1)S(1)}, bf16[384,768]{1,0:T(8,128)(2,1)S(1)}, u32[]{:S(2)}, u32[]{:S(2)}) collective-permute-start(bf16[384,768]{1,0:T(8,128)(2,1)S(1)} %constant_dynamic-update-slice_fusion.1.near.refs_1_), channel_id=1, source_target_pairs={{0,2},{1,3},{2,0},{3,1},{4,6},{5,7},{6,4},{7,5},{8,10},{9,11},{10,... | collective-permute-start | bytes 1769480 | tf_op jit(solution)/shard_map/ppermute | solution.py:500
  35.1 15.4 %collective-permute-start.7 = (bf16[256,768]{1,0:T(8,128)(2,1)S(1)}, bf16[256,768]{1,0:T(8,128)(2,1)S(1)}, u32[]{:S(2)}, u32[]{:S(2)}) collective-permute-start(bf16[256,768]{1,0:T(8,128)(2,1)S(1)} %pad_maximum_fusion.16), channel_id=1, source_target_pairs={{0,4},{4,0},{8,12},{12,8},{1,5},{5,1},{9,13},{13,9},{2,6},{6,2},{1... | collective-permute-start | bytes 1179656 | tf_op jit(solution)/shard_map/ppermute | solution.py:548
  38.4 11.3 %collective-permute-start.8 = (bf16[128,768]{1,0:T(8,128)(2,1)S(1)}, bf16[128,768]{1,0:T(8,128)(2,1)S(1)}, u32[]{:S(2)}, u32[]{:S(2)}) collective-permute-start(bf16[128,768]{1,0:T(8,128)(2,1)S(1)} %get-tuple-element.294.refs_18_), channel_id=1, source_target_pairs={{0,8},{4,12},{8,0},{12,4},{1,9},{5,13},{9,1},{13,5},{2,10},{6,14},... | collective-permute-start | bytes 589832 | tf_op jit(solution)/shard_map/ppermute | solution.py:548
  51.7 6.8 %collective-permute-start.9 = (bf16[768,768]{1,0:T(8,128)(2,1)}, bf16[768,768]{1,0:T(8,128)(2,1)}, u32[]{:S(2)}, u32[]{:S(2)}) collective-permute-start(bf16[768,768]{1,0:T(8,128)(2,1)} %pad_maximum_fusion.5), channel_id=1, source_target_pairs={{0,1},{1,0},{2,3},{3,2},{4,5},{5,4},{6,7},{7,6},{8,9},{9,8},{10,11... | collective-permute-start | bytes 3538952 | tf_op jit(solution)/shard_map/ppermute | solution.py:504
  52.7 20.2 %collective-permute-start.12 = (bf16[384,768]{1,0:T(8,128)(2,1)S(1)}, bf16[384,768]{1,0:T(8,128)(2,1)S(1)}, u32[]{:S(2)}, u32[]{:S(2)}) collective-permute-start(bf16[384,768]{1,0:T(8,128)(2,1)S(1)} %constant_dynamic-update-slice_fusion.3.near.refs_1_), channel_id=1, source_target_pairs={{0,2},{1,3},{2,0},{3,1},{4,6},{5,7},{6,4},{7,5},{8,10},{9,11},{10,... | collective-permute-start | bytes 1769480 | tf_op jit(solution)/shard_map/ppermute | solution.py:500
  54.3 18.7 %collective-permute-start.11 = (bf16[384,768]{1,0:T(8,128)(2,1)}, bf16[384,768]{1,0:T(8,128)(2,1)S(1)}, u32[]{:S(2)}, u32[]{:S(2)}) collective-permute-start(bf16[384,768]{1,0:T(8,128)(2,1)} %bitcast.13.refs_8_), channel_id=1, source_target_pairs={{0,16},{16,0},{1,17},{17,1},{2,18},{18,2},{3,19},{19,3},{4,20},{20... | collective-permute-start | bytes 1769480 | tf_op jit(solution)/shard_map/ppermute | solution.py:496
  56.5 16.5 %collective-permute-start.13 = (bf16[256,768]{1,0:T(8,128)(2,1)S(1)}, bf16[256,768]{1,0:T(8,128)(2,1)S(1)}, u32[]{:S(2)}, u32[]{:S(2)}) collective-permute-start(bf16[256,768]{1,0:T(8,128)(2,1)S(1)} %pad_maximum_fusion.17), channel_id=1, source_target_pairs={{0,4},{4,0},{8,12},{12,8},{1,5},{5,1},{9,13},{13,9},{2,6},{6,2},{1... | collective-permute-start | bytes 1179656 | tf_op jit(solution)/shard_map/ppermute | solution.py:548
  58.4 16.4 %collective-permute-start.10 = (bf16[192,768]{1,0:T(8,128)(2,1)S(1)}, bf16[192,768]{1,0:T(8,128)(2,1)S(1)}, u32[]{:S(2)}, u32[]{:S(2)}) collective-permute-start(bf16[192,768]{1,0:T(8,128)(2,1)S(1)} %slice.331), channel_id=1, source_target_pairs={{0,2},{1,3},{2,0},{3,1},{4,6},{5,7},{6,4},{7,5},{8,10},{9,11},{10,... | collective-permute-start | bytes 884744 | tf_op jit(solution)/shard_map/ppermute | solution.py:500
  75.6 19.2 %collective-permute-start.19 = (bf16[384,768]{1,0:T(8,128)(2,1)S(1)}, bf16[384,768]{1,0:T(8,128)(2,1)S(1)}, u32[]{:S(2)}, u32[]{:S(2)}) collective-permute-start(bf16[384,768]{1,0:T(8,128)(2,1)S(1)} %constant_dynamic-update-slice_fusion.5.near.refs_1_), channel_id=1, source_target_pairs={{0,2},{1,3},{2,0},{3,1},{4,6},{5,7},{6,4},{7,5},{8,10},{9,11},{10,... | collective-permute-start | bytes 1769480 | tf_op jit(solution)/shard_map/ppermute | solution.py:500
  78.1 16.7 %collective-permute-start.17 = (bf16[400,768]{1,0:T(8,128)(2,1)}, bf16[400,768]{1,0:T(8,128)(2,1)S(1)}, u32[]{:S(2)}, u32[]{:S(2)}) collective-permute-start(bf16[400,768]{1,0:T(8,128)(2,1)} %pad_maximum_fusion.13.refs_0_), channel_id=1, source_target_pairs={{0,1},{1,0},{2,3},{3,2},{4,5},{5,4},{6,7},{7,6},{8,9},{9,8},{10,11... | collective-permute-start | bytes 1843208 | tf_op jit(solution)/shard_map/ppermute | solution.py:504
  78.2 16.7 %collective-permute-start.18 = (bf16[400,768]{1,0:T(8,128)(2,1)}, bf16[400,768]{1,0:T(8,128)(2,1)}, u32[]{:S(2)}, u32[]{:S(2)}) collective-permute-start(bf16[400,768]{1,0:T(8,128)(2,1)} %collective-permute-done.2.refs_2_), channel_id=1, source_target_pairs={{0,16},{16,0},{1,17},{17,1},{2,18},{18,2},{3,19},{19,3},{4,20},{20... | collective-permute-start | bytes 1843208 | tf_op jit(solution)/shard_map/ppermute | solution.py:496
  80.1 17.2 %collective-permute-start.16 = (bf16[192,768]{1,0:T(8,128)(2,1)S(1)}, bf16[192,768]{1,0:T(8,128)(2,1)S(1)}, u32[]{:S(2)}, u32[]{:S(2)}) collective-permute-start(bf16[192,768]{1,0:T(8,128)(2,1)S(1)} %slice.332), channel_id=1, source_target_pairs={{0,2},{1,3},{2,0},{3,1},{4,6},{5,7},{6,4},{7,5},{8,10},{9,11},{10,... | collective-permute-start | bytes 884744 | tf_op jit(solution)/shard_map/ppermute | solution.py:500
  98.0 18.4 %collective-permute-start.22 = (bf16[128,768]{1,0:T(8,128)(2,1)S(1)}, bf16[128,768]{1,0:T(8,128)(2,1)S(1)}, u32[]{:S(2)}, u32[]{:S(2)}) collective-permute-start(bf16[128,768]{1,0:T(8,128)(2,1)S(1)} %add_convert_fusion.22), channel_id=1, source_target_pairs={{0,2},{1,3},{2,0},{3,1},{4,6},{5,7},{6,4},{7,5},{8,10},{9,11},{10,... | collective-permute-start | bytes 589832 | tf_op jit(solution)/shard_map/ppermute | solution.py:500
  99.6 16.8 %collective-permute-start.21 = (bf16[384,768]{1,0:T(8,128)(2,1)S(1)}, bf16[384,768]{1,0:T(8,128)(2,1)}, u32[]{:S(2)}, u32[]{:S(2)}) collective-permute-start(bf16[384,768]{1,0:T(8,128)(2,1)S(1)} %constant_dynamic-update-slice_fusion.7.refs_10_), channel_id=1, source_target_pairs={{0,16},{16,0},{1,17},{17,1},{2,18},{18,2},{3,19},{19,3},{4,20},{20... | collective-permute-start | bytes 1769480 | tf_op jit(solution)/shard_map/ppermute | solution.py:496
  100.7 15.7 %collective-permute-start.20 = (bf16[384,768]{1,0:T(8,128)(2,1)}, bf16[384,768]{1,0:T(8,128)(2,1)S(1)}, u32[]{:S(2)}, u32[]{:S(2)}) collective-permute-start(bf16[384,768]{1,0:T(8,128)(2,1)} %bitcast.13.refs_8_), channel_id=1, source_target_pairs={{0,1},{1,0},{2,3},{3,2},{4,5},{5,4},{6,7},{7,6},{8,9},{9,8},{10,11... | collective-permute-start | bytes 1769480 | tf_op jit(solution)/shard_map/ppermute | solution.py:504
  100.9 15.5 %collective-permute-start.25 = (bf16[128,768]{1,0:T(8,128)(2,1)S(1)}, bf16[128,768]{1,0:T(8,128)(2,1)S(1)}, u32[]{:S(2)}, u32[]{:S(2)}) collective-permute-start(bf16[128,768]{1,0:T(8,128)(2,1)S(1)} %add_convert_fusion.21), channel_id=1, source_target_pairs={{0,2},{1,3},{2,0},{3,1},{4,6},{5,7},{6,4},{7,5},{8,10},{9,11},{10,... | collective-permute-start | bytes 589832 | tf_op jit(solution)/shard_map/ppermute | solution.py:500
  117.1 10.9 %collective-permute-start.26 = (bf16[400,768]{1,0:T(8,128)(2,1)}, bf16[400,768]{1,0:T(8,128)(2,1)}, u32[]{:S(2)}, u32[]{:S(2)}) collective-permute-start(bf16[400,768]{1,0:T(8,128)(2,1)} %collective-permute-done.5.refs_1_), channel_id=1, source_target_pairs={{0,1},{1,0},{2,3},{3,2},{4,5},{5,4},{6,7},{7,6},{8,9},{9,8},{10,11... | collective-permute-start | bytes 1843208 | tf_op jit(solution)/shard_map/ppermute | solution.py:504
  117.5 10.5 %collective-permute-start.27 = (bf16[400,768]{1,0:T(8,128)(2,1)}, bf16[400,768]{1,0:T(8,128)(2,1)}, u32[]{:S(2)}, u32[]{:S(2)}) collective-permute-start(bf16[400,768]{1,0:T(8,128)(2,1)} %collective-permute-done.2.refs_2_), channel_id=1, source_target_pairs={{0,1},{1,0},{2,3},{3,2},{4,5},{5,4},{6,7},{7,6},{8,9},{9,8},{10,11... | collective-permute-start | bytes 1843208 | tf_op jit(solution)/shard_map/ppermute | solution.py:504
  120.3 7.7 %collective-permute-start.28 = (bf16[400,768]{1,0:T(8,128)(2,1)}, bf16[400,768]{1,0:T(8,128)(2,1)}, u32[]{:S(2)}, u32[]{:S(2)}) collective-permute-start(bf16[400,768]{1,0:T(8,128)(2,1)} %collective-permute-done.18.refs_3_), channel_id=1, source_target_pairs={{0,1},{1,0},{2,3},{3,2},{4,5},{5,4},{6,7},{7,6},{8,9},{9,8},{10,11... | collective-permute-start | bytes 1843208 | tf_op jit(solution)/shard_map/ppermute | solution.py:504
  121.0 7.0 %collective-permute-start.33 = (bf16[128,768]{1,0:T(8,128)(2,1)S(1)}, bf16[128,768]{1,0:T(8,128)(2,1)S(1)}, u32[]{:S(2)}, u32[]{:S(2)}) collective-permute-start(bf16[128,768]{1,0:T(8,128)(2,1)S(1)} %add_convert_fusion.20), channel_id=1, source_target_pairs={{0,2},{1,3},{2,0},{3,1},{4,6},{5,7},{6,4},{7,5},{8,10},{9,11},{10,... | collective-permute-start | bytes 589832 | tf_op jit(solution)/shard_map/ppermute | solution.py:500
  149.2 9.0 %collective-permute-start.34 = (bf16[128,768]{1,0:T(8,128)(2,1)S(1)}, bf16[128,768]{1,0:T(8,128)(2,1)S(1)}, u32[]{:S(2)}, u32[]{:S(2)}) collective-permute-start(bf16[128,768]{1,0:T(8,128)(2,1)S(1)} %get-tuple-element.375.g_own), channel_id=1, source_target_pairs={{0,2},{1,3},{2,0},{3,1},{4,6},{5,7},{6,4},{7,5},{8,10},{9,11},{10,... | collective-permute-start | bytes 589832 | tf_op jit(solution)/shard_map/ppermute | solution.py:500
  158.2 9.0 %collective-permute-start.37 = (bf16[2,2,448,768]{3,2,1,0:T(8,128)(2,1)}, bf16[2,2,448,768]{3,2,1,0:T(8,128)(2,1)S(1)}, u32[]{:S(2)}, u32[]{:S(2)}) collective-permute-start(bf16[2,2,448,768]{3,2,1,0:T(8,128)(2,1)} %get-tuple-element.361), channel_id=1, source_target_pairs={{0,1},{1,0},{2,3},{3,2},{4,5},{5,4},{6,7},{7,6},{8,9},{9,8},{10,11... | collective-permute-start | bytes 8257544 | tf_op jit(solution)/shard_map/ppermute | solution.py:504
  158.2 9.0 %collective-permute-start.38 = (bf16[2,2,384,768]{3,2,1,0:T(8,128)(2,1)}, bf16[2,2,384,768]{3,2,1,0:T(8,128)(2,1)}, u32[]{:S(2)}, u32[]{:S(2)}) collective-permute-start(bf16[2,2,384,768]{3,2,1,0:T(8,128)(2,1)} %get-tuple-element.362), channel_id=1, source_target_pairs={{0,1},{1,0},{2,3},{3,2},{4,5},{5,4},{6,7},{7,6},{8,9},{9,8},{10,11... | collective-permute-start | bytes 7077896 | tf_op jit(solution)/shard_map/ppermute | solution.py:504
  158.7 8.5 %collective-permute-start.36 = (bf16[256,768]{1,0:T(8,128)(2,1)S(1)}, bf16[256,768]{1,0:T(8,128)(2,1)S(1)}, u32[]{:S(2)}, u32[]{:S(2)}) collective-permute-start(bf16[256,768]{1,0:T(8,128)(2,1)S(1)} %pad_maximum_fusion.18), channel_id=1, source_target_pairs={{0,1},{1,0},{2,3},{3,2},{4,5},{5,4},{6,7},{7,6},{8,9},{9,8},{10,11... | collective-permute-start | bytes 1179656 | tf_op jit(solution)/shard_map/ppermute | solution.py:504
  158.8 13.4 %collective-permute-start.35 = (bf16[256,768]{1,0:T(8,128)(2,1)S(1)}, bf16[256,768]{1,0:T(8,128)(2,1)S(1)}, u32[]{:S(2)}, u32[]{:S(2)}) collective-permute-start(bf16[256,768]{1,0:T(8,128)(2,1)S(1)} %copy-done.48), channel_id=1, source_target_pairs={{0,2},{1,3},{2,0},{3,1},{4,6},{5,7},{6,4},{7,5},{8,10},{9,11},{10,... | collective-permute-start | bytes 1179656 | tf_op jit(solution)/shard_map/ppermute | solution.py:500
  172.3 18.1 %collective-permute-start.41 = (bf16[512,768]{1,0:T(8,128)(2,1)S(1)}, bf16[512,768]{1,0:T(8,128)(2,1)}, u32[]{:S(2)}, u32[]{:S(2)}) collective-permute-start(bf16[512,768]{1,0:T(8,128)(2,1)S(1)} %pad_maximum_fusion.9), channel_id=1, source_target_pairs={{0,1},{1,0},{2,3},{3,2},{4,5},{5,4},{6,7},{7,6},{8,9},{9,8},{10,11... | collective-permute-start | bytes 2359304 | tf_op jit(solution)/shard_map/ppermute | solution.py:504
  172.6 17.8 %collective-permute-start.39 = (bf16[448,768]{1,0:T(8,128)(2,1)}, bf16[448,768]{1,0:T(8,128)(2,1)S(1)}, u32[]{:S(2)}, u32[]{:S(2)}) collective-permute-start(bf16[448,768]{1,0:T(8,128)(2,1)} %get-tuple-element.372), channel_id=1, source_target_pairs={{0,2},{1,3},{2,0},{3,1},{4,6},{5,7},{6,4},{7,5},{8,10},{9,11},{10,... | collective-permute-start | bytes 2064392 | tf_op jit(solution)/shard_map/ppermute | solution.py:500
  173.5 16.0 %collective-permute-start.40 = (bf16[384,768]{1,0:T(8,128)(2,1)S(1)}, bf16[384,768]{1,0:T(8,128)(2,1)}, u32[]{:S(2)}, u32[]{:S(2)}) collective-permute-start(bf16[384,768]{1,0:T(8,128)(2,1)S(1)} %get-tuple-element.373), channel_id=1, source_target_pairs={{0,16},{16,0},{1,17},{17,1},{2,18},{18,2},{3,19},{19,3},{4,20},{20... | collective-permute-start | bytes 1769480 | tf_op jit(solution)/shard_map/ppermute | solution.py:496
  190.4 21.5 %collective-permute-start.44 = (bf16[1024,768]{1,0:T(8,128)(2,1)}, bf16[1024,768]{1,0:T(8,128)(2,1)}, u32[]{:S(2)}, u32[]{:S(2)}) collective-permute-start(bf16[1024,768]{1,0:T(8,128)(2,1)} %get-tuple-element.394), channel_id=1, source_target_pairs={{0,1},{1,0},{2,3},{3,2},{4,5},{5,4},{6,7},{7,6},{8,9},{9,8},{10,11... | collective-permute-start | bytes 4718600 | tf_op jit(solution)/shard_map/ppermute | solution.py:504
  194.1 17.8 %collective-permute-start.42 = (bf16[448,768]{1,0:T(8,128)(2,1)S(1)}, bf16[448,768]{1,0:T(8,128)(2,1)S(1)}, u32[]{:S(2)}, u32[]{:S(2)}) collective-permute-start(bf16[448,768]{1,0:T(8,128)(2,1)S(1)} %copy-done.40), channel_id=1, source_target_pairs={{0,2},{1,3},{2,0},{3,1},{4,6},{5,7},{6,4},{7,5},{8,10},{9,11},{10,... | collective-permute-start | bytes 2064392 | tf_op jit(solution)/shard_map/ppermute | solution.py:500
  195.0 16.6 %collective-permute-start.43 = (bf16[384,768]{1,0:T(8,128)(2,1)S(1)}, bf16[384,768]{1,0:T(8,128)(2,1)S(1)}, u32[]{:S(2)}, u32[]{:S(2)}) collective-permute-start(bf16[384,768]{1,0:T(8,128)(2,1)S(1)} %get-tuple-element.393), channel_id=1, source_target_pairs={{0,16},{16,0},{1,17},{17,1},{2,18},{18,2},{3,19},{19,3},{4,20},{20... | collective-permute-start | bytes 1769480 | tf_op jit(solution)/shard_map/ppermute | solution.py:496
  213.5 8.8 %collective-permute-start.47 = (bf16[1024,768]{1,0:T(8,128)(2,1)}, bf16[1024,768]{1,0:T(8,128)(2,1)}, u32[]{:S(2)}, u32[]{:S(2)}) collective-permute-start(bf16[1024,768]{1,0:T(8,128)(2,1)} %get-tuple-element.427), channel_id=1, source_target_pairs={{0,1},{1,0},{2,3},{3,2},{4,5},{5,4},{6,7},{7,6},{8,9},{9,8},{10,11... | collective-permute-start | bytes 4718600 | tf_op jit(solution)/shard_map/ppermute | solution.py:504
  213.6 18.2 %collective-permute-start.45 = (bf16[448,768]{1,0:T(8,128)(2,1)}, bf16[448,768]{1,0:T(8,128)(2,1)}, u32[]{:S(2)}, u32[]{:S(2)}) collective-permute-start(bf16[448,768]{1,0:T(8,128)(2,1)} %fusion.3), channel_id=1, source_target_pairs={{0,16},{16,0},{1,17},{17,1},{2,18},{18,2},{3,19},{19,3},{4,20},{20... | collective-permute-start | bytes 2064392 | tf_op jit(solution)/shard_map/ppermute | solution.py:496
  214.7 16.5 %collective-permute-start.46 = (bf16[384,768]{1,0:T(8,128)(2,1)}, bf16[384,768]{1,0:T(8,128)(2,1)}, u32[]{:S(2)}, u32[]{:S(2)}) collective-permute-start(bf16[384,768]{1,0:T(8,128)(2,1)} %fusion.7), channel_id=1, source_target_pairs={{0,2},{1,3},{2,0},{3,1},{4,6},{5,7},{6,4},{7,5},{8,10},{9,11},{10,... | collective-permute-start | bytes 1769480 | tf_op jit(solution)/shard_map/ppermute | solution.py:500
  215.7 38.9 %collective-permute-start.49 = (bf16[512,768]{1,0:T(8,128)(2,1)S(1)}, bf16[512,768]{1,0:T(8,128)(2,1)S(1)}, u32[]{:S(2)}, u32[]{:S(2)}) collective-permute-start(bf16[512,768]{1,0:T(8,128)(2,1)S(1)} %add_convert_fusion.2), channel_id=1, source_target_pairs={{0,2},{1,3},{2,0},{3,1},{4,6},{5,7},{6,4},{7,5},{8,10},{9,11},{10,... | collective-permute-start | bytes 2359304 | tf_op jit(solution)/shard_map/ppermute | solution.py:500
  237.3 17.3 %collective-permute-start.48 = (bf16[416,768]{1,0:T(8,128)(2,1)S(1)}, bf16[416,768]{1,0:T(8,128)(2,1)S(1)}, u32[]{:S(2)}, u32[]{:S(2)}) collective-permute-start(bf16[416,768]{1,0:T(8,128)(2,1)S(1)} %get-tuple-element.439), channel_id=1, source_target_pairs={{0,4},{4,0},{8,12},{12,8},{1,5},{5,1},{9,13},{13,9},{2,6},{6,2},{1... | collective-permute-start | bytes 1916936 | tf_op jit(solution)/shard_map/ppermute | solution.py:548
  255.7 13.1 %collective-permute-start.50 = (bf16[1024,768]{1,0:T(8,128)(2,1)}, bf16[1024,768]{1,0:T(8,128)(2,1)S(1)}, u32[]{:S(2)}, u32[]{:S(2)}) collective-permute-start(bf16[1024,768]{1,0:T(8,128)(2,1)} %get-tuple-element.454), channel_id=1, source_target_pairs={{0,1},{1,0},{2,3},{3,2},{4,5},{5,4},{6,7},{7,6},{8,9},{9,8},{10,11... | collective-permute-start | bytes 4718600 | tf_op jit(solution)/shard_map/ppermute | solution.py:504
  255.8 20.2 %collective-permute-start.52 = (bf16[512,768]{1,0:T(8,128)(2,1)}, bf16[512,768]{1,0:T(8,128)(2,1)S(1)}, u32[]{:S(2)}, u32[]{:S(2)}) collective-permute-start(bf16[512,768]{1,0:T(8,128)(2,1)} %add_convert_fusion.1), channel_id=1, source_target_pairs={{0,2},{1,3},{2,0},{3,1},{4,6},{5,7},{6,4},{7,5},{8,10},{9,11},{10,... | collective-permute-start | bytes 2359304 | tf_op jit(solution)/shard_map/ppermute | solution.py:500
  259.6 18.2 %collective-permute-start.56 = (bf16[256,768]{1,0:T(8,128)(2,1)S(1)}, bf16[256,768]{1,0:T(8,128)(2,1)S(1)}, u32[]{:S(2)}, u32[]{:S(2)}) collective-permute-start(bf16[256,768]{1,0:T(8,128)(2,1)S(1)} %add_convert_fusion.11), channel_id=1, source_target_pairs={{0,4},{4,0},{8,12},{12,8},{1,5},{5,1},{9,13},{13,9},{2,6},{6,2},{1... | collective-permute-start | bytes 1179656 | tf_op jit(solution)/shard_map/ppermute | solution.py:548
  260.0 22.4 %collective-permute-start.55 = (bf16[208,768]{1,0:T(8,128)(2,1)S(1)}, bf16[208,768]{1,0:T(8,128)(2,1)S(1)}, u32[]{:S(2)}, u32[]{:S(2)}) collective-permute-start(bf16[208,768]{1,0:T(8,128)(2,1)S(1)} %constant_dynamic-slice_fusion.2), channel_id=1, source_target_pairs={{0,8},{4,12},{8,0},{12,4},{1,9},{5,13},{9,1},{13,5},{2,10},{6,14},... | collective-permute-start | bytes 958472 | tf_op jit(solution)/shard_map/ppermute | solution.py:548
  277.3 15.3 %collective-permute-start.53 = (bf16[256,768]{1,0:T(8,128)(2,1)S(1)}, bf16[256,768]{1,0:T(8,128)(2,1)S(1)}, u32[]{:S(2)}, u32[]{:S(2)}) collective-permute-start(bf16[256,768]{1,0:T(8,128)(2,1)S(1)} %add_convert_fusion.10), channel_id=1, source_target_pairs={{0,4},{4,0},{8,12},{12,8},{1,5},{5,1},{9,13},{13,9},{2,6},{6,2},{1... | collective-permute-start | bytes 1179656 | tf_op jit(solution)/shard_map/ppermute | solution.py:548
  277.8 12.1 %collective-permute-start.54 = (bf16[256,768]{1,0:T(8,128)(2,1)S(1)}, bf16[256,768]{1,0:T(8,128)(2,1)S(1)}, u32[]{:S(2)}, u32[]{:S(2)}) collective-permute-start(bf16[256,768]{1,0:T(8,128)(2,1)S(1)} %get-tuple-element.576), channel_id=1, source_target_pairs={{0,2},{1,3},{2,0},{3,1},{4,6},{5,7},{6,4},{7,5},{8,10},{9,11},{10,... | collective-permute-start | bytes 1179656 | tf_op jit(solution)/shard_map/ppermute | solution.py:500
  279.9 37.7 %collective-permute-start.59 = (bf16[128,768]{1,0:T(8,128)(2,1)S(1)}, bf16[128,768]{1,0:T(8,128)(2,1)S(1)}, u32[]{:S(2)}, u32[]{:S(2)}) collective-permute-start(bf16[128,768]{1,0:T(8,128)(2,1)S(1)} %add_convert_fusion.19), channel_id=1, source_target_pairs={{0,8},{4,12},{8,0},{12,4},{1,9},{5,13},{9,1},{13,5},{2,10},{6,14},... | collective-permute-start | bytes 589832 | tf_op jit(solution)/shard_map/ppermute | solution.py:548
  282.4 15.2 %collective-permute-start.51 = (bf16[832,384]{1,0:T(8,128)(2,1)S(1)}, bf16[832,384]{1,0:T(8,128)(2,1)S(1)}, u32[]{:S(2)}, u32[]{:S(2)}) collective-permute-start(bf16[832,384]{1,0:T(8,128)(2,1)S(1)} %copy-done.64), channel_id=1, source_target_pairs={{0,16},{16,0},{1,17},{17,1},{2,18},{18,2},{3,19},{19,3},{4,20},{20... | collective-permute-start | bytes 1916936 | tf_op jit(solution)/shard_map/ppermute | solution.py:496
  283.4 14.9 %collective-permute-start.61 = (bf16[256,768]{1,0:T(8,128)(2,1)S(1)}, bf16[256,768]{1,0:T(8,128)(2,1)S(1)}, u32[]{:S(2)}, u32[]{:S(2)}) collective-permute-start(bf16[256,768]{1,0:T(8,128)(2,1)S(1)} %get-tuple-element.575), channel_id=1, source_target_pairs={{0,2},{1,3},{2,0},{3,1},{4,6},{5,7},{6,4},{7,5},{8,10},{9,11},{10,... | collective-permute-start | bytes 1179656 | tf_op jit(solution)/shard_map/ppermute | solution.py:500
  289.8 27.7 %collective-permute-start.58 = (bf16[208,768]{1,0:T(8,128)(2,1)S(1)}, bf16[208,768]{1,0:T(8,128)(2,1)S(1)}, u32[]{:S(2)}, u32[]{:S(2)}) collective-permute-start(bf16[208,768]{1,0:T(8,128)(2,1)S(1)} %add_convert_fusion.13), channel_id=1, source_target_pairs={{0,8},{4,12},{8,0},{12,4},{1,9},{5,13},{9,1},{13,5},{2,10},{6,14},... | collective-permute-start | bytes 958472 | tf_op jit(solution)/shard_map/ppermute | solution.py:548
  292.5 22.3 %collective-permute-start.60 = (bf16[256,768]{1,0:T(8,128)(2,1)S(1)}, bf16[256,768]{1,0:T(8,128)(2,1)S(1)}, u32[]{:S(2)}, u32[]{:S(2)}) collective-permute-start(bf16[256,768]{1,0:T(8,128)(2,1)S(1)} %add_convert_fusion.9), channel_id=1, source_target_pairs={{0,4},{4,0},{8,12},{12,8},{1,5},{5,1},{9,13},{13,9},{2,6},{6,2},{1... | collective-permute-start | bytes 1179656 | tf_op jit(solution)/shard_map/ppermute | solution.py:548
  297.6 25.9 %collective-permute-start.63 = (bf16[128,768]{1,0:T(8,128)(2,1)S(1)}, bf16[128,768]{1,0:T(8,128)(2,1)S(1)}, u32[]{:S(2)}, u32[]{:S(2)}) collective-permute-start(bf16[128,768]{1,0:T(8,128)(2,1)S(1)} %add_convert_fusion.18), channel_id=1, source_target_pairs={{0,8},{4,12},{8,0},{12,4},{1,9},{5,13},{9,1},{13,5},{2,10},{6,14},... | collective-permute-start | bytes 589832 | tf_op jit(solution)/shard_map/ppermute | solution.py:548
  298.3 25.1 %collective-permute-start.57 = (bf16[416,384]{1,0:T(8,128)(2,1)S(1)}, bf16[416,384]{1,0:T(8,128)(2,1)S(1)}, u32[]{:S(2)}, u32[]{:S(2)}) collective-permute-start(bf16[416,384]{1,0:T(8,128)(2,1)S(1)} %constant_dynamic-slice_fusion.1), channel_id=1, source_target_pairs={{0,4},{4,0},{8,12},{12,8},{1,5},{5,1},{9,13},{13,9},{2,6},{6,2},{1... | collective-permute-start | bytes 958472 | tf_op jit(solution)/shard_map/ppermute | solution.py:548
  314.9 10.9 %collective-permute-start.65 = (bf16[128,768]{1,0:T(8,128)(2,1)S(1)}, bf16[128,768]{1,0:T(8,128)(2,1)S(1)}, u32[]{:S(2)}, u32[]{:S(2)}) collective-permute-start(bf16[128,768]{1,0:T(8,128)(2,1)S(1)} %add_convert_fusion.17), channel_id=1, source_target_pairs={{0,8},{4,12},{8,0},{12,4},{1,9},{5,13},{9,1},{13,5},{2,10},{6,14},... | collective-permute-start | bytes 589832 | tf_op jit(solution)/shard_map/ppermute | solution.py:548
  324.7 8.3 %collective-permute-start.64 = (bf16[2,128,768]{2,1,0:T(8,128)(2,1)S(1)}, bf16[2,128,768]{2,1,0:T(8,128)(2,1)S(1)}, u32[]{:S(2)}, u32[]{:S(2)}) collective-permute-start(bf16[2,128,768]{2,1,0:T(8,128)(2,1)S(1)} %bitcast.208), channel_id=1, source_target_pairs={{0,2},{1,3},{2,0},{3,1},{4,6},{5,7},{6,4},{7,5},{8,10},{9,11},{10,... | collective-permute-start | bytes 1179656 | tf_op jit(solution)/shard_map/ppermute | solution.py:500
  325.9 6.9 %collective-permute-start.62 = (bf16[208,384]{1,0:T(8,128)(2,1)S(1)}, bf16[208,384]{1,0:T(8,128)(2,1)S(1)}, u32[]{:S(2)}, u32[]{:S(2)}) collective-permute-start(bf16[208,384]{1,0:T(8,128)(2,1)S(1)} %constant_dynamic-slice_fusion), channel_id=1, source_target_pairs={{0,8},{4,12},{8,0},{12,4},{1,9},{5,13},{9,1},{13,5},{2,10},{6,14},... | collective-permute-start | bytes 479240 | tf_op jit(solution)/shard_map/ppermute | solution.py:548
  333.0 4.6 %collective-permute-start.68 = (bf16[2,2,128,768]{3,2,1,0:T(8,128)(2,1)S(1)}, bf16[2,2,128,768]{3,2,1,0:T(8,128)(2,1)}, u32[]{:S(2)}, u32[]{:S(2)}) collective-permute-start(bf16[2,2,128,768]{3,2,1,0:T(8,128)(2,1)S(1)} %pad_maximum_fusion.10), channel_id=1, source_target_pairs={{0,1},{1,0},{2,3},{3,2},{4,5},{5,4},{6,7},{7,6},{8,9},{9,8},{10,11... | collective-permute-start | bytes 2359304 | tf_op jit(solution)/shard_map/ppermute | solution.py:504
  333.1 22.8 %collective-permute-start.72 = (bf16[416,768]{1,0:T(8,128)(2,1)S(1)}, bf16[416,768]{1,0:T(8,128)(2,1)S(1)}, u32[]{:S(2)}, u32[]{:S(2)}) collective-permute-start(bf16[416,768]{1,0:T(8,128)(2,1)S(1)} %pad_maximum_fusion.12), channel_id=1, source_target_pairs={{0,4},{4,0},{8,12},{12,8},{1,5},{5,1},{9,13},{13,9},{2,6},{6,2},{1... | collective-permute-start | bytes 1916936 | tf_op jit(solution)/shard_map/ppermute | solution.py:548
  333.2 19.9 %collective-permute-start.69 = (bf16[3,128,768]{2,1,0:T(8,128)(2,1)S(1)}, bf16[3,128,768]{2,1,0:T(8,128)(2,1)S(1)}, u32[]{:S(2)}, u32[]{:S(2)}) collective-permute-start(bf16[3,128,768]{2,1,0:T(8,128)(2,1)S(1)} %bitcast.213), channel_id=1, source_target_pairs={{0,2},{1,3},{2,0},{3,1},{4,6},{5,7},{6,4},{7,5},{8,10},{9,11},{10,... | collective-permute-start | bytes 1769480 | tf_op jit(solution)/shard_map/ppermute | solution.py:500
  334.5 18.7 %collective-permute-start.66 = (bf16[1,128,768]{2,1,0:T(8,128)(2,1)S(1)}, bf16[1,128,768]{2,1,0:T(8,128)(2,1)S(1)}, u32[]{:S(2)}, u32[]{:S(2)}) collective-permute-start(bf16[1,128,768]{2,1,0:T(8,128)(2,1)S(1)} %bitcast.217), channel_id=1, source_target_pairs={{0,2},{1,3},{2,0},{3,1},{4,6},{5,7},{6,4},{7,5},{8,10},{9,11},{10,... | collective-permute-start | bytes 589832 | tf_op jit(solution)/shard_map/ppermute | solution.py:500
  335.4 17.7 %collective-permute-start.67 = (bf16[208,384]{1,0:T(8,128)(2,1)S(1)}, bf16[208,384]{1,0:T(8,128)(2,1)S(1)}, u32[]{:S(2)}, u32[]{:S(2)}) collective-permute-start(bf16[208,384]{1,0:T(8,128)(2,1)S(1)} %add_convert_fusion.23), channel_id=1, source_target_pairs={{0,8},{4,12},{8,0},{12,4},{1,9},{5,13},{9,1},{13,5},{2,10},{6,14},... | collective-permute-start | bytes 479240 | tf_op jit(solution)/shard_map/ppermute | solution.py:548
  354.0 9.5 %collective-permute-start.70 = (bf16[416,384]{1,0:T(8,128)(2,1)S(1)}, bf16[416,384]{1,0:T(8,128)(2,1)S(1)}, u32[]{:S(2)}, u32[]{:S(2)}) collective-permute-start(bf16[416,384]{1,0:T(8,128)(2,1)S(1)} %pad_maximum_fusion.21), channel_id=1, source_target_pairs={{0,4},{4,0},{8,12},{12,8},{1,5},{5,1},{9,13},{13,9},{2,6},{6,2},{1... | collective-permute-start | bytes 958472 | tf_op jit(solution)/shard_map/ppermute | solution.py:548
  (86 other events, 599.5 us)

commit v6 on v5

--- a/solution.py
+++ b/solution.py
@@ -821,12 +821,16 @@
     feed_got, last = stage(feed_got, last)
     feed = join(feed, feed_got, masks[0])
     outputs = whole(result.reshape(result_x.shape), result_x)
-    attn_got, outputs, last, feed = stage(attn_got, outputs, last, feed)
+    input_grad = jnp.concatenate([early, last], axis=0)
+    feed = feed.astype(F32)
+    vector_sums = feed[depth : depth + 7]
+    up_grad = feed[:depth]
+    down_grad = feed[depth + SUMS :].T
+    attn_got, outputs, input_grad, vector_sums, up_grad, down_grad = stage(
+        attn_got, outputs, input_grad, vector_sums, up_grad, down_grad)
     attn = join(attn, attn_got, masks[0])
-    input_grad = jnp.concatenate([early, last], axis=0)
-
-    feed, attn = feed.astype(F32), attn.astype(F32)
-    vector_sums = feed[depth : depth + 7]
+
+    attn = attn.astype(F32)
     bias_sums = attn[4 * cols :].reshape(-1)[: 2 * cols]
     matrices = attn[: 4 * cols].reshape(4, cols, depth)
     return (
@@ -841,9 +845,9 @@
         vector_sums[0],
         vector_sums[1],
         vector_sums[2],
-        feed[:depth],
+        up_grad,
         vector_sums[6],
-        feed[depth + SUMS :].T,
+        down_grad,
         vector_sums[3],
         vector_sums[4],
         vector_sums[5],

time: 375 us -> 375 us (level)
  other arithmetic: 39.1 us -> 43.9 us
    unnamed x163 -> x149, local copies, waits for them, and re-layouts: 8.84 us -> 12 us
  transfers between devices with their start and end apart: 74 -> 74, of which waited for: 28 -> 25; matrix products, arithmetic and copies ran while one was open for 11% -> 12% of each run, Pallas kernels for 32% -> 32%
where the time goes in v6:
time: 375 us; the launch traced here: 371 us
  Pallas kernels  139 us (37%)
  waiting for transfers between devices  94.2 us (25%)
  starting transfers between devices  71.1 us (19%)
  other arithmetic  43.9 us (12%)
  local copies, waits for them, and re-layouts  20.6 us (5%)
    ppermute x20, waiting for transfers between devices, along(): lax.ppermute(value, 'context', [(i, i ^ mask) for i in range(contexts)])  50.7 us
    pallas_call x3, Pallas kernels, attention_backward(): pl.pallas_call(functools.partial(backward_body, heads, nears, index), out...  45.6 us
    pallas_call x3, Pallas kernels, attention_forward(): pl.pallas_call(functools.partial(forward_body, heads, index), out_shape=(...  41.4 us
    ppermute x21, waiting for transfers between devices, across(): return lax.ppermute(value, 'tensor', [(i, i ^ 2) for i in range(4)])  36.1 us
    ppermute x20, starting transfers between devices, along(): lax.ppermute(value, 'context', [(i, i ^ mask) for i in range(contexts)])  34.6 us
    convert_element_type x26, other arithmetic, low_sum(): return added(*values).astype(BF16)  28 us
    ppermute x21, starting transfers between devices, across(): return lax.ppermute(value, 'tensor', [(i, i ^ 2) for i in range(4)])  22.7 us
    pallas_call x1, Pallas kernels, feed_forward(): pl.pallas_call(functools.partial(feed_body, blocks, pieces, seqs), out_sh...  20.5 us
  transfers between devices with their start and end apart: 74, of which 25 were waited for; matrix products, arithmetic and copies ran while one was open for 12% of the time, Pallas kernels for 32%

profile of v6, /device:TPU:0, one launch (start us, length us, event | category | flops | bytes accessed | tf_op | source)
XLA Modules:
  0.0 371.0 jit_solution(3135120393500383401)
XLA Ops:
  0.7 1.8 fusion.20
  2.6 4.1 %collective-permute-start = (bf16[128,768]{1,0:T(8,128)(2,1)S(1)}, bf16[128,768]{1,0:T(8,128)(2,1)S(1)}, u32[]{:S(2)}, u32[]{:S(2)}) collective-permute-start(bf16[128,768]{1,0:T(8,128)(2,1)S(1)} %dynamic-slice_bitcast_fusion.2.refs_16_), channel_id=1, source_target_pairs={{0,8},{4,12},{8,0},{12,4},{1,9},{5,13},{9,1},{13,5},{2,10},{6,14},... | collective-permute-start | bytes 589832 | tf_op jit(solution)/shard_map/ppermute | solution.py:548
  9.4 2.0 pad_maximum_fusion.12.refs_0_
  11.3 4.5 %collective-permute-done = bf16[128,768]{1,0:T(8,128)(2,1)S(1)} collective-permute-done((bf16[128,768]{1,0:T(8,128)(2,1)S(1)}, bf16[128,768]{1,0:T(8,128)(2,1)S(1)}, u32[]{:S(2)}, u32[]{:S(2)}) %collective-permute-start) | collective-permute-done | bytes 196640 | tf_op jit(solution)/shard_map/ppermute | solution.py:548
  15.8 1.5 collective-permute-start.2
  17.4 1.5 collective-permute-start.1
  19.7 3.4 collective-permute-start.4
  23.0 8.8 %collective-permute-done.4 = bf16[128,768]{1,0:T(8,128)(2,1)S(1)} collective-permute-done((bf16[128,768]{1,0:T(8,128)(2,1)S(1)}, bf16[128,768]{1,0:T(8,128)(2,1)S(1)}, u32[]{:S(2)}, u32[]{:S(2)}) %collective-permute-start.4) | collective-permute-done | bytes 196640 | tf_op jit(solution)/shard_map/ppermute | solution.py:548
  34.2 3.4 collective-permute-start.7
  37.6 1.7 collective-permute-start.8
  41.7 7.3 %collective-permute-done.8 = bf16[128,768]{1,0:T(8,128)(2,1)S(1)} collective-permute-done((bf16[128,768]{1,0:T(8,128)(2,1)S(1)}, bf16[128,768]{1,0:T(8,128)(2,1)S(1)}, u32[]{:S(2)}, u32[]{:S(2)}) %collective-permute-start.8) | collective-permute-done | bytes 196640 | tf_op jit(solution)/shard_map/ppermute | solution.py:548
  52.0 1.6 collective-permute-start.12
  55.7 1.9 collective-permute-start.13
  58.3 13.9 %attention_forward.3 = (bf16[512,192]{1,0:T(8,128)(2,1)S(1)}, bf16[2048,192]{1,0:T(8,128)(2,1)}, bf16[2048,192]{1,0:T(8,128)(2,1)}, bf16[512,192]{1,0:T(8,128)(2...) custom-call(s32[4]{0:T(128)S(1)} %pad_add_fusion.places, ...), custom_call_target="tpu_custom_call" | custom-call | flops 4429185024 | bytes 5505024 | tf_op jit(solution)/shard_map/attention_forward/pallas_call | solution.py:189
  72.3 1.8 collective-permute-done.10
  74.8 1.6 collective-permute-start.19
  80.3 13.7 %attention_forward.4 = (bf16[512,192]{1,0:T(8,128)(2,1)S(1)}, bf16[2048,192]{1,0:T(8,128)(2,1)}, bf16[2048,192]{1,0:T(8,128)(2,1)}, bf16[512,192]{1,0:T(8,128)(2...) custom-call(s32[4]{0:T(128)S(1)} %pad_add_fusion.places, ...), custom_call_target="tpu_custom_call" | custom-call | flops 4429185024 | bytes 5505024 | tf_op jit(solution)/shard_map/attention_forward/pallas_call | solution.py:189
  94.1 2.5 collective-permute-done.16
  97.2 1.6 collective-permute-start.22
  100.9 1.5 collective-permute-start.25
  102.4 13.9 %attention_forward.5 = (bf16[512,192]{1,0:T(8,128)(2,1)S(1)}, bf16[2048,192]{1,0:T(8,128)(2,1)}, bf16[2048,192]{1,0:T(8,128)(2,1)}, bf16[512,192]{1,0:T(8,128)(2...) custom-call(s32[4]{0:T(128)S(1)} %pad_add_fusion.places, ...), custom_call_target="tpu_custom_call" | custom-call | flops 4429185024 | bytes 5505024 | tf_op jit(solution)/shard_map/attention_forward/pallas_call | solution.py:189
  117.5 2.7 collective-permute-done.32.refs_24_
  122.1 1.5 collective-permute-done.31.refs_15_
  123.7 4.2 %collective-permute-done.33.refs_27_ = bf16[128,768]{1,0:T(8,128)(2,1)S(1)} collective-permute-done((bf16[128,768]{1,0:T(8,128)(2,1)S(1)}, bf16[128,768]{1,0:T(8,128)(2,1)S(1)}, u32[]{:S(2)}, u32[]{:S(2)}) %collective-permute-start.33) | collective-permute-done | bytes 196640 | tf_op jit(solution)/shard_map/ppermute | solution.py:500
  128.6 20.5 %feed_forward.1 = (bf16[384,768]{1,0:T(8,128)(2,1)}, bf16[128,768]{1,0:T(8,128)(2,1)S(1)}, bf16[256,768]{1,0:T(8,128)(2,1)}, f32[384,768]{1,0:T(8,128)}, bf16[4,...) custom-call(s32[5]{0:T(128)S(1)} %concatenate.73.order.refs_8_, ...), custom_call_target="tpu_custom_call" | custom-call | flops 7247757312 | bytes 14155776 | tf_op jit(solution)/shard_map/feed_forward/pallas_call | solution.py:411
  151.3 6.7 %feed_gradients.2 = (bf16[2,2,448,768]{3,2,1,0:T(8,128)(2,1)}, bf16[2,2,384,768]{3,2,1,0:T(8,128)(2,1)}) custom-call(s32[5]{0:T(128)S(1)} %concatenate.73.order.refs_8_, bf16[4,384,768]{2,1,0:T(8,128)(2,1)} %get-tuple-element.353.act, bf16[4,384,768]{2,1,0:T(8,128)(2,1)} %get-tuple-element.365.d_inner, bf16[384,768]{1,0:T(8,128)(2,1)S(1)} %copy-done.11, ...), custom_call_target="tpu_custom_call" | custom-call | flops 1811939328 | bytes 4718592 | tf_op jit(solution)/shard_map/feed_gradients/pallas_call | solution.py:474
  159.7 7.1 %feed_gradients.3 = (bf16[2,2,448,768]{3,2,1,0:T(8,128)(2,1)}, bf16[2,2,384,768]{3,2,1,0:T(8,128)(2,1)}) custom-call(s32[5]{0:T(128)S(1)} %concatenate.73.order.refs_8_, bf16[4,384,768]{2,1,0:T(8,128)(2,1)} %get-tuple-element.353.act, bf16[4,384,768]{2,1,0:T(8,128)(2,1)} %get-tuple-element.365.d_inner, bf16[384,768]{1,0:T(8,128)(2,1)S(1)} %copy-done.11, ...), custom_call_target="tpu_custom_call" | custom-call | flops 1811939328 | bytes 4718592 | tf_op jit(solution)/shard_map/feed_gradients/pallas_call | solution.py:474
  167.3 1.4 copy-done.16
  168.7 3.1 fusion.13
  175.8 14.8 %attention_backward.3 = (bf16[512,192]{1,0:T(8,128)(2,1)S(1)}, bf16[2048,192]{1,0:T(8,128)(2,1)}, bf16[2048,192]{1,0:T(8,128)(2,1)}, bf16[1024,768]{1,0:T(8,128)...) custom-call(s32[4]{0:T(128)S(1)} %pad_add_fusion.places, ...), custom_call_target="tpu_custom_call" | custom-call | flops 9261023232 | bytes 7077888 | tf_op jit(solution)/shard_map/attention_backward/pallas_call | solution.py:220
  191.6 2.5 fusion.7
  197.1 15.4 %attention_backward.4 = (bf16[512,192]{1,0:T(8,128)(2,1)S(1)}, bf16[2048,192]{1,0:T(8,128)(2,1)}, bf16[2048,192]{1,0:T(8,128)(2,1)}, bf16[1024,768]{1,0:T(8,128)...) custom-call(s32[4]{0:T(128)S(1)} %pad_add_fusion.places, ...), custom_call_target="tpu_custom_call" | custom-call | flops 9261023232 | bytes 7077888 | tf_op jit(solution)/shard_map/attention_backward/pallas_call | solution.py:220
  218.7 5.5 %attention_gradients.3.refs_7_ = f32[3,192,768]{2,1,0:T(8,128)} custom-call(bf16[3,512,768]{2,1,0:T(8,128)(2,1)} %refs_0_.5, bf16[384,768]{1,0:T(8,128)(2,1)S(1)} %copy-done.1, bf16[384,768]{1,0:T(8,128)(2,1)} %copy-done.15, bf16[768,768]{1,0:T(8,128)(2,1)} %collective-permute-done.9.sib.refs_3_, bf16[512,192]{1,0:T(8,128)(2,1)S(1)} %get-tuple-element.430.refs_4_, ...), custom_call_target="tpu_custom_call" | custom-call | flops 1207959552 | bytes 4718592 | tf_op jit(solution)/shard_map/attention_gradients/pallas_call | solution.py:299
  224.2 2.3 add_convert_fusion.1
  226.6 5.9 %attention_gradients.4.refs_7_ = f32[3,192,768]{2,1,0:T(8,128)} custom-call(bf16[3,512,768]{2,1,0:T(8,128)(2,1)} %refs_0_.5, bf16[384,768]{1,0:T(8,128)(2,1)S(1)} %copy-done.3, bf16[384,768]{1,0:T(8,128)(2,1)} %copy-done.19, bf16[768,768]{1,0:T(8,128)(2,1)} %copy-done.34, bf16[512,192]{1,0:T(8,128)(2,1)S(1)} %get-tuple-element.434.refs_4_, ...), custom_call_target="tpu_custom_call" | custom-call | flops 1207959552 | bytes 4718592 | tf_op jit(solution)/shard_map/attention_gradients/pallas_call | solution.py:299
  233.7 1.8 fusion.6
  235.5 2.0 fusion.2
  237.5 1.8 fusion.10
  239.2 1.9 collective-permute-start.48
  241.1 15.4 %attention_backward.5 = (bf16[512,192]{1,0:T(8,128)(2,1)S(1)}, bf16[2048,192]{1,0:T(8,128)(2,1)}, bf16[2048,192]{1,0:T(8,128)(2,1)}, bf16[1024,768]{1,0:T(8,128)...) custom-call(s32[4]{0:T(128)S(1)} %pad_add_fusion.places, ...), custom_call_target="tpu_custom_call" | custom-call | flops 9261023232 | bytes 7077888 | tf_op jit(solution)/shard_map/attention_backward/pallas_call | solution.py:220
  258.5 1.2 add_convert_fusion.6
  259.8 1.2 add_convert_fusion.11
  261.6 2.3 collective-permute-start.55
  263.9 6.2 %attention_gradients.5 = (bf16[832,384]{1,0:T(8,128)(2,1)}, bf16[832,384]{1,0:T(8,128)(2,1)}) custom-call(bf16[3,512,768]{2,1,0:T(8,128)(2,1)} %refs_0_.5, bf16[384,768]{1,0:T(8,128)(2,1)S(1)} %copy-done.5, bf16[384,768]{1,0:T(8,128)(2,1)} %copy-done.18, bf16[768,768]{1,0:T(8,128)(2,1)} %copy-done.33, bf16[512,192]{1,0:T(8,128)(2,1)S(1)} %get-tuple-element.464.refs_4_, ...), custom_call_target="tpu_custom_call" | custom-call | flops 1207959552 | bytes 4718592 | tf_op jit(solution)/shard_map/attention_gradients/pallas_call | solution.py:299
  270.2 1.4 add_convert_fusion
  271.6 6.2 %collective-permute-done.52 = bf16[512,768]{1,0:T(8,128)(2,1)S(1)} collective-permute-done((bf16[512,768]{1,0:T(8,128)(2,1)}, bf16[512,768]{1,0:T(8,128)(2,1)S(1)}, u32[]{:S(2)}, u32[]{:S(2)}) %collective-permute-start.52) | collective-permute-done | bytes 786464 | tf_op jit(solution)/shard_map/ppermute | solution.py:500
  281.5 2.3 collective-permute-start.59
  286.1 5.5 %collective-permute-done.54 = bf16[256,768]{1,0:T(8,128)(2,1)S(1)} collective-permute-done((bf16[256,768]{1,0:T(8,128)(2,1)S(1)}, bf16[256,768]{1,0:T(8,128)(2,1)S(1)}, u32[]{:S(2)}, u32[]{:S(2)}) %collective-permute-start.54) | collective-permute-done | bytes 393248 | tf_op jit(solution)/shard_map/ppermute | solution.py:500
  291.6 2.3 collective-permute-start.58
  297.1 2.0 collective-permute-done.51
  299.9 1.5 collective-permute-start.57
  301.5 18.8 %collective-permute-done.60 = bf16[256,768]{1,0:T(8,128)(2,1)S(1)} collective-permute-done((bf16[256,768]{1,0:T(8,128)(2,1)S(1)}, bf16[256,768]{1,0:T(8,128)(2,1)S(1)}, u32[]{:S(2)}, u32[]{:S(2)}) %collective-permute-start.60) | collective-permute-done | bytes 393248 | tf_op jit(solution)/shard_map/ppermute | solution.py:548
  326.1 1.5 collective-permute-start.62
  327.6 6.4 %collective-permute-done.65 = bf16[128,768]{1,0:T(8,128)(2,1)S(1)} collective-permute-done((bf16[128,768]{1,0:T(8,128)(2,1)S(1)}, bf16[128,768]{1,0:T(8,128)(2,1)S(1)}, u32[]{:S(2)}, u32[]{:S(2)}) %collective-permute-start.65) | collective-permute-done | bytes 196640 | tf_op jit(solution)/shard_map/ppermute | solution.py:548
  336.9 1.2 collective-permute-start.66
  338.1 2.6 collective-permute-start.67
  340.7 1.2 select_bitcast_fusion.7
  342.3 13.5 %collective-permute-done.66 = bf16[1,128,768]{2,1,0:T(8,128)(2,1)S(1)} collective-permute-done((bf16[1,128,768]{2,1,0:T(8,128)(2,1)S(1)}, bf16[1,128,768]{2,1,0:T(8,128)(2,1)S(1)}, u32[]{:S(2)}, u32[]{:S(2)}) %collective-permute-start.66) | collective-permute-done | bytes 196640 | tf_op jit(solution)/shard_map/ppermute | solution.py:500
  356.7 1.8 collective-permute-start.70
  358.9 1.2 convert_bitcast_fusion
  360.0 1.6 pad_maximum_fusion.1
  362.2 1.6 copy.36
  363.8 2.5 collective-permute-done.70
  368.8 1.4 copy.37
  (336 shorter events, 70.9 us)
Async XLA Ops:
  2.6 13.2 %collective-permute-start = (bf16[128,768]{1,0:T(8,128)(2,1)S(1)}, bf16[128,768]{1,0:T(8,128)(2,1)S(1)}, u32[]{:S(2)}, u32[]{:S(2)}) collective-permute-start(bf16[128,768]{1,0:T(8,128)(2,1)S(1)} %dynamic-slice_bitcast_fusion.2.refs_16_), channel_id=1, source_target_pairs={{0,8},{4,12},{8,0},{12,4},{1,9},{5,13},{9,1},{13,5},{2,10},{6,14},... | collective-permute-start | bytes 589832 | tf_op jit(solution)/shard_map/ppermute | solution.py:548
  15.8 16.8 %collective-permute-start.2 = (bf16[400,768]{1,0:T(8,128)(2,1)}, bf16[400,768]{1,0:T(8,128)(2,1)}, u32[]{:S(2)}, u32[]{:S(2)}) collective-permute-start(bf16[400,768]{1,0:T(8,128)(2,1)} %pad_maximum_fusion.12.refs_0_), channel_id=1, source_target_pairs={{0,2},{1,3},{2,0},{3,1},{4,6},{5,7},{6,4},{7,5},{8,10},{9,11},{10,... | collective-permute-start | bytes 1843208 | tf_op jit(solution)/shard_map/ppermute | solution.py:500
  17.4 15.3 %collective-permute-start.1 = (bf16[4,192,384]{2,1,0:T(8,128)(2,1)S(1)}, bf16[4,192,384]{2,1,0:T(8,128)(2,1)S(1)}, u32[]{:S(2)}, u32[]{:S(2)}) collective-permute-start(bf16[4,192,384]{2,1,0:T(8,128)(2,1)S(1)} %pad_maximum_fusion.14), channel_id=1, source_target_pairs={{0,16},{16,0},{1,17},{17,1},{2,18},{18,2},{3,19},{19,3},{4,20},{20... | collective-permute-start | bytes 1769480 | tf_op jit(solution)/shard_map/ppermute | solution.py:496
  18.9 13.7 %collective-permute-start.3 = (bf16[256,768]{1,0:T(8,128)(2,1)S(1)}, bf16[256,768]{1,0:T(8,128)(2,1)S(1)}, u32[]{:S(2)}, u32[]{:S(2)}) collective-permute-start(bf16[256,768]{1,0:T(8,128)(2,1)S(1)} %pad_maximum_fusion.15), channel_id=1, source_target_pairs={{0,4},{4,0},{8,12},{12,8},{1,5},{5,1},{9,13},{13,9},{2,6},{6,2},{1... | collective-permute-start | bytes 1179656 | tf_op jit(solution)/shard_map/ppermute | solution.py:548
  19.7 12.2 %collective-permute-start.4 = (bf16[128,768]{1,0:T(8,128)(2,1)S(1)}, bf16[128,768]{1,0:T(8,128)(2,1)S(1)}, u32[]{:S(2)}, u32[]{:S(2)}) collective-permute-start(bf16[128,768]{1,0:T(8,128)(2,1)S(1)} %get-tuple-element.285.refs_17_), channel_id=1, source_target_pairs={{0,8},{4,12},{8,0},{12,4},{1,9},{5,13},{9,1},{13,5},{2,10},{6,14},... | collective-permute-start | bytes 589832 | tf_op jit(solution)/shard_map/ppermute | solution.py:548
  32.7 17.0 %collective-permute-start.5 = (bf16[400,768]{1,0:T(8,128)(2,1)}, bf16[400,768]{1,0:T(8,128)(2,1)}, u32[]{:S(2)}, u32[]{:S(2)}) collective-permute-start(bf16[400,768]{1,0:T(8,128)(2,1)} %pad_maximum_fusion.12.refs_0_), channel_id=1, source_target_pairs={{0,16},{16,0},{1,17},{17,1},{2,18},{18,2},{3,19},{19,3},{4,20},{20... | collective-permute-start | bytes 1843208 | tf_op jit(solution)/shard_map/ppermute | solution.py:496
  33.6 16.1 %collective-permute-start.6 = (bf16[384,768]{1,0:T(8,128)(2,1)S(1)}, bf16[384,768]{1,0:T(8,128)(2,1)S(1)}, u32[]{:S(2)}, u32[]{:S(2)}) collective-permute-start(bf16[384,768]{1,0:T(8,128)(2,1)S(1)} %constant_dynamic-update-slice_fusion.1.near.refs_1_), channel_id=1, source_target_pairs={{0,2},{1,3},{2,0},{3,1},{4,6},{5,7},{6,4},{7,5},{8,10},{9,11},{10,... | collective-permute-start | bytes 1769480 | tf_op jit(solution)/shard_map/ppermute | solution.py:500
  34.2 15.5 %collective-permute-start.7 = (bf16[256,768]{1,0:T(8,128)(2,1)S(1)}, bf16[256,768]{1,0:T(8,128)(2,1)S(1)}, u32[]{:S(2)}, u32[]{:S(2)}) collective-permute-start(bf16[256,768]{1,0:T(8,128)(2,1)S(1)} %pad_maximum_fusion.16), channel_id=1, source_target_pairs={{0,4},{4,0},{8,12},{12,8},{1,5},{5,1},{9,13},{13,9},{2,6},{6,2},{1... | collective-permute-start | bytes 1179656 | tf_op jit(solution)/shard_map/ppermute | solution.py:548
  37.6 11.3 %collective-permute-start.8 = (bf16[128,768]{1,0:T(8,128)(2,1)S(1)}, bf16[128,768]{1,0:T(8,128)(2,1)S(1)}, u32[]{:S(2)}, u32[]{:S(2)}) collective-permute-start(bf16[128,768]{1,0:T(8,128)(2,1)S(1)} %get-tuple-element.296.refs_18_), channel_id=1, source_target_pairs={{0,8},{4,12},{8,0},{12,4},{1,9},{5,13},{9,1},{13,5},{2,10},{6,14},... | collective-permute-start | bytes 589832 | tf_op jit(solution)/shard_map/ppermute | solution.py:548
  50.9 6.8 %collective-permute-start.9 = (bf16[768,768]{1,0:T(8,128)(2,1)}, bf16[768,768]{1,0:T(8,128)(2,1)}, u32[]{:S(2)}, u32[]{:S(2)}) collective-permute-start(bf16[768,768]{1,0:T(8,128)(2,1)} %pad_maximum_fusion.4), channel_id=1, source_target_pairs={{0,1},{1,0},{2,3},{3,2},{4,5},{5,4},{6,7},{7,6},{8,9},{9,8},{10,11... | collective-permute-start | bytes 3538952 | tf_op jit(solution)/shard_map/ppermute | solution.py:504
  52.0 20.2 %collective-permute-start.12 = (bf16[384,768]{1,0:T(8,128)(2,1)S(1)}, bf16[384,768]{1,0:T(8,128)(2,1)S(1)}, u32[]{:S(2)}, u32[]{:S(2)}) collective-permute-start(bf16[384,768]{1,0:T(8,128)(2,1)S(1)} %constant_dynamic-update-slice_fusion.3.near.refs_1_), channel_id=1, source_target_pairs={{0,2},{1,3},{2,0},{3,1},{4,6},{5,7},{6,4},{7,5},{8,10},{9,11},{10,... | collective-permute-start | bytes 1769480 | tf_op jit(solution)/shard_map/ppermute | solution.py:500
  53.6 18.6 %collective-permute-start.11 = (bf16[384,768]{1,0:T(8,128)(2,1)}, bf16[384,768]{1,0:T(8,128)(2,1)S(1)}, u32[]{:S(2)}, u32[]{:S(2)}) collective-permute-start(bf16[384,768]{1,0:T(8,128)(2,1)} %bitcast.13.refs_8_), channel_id=1, source_target_pairs={{0,16},{16,0},{1,17},{17,1},{2,18},{18,2},{3,19},{19,3},{4,20},{20... | collective-permute-start | bytes 1769480 | tf_op jit(solution)/shard_map/ppermute | solution.py:496
  55.7 16.5 %collective-permute-start.13 = (bf16[256,768]{1,0:T(8,128)(2,1)S(1)}, bf16[256,768]{1,0:T(8,128)(2,1)S(1)}, u32[]{:S(2)}, u32[]{:S(2)}) collective-permute-start(bf16[256,768]{1,0:T(8,128)(2,1)S(1)} %pad_maximum_fusion.17), channel_id=1, source_target_pairs={{0,4},{4,0},{8,12},{12,8},{1,5},{5,1},{9,13},{13,9},{2,6},{6,2},{1... | collective-permute-start | bytes 1179656 | tf_op jit(solution)/shard_map/ppermute | solution.py:548
  57.6 16.5 %collective-permute-start.10 = (bf16[192,768]{1,0:T(8,128)(2,1)S(1)}, bf16[192,768]{1,0:T(8,128)(2,1)S(1)}, u32[]{:S(2)}, u32[]{:S(2)}) collective-permute-start(bf16[192,768]{1,0:T(8,128)(2,1)S(1)} %slice.326), channel_id=1, source_target_pairs={{0,2},{1,3},{2,0},{3,1},{4,6},{5,7},{6,4},{7,5},{8,10},{9,11},{10,... | collective-permute-start | bytes 884744 | tf_op jit(solution)/shard_map/ppermute | solution.py:500
  74.8 19.2 %collective-permute-start.19 = (bf16[384,768]{1,0:T(8,128)(2,1)S(1)}, bf16[384,768]{1,0:T(8,128)(2,1)S(1)}, u32[]{:S(2)}, u32[]{:S(2)}) collective-permute-start(bf16[384,768]{1,0:T(8,128)(2,1)S(1)} %constant_dynamic-update-slice_fusion.5.near.refs_1_), channel_id=1, source_target_pairs={{0,2},{1,3},{2,0},{3,1},{4,6},{5,7},{6,4},{7,5},{8,10},{9,11},{10,... | collective-permute-start | bytes 1769480 | tf_op jit(solution)/shard_map/ppermute | solution.py:500
  77.4 16.7 %collective-permute-start.17 = (bf16[400,768]{1,0:T(8,128)(2,1)}, bf16[400,768]{1,0:T(8,128)(2,1)S(1)}, u32[]{:S(2)}, u32[]{:S(2)}) collective-permute-start(bf16[400,768]{1,0:T(8,128)(2,1)} %pad_maximum_fusion.12.refs_0_), channel_id=1, source_target_pairs={{0,1},{1,0},{2,3},{3,2},{4,5},{5,4},{6,7},{7,6},{8,9},{9,8},{10,11... | collective-permute-start | bytes 1843208 | tf_op jit(solution)/shard_map/ppermute | solution.py:504
  77.5 16.6 %collective-permute-start.18 = (bf16[400,768]{1,0:T(8,128)(2,1)}, bf16[400,768]{1,0:T(8,128)(2,1)}, u32[]{:S(2)}, u32[]{:S(2)}) collective-permute-start(bf16[400,768]{1,0:T(8,128)(2,1)} %collective-permute-done.2.refs_2_), channel_id=1, source_target_pairs={{0,16},{16,0},{1,17},{17,1},{2,18},{18,2},{3,19},{19,3},{4,20},{20... | collective-permute-start | bytes 1843208 | tf_op jit(solution)/shard_map/ppermute | solution.py:496
  79.3 17.2 %collective-permute-start.16 = (bf16[192,768]{1,0:T(8,128)(2,1)S(1)}, bf16[192,768]{1,0:T(8,128)(2,1)S(1)}, u32[]{:S(2)}, u32[]{:S(2)}) collective-permute-start(bf16[192,768]{1,0:T(8,128)(2,1)S(1)} %slice.327), channel_id=1, source_target_pairs={{0,2},{1,3},{2,0},{3,1},{4,6},{5,7},{6,4},{7,5},{8,10},{9,11},{10,... | collective-permute-start | bytes 884744 | tf_op jit(solution)/shard_map/ppermute | solution.py:500
  97.2 19.0 %collective-permute-start.22 = (bf16[128,768]{1,0:T(8,128)(2,1)S(1)}, bf16[128,768]{1,0:T(8,128)(2,1)S(1)}, u32[]{:S(2)}, u32[]{:S(2)}) collective-permute-start(bf16[128,768]{1,0:T(8,128)(2,1)S(1)} %add_convert_fusion.22), channel_id=1, source_target_pairs={{0,2},{1,3},{2,0},{3,1},{4,6},{5,7},{6,4},{7,5},{8,10},{9,11},{10,... | collective-permute-start | bytes 589832 | tf_op jit(solution)/shard_map/ppermute | solution.py:500
  98.8 17.5 %collective-permute-start.21 = (bf16[384,768]{1,0:T(8,128)(2,1)S(1)}, bf16[384,768]{1,0:T(8,128)(2,1)}, u32[]{:S(2)}, u32[]{:S(2)}) collective-permute-start(bf16[384,768]{1,0:T(8,128)(2,1)S(1)} %constant_dynamic-update-slice_fusion.7.refs_10_), channel_id=1, source_target_pairs={{0,16},{16,0},{1,17},{17,1},{2,18},{18,2},{3,19},{19,3},{4,20},{20... | collective-permute-start | bytes 1769480 | tf_op jit(solution)/shard_map/ppermute | solution.py:496
  99.9 16.4 %collective-permute-start.20 = (bf16[384,768]{1,0:T(8,128)(2,1)}, bf16[384,768]{1,0:T(8,128)(2,1)S(1)}, u32[]{:S(2)}, u32[]{:S(2)}) collective-permute-start(bf16[384,768]{1,0:T(8,128)(2,1)} %bitcast.13.refs_8_), channel_id=1, source_target_pairs={{0,1},{1,0},{2,3},{3,2},{4,5},{5,4},{6,7},{7,6},{8,9},{9,8},{10,11... | collective-permute-start | bytes 1769480 | tf_op jit(solution)/shard_map/ppermute | solution.py:504
  100.9 15.4 %collective-permute-start.25 = (bf16[128,768]{1,0:T(8,128)(2,1)S(1)}, bf16[128,768]{1,0:T(8,128)(2,1)S(1)}, u32[]{:S(2)}, u32[]{:S(2)}) collective-permute-start(bf16[128,768]{1,0:T(8,128)(2,1)S(1)} %add_convert_fusion.21), channel_id=1, source_target_pairs={{0,2},{1,3},{2,0},{3,1},{4,6},{5,7},{6,4},{7,5},{8,10},{9,11},{10,... | collective-permute-start | bytes 589832 | tf_op jit(solution)/shard_map/ppermute | solution.py:500
  117.0 10.9 %collective-permute-start.26 = (bf16[400,768]{1,0:T(8,128)(2,1)}, bf16[400,768]{1,0:T(8,128)(2,1)}, u32[]{:S(2)}, u32[]{:S(2)}) collective-permute-start(bf16[400,768]{1,0:T(8,128)(2,1)} %collective-permute-done.5.refs_1_), channel_id=1, source_target_pairs={{0,1},{1,0},{2,3},{3,2},{4,5},{5,4},{6,7},{7,6},{8,9},{9,8},{10,11... | collective-permute-start | bytes 1843208 | tf_op jit(solution)/shard_map/ppermute | solution.py:504
  117.5 10.4 %collective-permute-start.27 = (bf16[400,768]{1,0:T(8,128)(2,1)}, bf16[400,768]{1,0:T(8,128)(2,1)}, u32[]{:S(2)}, u32[]{:S(2)}) collective-permute-start(bf16[400,768]{1,0:T(8,128)(2,1)} %collective-permute-done.2.refs_2_), channel_id=1, source_target_pairs={{0,1},{1,0},{2,3},{3,2},{4,5},{5,4},{6,7},{7,6},{8,9},{9,8},{10,11... | collective-permute-start | bytes 1843208 | tf_op jit(solution)/shard_map/ppermute | solution.py:504
  120.2 7.7 %collective-permute-start.28 = (bf16[400,768]{1,0:T(8,128)(2,1)}, bf16[400,768]{1,0:T(8,128)(2,1)}, u32[]{:S(2)}, u32[]{:S(2)}) collective-permute-start(bf16[400,768]{1,0:T(8,128)(2,1)} %collective-permute-done.18.refs_3_), channel_id=1, source_target_pairs={{0,1},{1,0},{2,3},{3,2},{4,5},{5,4},{6,7},{7,6},{8,9},{9,8},{10,11... | collective-permute-start | bytes 1843208 | tf_op jit(solution)/shard_map/ppermute | solution.py:504
  120.9 7.0 %collective-permute-start.33 = (bf16[128,768]{1,0:T(8,128)(2,1)S(1)}, bf16[128,768]{1,0:T(8,128)(2,1)S(1)}, u32[]{:S(2)}, u32[]{:S(2)}) collective-permute-start(bf16[128,768]{1,0:T(8,128)(2,1)S(1)} %add_convert_fusion.20), channel_id=1, source_target_pairs={{0,2},{1,3},{2,0},{3,1},{4,6},{5,7},{6,4},{7,5},{8,10},{9,11},{10,... | collective-permute-start | bytes 589832 | tf_op jit(solution)/shard_map/ppermute | solution.py:500
  149.1 9.0 %collective-permute-start.34 = (bf16[128,768]{1,0:T(8,128)(2,1)S(1)}, bf16[128,768]{1,0:T(8,128)(2,1)S(1)}, u32[]{:S(2)}, u32[]{:S(2)}) collective-permute-start(bf16[128,768]{1,0:T(8,128)(2,1)S(1)} %get-tuple-element.377.g_own), channel_id=1, source_target_pairs={{0,2},{1,3},{2,0},{3,1},{4,6},{5,7},{6,4},{7,5},{8,10},{9,11},{10,... | collective-permute-start | bytes 589832 | tf_op jit(solution)/shard_map/ppermute | solution.py:500
  158.0 9.3 %collective-permute-start.37 = (bf16[2,2,448,768]{3,2,1,0:T(8,128)(2,1)}, bf16[2,2,448,768]{3,2,1,0:T(8,128)(2,1)S(1)}, u32[]{:S(2)}, u32[]{:S(2)}) collective-permute-start(bf16[2,2,448,768]{3,2,1,0:T(8,128)(2,1)} %get-tuple-element.363), channel_id=1, source_target_pairs={{0,1},{1,0},{2,3},{3,2},{4,5},{5,4},{6,7},{7,6},{8,9},{9,8},{10,11... | collective-permute-start | bytes 8257544 | tf_op jit(solution)/shard_map/ppermute | solution.py:504
  158.0 9.2 %collective-permute-start.38 = (bf16[2,2,384,768]{3,2,1,0:T(8,128)(2,1)}, bf16[2,2,384,768]{3,2,1,0:T(8,128)(2,1)S(1)}, u32[]{:S(2)}, u32[]{:S(2)}) collective-permute-start(bf16[2,2,384,768]{3,2,1,0:T(8,128)(2,1)} %get-tuple-element.364), channel_id=1, source_target_pairs={{0,1},{1,0},{2,3},{3,2},{4,5},{5,4},{6,7},{7,6},{8,9},{9,8},{10,11... | collective-permute-start | bytes 7077896 | tf_op jit(solution)/shard_map/ppermute | solution.py:504
  158.6 8.2 %collective-permute-start.36 = (bf16[256,768]{1,0:T(8,128)(2,1)S(1)}, bf16[256,768]{1,0:T(8,128)(2,1)S(1)}, u32[]{:S(2)}, u32[]{:S(2)}) collective-permute-start(bf16[256,768]{1,0:T(8,128)(2,1)S(1)} %pad_maximum_fusion.18), channel_id=1, source_target_pairs={{0,1},{1,0},{2,3},{3,2},{4,5},{5,4},{6,7},{7,6},{8,9},{9,8},{10,11... | collective-permute-start | bytes 1179656 | tf_op jit(solution)/shard_map/ppermute | solution.py:504
  158.7 14.2 %collective-permute-start.35 = (bf16[256,768]{1,0:T(8,128)(2,1)S(1)}, bf16[256,768]{1,0:T(8,128)(2,1)S(1)}, u32[]{:S(2)}, u32[]{:S(2)}) collective-permute-start(bf16[256,768]{1,0:T(8,128)(2,1)S(1)} %copy-done.43), channel_id=1, source_target_pairs={{0,2},{1,3},{2,0},{3,1},{4,6},{5,7},{6,4},{7,5},{8,10},{9,11},{10,... | collective-permute-start | bytes 1179656 | tf_op jit(solution)/shard_map/ppermute | solution.py:500
  173.7 17.9 %collective-permute-start.41 = (bf16[512,768]{1,0:T(8,128)(2,1)S(1)}, bf16[512,768]{1,0:T(8,128)(2,1)}, u32[]{:S(2)}, u32[]{:S(2)}) collective-permute-start(bf16[512,768]{1,0:T(8,128)(2,1)S(1)} %pad_maximum_fusion.8), channel_id=1, source_target_pairs={{0,1},{1,0},{2,3},{3,2},{4,5},{5,4},{6,7},{7,6},{8,9},{9,8},{10,11... | collective-permute-start | bytes 2359304 | tf_op jit(solution)/shard_map/ppermute | solution.py:504
  173.8 17.7 %collective-permute-start.39 = (bf16[448,768]{1,0:T(8,128)(2,1)S(1)}, bf16[448,768]{1,0:T(8,128)(2,1)S(1)}, u32[]{:S(2)}, u32[]{:S(2)}) collective-permute-start(bf16[448,768]{1,0:T(8,128)(2,1)S(1)} %get-tuple-element.374), channel_id=1, source_target_pairs={{0,2},{1,3},{2,0},{3,1},{4,6},{5,7},{6,4},{7,5},{8,10},{9,11},{10,... | collective-permute-start | bytes 2064392 | tf_op jit(solution)/shard_map/ppermute | solution.py:500
  174.8 15.8 %collective-permute-start.40 = (bf16[384,768]{1,0:T(8,128)(2,1)S(1)}, bf16[384,768]{1,0:T(8,128)(2,1)}, u32[]{:S(2)}, u32[]{:S(2)}) collective-permute-start(bf16[384,768]{1,0:T(8,128)(2,1)S(1)} %get-tuple-element.375), channel_id=1, source_target_pairs={{0,16},{16,0},{1,17},{17,1},{2,18},{18,2},{3,19},{19,3},{4,20},{20... | collective-permute-start | bytes 1769480 | tf_op jit(solution)/shard_map/ppermute | solution.py:496
  191.6 21.7 %collective-permute-start.44 = (bf16[1024,768]{1,0:T(8,128)(2,1)}, bf16[1024,768]{1,0:T(8,128)(2,1)S(1)}, u32[]{:S(2)}, u32[]{:S(2)}) collective-permute-start(bf16[1024,768]{1,0:T(8,128)(2,1)} %get-tuple-element.396), channel_id=1, source_target_pairs={{0,1},{1,0},{2,3},{3,2},{4,5},{5,4},{6,7},{7,6},{8,9},{9,8},{10,11... | collective-permute-start | bytes 4718600 | tf_op jit(solution)/shard_map/ppermute | solution.py:504
  195.2 18.1 %collective-permute-start.42 = (bf16[448,768]{1,0:T(8,128)(2,1)}, bf16[448,768]{1,0:T(8,128)(2,1)S(1)}, u32[]{:S(2)}, u32[]{:S(2)}) collective-permute-start(bf16[448,768]{1,0:T(8,128)(2,1)} %get-tuple-element.394), channel_id=1, source_target_pairs={{0,2},{1,3},{2,0},{3,1},{4,6},{5,7},{6,4},{7,5},{8,10},{9,11},{10,... | collective-permute-start | bytes 2064392 | tf_op jit(solution)/shard_map/ppermute | solution.py:500
  196.2 16.4 %collective-permute-start.43 = (bf16[384,768]{1,0:T(8,128)(2,1)}, bf16[384,768]{1,0:T(8,128)(2,1)S(1)}, u32[]{:S(2)}, u32[]{:S(2)}) collective-permute-start(bf16[384,768]{1,0:T(8,128)(2,1)} %get-tuple-element.395), channel_id=1, source_target_pairs={{0,16},{16,0},{1,17},{17,1},{2,18},{18,2},{3,19},{19,3},{4,20},{20... | collective-permute-start | bytes 1769480 | tf_op jit(solution)/shard_map/ppermute | solution.py:496
  215.5 8.7 %collective-permute-start.47 = (bf16[1024,768]{1,0:T(8,128)(2,1)}, bf16[1024,768]{1,0:T(8,128)(2,1)}, u32[]{:S(2)}, u32[]{:S(2)}) collective-permute-start(bf16[1024,768]{1,0:T(8,128)(2,1)} %get-tuple-element.429), channel_id=1, source_target_pairs={{0,1},{1,0},{2,3},{3,2},{4,5},{5,4},{6,7},{7,6},{8,9},{9,8},{10,11... | collective-permute-start | bytes 4718600 | tf_op jit(solution)/shard_map/ppermute | solution.py:504
  215.5 18.2 %collective-permute-start.45 = (bf16[448,768]{1,0:T(8,128)(2,1)}, bf16[448,768]{1,0:T(8,128)(2,1)}, u32[]{:S(2)}, u32[]{:S(2)}) collective-permute-start(bf16[448,768]{1,0:T(8,128)(2,1)} %fusion.3), channel_id=1, source_target_pairs={{0,16},{16,0},{1,17},{17,1},{2,18},{18,2},{3,19},{19,3},{4,20},{20... | collective-permute-start | bytes 2064392 | tf_op jit(solution)/shard_map/ppermute | solution.py:496
  216.7 16.5 %collective-permute-start.46 = (bf16[384,768]{1,0:T(8,128)(2,1)}, bf16[384,768]{1,0:T(8,128)(2,1)}, u32[]{:S(2)}, u32[]{:S(2)}) collective-permute-start(bf16[384,768]{1,0:T(8,128)(2,1)} %fusion.7), channel_id=1, source_target_pairs={{0,2},{1,3},{2,0},{3,1},{4,6},{5,7},{6,4},{7,5},{8,10},{9,11},{10,... | collective-permute-start | bytes 1769480 | tf_op jit(solution)/shard_map/ppermute | solution.py:500
  217.5 39.0 %collective-permute-start.49 = (bf16[512,768]{1,0:T(8,128)(2,1)}, bf16[512,768]{1,0:T(8,128)(2,1)}, u32[]{:S(2)}, u32[]{:S(2)}) collective-permute-start(bf16[512,768]{1,0:T(8,128)(2,1)} %add_convert_fusion.2), channel_id=1, source_target_pairs={{0,2},{1,3},{2,0},{3,1},{4,6},{5,7},{6,4},{7,5},{8,10},{9,11},{10,... | collective-permute-start | bytes 2359304 | tf_op jit(solution)/shard_map/ppermute | solution.py:500
  239.2 17.3 %collective-permute-start.48 = (bf16[416,768]{1,0:T(8,128)(2,1)S(1)}, bf16[416,768]{1,0:T(8,128)(2,1)S(1)}, u32[]{:S(2)}, u32[]{:S(2)}) collective-permute-start(bf16[416,768]{1,0:T(8,128)(2,1)S(1)} %get-tuple-element.441), channel_id=1, source_target_pairs={{0,4},{4,0},{8,12},{12,8},{1,5},{5,1},{9,13},{13,9},{2,6},{6,2},{1... | collective-permute-start | bytes 1916936 | tf_op jit(solution)/shard_map/ppermute | solution.py:548
  257.4 12.8 %collective-permute-start.50 = (bf16[1024,768]{1,0:T(8,128)(2,1)}, bf16[1024,768]{1,0:T(8,128)(2,1)}, u32[]{:S(2)}, u32[]{:S(2)}) collective-permute-start(bf16[1024,768]{1,0:T(8,128)(2,1)} %get-tuple-element.456), channel_id=1, source_target_pairs={{0,1},{1,0},{2,3},{3,2},{4,5},{5,4},{6,7},{7,6},{8,9},{9,8},{10,11... | collective-permute-start | bytes 4718600 | tf_op jit(solution)/shard_map/ppermute | solution.py:504
  257.5 20.2 %collective-permute-start.52 = (bf16[512,768]{1,0:T(8,128)(2,1)}, bf16[512,768]{1,0:T(8,128)(2,1)S(1)}, u32[]{:S(2)}, u32[]{:S(2)}) collective-permute-start(bf16[512,768]{1,0:T(8,128)(2,1)} %add_convert_fusion.1), channel_id=1, source_target_pairs={{0,2},{1,3},{2,0},{3,1},{4,6},{5,7},{6,4},{7,5},{8,10},{9,11},{10,... | collective-permute-start | bytes 2359304 | tf_op jit(solution)/shard_map/ppermute | solution.py:500
  261.0 18.6 %collective-permute-start.56 = (bf16[256,768]{1,0:T(8,128)(2,1)S(1)}, bf16[256,768]{1,0:T(8,128)(2,1)S(1)}, u32[]{:S(2)}, u32[]{:S(2)}) collective-permute-start(bf16[256,768]{1,0:T(8,128)(2,1)S(1)} %add_convert_fusion.11), channel_id=1, source_target_pairs={{0,4},{4,0},{8,12},{12,8},{1,5},{5,1},{9,13},{13,9},{2,6},{6,2},{1... | collective-permute-start | bytes 1179656 | tf_op jit(solution)/shard_map/ppermute | solution.py:548
  261.6 22.2 %collective-permute-start.55 = (bf16[208,768]{1,0:T(8,128)(2,1)S(1)}, bf16[208,768]{1,0:T(8,128)(2,1)S(1)}, u32[]{:S(2)}, u32[]{:S(2)}) collective-permute-start(bf16[208,768]{1,0:T(8,128)(2,1)S(1)} %constant_dynamic-slice_fusion.2), channel_id=1, source_target_pairs={{0,8},{4,12},{8,0},{12,4},{1,9},{5,13},{9,1},{13,5},{2,10},{6,14},... | collective-permute-start | bytes 958472 | tf_op jit(solution)/shard_map/ppermute | solution.py:548
  279.0 16.1 %collective-permute-start.53 = (bf16[256,768]{1,0:T(8,128)(2,1)S(1)}, bf16[256,768]{1,0:T(8,128)(2,1)S(1)}, u32[]{:S(2)}, u32[]{:S(2)}) collective-permute-start(bf16[256,768]{1,0:T(8,128)(2,1)S(1)} %add_convert_fusion.10), channel_id=1, source_target_pairs={{0,4},{4,0},{8,12},{12,8},{1,5},{5,1},{9,13},{13,9},{2,6},{6,2},{1... | collective-permute-start | bytes 1179656 | tf_op jit(solution)/shard_map/ppermute | solution.py:548
  279.6 12.1 %collective-permute-start.54 = (bf16[256,768]{1,0:T(8,128)(2,1)S(1)}, bf16[256,768]{1,0:T(8,128)(2,1)S(1)}, u32[]{:S(2)}, u32[]{:S(2)}) collective-permute-start(bf16[256,768]{1,0:T(8,128)(2,1)S(1)} %get-tuple-element.582), channel_id=1, source_target_pairs={{0,2},{1,3},{2,0},{3,1},{4,6},{5,7},{6,4},{7,5},{8,10},{9,11},{10,... | collective-permute-start | bytes 1179656 | tf_op jit(solution)/shard_map/ppermute | solution.py:500
  281.5 39.8 %collective-permute-start.59 = (bf16[128,768]{1,0:T(8,128)(2,1)S(1)}, bf16[128,768]{1,0:T(8,128)(2,1)S(1)}, u32[]{:S(2)}, u32[]{:S(2)}) collective-permute-start(bf16[128,768]{1,0:T(8,128)(2,1)S(1)} %add_convert_fusion.19), channel_id=1, source_target_pairs={{0,8},{4,12},{8,0},{12,4},{1,9},{5,13},{9,1},{13,5},{2,10},{6,14},... | collective-permute-start | bytes 589832 | tf_op jit(solution)/shard_map/ppermute | solution.py:548
  283.9 15.2 %collective-permute-start.51 = (bf16[832,384]{1,0:T(8,128)(2,1)S(1)}, bf16[832,384]{1,0:T(8,128)(2,1)S(1)}, u32[]{:S(2)}, u32[]{:S(2)}) collective-permute-start(bf16[832,384]{1,0:T(8,128)(2,1)S(1)} %copy-done.57), channel_id=1, source_target_pairs={{0,16},{16,0},{1,17},{17,1},{2,18},{18,2},{3,19},{19,3},{4,20},{20... | collective-permute-start | bytes 1916936 | tf_op jit(solution)/shard_map/ppermute | solution.py:496
  284.9 15.0 %collective-permute-start.61 = (bf16[256,768]{1,0:T(8,128)(2,1)S(1)}, bf16[256,768]{1,0:T(8,128)(2,1)S(1)}, u32[]{:S(2)}, u32[]{:S(2)}) collective-permute-start(bf16[256,768]{1,0:T(8,128)(2,1)S(1)} %get-tuple-element.581), channel_id=1, source_target_pairs={{0,2},{1,3},{2,0},{3,1},{4,6},{5,7},{6,4},{7,5},{8,10},{9,11},{10,... | collective-permute-start | bytes 1179656 | tf_op jit(solution)/shard_map/ppermute | solution.py:500
  291.6 29.7 %collective-permute-start.58 = (bf16[208,768]{1,0:T(8,128)(2,1)S(1)}, bf16[208,768]{1,0:T(8,128)(2,1)S(1)}, u32[]{:S(2)}, u32[]{:S(2)}) collective-permute-start(bf16[208,768]{1,0:T(8,128)(2,1)S(1)} %add_convert_fusion.13), channel_id=1, source_target_pairs={{0,8},{4,12},{8,0},{12,4},{1,9},{5,13},{9,1},{13,5},{2,10},{6,14},... | collective-permute-start | bytes 958472 | tf_op jit(solution)/shard_map/ppermute | solution.py:548
  295.1 25.1 %collective-permute-start.60 = (bf16[256,768]{1,0:T(8,128)(2,1)S(1)}, bf16[256,768]{1,0:T(8,128)(2,1)S(1)}, u32[]{:S(2)}, u32[]{:S(2)}) collective-permute-start(bf16[256,768]{1,0:T(8,128)(2,1)S(1)} %add_convert_fusion.9), channel_id=1, source_target_pairs={{0,4},{4,0},{8,12},{12,8},{1,5},{5,1},{9,13},{13,9},{2,6},{6,2},{1... | collective-permute-start | bytes 1179656 | tf_op jit(solution)/shard_map/ppermute | solution.py:548
  299.0 25.0 %collective-permute-start.63 = (bf16[128,768]{1,0:T(8,128)(2,1)S(1)}, bf16[128,768]{1,0:T(8,128)(2,1)S(1)}, u32[]{:S(2)}, u32[]{:S(2)}) collective-permute-start(bf16[128,768]{1,0:T(8,128)(2,1)S(1)} %add_convert_fusion.18), channel_id=1, source_target_pairs={{0,8},{4,12},{8,0},{12,4},{1,9},{5,13},{9,1},{13,5},{2,10},{6,14},... | collective-permute-start | bytes 589832 | tf_op jit(solution)/shard_map/ppermute | solution.py:548
  299.9 24.0 %collective-permute-start.57 = (bf16[416,384]{1,0:T(8,128)(2,1)S(1)}, bf16[416,384]{1,0:T(8,128)(2,1)S(1)}, u32[]{:S(2)}, u32[]{:S(2)}) collective-permute-start(bf16[416,384]{1,0:T(8,128)(2,1)S(1)} %constant_dynamic-slice_fusion.1), channel_id=1, source_target_pairs={{0,4},{4,0},{8,12},{12,8},{1,5},{5,1},{9,13},{13,9},{2,6},{6,2},{1... | collective-permute-start | bytes 958472 | tf_op jit(solution)/shard_map/ppermute | solution.py:548
  321.3 12.7 %collective-permute-start.65 = (bf16[128,768]{1,0:T(8,128)(2,1)S(1)}, bf16[128,768]{1,0:T(8,128)(2,1)S(1)}, u32[]{:S(2)}, u32[]{:S(2)}) collective-permute-start(bf16[128,768]{1,0:T(8,128)(2,1)S(1)} %add_convert_fusion.17), channel_id=1, source_target_pairs={{0,8},{4,12},{8,0},{12,4},{1,9},{5,13},{9,1},{13,5},{2,10},{6,14},... | collective-permute-start | bytes 589832 | tf_op jit(solution)/shard_map/ppermute | solution.py:548
  325.1 10.6 %collective-permute-start.64 = (bf16[2,128,768]{2,1,0:T(8,128)(2,1)S(1)}, bf16[2,128,768]{2,1,0:T(8,128)(2,1)S(1)}, u32[]{:S(2)}, u32[]{:S(2)}) collective-permute-start(bf16[2,128,768]{2,1,0:T(8,128)(2,1)S(1)} %bitcast.208), channel_id=1, source_target_pairs={{0,2},{1,3},{2,0},{3,1},{4,6},{5,7},{6,4},{7,5},{8,10},{9,11},{10,... | collective-permute-start | bytes 1179656 | tf_op jit(solution)/shard_map/ppermute | solution.py:500
  326.1 9.6 %collective-permute-start.62 = (bf16[208,384]{1,0:T(8,128)(2,1)S(1)}, bf16[208,384]{1,0:T(8,128)(2,1)S(1)}, u32[]{:S(2)}, u32[]{:S(2)}) collective-permute-start(bf16[208,384]{1,0:T(8,128)(2,1)S(1)} %constant_dynamic-slice_fusion), channel_id=1, source_target_pairs={{0,8},{4,12},{8,0},{12,4},{1,9},{5,13},{9,1},{13,5},{2,10},{6,14},... | collective-permute-start | bytes 479240 | tf_op jit(solution)/shard_map/ppermute | solution.py:548
  335.9 22.8 %collective-permute-start.72 = (bf16[416,768]{1,0:T(8,128)(2,1)S(1)}, bf16[416,768]{1,0:T(8,128)(2,1)S(1)}, u32[]{:S(2)}, u32[]{:S(2)}) collective-permute-start(bf16[416,768]{1,0:T(8,128)(2,1)S(1)} %pad_maximum_fusion.11), channel_id=1, source_target_pairs={{0,4},{4,0},{8,12},{12,8},{1,5},{5,1},{9,13},{13,9},{2,6},{6,2},{1... | collective-permute-start | bytes 1916936 | tf_op jit(solution)/shard_map/ppermute | solution.py:548
  336.0 19.8 %collective-permute-start.69 = (bf16[3,128,768]{2,1,0:T(8,128)(2,1)S(1)}, bf16[3,128,768]{2,1,0:T(8,128)(2,1)S(1)}, u32[]{:S(2)}, u32[]{:S(2)}) collective-permute-start(bf16[3,128,768]{2,1,0:T(8,128)(2,1)S(1)} %bitcast.213), channel_id=1, source_target_pairs={{0,2},{1,3},{2,0},{3,1},{4,6},{5,7},{6,4},{7,5},{8,10},{9,11},{10,... | collective-permute-start | bytes 1769480 | tf_op jit(solution)/shard_map/ppermute | solution.py:500
  336.9 18.9 %collective-permute-start.66 = (bf16[1,128,768]{2,1,0:T(8,128)(2,1)S(1)}, bf16[1,128,768]{2,1,0:T(8,128)(2,1)S(1)}, u32[]{:S(2)}, u32[]{:S(2)}) collective-permute-start(bf16[1,128,768]{2,1,0:T(8,128)(2,1)S(1)} %bitcast.217), channel_id=1, source_target_pairs={{0,2},{1,3},{2,0},{3,1},{4,6},{5,7},{6,4},{7,5},{8,10},{9,11},{10,... | collective-permute-start | bytes 589832 | tf_op jit(solution)/shard_map/ppermute | solution.py:500
  338.1 17.7 %collective-permute-start.67 = (bf16[208,384]{1,0:T(8,128)(2,1)S(1)}, bf16[208,384]{1,0:T(8,128)(2,1)S(1)}, u32[]{:S(2)}, u32[]{:S(2)}) collective-permute-start(bf16[208,384]{1,0:T(8,128)(2,1)S(1)} %add_convert_fusion.23), channel_id=1, source_target_pairs={{0,8},{4,12},{8,0},{12,4},{1,9},{5,13},{9,1},{13,5},{2,10},{6,14},... | collective-permute-start | bytes 479240 | tf_op jit(solution)/shard_map/ppermute | solution.py:548
  356.1 5.6 %collective-permute-start.71 = (bf16[2,3,128,768]{3,2,1,0:T(8,128)(2,1)S(1)}, bf16[2,3,128,768]{3,2,1,0:T(8,128)(2,1)S(1)}, u32[]{:S(2)}, u32[]{:S(2)}) collective-permute-start(bf16[2,3,128,768]{3,2,1,0:T(8,128)(2,1)S(1)} %pad_maximum_fusion.7), channel_id=1, source_target_pairs={{0,1},{1,0},{2,3},{3,2},{4,5},{5,4},{6,7},{7,6},{8,9},{9,8},{10,11... | collective-permute-start | bytes 3538952 | tf_op jit(solution)/shard_map/ppermute | solution.py:504
  356.7 9.6 %collective-permute-start.70 = (bf16[416,384]{1,0:T(8,128)(2,1)S(1)}, bf16[416,384]{1,0:T(8,128)(2,1)S(1)}, u32[]{:S(2)}, u32[]{:S(2)}) collective-permute-start(bf16[416,384]{1,0:T(8,128)(2,1)S(1)} %pad_maximum_fusion.21), channel_id=1, source_target_pairs={{0,4},{4,0},{8,12},{12,8},{1,5},{5,1},{9,13},{13,9},{2,6},{6,2},{1... | collective-permute-start | bytes 958472 | tf_op jit(solution)/shard_map/ppermute | solution.py:548
  (79 other events, 498.2 us)
